TPU v7x, 32 devices: a whole 2x2x4 slice. The times are simulated.
32 devices in a mesh: groups: 2 (over x), utt: 16 (over z, y, core).
Axes of the slice: x: 2, y: 2, z: 4, core: 2. Of those that a mesh axis runs over, the one named last changes fastest.
Arguments:
- waveforms: float32 [64, 90], P(('groups', 'utt')), parts along dimension 0, may hold values from -6 to 6
- lengths: int32 [64], P(('groups', 'utt')), parts along dimension 0, may hold values from 1 to 7, as said below
- take_list: int32 [64], P(('groups', 'utt')), parts along dimension 0, may hold values from 0 to 31, as said below
- conv_first: float32 [3, 10, 512], replicated, may hold values from -2 to 2
- conv_second: bfloat16 [3, 1536, 512], replicated, may hold values from -0.15625 to 0.15625
- norm_gain: float32 [3, 2, 512], replicated, may hold values from 0.5 to 1.5
- norm_shift: float32 [3, 2, 512], replicated, may hold values from -2 to 2
- enc_weight: bfloat16 [1536, 8192], P(None, 'utt'), may hold values from -0.15625 to 0.15625
- enc_bias: float32 [8192], P('utt'), may hold values from -2 to 2
- dec_weight: bfloat16 [8192, 1536], P('utt'), may hold values from -0.0625 to 0.0625
- dec_bias: float32 [1536], replicated, may hold values from -2 to 2
Outputs:
- enc_grad: bfloat16 [3072, 8192], P('groups', 'utt'), parts along dimension 0
- dec_grad: bfloat16 [16384, 1536], P(('groups', 'utt')), parts along dimension 0
- enc_bias_grad: float32 [16384], P(('groups', 'utt')), parts along dimension 0
- dec_bias_grad: float32 [3072], P('groups'), parts along dimension 0
- mean_loss: float32 [2], P('groups'), parts along dimension 0
- errors_out: bfloat16 [256, 1536], P(('groups', 'utt')), parts along dimension 0
There are 2 independent parts, one for each index of `groups`. A program takes and returns all parts, laid end to end along the dimension named above; an argument that names none is the same for every part. Nothing has to cross between parts.
Inputs may be any that keep to these rules, and one draw needn't show every extreme that they name: Valid frames of each utterance; the 32 lengths sum to 128, and some utterance has exactly 7. `take_list`: a permutation of the utterances: entry d * 2 + k names the utterance that slot k of device d takes; the utterances taken by the slots of one device have 8 valid frames together.
All inputs are finite; a program needn't handle non-finite values.
Results may differ from a plain program's by a relative error of at most 0.0095.
Values may be sent and summed in bfloat16 or wider, within the bound.
No kernel may reach another device: no remote copies, remote signals or barrier semaphores. Data moves between devices by JAX's collectives and lax.ppermute only.
A program may use at most 128 MiB of HBM per device.

v0:
```python
import jax
import jax.numpy as jnp
from jax import lax
from jax.sharding import PartitionSpec as P

ROWS_DEV = 8


sparsity = 0.5
epsilon = 1e-05


def normalize(values, gain, shift):
    center = values - jnp.mean(values, axis=-1, keepdims=True)
    spread = jnp.mean(center * center, axis=-1, keepdims=True)
    return center * lax.rsqrt(spread + epsilon) * gain + shift


def extract(chosen, conv_first, conv_second, norm_gain, norm_shift):
    count = chosen.shape[0]
    frames = (chosen.shape[1] - 10) // 10
    checkpoints = conv_first.shape[0]
    channels = conv_first.shape[2]
    blocks = chosen.reshape(count, 2 * frames + 2, 5)
    windows = jnp.concatenate([blocks[:, :-1], blocks[:, 1:]], axis=-1)
    first = jnp.einsum("ntk,ckd->cntd", windows, conv_first, precision=lax.Precision.HIGHEST)
    first = normalize(first, norm_gain[:, 0][:, None, None, :], norm_shift[:, 0][:, None, None, :])
    first = jax.nn.gelu(first, approximate=False).astype(jnp.bfloat16)
    paired = first[:, :, :-1].reshape(checkpoints, count, frames, 2 * channels)
    columns = jnp.concatenate([paired, first[:, :, 2::2]], axis=-1)
    second = jnp.einsum("cntk,ckd->cntd", columns, conv_second, preferred_element_type=jnp.float32)
    second = normalize(
        second, norm_gain[:, 1][:, None, None, :], norm_shift[:, 1][:, None, None, :]
    )
    second = jax.nn.gelu(second, approximate=False).astype(jnp.bfloat16)
    return second.transpose(1, 2, 0, 3).reshape(count, frames, checkpoints * channels)


def shards(
    waveforms,
    lengths,
    take_list,
    conv_first,
    conv_second,
    norm_gain,
    norm_shift,
    enc_weight,
    enc_bias,
    dec_weight,
    dec_bias,
):
    slots = take_list.shape[0]
    devices = lax.axis_size("utt")
    tokens = ROWS_DEV * devices
    position = lax.axis_index("utt")
    piece_sound = lax.all_gather(waveforms, "utt", axis=0, tiled=True)
    piece_length = lax.all_gather(lengths, "utt", axis=0, tiled=True)
    labels = jnp.arange(piece_sound.shape[0], dtype=jnp.int32)
    match = take_list[:, None] == labels[None, :]
    sound_sum = jnp.dot(match.astype(jnp.float32), piece_sound, precision=lax.Precision.HIGHEST)
    length_sum = jnp.sum(jnp.where(match, piece_length[None, :], 0), axis=1).astype(jnp.int32)
    frames = extract(sound_sum, conv_first, conv_second, norm_gain, norm_shift)
    frame_count = frames.shape[1]
    feature = frames.shape[2]
    flat_frames = frames.reshape(slots * frame_count, feature)
    local_start = jnp.cumsum(length_sum) - length_sum
    frame_index = jnp.arange(frame_count, dtype=jnp.int32)
    valid = frame_index[None, :] < length_sum[:, None]
    before = position * ROWS_DEV
    targets = jnp.where(valid, before + local_start[:, None] + frame_index[None, :], tokens)
    targets = targets.reshape(-1)
    all_frames, all_targets = (
        lax.all_gather(flat_frames, "utt", axis=0, tiled=True),
        lax.all_gather(targets, "utt", axis=0, tiled=True),
    )
    inputs = jnp.zeros((tokens + 1, feature), jnp.bfloat16).at[all_targets].set(all_frames)[:tokens]
    latents_dev = enc_weight.shape[1]
    checkpoints = conv_first.shape[0]
    channels = conv_first.shape[2]
    preact = jnp.dot(inputs, enc_weight, preferred_element_type=jnp.float32) + enc_bias
    latent = jnp.maximum(preact, 0.0)
    latent_b = latent.astype(jnp.bfloat16)
    decoder = dec_weight.astype(jnp.float32).reshape(latents_dev, checkpoints, channels)
    norms = jnp.sqrt(jnp.sum(decoder * decoder, axis=-1) + 1e-06)
    weights_sum = jnp.sum(norms, axis=-1)
    partial_recon = jnp.dot(latent_b, dec_weight, preferred_element_type=jnp.float32)
    recon = lax.psum(partial_recon, "utt")
    errors = recon + dec_bias - inputs.astype(jnp.float32)
    errors_b = errors.astype(jnp.bfloat16)
    own_errors = lax.dynamic_slice_in_dim(errors, position * ROWS_DEV, ROWS_DEV, 0)
    loss_part = jnp.sum(own_errors * own_errors) + sparsity * jnp.sum(latent * weights_sum)
    bias_part = jnp.sum(2.0 * own_errors, axis=0)
    dec_bias_grad, loss_total = lax.psum((bias_part, loss_part), "utt")
    mean_loss = (loss_total / (tokens * feature)).reshape(1)
    activity = jnp.sum(latent, axis=0)
    dec_grad = 2.0 * jnp.dot(latent_b.T, errors_b, preferred_element_type=jnp.float32)
    dec_grad = dec_grad + sparsity * (
        activity[:, None, None] * decoder / norms[:, :, None]
    ).reshape(latents_dev, feature)
    upstream = (
        2.0 * jnp.dot(errors_b, dec_weight.T, preferred_element_type=jnp.float32)
        + sparsity * weights_sum
    )
    through = jnp.where(preact > 0.0, upstream, 0.0)
    enc_grad = jnp.dot(inputs.T, through.astype(jnp.bfloat16), preferred_element_type=jnp.float32)
    return (
        enc_grad.astype(jnp.bfloat16),
        dec_grad.astype(jnp.bfloat16),
        jnp.sum(through, axis=0),
        dec_bias_grad,
        mean_loss,
        own_errors.astype(jnp.bfloat16),
    )


def solution(mesh):
    return jax.shard_map(
        shards,
        mesh=mesh,
        in_specs=(
            P(("groups", "utt"), None),
            P(("groups", "utt")),
            P(("groups", "utt")),
            P(),
            P(),
            P(),
            P(),
            P(None, "utt"),
            P("utt"),
            P("utt", None),
            P(),
        ),
        out_specs=(
            P("groups", "utt"),
            P(("groups", "utt"), None),
            P(("groups", "utt")),
            P("groups"),
            P("groups"),
            P(("groups", "utt"), None),
        ),
        check_vma=False,
    )
```

profile of v0, /device:TPU:0, one launch (start us, length us, event | category | flops | bytes accessed | tf_op | source)
XLA Modules:
  0.0 240.3 jit_solution(2240350737570929996)
XLA Ops:
  7.2 23.5 %all-gather = f32[16,2,90]{2,1,0:T(2,128)S(1)} all-gather(f32[1,2,90]{2,1,0:T(2,128)} %bitcast.74), channel_id=1, replica_groups=mesh['groups'=2,'utt'=16] {'utt'}, dimensions={0}, use_global_device_ids=true | all-gather | bytes 12240 | tf_op jit(solution)/shard_map/all_gather | solution.py:56
  30.7 0.8 fusion.44
  31.8 1.4 fusion.55
  33.5 0.8 fusion.54
  34.3 0.8 fusion.53
  35.1 0.8 fusion.12
  36.1 3.3 %fusion.56 = (f32[3,2,8]{2,1,0:T(2,128)S(1)}, f32[3,2,8,512]{3,2,1,0:T(8,128)S(1)}) fusion(bf16[3,1536,512]{2,1,0:T(8,128)(2,1)} %param.15, bf16[3,2,8,512]{3,2,0,1:T(8,128)(2,1)S(1)} %slice.32, bf16[3,2,8,1024]{3,2,0,1:T(8,128)(2,1)S(1)} %reshape.107), kind=kOutput, calls=%fused_computation.111 | convolution fusion | flops 75816912 | bytes 4964544 | tf_op jit(solution)/shard_map/cntk,ckd->cntd/dot_general | solution.py:31
  40.0 21.0 %all_gather.15 = bf16[256,1536]{1,0:T(8,128)(2,1)} all-gather(bf16[16,1536]{1,0:T(8,128)(2,1)S(1)} %bitcast.71), channel_id=1, replica_groups=mesh['groups'=2,'utt'=16] {'utt'}, dimensions={0}, use_global_device_ids=true | all-gather | bytes 835584 | tf_op jit(solution)/shard_map/all_gather | solution.py:73
  62.5 9.6 %all-reduce = s32[32]{0:T(128)S(1)} all-reduce(s32[32]{0:T(128)S(1)} %dynamic-update-slice), channel_id=1, replica_groups=mesh['groups'=2,'utt'=16] {'utt'}, use_global_device_ids=true, to_apply=%add | all-reduce | flops 32 | bytes 256
  73.5 11.2 %all-reduce.1 = s32[256]{0:T(256)S(1)} all-reduce(s32[256]{0:T(256)S(1)} %dynamic-update-slice.1), channel_id=1, replica_groups=mesh['groups'=2,'utt'=16] {'utt'}, use_global_device_ids=true, to_apply=%add.1 | all-reduce | flops 256 | bytes 2048
  84.8 2.1 convert_multiply_fusion.1
  86.9 3.6 %copy.44 = f32[512,1536]{0,1:T(8,128)} copy(f32[512,1536]{1,0:T(8,128)} %convert_multiply_fusion.1) | data formatting | bytes 6291456 | tf_op jit(solution)/shard_map/mul | solution.py:84
  90.5 2.1 reduce_sum.113
  92.6 3.1 %scatter_custom_fusion = bf16[129,1536]{1,0:T(8,128)(2,1)} fusion(s32[256]{0:T(256)S(1)} %compare_select_fusion, bf16[256,1536]{1,0:T(8,128)(2,1)} %all_gather.15, bf16[]{:T(256)} %constant.40.clone.1), kind=kCustom, calls=%fused_computation.43 | custom fusion | bytes 396800 | tf_op jit(solution)/shard_map/scatter | solution.py:76
  95.7 2.0 multiply_reduce_fusion.1
  97.7 1.3 fusion.41
  99.0 2.1 div.33
  101.1 3.6 %copy.45 = f32[512,1536]{1,0:T(8,128)} copy(f32[512,1536]{0,1:T(8,128)} %bitcast.70) | data formatting | bytes 6291456 | tf_op jit(solution)/shard_map/div | solution.py:98
  105.4 83.7 %all-reduce.5.cloned.1.call-done = f32[128,1536]{1,0:T(8,128)} async-done(((f32[128,1536]{1,0:T(8,128)}), f32[128,1536]{1,0:T(8,128)}) %all-reduce.5.cloned.1.call-update) | async-done | bytes 786448 | tf_op jit(solution)/shard_map/psum | solution.py:87
  189.1 1.4 convert_subtract_fusion
  191.9 1.3 fusion.57
  193.1 1.7 convolution_convert_fusion
  195.5 31.9 %all-reduce.2 = (f32[1536]{0:T(1024)}, f32[]{:T(128)}) all-reduce(f32[1536]{0:T(1024)S(1)} %get-tuple-element.7, f32[]{:T(128)S(6)} %add.150), channel_id=1, replica_groups=mesh['groups'=2,'utt'=16] {'utt'}, use_global_device_ids=true, to_apply=%region_13.14 | all-reduce | flops 1537 | bytes 12296 | tf_op jit(solution)/shard_map/psum | solution.py:93
  228.1 4.2 %fusion.5 = bf16[512,1536]{1,0:T(8,128)(2,1)} fusion(f32[512,1536]{1,0:T(8,128)} %copy.45, bf16[512,1536]{1,0:T(8,128)(2,1)S(1)} %copy-done.1, f32[512]{0:T(512)S(1)} %get-tuple-element.9, f32[128,1536]{1,0:T(8,128)} %copy-done.3, f32[128,512]{1,0:T(8,128)S(1)} %get-tuple-element.26), kind=kOutput, calls=%fused_computation.9 | convolution fusion | flops 207159296 | bytes 7342080 | tf_op jit(solution)/shard_map/dot_general | solution.py:96
  (53 shorter events, 4.3 us)
Async XLA Ops:
  7.2 88.5 %copy-start = (bf16[1536,512]{1,0:T(8,128)(2,1)S(1)}, bf16[1536,512]{1,0:T(8,128)(2,1)}, u32[]{:S(2)}) copy-start(bf16[1536,512]{1,0:T(8,128)(2,1)} %param.18) | copy-start | bytes 4718596
  7.2 181.9 %all-reduce.5.cloned.1.call-start = ((), (), s32[]{:S(2)}) async-start(), calls=%async_computation | async-start | bytes 1572864 | tf_op jit(solution)/shard_map/psum | solution.py:87
  36.1 24.9 %copy-start.8 = (u32[32]{0:T(128)S(1)}, u32[32]{0:T(128)}, u32[]{:S(2)}) copy-start(u32[32]{0:T(128)} %constant.13) | copy-start | bytes 388
  36.1 26.1 %copy-start.6 = (s32[2]{0:T(128)S(1)}, s32[2]{0:T(128)}, u32[]{:S(2)}) copy-start(s32[2]{0:T(128)} %param.12) | copy-start | bytes 28
  36.1 36.0 %copy-start.7 = (s32[2]{0:T(128)S(1)}, s32[2]{0:T(128)}, u32[]{:S(2)}) copy-start(s32[2]{0:T(128)} %param.13) | copy-start | bytes 28
  36.1 48.7 %copy-start.1 = (bf16[512,1536]{1,0:T(8,128)(2,1)S(1)}, bf16[512,1536]{1,0:T(8,128)(2,1)}, u32[]{:S(2)}) copy-start(bf16[512,1536]{1,0:T(8,128)(2,1)} %param.20) | copy-start | bytes 4718596
  90.5 5.3 %copy-start.5 = (f32[512]{0:T(512)S(1)}, f32[512]{0:T(512)}, u32[]{:S(2)}) copy-start(f32[512]{0:T(512)} %param.19) | copy-start | bytes 6148
  101.1 88.0 %copy-start.4 = (f32[1536]{0:T(1024)S(1)}, f32[1536]{0:T(1024)}, u32[]{:S(2)}) copy-start(f32[1536]{0:T(1024)} %param.21) | copy-start | bytes 18436
  189.1 4.0 %copy-start.2 = (bf16[129,1536]{1,0:T(8,128)(2,1)S(1)}, bf16[129,1536]{1,0:T(8,128)(2,1)}, u32[]{:S(2)}) copy-start(bf16[129,1536]{1,0:T(8,128)(2,1)} %scatter_custom_fusion) | copy-start | bytes 1188868
  190.5 4.4 %copy-start.3 = (f32[128,1536]{1,0:T(8,128)}, f32[128,1536]{1,0:T(8,128)S(1)}, u32[]{:S(2)}) copy-start(f32[128,1536]{1,0:T(8,128)S(1)} %convert_subtract_fusion) | copy-start | bytes 2359300
Sparse Core Ops, SparseCore 0:
  99.1 89.9 all-reduce.4
where the time goes:
time: 241 us; the launch traced here: 240 us
  blocking collectives  97.2 us (40%)
  waiting for transfers between devices  83.8 us (35%)
  between operations  18.7 us (8%)
  local copies, waits for them, and re-layouts  16.3 us (7%)
  matrix products  16 us (7%)
  other arithmetic  8.29 us (3%)
    psum x1, waiting for transfers between devices, shards(): recon = lax.psum(partial_recon, 'utt')  83.7 us
    psum x1, blocking collectives, shards(): dec_bias_grad, loss_total = lax.psum((bias_part, loss_part), 'utt')  31.9 us
    all_gather x1, blocking collectives, shards(): piece_sound = lax.all_gather(waveforms, 'utt', axis=0, tiled=True)  23.5 us
    all_gather x1, blocking collectives, shards(): lax.all_gather(flat_frames, 'utt', axis=0, tiled=True)  21 us
    unnamed x2, blocking collectives  20.8 us
    div x2, local copies, waits for them, and re-layouts, shards(): activity[:, None, None] * decoder / norms[:, :, None]  5.7 us
  transfers between devices with their start and end apart: 1, of which 1 were waited for; matrix products, arithmetic and copies ran while one was open for 2% of the time, Pallas kernels for 0%

commit v1 on v0

--- a/solution.py
+++ b/solution.py
@@ -4,7 +4,7 @@
 from jax.sharding import PartitionSpec as P
 
 ROWS_DEV = 8
-
+EXTRA = 128
 
 sparsity = 0.5
 epsilon = 1e-05
@@ -36,6 +36,35 @@
     return second.transpose(1, 2, 0, 3).reshape(count, frames, checkpoints * channels)
 
 
+def levels(devices):
+    chips = devices // 2
+    outer = 1
+    while outer * outer < chips:
+        outer *= 2
+    return outer, chips // outer
+
+
+def exchange(value, bit):
+    devices = lax.axis_size("utt")
+    return lax.ppermute(value, "utt", [(i, i ^ bit) for i in range(devices)])
+
+
+def tree(parts):
+    while len(parts) > 1:
+        parts = [parts[i] + parts[i + 1] for i in range(0, len(parts), 2)]
+    return parts[0]
+
+
+def gather_frames(own, outer, inner):
+    step = 2 * inner
+    held = jnp.concatenate([own] + [exchange(own, step * k) for k in range(1, outer)], axis=0)
+    bit = 2
+    while bit < step:
+        held = jnp.concatenate([held, exchange(held, bit)], axis=0)
+        bit *= 2
+    return jnp.concatenate([held, exchange(held, 1)], axis=0)
+
+
 def shards(
     waveforms,
     lengths,
@@ -51,47 +80,97 @@
 ):
     slots = take_list.shape[0]
     devices = lax.axis_size("utt")
+    outer, inner = levels(devices)
+    step = 2 * inner
     tokens = ROWS_DEV * devices
     position = lax.axis_index("utt")
-    piece_sound = lax.all_gather(waveforms, "utt", axis=0, tiled=True)
-    piece_length = lax.all_gather(lengths, "utt", axis=0, tiled=True)
-    labels = jnp.arange(piece_sound.shape[0], dtype=jnp.int32)
-    match = take_list[:, None] == labels[None, :]
-    sound_sum = jnp.dot(match.astype(jnp.float32), piece_sound, precision=lax.Precision.HIGHEST)
-    length_sum = jnp.sum(jnp.where(match, piece_length[None, :], 0), axis=1).astype(jnp.int32)
-    frames = extract(sound_sum, conv_first, conv_second, norm_gain, norm_shift)
-    frame_count = frames.shape[1]
-    feature = frames.shape[2]
-    flat_frames = frames.reshape(slots * frame_count, feature)
-    local_start = jnp.cumsum(length_sum) - length_sum
-    frame_index = jnp.arange(frame_count, dtype=jnp.int32)
-    valid = frame_index[None, :] < length_sum[:, None]
-    before = position * ROWS_DEV
-    targets = jnp.where(valid, before + local_start[:, None] + frame_index[None, :], tokens)
-    targets = targets.reshape(-1)
-    all_frames, all_targets = (
-        lax.all_gather(flat_frames, "utt", axis=0, tiled=True),
-        lax.all_gather(targets, "utt", axis=0, tiled=True),
-    )
-    inputs = jnp.zeros((tokens + 1, feature), jnp.bfloat16).at[all_targets].set(all_frames)[:tokens]
     latents_dev = enc_weight.shape[1]
     checkpoints = conv_first.shape[0]
     channels = conv_first.shape[2]
+
+    frames = extract(waveforms, conv_first, conv_second, norm_gain, norm_shift)
+    frame_count = frames.shape[1]
+    feature = frames.shape[2]
+    lane = lax.broadcasted_iota(jnp.int32, (slots, frame_count, feature), 2)
+    row = lax.broadcasted_iota(jnp.int32, (slots, frame_count, feature), 1)
+    notes = jnp.where(lane == 0, lengths[:, None, None], take_list[:, None, None])
+    packed = jnp.where(row == frame_count - 1, notes.astype(jnp.bfloat16), frames)
+    every = gather_frames(packed.reshape(slots * frame_count, feature), outer, inner)
+
+    place = jnp.arange(devices, dtype=jnp.int32)
+    core_rel = place // (devices // 2)
+    inner_rel = (place // outer) % inner
+    outer_rel = place % outer
+    owner = position ^ (outer_rel * step + inner_rel * 2 + core_rel)
+    notes = every.reshape(devices, slots, frame_count, feature)[:, :, frame_count - 1, :2]
+    notes = notes.astype(jnp.float32).astype(jnp.int32)
+    size_of = notes[:, :, 0].reshape(-1)
+    takes = notes[:, :, 1].reshape(-1)
+    kinds = jnp.arange(slots, dtype=jnp.int32)
+    label = (owner[:, None] * slots + kinds[None, :]).reshape(-1)
+    match = takes[:, None] == label[None, :]
+    device_start = jnp.sum(jnp.where(match, ROWS_DEV * (label // slots)[:, None], 0), axis=0)
+    second_slot = jnp.sum(jnp.where(match, (label % slots)[:, None], 0), axis=0)
+    begin = device_start + second_slot * (ROWS_DEV - size_of)
+    frame_index = jnp.arange(frame_count, dtype=jnp.int32)
+    target = jnp.where(frame_index[None, :] < size_of[:, None], begin[:, None] + frame_index[None, :], -1)
+    target = target.reshape(-1)
+
+    core_of = place // (devices // 2)
+    outer_of = (place // inner) % outer
+    inner_of = place % inner
+    holder = position ^ (outer_of * step + inner_of * 2 + core_of)
+    token = (holder[:, None] * ROWS_DEV + jnp.arange(ROWS_DEV, dtype=jnp.int32)[None, :]).reshape(-1)
+    pick = (token[:, None] == target[None, :]).astype(jnp.bfloat16)
+    inputs = jnp.dot(pick, every, preferred_element_type=jnp.float32).astype(jnp.bfloat16)
+
     preact = jnp.dot(inputs, enc_weight, preferred_element_type=jnp.float32) + enc_bias
     latent = jnp.maximum(preact, 0.0)
     latent_b = latent.astype(jnp.bfloat16)
     decoder = dec_weight.astype(jnp.float32).reshape(latents_dev, checkpoints, channels)
     norms = jnp.sqrt(jnp.sum(decoder * decoder, axis=-1) + 1e-06)
     weights_sum = jnp.sum(norms, axis=-1)
-    partial_recon = jnp.dot(latent_b, dec_weight, preferred_element_type=jnp.float32)
-    recon = lax.psum(partial_recon, "utt")
-    errors = recon + dec_bias - inputs.astype(jnp.float32)
-    errors_b = errors.astype(jnp.bfloat16)
-    own_errors = lax.dynamic_slice_in_dim(errors, position * ROWS_DEV, ROWS_DEV, 0)
-    loss_part = jnp.sum(own_errors * own_errors) + sparsity * jnp.sum(latent * weights_sum)
-    bias_part = jnp.sum(2.0 * own_errors, axis=0)
-    dec_bias_grad, loss_total = lax.psum((bias_part, loss_part), "utt")
+    part = jnp.dot(latent_b, dec_weight, preferred_element_type=jnp.float32)
+    weight_part = jnp.sum(latent * weights_sum, axis=1, keepdims=True)
+    part = jnp.concatenate([part, jnp.broadcast_to(weight_part, (tokens, EXTRA))], axis=1)
+
+    half = tokens // 2
+    part = part[:half] + exchange(part[half:], 1)
+    chunk = half // outer
+    small = part.astype(jnp.bfloat16)
+    pieces = [part[:chunk]]
+    for k in range(1, outer):
+        pieces.append(exchange(small[k * chunk : (k + 1) * chunk], step * k).astype(jnp.float32))
+    part = sum(pieces[1:], pieces[0])
+    rows = chunk // inner
+    bit = 2
+    while bit < step:
+        other = exchange(part, bit)
+        width = (bit // 2) * rows
+        other = other.reshape(-1, 2, width, feature + EXTRA)[:, ::-1].reshape(chunk, feature + EXTRA)
+        part = part + other
+        bit *= 2
+    errors = part[:, :feature] + dec_bias - inputs[:chunk].astype(jnp.float32)
+    coarse = part[:, feature:].astype(jnp.bfloat16)
+    fine = (part[:, feature:] - coarse.astype(jnp.float32)).astype(jnp.bfloat16)
+    spot = lax.broadcasted_iota(jnp.int32, (chunk, EXTRA), 1)
+    payload = jnp.concatenate([errors.astype(jnp.bfloat16), jnp.where(spot == 0, coarse, fine)], axis=1)
+    held = jnp.concatenate([payload] + [exchange(payload, step * k) for k in range(1, outer)], axis=0)
+    held = jnp.concatenate([held, exchange(held, 1)], axis=0)
+    errors_b = held[:, :feature]
+
+    wide = errors_b.astype(jnp.float32).reshape(devices, ROWS_DEV, feature)
+    extra = held[:, feature:].astype(jnp.float32).reshape(devices, ROWS_DEV, EXTRA)
+    totals = jnp.sum(wide, axis=1)
+    squares = jnp.sum(wide * wide, axis=1)
+    extras = jnp.sum(extra, axis=1)
+    totals = tree([totals[i] for i in range(devices)])
+    squares = tree([squares[i] for i in range(devices)])
+    extras = tree([extras[i] for i in range(devices)])
+    dec_bias_grad = 2.0 * totals
+    loss_total = jnp.sum(squares) + sparsity * (extras[0] + extras[1])
     mean_loss = (loss_total / (tokens * feature)).reshape(1)
+
     activity = jnp.sum(latent, axis=0)
     dec_grad = 2.0 * jnp.dot(latent_b.T, errors_b, preferred_element_type=jnp.float32)
     dec_grad = dec_grad + sparsity * (
@@ -109,7 +188,7 @@
         jnp.sum(through, axis=0),
         dec_bias_grad,
         mean_loss,
-        own_errors.astype(jnp.bfloat16),
+        errors_b[:ROWS_DEV],
     )
 
 

time: 241 us -> 93.4 us (0.39)
  blocking collectives: 97.2 us -> 0 us
  waiting for transfers between devices: 83.8 us -> 14.8 us
  starting transfers between devices: 0.04 us -> 18.1 us
  between operations: 18.7 us -> 4.08 us
  local copies, waits for them, and re-layouts: 16.3 us -> 26.4 us
  other arithmetic: 8.29 us -> 12.7 us
    psum x1 -> x0, waiting for transfers between devices: 83.7 us -> none  [shards(): recon = lax.psum(partial_recon, 'utt')]
    all_gather x2 -> x0, blocking collectives: 44.5 us -> none  [the longest x1 23.5 us: shards(): piece_sound = lax.all_gather(waveforms, 'utt', axis=0, tiled=True)]
    psum x1 -> x0, blocking collectives: 31.9 us -> none  [shards(): dec_bias_grad, loss_total = lax.psum((bias_part, loss_part), 'utt')]
    unnamed x2 -> x0, blocking collectives: 20.8 us -> none
    ppermute x0 -> x14, starting transfers between devices: none -> 18.1 us  [exchange(): return lax.ppermute(value, 'utt', [(i, i ^ bit) for i in range(devices)])]
    ppermute x0 -> x14, waiting for transfers between devices: none -> 14.8 us  [exchange(): return lax.ppermute(value, 'utt', [(i, i ^ bit) for i in range(devices)])]
    unnamed x28 -> x31, local copies, waits for them, and re-layouts: 1.34 us -> 7.81 us
    scatter x1 -> x0, local copies, waits for them, and re-layouts: 3.08 us -> none  [shards(): jnp.zeros((tokens + 1, feature), jnp.bfloat16).at[all_targets]]
  transfers between devices with their start and end apart: 1 -> 14, of which waited for: 1 -> 6; matrix products, arithmetic and copies ran while one was open for 2% -> 25% of each run, Pallas kernels for 0% -> 0%
where the time goes in v1:
time: 93.4 us; the launch traced here: 92.5 us
  local copies, waits for them, and re-layouts  26.4 us (28%)
  starting transfers between devices  18.1 us (19%)
  matrix products  16.5 us (18%)
  waiting for transfers between devices  14.8 us (16%)
  other arithmetic  12.7 us (14%)
  between operations  4.08 us (4%)
    ppermute x14, starting transfers between devices, exchange(): return lax.ppermute(value, 'utt', [(i, i ^ bit) for i in range(devices)])  18.1 us
    ppermute x14, waiting for transfers between devices, exchange(): return lax.ppermute(value, 'utt', [(i, i ^ bit) for i in range(devices)])  14.8 us
    unnamed x31, local copies, waits for them, and re-layouts  7.81 us
    div x2, local copies, waits for them, and re-layouts, shards(): activity[:, None, None] * decoder / norms[:, :, None]  5.65 us
    dot_general x1, matrix products, shards(): jnp.dot(latent_b.T, errors_b, preferred_element_type=jnp.float32)  4.16 us
    mul x1, local copies, waits for them, and re-layouts, shards(): norms = jnp.sqrt(jnp.sum(decoder * decoder, axis=-1) + 1e-06)  3.58 us
    dot_general x1, matrix products, extract(): jnp.einsum('cntk,ckd->cntd', columns, conv_second, preferred_element_type...  3.26 us
    dot_general x1, matrix products, shards(): jnp.dot(errors_b, dec_weight.T, preferred_element_type=jnp.float32)  2.31 us
  transfers between devices with their start and end apart: 14, of which 6 were waited for; matrix products, arithmetic and copies ran while one was open for 25% of the time, Pallas kernels for 0%

profile of v1, /device:TPU:0, one launch (start us, length us, event | category | flops | bytes accessed | tf_op | source)
XLA Modules:
  0.0 92.5 jit_solution(7710528053459826641)
XLA Ops:
  6.0 3.3 %fusion.100 = (f32[3,2,8]{2,1,0:T(2,128)S(1)}, f32[3,2,8,512]{3,2,1,0:T(8,128)S(1)}) fusion(bf16[3,1536,512]{2,1,0:T(8,128)(2,1)} %param.15, bf16[3,2,8,512]{3,2,0,1:T(8,128)(2,1)S(1)} %slice.234, bf16[3,2,8,1024]{3,2,0,1:T(8,128)(2,1)S(1)} %reshape.349), kind=kOutput, calls=%fused_computation.238 | convolution fusion | flops 75816912 | bytes 4964544 | tf_op jit(solution)/shard_map/cntk,ckd->cntd/dot_general | solution.py:31
  11.0 3.0 %collective-permute-start = (bf16[16,1536]{1,0:T(8,128)(2,1)S(1)}, bf16[16,1536]{1,0:T(8,128)(2,1)S(1)}, u32[]{:S(2)}, u32[]{:S(2)}) collective-permute-start(bf16[16,1536]{1,0:T(8,128)(2,1)S(1)} %get-tuple-element.15), channel_id=1, source_target_pairs={{0,4},{1,5},{2,6},{3,7},{4,0},{5,1},{6,2},{7,3},{8,12},{9,13},{10,... | collective-permute-start | bytes 147464 | tf_op jit(solution)/shard_map/ppermute | solution.py:49
  14.0 2.6 %collective-permute-start.1 = (bf16[16,1536]{1,0:T(8,128)(2,1)S(1)}, bf16[16,1536]{1,0:T(8,128)(2,1)S(1)}, u32[]{:S(2)}, u32[]{:S(2)}) collective-permute-start(bf16[16,1536]{1,0:T(8,128)(2,1)S(1)} %get-tuple-element.15), channel_id=1, source_target_pairs={{0,8},{1,9},{2,10},{3,11},{4,12},{5,13},{6,14},{7,15},{8,0},{9,1},... | collective-permute-start | bytes 147464 | tf_op jit(solution)/shard_map/ppermute | solution.py:49
  17.3 2.1 %convert_multiply_fusion.1 = f32[512,1536]{1,0:T(8,128)} fusion(bf16[512,1536]{1,0:T(8,128)(2,1)S(1)} %copy-done.1), kind=kLoop, calls=%fused_computation.3 | loop fusion | flops 1572864 | bytes 4718592 | tf_op jit(solution)/shard_map/mul | solution.py:131
  20.2 3.6 %copy.53 = f32[512,1536]{0,1:T(8,128)} copy(f32[512,1536]{1,0:T(8,128)} %convert_multiply_fusion.1) | data formatting | bytes 6291456 | tf_op jit(solution)/shard_map/mul | solution.py:131
  23.8 2.1 %reduce_sum.141 = f32[512,3]{0,1:T(4,128)S(1)} reduce(f32[512,3,512]{0,2,1:T(8,128)} %bitcast.82, f32[]{:T(128)} %constant.90.clone.1), dimensions={2}, to_apply=%region_6.7 | reduce | flops 784896 | bytes 3151876 | tf_op jit(solution)/shard_map/reduce_sum | solution.py:131
  25.9 1.8 %collective-permute-start.3 = (bf16[64,1536]{1,0:T(8,128)(2,1)S(1)}, bf16[64,1536]{1,0:T(8,128)(2,1)S(1)}, u32[]{:S(2)}, u32[]{:S(2)}) collective-permute-start(bf16[64,1536]{1,0:T(8,128)(2,1)S(1)} %pad_maximum_fusion.2), channel_id=1, source_target_pairs={{0,2},{1,3},{2,0},{3,1},{4,6},{5,7},{6,4},{7,5},{8,10},{9,11},{10,... | collective-permute-start | bytes 589832 | tf_op jit(solution)/shard_map/ppermute | solution.py:49
  29.7 2.4 %collective-permute-done.3 = bf16[64,1536]{1,0:T(8,128)(2,1)S(1)} collective-permute-done((bf16[64,1536]{1,0:T(8,128)(2,1)S(1)}, bf16[64,1536]{1,0:T(8,128)(2,1)S(1)}, u32[]{:S(2)}, u32[]{:S(2)}) %collective-permute-start.3) | collective-permute-done | bytes 196640 | tf_op jit(solution)/shard_map/ppermute | solution.py:49
  32.9 1.9 %collective-permute-done.4 = bf16[128,1536]{1,0:T(8,128)(2,1)S(1)} collective-permute-done((bf16[128,1536]{1,0:T(8,128)(2,1)}, bf16[128,1536]{1,0:T(8,128)(2,1)S(1)}, u32[]{:S(2)}, u32[]{:S(2)}) %collective-permute-start.4) | collective-permute-done | bytes 393248 | tf_op jit(solution)/shard_map/ppermute | solution.py:49
  37.2 1.5 %convolution_convert_fusion.1 = bf16[128,1536]{1,0:T(8,128)(2,1)S(1)} fusion(bf16[256,1536]{1,0:T(8,128)(2,1)} %constant_dynamic-update-slice_fusion.5, s32[256]{0:T(256)S(1)} %select_n.133, s32[128]{0:T(128)} %add.459), kind=kOutput, calls=%fused_computation.10 | convolution fusion | flops 100892672 | bytes 1181184 | tf_op jit(solution)/shard_map/dot_general | solution.py:125
  38.7 1.7 %maximum_reduce_fusion = (f32[512]{0:T(512)}, f32[128]{0:T(128)S(1)}, f32[128,512]{1,0:T(8,128)S(1)}) fusion(f32[512]{0:T(512)S(1)} %get-tuple-element.36, f32[512]{0:T(512)} %param.19, bf16[128,1536]{1,0:T(8,128)(2,1)S(1)} %convolution_convert_fusion.1, bf16[1536,512]{1,0:T(8,128)(2,1)S(1)} %copy-done), kind=kOutput, calls=%fused_computation.48 | convolution fusion | flops 201653632 | bytes 2234880 | tf_op jit(solution)/shard_map/dot_general | solution.py:127
  41.1 1.6 %collective-permute-done.5 = f32[64,1664]{1,0:T(8,128)S(1)} collective-permute-done((f32[64,1664]{1,0:T(8,128)S(1)}, f32[64,1664]{1,0:T(8,128)S(1)}, u32[]{:S(2)}, u32[]{:S(2)}) %collective-permute-start.5) | collective-permute-done | bytes 426016 | tf_op jit(solution)/shard_map/ppermute | solution.py:49
  43.5 3.5 %collective-permute-start.7 = (bf16[16,1664]{1,0:T(8,128)(2,1)S(1)}, bf16[16,1664]{1,0:T(8,128)(2,1)S(1)}, u32[]{:S(2)}, u32[]{:S(2)}) collective-permute-start(bf16[16,1664]{1,0:T(8,128)(2,1)S(1)} %get-tuple-element.18), channel_id=1, source_target_pairs={{0,8},{1,9},{2,10},{3,11},{4,12},{5,13},{6,14},{7,15},{8,0},{9,1},... | collective-permute-start | bytes 159752 | tf_op jit(solution)/shard_map/ppermute | solution.py:49
  47.3 3.1 %collective-permute-done.7 = bf16[16,1664]{1,0:T(8,128)(2,1)S(1)} collective-permute-done((bf16[16,1664]{1,0:T(8,128)(2,1)S(1)}, bf16[16,1664]{1,0:T(8,128)(2,1)S(1)}, u32[]{:S(2)}, u32[]{:S(2)}) %collective-permute-start.7) | collective-permute-done | bytes 53280 | tf_op jit(solution)/shard_map/ppermute | solution.py:49
  50.4 2.5 %collective-permute-done.8 = bf16[16,1664]{1,0:T(8,128)(2,1)S(1)} collective-permute-done((bf16[16,1664]{1,0:T(8,128)(2,1)S(1)}, bf16[16,1664]{1,0:T(8,128)(2,1)S(1)}, u32[]{:S(2)}, u32[]{:S(2)}) %collective-permute-start.8) | collective-permute-done | bytes 53280 | tf_op jit(solution)/shard_map/ppermute | solution.py:49
  52.9 1.6 %collective-permute-start.9 = (f32[16,1664]{1,0:T(8,128)S(1)}, f32[16,1664]{1,0:T(8,128)S(1)}, u32[]{:S(2)}, u32[]{:S(2)}) collective-permute-start(f32[16,1664]{1,0:T(8,128)S(1)} %fusion.27), channel_id=1, source_target_pairs={{0,2},{1,3},{2,0},{3,1},{4,6},{5,7},{6,4},{7,5},{8,10},{9,11},{10,... | collective-permute-start | bytes 319496 | tf_op jit(solution)/shard_map/ppermute | solution.py:49
  54.5 3.2 %collective-permute-done.9 = f32[16,1664]{1,0:T(8,128)S(1)} collective-permute-done((f32[16,1664]{1,0:T(8,128)S(1)}, f32[16,1664]{1,0:T(8,128)S(1)}, u32[]{:S(2)}, u32[]{:S(2)}) %collective-permute-start.9) | collective-permute-done | bytes 106528 | tf_op jit(solution)/shard_map/ppermute | solution.py:49
  59.0 1.8 %collective-permute-start.11 = (bf16[16,1664]{1,0:T(8,128)(2,1)}, bf16[16,1664]{1,0:T(8,128)(2,1)}, u32[]{:S(2)}, u32[]{:S(2)}) collective-permute-start(bf16[16,1664]{1,0:T(8,128)(2,1)} %get-tuple-element.21), channel_id=1, source_target_pairs={{0,8},{1,9},{2,10},{3,11},{4,12},{5,13},{6,14},{7,15},{8,0},{9,1},... | collective-permute-start | bytes 159752 | tf_op jit(solution)/shard_map/ppermute | solution.py:49
  60.8 2.6 %collective-permute-start.12 = (bf16[16,1664]{1,0:T(8,128)(2,1)}, bf16[16,1664]{1,0:T(8,128)(2,1)}, u32[]{:S(2)}, u32[]{:S(2)}) collective-permute-start(bf16[16,1664]{1,0:T(8,128)(2,1)} %get-tuple-element.21), channel_id=1, source_target_pairs={{0,12},{1,13},{2,14},{3,15},{4,8},{5,9},{6,10},{7,11},{8,4},{9,5},... | collective-permute-start | bytes 159752 | tf_op jit(solution)/shard_map/ppermute | solution.py:49
  64.0 2.1 %div.67 = f32[512,3,512]{0,2,1:T(8,128)} broadcast(f32[512,3]{0,1:T(4,128)S(1)} %get-tuple-element.35), dimensions={0,1} | broadcast | bytes 3151872 | tf_op jit(solution)/shard_map/div | solution.py:177
  66.1 3.6 %copy.54 = f32[512,1536]{1,0:T(8,128)} copy(f32[512,1536]{0,1:T(8,128)} %bitcast.83) | data formatting | bytes 6291456 | tf_op jit(solution)/shard_map/div | solution.py:177
  80.5 2.3 %fusion.101 = (f32[512]{0:T(512)}, bf16[128,512]{1,0:T(8,128)(2,1)S(1)}) fusion(f32[512]{0:T(512)S(1)} %copy-done.4, bf16[512,1536]{1,0:T(8,128)(2,1)S(1)} %copy-done.1, bf16[128,1664]{1,0:T(8,128)(2,1)} %constant_dynamic-update-slice_fusion.11, f32[128,512]{1,0:T(8,128)} %copy-done.2), kind=kOutput, calls=%fused_computation.239 | convolution fusion | flops 201719296 | bytes 2363392 | tf_op jit(solution)/shard_map/dot_general | solution.py:180
  82.8 1.7 %convolution_convert_fusion = bf16[1536,512]{1,0:T(8,128)(2,1)} fusion(bf16[128,1536]{1,0:T(8,128)(2,1)S(1)} %convolution_convert_fusion.1, bf16[128,512]{1,0:T(8,128)(2,1)S(1)} %get-tuple-element.51), kind=kOutput, calls=%fused_computation.9 | convolution fusion | flops 202113024 | bytes 2097152 | tf_op jit(solution)/shard_map/dot_general | solution.py:184
  87.2 4.2 %fusion.5 = bf16[512,1536]{1,0:T(8,128)(2,1)} fusion(f32[512,1536]{1,0:T(8,128)} %copy.54, bf16[512,1536]{1,0:T(8,128)(2,1)S(1)} %copy-done.1, f32[512]{0:T(512)S(1)} %copy-done.6, bf16[128,1664]{1,0:T(8,128)(2,1)} %constant_dynamic-update-slice_fusion.11, f32[128,512]{1,0:T(8,128)} %copy-done.2), kind=kOutput, calls=%fused_computation.8 | convolution fusion | flops 206962688 | bytes 6948864 | tf_op jit(solution)/shard_map/dot_general | solution.py:175
  (114 shorter events, 28.7 us)
Async XLA Ops:
  0.6 38.0 %copy-start = (bf16[1536,512]{1,0:T(8,128)(2,1)S(1)}, bf16[1536,512]{1,0:T(8,128)(2,1)}, u32[]{:S(2)}) copy-start(bf16[1536,512]{1,0:T(8,128)(2,1)} %param.18) | copy-start | bytes 4718596
  5.0 4.9 %copy-start.7 = (s32[2]{0:T(128)S(1)}, s32[2]{0:T(128)}, u32[]{:S(2)}) copy-start(s32[2]{0:T(128)} %param.12) | copy-start | bytes 28
  5.0 5.0 %copy-start.8 = (s32[2]{0:T(128)S(1)}, s32[2]{0:T(128)}, u32[]{:S(2)}) copy-start(s32[2]{0:T(128)} %param.13) | copy-start | bytes 28
  5.8 11.5 %copy-start.1 = (bf16[512,1536]{1,0:T(8,128)(2,1)S(1)}, bf16[512,1536]{1,0:T(8,128)(2,1)}, u32[]{:S(2)}) copy-start(bf16[512,1536]{1,0:T(8,128)(2,1)} %param.20) | copy-start | bytes 4718596
  11.0 14.9 %collective-permute-start = (bf16[16,1536]{1,0:T(8,128)(2,1)S(1)}, bf16[16,1536]{1,0:T(8,128)(2,1)S(1)}, u32[]{:S(2)}, u32[]{:S(2)}) collective-permute-start(bf16[16,1536]{1,0:T(8,128)(2,1)S(1)} %get-tuple-element.15), channel_id=1, source_target_pairs={{0,4},{1,5},{2,6},{3,7},{4,0},{5,1},{6,2},{7,3},{8,12},{9,13},{10,... | collective-permute-start | bytes 147464 | tf_op jit(solution)/shard_map/ppermute | solution.py:49
  14.0 11.9 %collective-permute-start.1 = (bf16[16,1536]{1,0:T(8,128)(2,1)S(1)}, bf16[16,1536]{1,0:T(8,128)(2,1)S(1)}, u32[]{:S(2)}, u32[]{:S(2)}) collective-permute-start(bf16[16,1536]{1,0:T(8,128)(2,1)S(1)} %get-tuple-element.15), channel_id=1, source_target_pairs={{0,8},{1,9},{2,10},{3,11},{4,12},{5,13},{6,14},{7,15},{8,0},{9,1},... | collective-permute-start | bytes 147464 | tf_op jit(solution)/shard_map/ppermute | solution.py:49
  16.6 9.3 %collective-permute-start.2 = (bf16[16,1536]{1,0:T(8,128)(2,1)S(1)}, bf16[16,1536]{1,0:T(8,128)(2,1)S(1)}, u32[]{:S(2)}, u32[]{:S(2)}) collective-permute-start(bf16[16,1536]{1,0:T(8,128)(2,1)S(1)} %get-tuple-element.15), channel_id=1, source_target_pairs={{0,12},{1,13},{2,14},{3,15},{4,8},{5,9},{6,10},{7,11},{8,4},{9,5},... | collective-permute-start | bytes 147464 | tf_op jit(solution)/shard_map/ppermute | solution.py:49
  25.9 6.1 %collective-permute-start.3 = (bf16[64,1536]{1,0:T(8,128)(2,1)S(1)}, bf16[64,1536]{1,0:T(8,128)(2,1)S(1)}, u32[]{:S(2)}, u32[]{:S(2)}) collective-permute-start(bf16[64,1536]{1,0:T(8,128)(2,1)S(1)} %pad_maximum_fusion.2), channel_id=1, source_target_pairs={{0,2},{1,3},{2,0},{3,1},{4,6},{5,7},{6,4},{7,5},{8,10},{9,11},{10,... | collective-permute-start | bytes 589832 | tf_op jit(solution)/shard_map/ppermute | solution.py:49
  32.9 1.9 %collective-permute-start.4 = (bf16[128,1536]{1,0:T(8,128)(2,1)}, bf16[128,1536]{1,0:T(8,128)(2,1)S(1)}, u32[]{:S(2)}, u32[]{:S(2)}) collective-permute-start(bf16[128,1536]{1,0:T(8,128)(2,1)} %get-tuple-element.19), channel_id=1, source_target_pairs={{0,1},{1,0},{2,3},{3,2},{4,5},{5,4},{6,7},{7,6},{8,9},{9,8},{10,11... | collective-permute-start | bytes 1179656 | tf_op jit(solution)/shard_map/ppermute | solution.py:49
  40.4 12.6 %copy-start.2 = (f32[128,512]{1,0:T(8,128)}, f32[128,512]{1,0:T(8,128)S(1)}, u32[]{:S(2)}) copy-start(f32[128,512]{1,0:T(8,128)S(1)} %get-tuple-element.49) | copy-start | bytes 786436
  40.4 17.3 %copy-start.5 = (f32[1536]{0:T(1024)S(1)}, f32[1536]{0:T(1024)}, u32[]{:S(2)}) copy-start(f32[1536]{0:T(1024)} %param.21) | copy-start | bytes 18436
  40.9 1.8 %collective-permute-start.5 = (f32[64,1664]{1,0:T(8,128)S(1)}, f32[64,1664]{1,0:T(8,128)S(1)}, u32[]{:S(2)}, u32[]{:S(2)}) collective-permute-start(f32[64,1664]{1,0:T(8,128)S(1)} %pad_maximum_fusion), channel_id=1, source_target_pairs={{0,1},{1,0},{2,3},{3,2},{4,5},{5,4},{6,7},{7,6},{8,9},{9,8},{10,11... | collective-permute-start | bytes 1277960 | tf_op jit(solution)/shard_map/ppermute | solution.py:49
  42.8 4.5 %collective-permute-start.6 = (bf16[16,1664]{1,0:T(8,128)(2,1)S(1)}, bf16[16,1664]{1,0:T(8,128)(2,1)S(1)}, u32[]{:S(2)}, u32[]{:S(2)}) collective-permute-start(bf16[16,1664]{1,0:T(8,128)(2,1)S(1)} %get-tuple-element.16), channel_id=1, source_target_pairs={{0,4},{1,5},{2,6},{3,7},{4,0},{5,1},{6,2},{7,3},{8,12},{9,13},{10,... | collective-permute-start | bytes 159752 | tf_op jit(solution)/shard_map/ppermute | solution.py:49
  43.5 6.9 %collective-permute-start.7 = (bf16[16,1664]{1,0:T(8,128)(2,1)S(1)}, bf16[16,1664]{1,0:T(8,128)(2,1)S(1)}, u32[]{:S(2)}, u32[]{:S(2)}) collective-permute-start(bf16[16,1664]{1,0:T(8,128)(2,1)S(1)} %get-tuple-element.18), channel_id=1, source_target_pairs={{0,8},{1,9},{2,10},{3,11},{4,12},{5,13},{6,14},{7,15},{8,0},{9,1},... | collective-permute-start | bytes 159752 | tf_op jit(solution)/shard_map/ppermute | solution.py:49
  47.0 5.9 %collective-permute-start.8 = (bf16[16,1664]{1,0:T(8,128)(2,1)S(1)}, bf16[16,1664]{1,0:T(8,128)(2,1)S(1)}, u32[]{:S(2)}, u32[]{:S(2)}) collective-permute-start(bf16[16,1664]{1,0:T(8,128)(2,1)S(1)} %get-tuple-element.17), channel_id=1, source_target_pairs={{0,12},{1,13},{2,14},{3,15},{4,8},{5,9},{6,10},{7,11},{8,4},{9,5},... | collective-permute-start | bytes 159752 | tf_op jit(solution)/shard_map/ppermute | solution.py:49
  52.9 4.8 %collective-permute-start.9 = (f32[16,1664]{1,0:T(8,128)S(1)}, f32[16,1664]{1,0:T(8,128)S(1)}, u32[]{:S(2)}, u32[]{:S(2)}) collective-permute-start(f32[16,1664]{1,0:T(8,128)S(1)} %fusion.27), channel_id=1, source_target_pairs={{0,2},{1,3},{2,0},{3,1},{4,6},{5,7},{6,4},{7,5},{8,10},{9,11},{10,... | collective-permute-start | bytes 319496 | tf_op jit(solution)/shard_map/ppermute | solution.py:49
  57.8 0.6 copy-start.3
  59.0 12.0 %collective-permute-start.10 = (bf16[16,1664]{1,0:T(8,128)(2,1)}, bf16[16,1664]{1,0:T(8,128)(2,1)}, u32[]{:S(2)}, u32[]{:S(2)}) collective-permute-start(bf16[16,1664]{1,0:T(8,128)(2,1)} %get-tuple-element.21), channel_id=1, source_target_pairs={{0,4},{1,5},{2,6},{3,7},{4,0},{5,1},{6,2},{7,3},{8,12},{9,13},{10,... | collective-permute-start | bytes 159752 | tf_op jit(solution)/shard_map/ppermute | solution.py:49
  59.0 12.0 %collective-permute-start.11 = (bf16[16,1664]{1,0:T(8,128)(2,1)}, bf16[16,1664]{1,0:T(8,128)(2,1)}, u32[]{:S(2)}, u32[]{:S(2)}) collective-permute-start(bf16[16,1664]{1,0:T(8,128)(2,1)} %get-tuple-element.21), channel_id=1, source_target_pairs={{0,8},{1,9},{2,10},{3,11},{4,12},{5,13},{6,14},{7,15},{8,0},{9,1},... | collective-permute-start | bytes 159752 | tf_op jit(solution)/shard_map/ppermute | solution.py:49
  60.8 10.2 %collective-permute-start.12 = (bf16[16,1664]{1,0:T(8,128)(2,1)}, bf16[16,1664]{1,0:T(8,128)(2,1)}, u32[]{:S(2)}, u32[]{:S(2)}) collective-permute-start(bf16[16,1664]{1,0:T(8,128)(2,1)} %get-tuple-element.21), channel_id=1, source_target_pairs={{0,12},{1,13},{2,14},{3,15},{4,8},{5,9},{6,10},{7,11},{8,4},{9,5},... | collective-permute-start | bytes 159752 | tf_op jit(solution)/shard_map/ppermute | solution.py:49
  66.1 14.4 %copy-start.4 = (f32[512]{0:T(512)S(1)}, f32[512]{0:T(512)}, u32[]{:S(2)}) copy-start(f32[512]{0:T(512)} %broadcast_multiply_fusion.2) | copy-start | bytes 6148
  71.0 16.2 %copy-start.6 = (f32[512]{0:T(512)S(1)}, f32[512]{0:T(512)}, u32[]{:S(2)}) copy-start(f32[512]{0:T(512)} %get-tuple-element.8) | copy-start | bytes 6148
  71.9 4.4 %collective-permute-start.13 = (bf16[64,1664]{1,0:T(8,128)(2,1)S(1)}, bf16[64,1664]{1,0:T(8,128)(2,1)S(1)}, u32[]{:S(2)}, u32[]{:S(2)}) collective-permute-start(bf16[64,1664]{1,0:T(8,128)(2,1)S(1)} %pad_maximum_fusion.1), channel_id=1, source_target_pairs={{0,1},{1,0},{2,3},{3,2},{4,5},{5,4},{6,7},{7,6},{8,9},{9,8},{10,11... | collective-permute-start | bytes 638984 | tf_op jit(solution)/shard_map/ppermute | solution.py:49

commit v2 on v0

v2 whole, which is shorter than its diff:
```python
import jax
import jax.numpy as jnp
from jax import lax
from jax.experimental import pallas as pl
from jax.experimental.pallas import tpu as pltpu
from jax.sharding import PartitionSpec as P

ROWS_DEV = 8
EXTRA = 128
LANES = 128
VMEM_BYTES = 56 << 20

sparsity = 0.5
epsilon = 1e-05

F32 = jnp.float32
BF16 = jnp.bfloat16

ERF_LIMIT = 3.7439211627767994
ERF_TOP = (
    0.00022905065861350646,
    0.0034082910107109506,
    0.050955695062380861,
    0.18520832239976145,
    1.128379143519084,
)
ERF_BOTTOM = (
    -1.1791602954361697e-7,
    0.000023547966471313185,
    0.0010179625278914885,
    0.014070470171167667,
    0.11098505178285362,
    0.49746925110067538,
    1.0,
)


def polynomial(x, terms):
    total = jnp.full_like(x, terms[0])
    for term in terms[1:]:
        total = total * x + term
    return total


def gelu(x):
    z = jnp.clip(x * 0.7071067811865476, -ERF_LIMIT, ERF_LIMIT)
    square = z * z
    erf = z * polynomial(square, ERF_TOP) / polynomial(square, ERF_BOTTOM)
    return 0.5 * x * (1.0 + erf)


def normalize(values, gain, shift):
    center = values - jnp.mean(values, axis=-1, keepdims=True)
    spread = jnp.mean(center * center, axis=-1, keepdims=True)
    return center * lax.rsqrt(spread + epsilon) * gain + shift


def levels(devices):
    chips = devices // 2
    outer = 1
    while outer * outer < chips:
        outer *= 2
    return outer, chips // outer


def exchange(value, bit):
    devices = lax.axis_size("utt")
    return lax.ppermute(value, "utt", [(i, i ^ bit) for i in range(devices)])


def tree(parts):
    while len(parts) > 1:
        parts = [parts[i] + parts[i + 1] for i in range(0, len(parts), 2)]
    return parts[0]


def iota(shape, dim):
    return lax.broadcasted_iota(jnp.int32, shape, dim)


def log2(n):
    return n.bit_length() - 1


def vmem():
    return pl.BlockSpec(memory_space=pltpu.VMEM)


def smem():
    return pl.BlockSpec(memory_space=pltpu.SMEM)


def call(kernel, name, out_shape, in_specs, out_specs, scratch=(), flops=0, moved=0):
    return pl.pallas_call(
        kernel,
        name=name,
        out_shape=out_shape,
        in_specs=in_specs,
        out_specs=out_specs,
        scratch_shapes=list(scratch),
        compiler_params=pltpu.CompilerParams(vmem_limit_bytes=VMEM_BYTES),
        cost_estimate=pl.CostEstimate(flops=flops, bytes_accessed=moved, transcendentals=0),
    )


def shape(dims, kind):
    return jax.ShapeDtypeStruct(dims, kind)


def features_kernel(length, take, wave, first_w, gain, shift, second_hbm, out, second_w, sems):
    checkpoints, taps_first, channels = first_w.shape
    slots, samples = wave.shape
    frames = out.shape[0] // slots
    copies = []
    for c in range(checkpoints):
        copies.append(pltpu.make_async_copy(second_hbm.at[c], second_w.at[c], sems.at[c]))
        copies[-1].start()
    lane = iota((frames, samples), 1)
    start = iota((frames, samples), 0) * 10
    columns = []
    for s in range(slots):
        row = jnp.broadcast_to(wave[s : s + 1, :], (frames, samples))
        columns.append(
            [
                jnp.sum(jnp.where(lane == start + o, row, 0.0), axis=1, keepdims=True)
                for o in range(taps_first + 10)
            ]
        )
    taps = [
        jnp.concatenate(
            [columns[s][5 * tap + k] for tap in range(3) for s in range(slots)], axis=0
        )
        for k in range(taps_first)
    ]
    hidden = []
    for c in range(checkpoints):
        total = taps[0] * first_w[c, 0:1, :]
        for k in range(1, taps_first):
            total = total + taps[k] * first_w[c, k : k + 1, :]
        total = normalize(total, gain[c, 0:1, :], shift[c, 0:1, :])
        hidden.append(gelu(total).astype(BF16))
    rows = slots * frames
    for c in range(checkpoints):
        copies[c].wait()
        total = jnp.zeros((rows, channels), F32)
        for tap in range(3):
            total = total + jnp.dot(
                hidden[c][tap * rows : (tap + 1) * rows],
                second_w[c, tap * channels : (tap + 1) * channels, :],
                preferred_element_type=F32,
            )
        total = gelu(normalize(total, gain[c, 1:2, :], shift[c, 1:2, :]))
        if c == 0:
            spot = iota((rows, channels), 1)
            line = iota((rows, channels), 0)
            for s in range(slots):
                note = jnp.where(
                    spot == 0, length[s].astype(F32), take[s].astype(F32)
                )
                total = jnp.where(line == (s + 1) * frames - 1, note, total)
        out[:, c * channels : (c + 1) * channels] = total.astype(BF16)


def join_kernel(*refs):
    out = refs[-1]
    at = 0
    for ref in refs[:-1]:
        out[at : at + ref.shape[0], :] = ref[...]
        at += ref.shape[0]


def norms_kernel(dec, norms, row):
    latents, feature = dec.shape
    channels = 512
    spot = iota((latents, LANES), 1)
    packed = jnp.zeros((latents, LANES), F32)
    total = jnp.zeros((latents, 1), F32)
    for c in range(feature // channels):
        block = dec[:, c * channels : (c + 1) * channels].astype(F32)
        norm = jnp.sqrt(jnp.sum(block * block, axis=1, keepdims=True) + 1e-06)
        total = total + norm
        packed = jnp.where(spot == c, norm, packed)
    norms[...] = packed
    row[...] = jnp.broadcast_to(total, (latents, LANES)).T[:8]


def encode_kernel(count, outer, inner, slots, frames, rel, *refs):
    me_ref = refs[0]
    pieces = refs[1 : 1 + count]
    enc, bias, dec, weights_sum, dec_bias = refs[1 + count : 6 + count]
    own, send, shift, inputs_out, latent_out = refs[6 + count :]
    me = me_ref[0]
    step = 2 * inner
    tokens, feature = inputs_out.shape
    rows = pieces[0].shape[0]
    held = rows // frames
    shift_frames, shift_slots = log2(frames), log2(slots)
    choose = (iota((held, rows), 1) == iota((held, rows), 0) * frames + frames - 1).astype(BF16)
    takes, starts = [], []
    for piece, bits in zip(pieces, rel):
        notes = jnp.dot(choose, piece[:, :LANES], preferred_element_type=F32)
        takes.append(notes[:, 1:2].astype(jnp.int32))
        device = me ^ ((iota((held, 1), 0) >> shift_slots) * step + bits)
        starts.append(device * ROWS_DEV)
    takes = jnp.concatenate(takes, axis=0)
    starts = jnp.concatenate(starts, axis=0)
    kinds = iota(takes.shape, 0) & (slots - 1)
    r = iota((tokens, 1), 0) >> log2(ROWS_DEV)
    holder = (
        ((r >> log2(inner)) & (outer - 1)) * step + (r & (inner - 1)) * 2 + (r >> log2(outer * inner))
    )
    token = (me ^ holder) * ROWS_DEV + (iota((tokens, 1), 0) & (ROWS_DEV - 1))
    lane = iota((1, rows), 1)
    frame = lane & (frames - 1)
    last = (iota((rows, rows), 0) == (iota((rows, rows), 1) | (frames - 1))).astype(BF16)
    ident = (iota((16, LANES), 0) == iota((16, LANES), 1)).astype(BF16)
    total = jnp.zeros((tokens, feature), F32)
    for piece, bits in zip(pieces, rel):
        turned = lax.dot_general(
            ident, piece[:, :LANES], (((1,), (1,)), ((), ())), preferred_element_type=F32
        )
        turned = jnp.dot(turned.astype(BF16), last, preferred_element_type=F32)
        size = turned[0:1, :].astype(jnp.int32)
        device = me ^ ((lane >> (shift_frames + shift_slots)) * step + bits)
        label = device * slots + ((lane >> shift_frames) & (slots - 1))
        match = takes == label
        begin = jnp.sum(jnp.where(match, starts, 0), axis=0, keepdims=True)
        second = jnp.sum(jnp.where(match, kinds, 0), axis=0, keepdims=True)
        target = begin + second * (ROWS_DEV - size) + frame
        target = jnp.where(frame < size, target, -1)
        pick = jnp.where(token == target, 1.0, 0.0).astype(BF16)
        total = total + jnp.dot(pick, piece[...], preferred_element_type=F32)
    inputs = total.astype(BF16)
    inputs_out[...] = inputs
    latent = jnp.maximum(jnp.dot(inputs, enc[...], preferred_element_type=F32) + bias[...], 0.0)
    latent_out[...] = latent
    part = jnp.dot(latent.astype(BF16), dec[...], preferred_element_type=F32)
    weighted = latent * weights_sum[0:1, :]
    extra = weighted[:, :LANES]
    for q in range(1, weighted.shape[1] // LANES):
        extra = extra + weighted[:, q * LANES : (q + 1) * LANES]
    half = tokens // 2
    own[:, :feature] = part[:half]
    own[:, feature:] = extra[:half]
    send[:, :feature] = part[half:]
    send[:, feature:] = extra[half:]
    chunk = shift.shape[0]
    shift[:, :feature] = dec_bias[...] - inputs[:chunk].astype(F32)
    shift[:, feature:] = jnp.zeros((chunk, EXTRA), F32)


def turn_kernel(inputs, latent, norms, inputs_t, latent_t, scale):
    inputs_t[...] = inputs[...].astype(F32).T.astype(BF16)
    turned = latent[...].T
    latent_t[...] = turned.astype(BF16)
    activity = jnp.sum(turned, axis=1, keepdims=True)
    scale[...] = (sparsity * activity) / jnp.maximum(norms[...], 1e-30)


def gradients_kernel(count, inner, cells, *refs):
    pieces = refs[:count]
    dec, weights_sum, inputs_t, latent_t, latent, scale = refs[count : count + 6]
    enc_out, dec_out, enc_bias_out, dec_bias_out, loss_out, errors_out = refs[count + 6 : count + 12]
    enc_buf, dec_buf, sems = refs[count + 12 :]
    latents, feature = dec.shape
    channels = 512
    errors = jnp.concatenate([piece[:, :feature] for piece in pieces], axis=0)
    copies = []
    parts = 4
    size = latents // parts
    for i in range(parts):
        at = slice(i * size, (i + 1) * size)
        grad = 2.0 * jnp.dot(latent_t[at], errors, preferred_element_type=F32)
        for c in range(feature // channels):
            lanes = slice(c * channels, (c + 1) * channels)
            term = scale[at, c : c + 1] * dec[at, lanes].astype(F32)
            dec_buf[at, lanes] = (grad[:, lanes] + term).astype(BF16)
        copies.append(pltpu.make_async_copy(dec_buf.at[at], dec_out.at[at], sems.at[i]))
        copies[-1].start()
    upstream = lax.dot_general(
        errors, dec[...], (((1,), (1,)), ((), ())), preferred_element_type=F32
    )
    upstream = 2.0 * upstream + sparsity * weights_sum[0:1, :]
    through = jnp.where(latent[...] > 0.0, upstream, 0.0)
    enc_bias_out[...] = jnp.sum(through, axis=0, keepdims=True)
    through = through.astype(BF16)
    size = feature // parts
    for i in range(parts):
        at = slice(i * size, (i + 1) * size)
        grad = jnp.dot(inputs_t[at], through, preferred_element_type=F32)
        enc_buf[at] = grad.astype(BF16)
        copies.append(pltpu.make_async_copy(enc_buf.at[at], enc_out.at[at], sems.at[parts + i]))
        copies[-1].start()
    errors_out[...] = pieces[0][:ROWS_DEV, :feature]
    wide = [piece[...].astype(F32) for piece in pieces]
    plain = tree(wide)
    squares = tree([w[:, :feature] * w[:, :feature] for w in wide])
    plain = tree([plain[i * ROWS_DEV : (i + 1) * ROWS_DEV] for i in range(inner)])
    squares = tree([squares[i * ROWS_DEV : (i + 1) * ROWS_DEV] for i in range(inner)])
    dec_bias_out[...] = 2.0 * jnp.sum(plain[:, :feature], axis=0, keepdims=True)
    loss = jnp.sum(squares) + sparsity * jnp.sum(plain[:, feature:])
    loss_out[0] = loss / cells
    for copy in copies:
        copy.wait()


def shards(
    waveforms,
    lengths,
    take_list,
    conv_first,
    conv_second,
    norm_gain,
    norm_shift,
    enc_weight,
    enc_bias,
    dec_weight,
    dec_bias,
):
    slots = take_list.shape[0]
    devices = lax.axis_size("utt")
    outer, inner = levels(devices)
    step = 2 * inner
    tokens = ROWS_DEV * devices
    position = lax.axis_index("utt").astype(jnp.int32).reshape(1)
    feature, latents = enc_weight.shape
    checkpoints, _, channels = conv_first.shape
    frames = (waveforms.shape[1] - 10) // 10
    wide = feature + EXTRA

    packed = call(
        features_kernel,
        "features",
        shape((slots * frames, feature), BF16),
        [smem(), smem(), vmem(), vmem(), vmem(), vmem(), pl.BlockSpec(memory_space=pl.ANY)],
        vmem(),
        [pltpu.VMEM(conv_second.shape, BF16), pltpu.SemaphoreType.DMA((checkpoints,))],
        flops=2 * slots * frames * feature * 3 * channels,
        moved=2 * conv_second.size,
    )(lengths, take_list, waveforms, conv_first, norm_gain, norm_shift, conv_second)

    norms, weights_sum = call(
        norms_kernel,
        "norms",
        (shape((latents, LANES), F32), shape((8, latents), F32)),
        [vmem()],
        (vmem(), vmem()),
        flops=4 * dec_weight.size,
        moved=2 * dec_weight.size,
    )(dec_weight)

    blocks = [packed] + [exchange(packed, step * k) for k in range(1, outer)]
    pieces = [
        call(
            join_kernel,
            "join",
            shape((outer * slots * frames, feature), BF16),
            [vmem()] * outer,
            vmem(),
            moved=4 * outer * slots * frames * feature,
        )(*blocks)
    ]
    rel = [0]
    bit = 2
    while bit < step:
        pieces += [exchange(piece, bit) for piece in pieces]
        rel += [r ^ bit for r in rel]
        bit *= 2
    pieces += [exchange(piece, 1) for piece in pieces]
    rel += [r ^ 1 for r in rel]

    half = tokens // 2
    chunk = half // outer

    def encode(*refs):
        encode_kernel(len(pieces), outer, inner, slots, frames, rel, *refs)

    own, send, shift, inputs, latent = call(
        encode,
        "encode",
        (
            shape((half, wide), F32),
            shape((half, wide), F32),
            shape((chunk, wide), F32),
            shape((tokens, feature), BF16),
            shape((tokens, latents), F32),
        ),
        [smem()] + [vmem()] * (len(pieces) + 5),
        (vmem(),) * 5,
        flops=4 * tokens * feature * latents,
        moved=4 * dec_weight.size,
    )(
        position,
        *pieces,
        enc_weight,
        enc_bias.reshape(1, latents),
        dec_weight,
        weights_sum,
        dec_bias.reshape(1, feature),
    )

    inputs_t, latent_t, scale = call(
        turn_kernel,
        "turn",
        (shape((feature, tokens), BF16), shape((latents, tokens), BF16), shape((latents, LANES), F32)),
        [vmem()] * 3,
        (vmem(),) * 3,
        flops=2 * tokens * feature,
        moved=4 * tokens * feature,
    )(inputs, latent, norms)

    part = own + exchange(send, 1)
    small = part.astype(BF16)
    blocks = [part[:chunk]]
    for k in range(1, outer):
        blocks.append(exchange(small[k * chunk : (k + 1) * chunk], step * k).astype(F32))
    part = sum(blocks[1:], blocks[0])
    rows = chunk // inner
    bit = 2
    while bit < step:
        width = (bit // 2) * rows
        other = exchange(part, bit).reshape(-1, 2, width, wide)
        part = part + other[:, ::-1].reshape(chunk, wide)
        bit *= 2
    errors = (part + shift).astype(BF16)
    blocks = [errors] + [exchange(errors, step * k) for k in range(1, outer)]
    blocks += [exchange(block, 1) for block in blocks]

    def gradients(*refs):
        gradients_kernel(len(blocks), inner, float(tokens * feature), *refs)

    any_space = pl.BlockSpec(memory_space=pl.ANY)
    enc_grad, dec_grad, enc_bias_grad, dec_bias_grad, mean_loss, errors_own = call(
        gradients,
        "gradients",
        (
            shape((feature, latents), BF16),
            shape((latents, feature), BF16),
            shape((1, latents), F32),
            shape((1, feature), F32),
            shape((1,), F32),
            shape((ROWS_DEV, feature), BF16),
        ),
        [vmem()] * (len(blocks) + 6),
        (any_space, any_space, vmem(), vmem(), smem(), vmem()),
        [
            pltpu.VMEM((feature, latents), BF16),
            pltpu.VMEM((latents, feature), BF16),
            pltpu.SemaphoreType.DMA((8,)),
        ],
        flops=6 * tokens * feature * latents,
        moved=8 * dec_weight.size,
    )(*blocks, dec_weight, weights_sum, inputs_t, latent_t, latent, scale)
    return (
        enc_grad,
        dec_grad,
        enc_bias_grad.reshape(latents),
        dec_bias_grad.reshape(feature),
        mean_loss,
        errors_own,
    )


def solution(mesh):
    return jax.shard_map(
        shards,
        mesh=mesh,
        in_specs=(
            P(("groups", "utt"), None),
            P(("groups", "utt")),
            P(("groups", "utt")),
            P(),
            P(),
            P(),
            P(),
            P(None, "utt"),
            P("utt"),
            P("utt", None),
            P(),
        ),
        out_specs=(
            P("groups", "utt"),
            P(("groups", "utt"), None),
            P(("groups", "utt")),
            P("groups"),
            P("groups"),
            P(("groups", "utt"), None),
        ),
        check_vma=False,
    )
```

time: 241 us -> 70.3 us (0.29)
  blocking collectives: 97.2 us -> 0 us
  waiting for transfers between devices: 83.8 us -> 22.4 us
  Pallas kernels: 0 us -> 21.6 us
  between operations: 18.7 us -> 0.81 us
  starting transfers between devices: 0.04 us -> 17.8 us
  matrix products: 16 us -> 0 us
  local copies, waits for them, and re-layouts: 16.3 us -> 4.8 us
  other arithmetic: 8.29 us -> 2.47 us
    psum x1 -> x0, waiting for transfers between devices: 83.7 us -> none  [shards(): recon = lax.psum(partial_recon, 'utt')]
    all_gather x2 -> x0, blocking collectives: 44.5 us -> none  [the longest x1 23.5 us: shards(): piece_sound = lax.all_gather(waveforms, 'utt', axis=0, tiled=True)]
    psum x1 -> x0, blocking collectives: 31.9 us -> none  [shards(): dec_bias_grad, loss_total = lax.psum((bias_part, loss_part), 'utt')]
    ppermute x0 -> x18, waiting for transfers between devices: none -> 22.4 us  [exchange(): return lax.ppermute(value, 'utt', [(i, i ^ bit) for i in range(devices)])]
    pallas_call x0 -> x6, Pallas kernels: none -> 21.6 us  [the longest x1 5.31 us: shards(): call(gradients, 'gradients', (shape((feature, latents), BF16), shape((lat...]
    unnamed x2 -> x0, blocking collectives: 20.8 us -> none
    ppermute x0 -> x18, starting transfers between devices: none -> 17.8 us  [exchange(): return lax.ppermute(value, 'utt', [(i, i ^ bit) for i in range(devices)])]
    dot_general x8 -> x0, matrix products: 16 us -> none  [the longest x1 4.24 us: shards(): jnp.dot(latent_b.T, errors_b, preferred_element_type=jnp.float32)]
  transfers between devices with their start and end apart: 1 -> 18, of which waited for: 1 -> 10; matrix products, arithmetic and copies ran while one was open for 2% -> 1% of each run, Pallas kernels for 0% -> 7%
where the time goes in v2:
time: 70.3 us; the launch traced here: 69.9 us
  waiting for transfers between devices  22.4 us (32%)
  Pallas kernels  21.6 us (31%)
  starting transfers between devices  17.8 us (25%)
  local copies, waits for them, and re-layouts  4.8 us (7%)
  other arithmetic  2.47 us (4%)
  between operations  0.81 us (1%)
    ppermute x18, waiting for transfers between devices, exchange(): return lax.ppermute(value, 'utt', [(i, i ^ bit) for i in range(devices)])  22.4 us
    ppermute x18, starting transfers between devices, exchange(): return lax.ppermute(value, 'utt', [(i, i ^ bit) for i in range(devices)])  17.8 us
    pallas_call x1, Pallas kernels, shards(): call(gradients, 'gradients', (shape((feature, latents), BF16), shape((lat...  5.31 us
    pallas_call x1, Pallas kernels, shards(): call(encode, 'encode', (shape((half, wide), F32), shape((half, wide), F32...  5.2 us
    pallas_call x1, Pallas kernels, shards(): call(features_kernel, 'features', shape((slots * frames, feature), BF16),...  4.56 us
    unnamed x33, local copies, waits for them, and re-layouts  4.13 us
    pallas_call x1, Pallas kernels, shards(): call(norms_kernel, 'norms', (shape((latents, LANES), F32), shape((8, late...  2.78 us
    pallas_call x1, Pallas kernels, shards(): call(turn_kernel, 'turn', (shape((feature, tokens), BF16), shape((latents...  2.2 us
  transfers between devices with their start and end apart: 18, of which 10 were waited for; matrix products, arithmetic and copies ran while one was open for 1% of the time, Pallas kernels for 7%

profile of v2, /device:TPU:0, one launch (start us, length us, event | category | flops | bytes accessed | tf_op | source)
XLA Modules:
  0.0 69.9 jit_solution(8138326957846198947)
XLA Ops:
  0.6 1.5 %copy.17.first_w = f32[3,10,512]{2,1,0:T(8,128)} copy(f32[3,10,512]{2,0,1:T(4,128)} %param.14) | data formatting | bytes 122880 | tf_op args[3]
  2.2 4.6 %features.1.refs_0_ = bf16[16,1536]{1,0:T(8,128)(2,1)} custom-call(s32[2]{0:T(128)} %length.1, s32[2]{0:T(128)} %take.1, f32[2,90]{1,0:T(2,128)} %wave.1, f32[3,10,512]{2,1,0:T(8,128)} %copy.17.first_w, f32[3,2,512]{2,1,0:T(2,128)} %gain.1, f32[3,2,512]{2,1,0:T(2,128)} %shift.1, bf16[3,1536,512]{2,1,0:T(8,128)(2,1)} %second_hbm.1), custom_call_target="tpu_custom_call" | custom-call | flops 75497472 | bytes 4718592 | tf_op jit(solution)/shard_map/features/pallas_call | solution.py:331
  6.7 5.1 %collective-permute-start.2 = (bf16[16,1536]{1,0:T(8,128)(2,1)}, bf16[16,1536]{1,0:T(8,128)(2,1)S(1)}, u32[]{:S(2)}, u32[]{:S(2)}) collective-permute-start(bf16[16,1536]{1,0:T(8,128)(2,1)} %features.1.refs_0_), channel_id=1, source_target_pairs={{0,12},{1,13},{2,14},{3,15},{4,8},{5,9},{6,10},{7,11},{8,4},{9,5},... | collective-permute-start | bytes 147464 | tf_op jit(solution)/shard_map/ppermute | solution.py:68
  12.5 1.8 %collective-permute-done.2.refs_3_ = bf16[16,1536]{1,0:T(8,128)(2,1)S(1)} collective-permute-done((bf16[16,1536]{1,0:T(8,128)(2,1)}, bf16[16,1536]{1,0:T(8,128)(2,1)S(1)}, u32[]{:S(2)}, u32[]{:S(2)}) %collective-permute-start.2) | collective-permute-done | bytes 49184 | tf_op jit(solution)/shard_map/ppermute | solution.py:68
  14.3 2.8 %collective-permute-done.1.refs_2_ = bf16[16,1536]{1,0:T(8,128)(2,1)S(1)} collective-permute-done((bf16[16,1536]{1,0:T(8,128)(2,1)}, bf16[16,1536]{1,0:T(8,128)(2,1)S(1)}, u32[]{:S(2)}, u32[]{:S(2)}) %collective-permute-start.1) | collective-permute-done | bytes 49184 | tf_op jit(solution)/shard_map/ppermute | solution.py:68
  18.3 1.5 %join.1.refs_1_ = bf16[64,1536]{1,0:T(8,128)(2,1)} custom-call(bf16[16,1536]{1,0:T(8,128)(2,1)} %features.1.refs_0_, bf16[16,1536]{1,0:T(8,128)(2,1)} %copy-done.14, bf16[16,1536]{1,0:T(8,128)(2,1)} %copy-done.13, bf16[16,1536]{1,0:T(8,128)(2,1)} %copy-done.12), custom_call_target="tpu_custom_call" | custom-call | bytes 393216 | tf_op jit(solution)/shard_map/join/pallas_call | solution.py:354
  19.8 1.5 %collective-permute-start.3 = (bf16[64,1536]{1,0:T(8,128)(2,1)}, bf16[64,1536]{1,0:T(8,128)(2,1)S(1)}, u32[]{:S(2)}, u32[]{:S(2)}) collective-permute-start(bf16[64,1536]{1,0:T(8,128)(2,1)} %join.1.refs_1_), channel_id=1, source_target_pairs={{0,2},{1,3},{2,0},{3,1},{4,6},{5,7},{6,4},{7,5},{8,10},{9,11},{10,... | collective-permute-start | bytes 589832 | tf_op jit(solution)/shard_map/ppermute | solution.py:68
  21.4 4.4 %collective-permute-done.3.refs_2_ = bf16[64,1536]{1,0:T(8,128)(2,1)S(1)} collective-permute-done((bf16[64,1536]{1,0:T(8,128)(2,1)}, bf16[64,1536]{1,0:T(8,128)(2,1)S(1)}, u32[]{:S(2)}, u32[]{:S(2)}) %collective-permute-start.3) | collective-permute-done | bytes 196640 | tf_op jit(solution)/shard_map/ppermute | solution.py:68
  26.5 2.8 %norms.1 = (f32[512,128]{1,0:T(8,128)}, f32[8,512]{1,0:T(8,128)}) custom-call(bf16[512,1536]{1,0:T(8,128)(2,1)} %refs_8_.1), custom_call_target="tpu_custom_call" | custom-call | flops 3145728 | bytes 1572864 | tf_op jit(solution)/shard_map/norms/pallas_call | solution.py:342
  30.0 5.2 %encode.1 = (f32[64,1664]{1,0:T(8,128)}, f32[64,1664]{1,0:T(8,128)}, f32[16,1664]{1,0:T(8,128)}, bf16[128,1536]{1,0:T(8,128)(2,1)}, f32[128,512]{1,0:T(8,128)}) custom-call(s32[1]{0:T(128)} %bitcast.refs_0_, bf16[64,1536]{1,0:T(8,128)(2,1)} %join.1.refs_1_, bf16[64,1536]{1,0:T(8,128)(2,1)} %copy-done.1, bf16[64,1536]{1,0:T(8,128)(2,1)} %copy-done.2, ...), custom_call_target="tpu_custom_call" | custom-call | flops 402653184 | bytes 3145728 | tf_op jit(solution)/shard_map/encode/pallas_call | solution.py:378
  35.7 1.6 %collective-permute-done.6 = f32[64,1664]{1,0:T(8,128)S(1)} collective-permute-done((f32[64,1664]{1,0:T(8,128)}, f32[64,1664]{1,0:T(8,128)S(1)}, u32[]{:S(2)}, u32[]{:S(2)}) %collective-permute-start.6) | collective-permute-done | bytes 426016 | tf_op jit(solution)/shard_map/ppermute | solution.py:68
  37.3 1.1 %fusion.4 = (bf16[64,1664]{1,0:T(8,128)(2,1)S(1)}, f32[64,1664]{1,0:T(8,128)S(1)}) fusion(f32[64,1664]{1,0:T(8,128)} %get-tuple-element.23, f32[64,1664]{1,0:T(8,128)S(1)} %collective-permute-done.6), kind=kLoop, calls=%fused_computation.6 | loop fusion | flops 212992 | bytes 1490944 | tf_op jit(solution)/shard_map/convert_element_type | solution.py:413
  38.6 2.7 %collective-permute-start.9 = (bf16[16,1664]{1,0:T(8,128)(2,1)S(1)}, bf16[16,1664]{1,0:T(8,128)(2,1)S(1)}, u32[]{:S(2)}, u32[]{:S(2)}) collective-permute-start(bf16[16,1664]{1,0:T(8,128)(2,1)S(1)} %get-tuple-element.41), channel_id=1, source_target_pairs={{0,12},{1,13},{2,14},{3,15},{4,8},{5,9},{6,10},{7,11},{8,4},{9,5},... | collective-permute-start | bytes 159752 | tf_op jit(solution)/shard_map/ppermute | solution.py:68
  42.6 2.3 %collective-permute-done.9 = bf16[16,1664]{1,0:T(8,128)(2,1)S(1)} collective-permute-done((bf16[16,1664]{1,0:T(8,128)(2,1)S(1)}, bf16[16,1664]{1,0:T(8,128)(2,1)S(1)}, u32[]{:S(2)}, u32[]{:S(2)}) %collective-permute-start.9) | collective-permute-done | bytes 53280 | tf_op jit(solution)/shard_map/ppermute | solution.py:68
  44.9 2.5 %collective-permute-done.8 = bf16[16,1664]{1,0:T(8,128)(2,1)S(1)} collective-permute-done((bf16[16,1664]{1,0:T(8,128)(2,1)S(1)}, bf16[16,1664]{1,0:T(8,128)(2,1)S(1)}, u32[]{:S(2)}, u32[]{:S(2)}) %collective-permute-start.8) | collective-permute-done | bytes 53280 | tf_op jit(solution)/shard_map/ppermute | solution.py:68
  47.4 1.6 %collective-permute-start.10 = (f32[16,1664]{1,0:T(8,128)S(1)}, f32[16,1664]{1,0:T(8,128)S(1)}, u32[]{:S(2)}, u32[]{:S(2)}) collective-permute-start(f32[16,1664]{1,0:T(8,128)S(1)} %fusion.1), channel_id=1, source_target_pairs={{0,2},{1,3},{2,0},{3,1},{4,6},{5,7},{6,4},{7,5},{8,10},{9,11},{10,... | collective-permute-start | bytes 319496 | tf_op jit(solution)/shard_map/ppermute | solution.py:68
  49.0 3.2 %collective-permute-done.10 = f32[16,1664]{1,0:T(8,128)S(1)} collective-permute-done((f32[16,1664]{1,0:T(8,128)S(1)}, f32[16,1664]{1,0:T(8,128)S(1)}, u32[]{:S(2)}, u32[]{:S(2)}) %collective-permute-start.10) | collective-permute-done | bytes 106528 | tf_op jit(solution)/shard_map/ppermute | solution.py:68
  52.2 2.3 %collective-permute-start.13 = (bf16[16,1664]{1,0:T(8,128)(2,1)S(1)}, bf16[16,1664]{1,0:T(8,128)(2,1)S(1)}, u32[]{:S(2)}, u32[]{:S(2)}) collective-permute-start(bf16[16,1664]{1,0:T(8,128)(2,1)S(1)} %fusion.3.refs_0_), channel_id=1, source_target_pairs={{0,12},{1,13},{2,14},{3,15},{4,8},{5,9},{6,10},{7,11},{8,4},{9,5},... | collective-permute-start | bytes 159752 | tf_op jit(solution)/shard_map/ppermute | solution.py:68
  54.5 2.2 %collective-permute-start.11 = (bf16[16,1664]{1,0:T(8,128)(2,1)S(1)}, bf16[16,1664]{1,0:T(8,128)(2,1)S(1)}, u32[]{:S(2)}, u32[]{:S(2)}) collective-permute-start(bf16[16,1664]{1,0:T(8,128)(2,1)S(1)} %fusion.3.refs_0_), channel_id=1, source_target_pairs={{0,4},{1,5},{2,6},{3,7},{4,0},{5,1},{6,2},{7,3},{8,12},{9,13},{10,... | collective-permute-start | bytes 159752 | tf_op jit(solution)/shard_map/ppermute | solution.py:68
  56.7 1.9 %collective-permute-done.13.refs_3_ = bf16[16,1664]{1,0:T(8,128)(2,1)S(1)} collective-permute-done((bf16[16,1664]{1,0:T(8,128)(2,1)S(1)}, bf16[16,1664]{1,0:T(8,128)(2,1)S(1)}, u32[]{:S(2)}, u32[]{:S(2)}) %collective-permute-start.13) | collective-permute-done | bytes 53280 | tf_op jit(solution)/shard_map/ppermute | solution.py:68
  58.6 1.3 %collective-permute-done.12.refs_2_ = bf16[16,1664]{1,0:T(8,128)(2,1)S(1)} collective-permute-done((bf16[16,1664]{1,0:T(8,128)(2,1)S(1)}, bf16[16,1664]{1,0:T(8,128)(2,1)S(1)}, u32[]{:S(2)}, u32[]{:S(2)}) %collective-permute-start.12) | collective-permute-done | bytes 53280 | tf_op jit(solution)/shard_map/ppermute | solution.py:68
  60.4 2.2 %turn.1 = (bf16[1536,128]{1,0:T(8,128)(2,1)}, bf16[512,128]{1,0:T(8,128)(2,1)}, f32[512,128]{1,0:T(8,128)}) custom-call(bf16[128,1536]{1,0:T(8,128)(2,1)} %get-tuple-element.26.inputs, f32[128,512]{1,0:T(8,128)} %get-tuple-element.27.latent.refs_12_, f32[512,128]{1,0:T(8,128)} %get-tuple-element.28.norms), custom_call_target="tpu_custom_call" | custom-call | flops 393216 | bytes 786432 | tf_op jit(solution)/shard_map/turn/pallas_call | solution.py:402
  63.3 5.3 %gradients.1 = (bf16[1536,512]{1,0:T(8,128)(2,1)}, bf16[512,1536]{1,0:T(8,128)(2,1)}, f32[1,512]{1,0:T(1,128)}, f32[1,1536]{1,0:T(1,128)}, f32[1]{0:T(128)}, /*index=5*/bf16[8,1536]{1,0:T(8,128)(2,1)}) custom-call(bf16[16,1664]{1,0:T(8,128)(2,1)} %copy-done, bf16[16,1664]{1,0:T(8,128)(2,1)} %copy-done.7, bf16[16,1664]{1,0:T(8,128)(2,1)} %copy-done.6, ...), custom_call_target="tpu_custom_call" | custom-call | flops 603979776 | bytes 6291456 | tf_op jit(solution)/shard_map/gradients/pallas_call | solution.py:433
  68.6 1.3 %reduce = f32[1536]{0:T(1024)} reduce(f32[1,1536]{1,0:T(1,128)} %get-tuple-element.35, f32[]{:T(128)} %constant.7), dimensions={0}, to_apply=%get-tuple-element.35.reduce_sub_computation | reduce | bytes 12292 | tf_op jit(solution)/shard_map/gradients/pallas_call | solution.py:433
  (57 shorter events, 6.4 us)
Async XLA Ops:
  2.2 23.6 %copy-start.15 = (f32[1536]{0:T(1024)S(1)}, f32[1536]{0:T(1024)}, u32[]{:S(2)}) copy-start(f32[1536]{0:T(1024)} %param.21) | copy-start | bytes 18436
  6.7 7.6 %collective-permute-start.2 = (bf16[16,1536]{1,0:T(8,128)(2,1)}, bf16[16,1536]{1,0:T(8,128)(2,1)S(1)}, u32[]{:S(2)}, u32[]{:S(2)}) collective-permute-start(bf16[16,1536]{1,0:T(8,128)(2,1)} %features.1.refs_0_), channel_id=1, source_target_pairs={{0,12},{1,13},{2,14},{3,15},{4,8},{5,9},{6,10},{7,11},{8,4},{9,5},... | collective-permute-start | bytes 147464 | tf_op jit(solution)/shard_map/ppermute | solution.py:68
  11.9 5.2 %collective-permute-start.1 = (bf16[16,1536]{1,0:T(8,128)(2,1)}, bf16[16,1536]{1,0:T(8,128)(2,1)S(1)}, u32[]{:S(2)}, u32[]{:S(2)}) collective-permute-start(bf16[16,1536]{1,0:T(8,128)(2,1)} %features.1.refs_0_), channel_id=1, source_target_pairs={{0,8},{1,9},{2,10},{3,11},{4,12},{5,13},{6,14},{7,15},{8,0},{9,1},... | collective-permute-start | bytes 147464 | tf_op jit(solution)/shard_map/ppermute | solution.py:68
  11.9 5.2 %collective-permute-start = (bf16[16,1536]{1,0:T(8,128)(2,1)}, bf16[16,1536]{1,0:T(8,128)(2,1)S(1)}, u32[]{:S(2)}, u32[]{:S(2)}) collective-permute-start(bf16[16,1536]{1,0:T(8,128)(2,1)} %features.1.refs_0_), channel_id=1, source_target_pairs={{0,4},{1,5},{2,6},{3,7},{4,0},{5,1},{6,2},{7,3},{8,12},{9,13},{10,... | collective-permute-start | bytes 147464 | tf_op jit(solution)/shard_map/ppermute | solution.py:68
  19.8 6.0 %collective-permute-start.3 = (bf16[64,1536]{1,0:T(8,128)(2,1)}, bf16[64,1536]{1,0:T(8,128)(2,1)S(1)}, u32[]{:S(2)}, u32[]{:S(2)}) collective-permute-start(bf16[64,1536]{1,0:T(8,128)(2,1)} %join.1.refs_1_), channel_id=1, source_target_pairs={{0,2},{1,3},{2,0},{3,1},{4,6},{5,7},{6,4},{7,5},{8,10},{9,11},{10,... | collective-permute-start | bytes 589832 | tf_op jit(solution)/shard_map/ppermute | solution.py:68
  21.4 7.9 %collective-permute-start.4 = (bf16[64,1536]{1,0:T(8,128)(2,1)}, bf16[64,1536]{1,0:T(8,128)(2,1)S(1)}, u32[]{:S(2)}, u32[]{:S(2)}) collective-permute-start(bf16[64,1536]{1,0:T(8,128)(2,1)} %join.1.refs_1_), channel_id=1, source_target_pairs={{0,1},{1,0},{2,3},{3,2},{4,5},{5,4},{6,7},{7,6},{8,9},{9,8},{10,11... | collective-permute-start | bytes 589832 | tf_op jit(solution)/shard_map/ppermute | solution.py:68
  25.8 3.5 %copy-start.1 = (bf16[64,1536]{1,0:T(8,128)(2,1)}, bf16[64,1536]{1,0:T(8,128)(2,1)S(1)}, u32[]{:S(2)}) copy-start(bf16[64,1536]{1,0:T(8,128)(2,1)S(1)} %collective-permute-done.3.refs_2_) | copy-start | bytes 589828
  25.8 3.5 %collective-permute-start.5 = (bf16[64,1536]{1,0:T(8,128)(2,1)S(1)}, bf16[64,1536]{1,0:T(8,128)(2,1)S(1)}, u32[]{:S(2)}, u32[]{:S(2)}) collective-permute-start(bf16[64,1536]{1,0:T(8,128)(2,1)S(1)} %collective-permute-done.3.refs_2_), channel_id=1, source_target_pairs={{0,1},{1,0},{2,3},{3,2},{4,5},{5,4},{6,7},{7,6},{8,9},{9,8},{10,11... | collective-permute-start | bytes 589832 | tf_op jit(solution)/shard_map/ppermute | solution.py:68
  35.2 16.9 %copy-start.4 = (f32[16,1664]{1,0:T(8,128)S(1)}, f32[16,1664]{1,0:T(8,128)}, u32[]{:S(2)}) copy-start(f32[16,1664]{1,0:T(8,128)} %get-tuple-element.25) | copy-start | bytes 319492
  35.2 2.1 %collective-permute-start.6 = (f32[64,1664]{1,0:T(8,128)}, f32[64,1664]{1,0:T(8,128)S(1)}, u32[]{:S(2)}, u32[]{:S(2)}) collective-permute-start(f32[64,1664]{1,0:T(8,128)} %get-tuple-element.24), channel_id=1, source_target_pairs={{0,1},{1,0},{2,3},{3,2},{4,5},{5,4},{6,7},{7,6},{8,9},{9,8},{10,11... | collective-permute-start | bytes 1277960 | tf_op jit(solution)/shard_map/ppermute | solution.py:68
  38.4 4.2 %collective-permute-start.7 = (bf16[16,1664]{1,0:T(8,128)(2,1)S(1)}, bf16[16,1664]{1,0:T(8,128)(2,1)S(1)}, u32[]{:S(2)}, u32[]{:S(2)}) collective-permute-start(bf16[16,1664]{1,0:T(8,128)(2,1)S(1)} %get-tuple-element.40), channel_id=1, source_target_pairs={{0,4},{1,5},{2,6},{3,7},{4,0},{5,1},{6,2},{7,3},{8,12},{9,13},{10,... | collective-permute-start | bytes 159752 | tf_op jit(solution)/shard_map/ppermute | solution.py:68
  38.6 6.3 %collective-permute-start.9 = (bf16[16,1664]{1,0:T(8,128)(2,1)S(1)}, bf16[16,1664]{1,0:T(8,128)(2,1)S(1)}, u32[]{:S(2)}, u32[]{:S(2)}) collective-permute-start(bf16[16,1664]{1,0:T(8,128)(2,1)S(1)} %get-tuple-element.41), channel_id=1, source_target_pairs={{0,12},{1,13},{2,14},{3,15},{4,8},{5,9},{6,10},{7,11},{8,4},{9,5},... | collective-permute-start | bytes 159752 | tf_op jit(solution)/shard_map/ppermute | solution.py:68
  41.3 6.1 %collective-permute-start.8 = (bf16[16,1664]{1,0:T(8,128)(2,1)S(1)}, bf16[16,1664]{1,0:T(8,128)(2,1)S(1)}, u32[]{:S(2)}, u32[]{:S(2)}) collective-permute-start(bf16[16,1664]{1,0:T(8,128)(2,1)S(1)} %get-tuple-element.42), channel_id=1, source_target_pairs={{0,8},{1,9},{2,10},{3,11},{4,12},{5,13},{6,14},{7,15},{8,0},{9,1},... | collective-permute-start | bytes 159752 | tf_op jit(solution)/shard_map/ppermute | solution.py:68
  47.4 4.8 %collective-permute-start.10 = (f32[16,1664]{1,0:T(8,128)S(1)}, f32[16,1664]{1,0:T(8,128)S(1)}, u32[]{:S(2)}, u32[]{:S(2)}) collective-permute-start(f32[16,1664]{1,0:T(8,128)S(1)} %fusion.1), channel_id=1, source_target_pairs={{0,2},{1,3},{2,0},{3,1},{4,6},{5,7},{6,4},{7,5},{8,10},{9,11},{10,... | collective-permute-start | bytes 319496 | tf_op jit(solution)/shard_map/ppermute | solution.py:68
  52.2 10.5 %copy-start = (bf16[16,1664]{1,0:T(8,128)(2,1)}, bf16[16,1664]{1,0:T(8,128)(2,1)S(1)}, u32[]{:S(2)}) copy-start(bf16[16,1664]{1,0:T(8,128)(2,1)S(1)} %fusion.3.refs_0_) | copy-start | bytes 159748
  52.2 6.3 %collective-permute-start.13 = (bf16[16,1664]{1,0:T(8,128)(2,1)S(1)}, bf16[16,1664]{1,0:T(8,128)(2,1)S(1)}, u32[]{:S(2)}, u32[]{:S(2)}) collective-permute-start(bf16[16,1664]{1,0:T(8,128)(2,1)S(1)} %fusion.3.refs_0_), channel_id=1, source_target_pairs={{0,12},{1,13},{2,14},{3,15},{4,8},{5,9},{6,10},{7,11},{8,4},{9,5},... | collective-permute-start | bytes 159752 | tf_op jit(solution)/shard_map/ppermute | solution.py:68
  54.5 5.4 %collective-permute-start.12 = (bf16[16,1664]{1,0:T(8,128)(2,1)S(1)}, bf16[16,1664]{1,0:T(8,128)(2,1)S(1)}, u32[]{:S(2)}, u32[]{:S(2)}) collective-permute-start(bf16[16,1664]{1,0:T(8,128)(2,1)S(1)} %fusion.3.refs_0_), channel_id=1, source_target_pairs={{0,8},{1,9},{2,10},{3,11},{4,12},{5,13},{6,14},{7,15},{8,0},{9,1},... | collective-permute-start | bytes 159752 | tf_op jit(solution)/shard_map/ppermute | solution.py:68
  54.5 5.4 %collective-permute-start.11 = (bf16[16,1664]{1,0:T(8,128)(2,1)S(1)}, bf16[16,1664]{1,0:T(8,128)(2,1)S(1)}, u32[]{:S(2)}, u32[]{:S(2)}) collective-permute-start(bf16[16,1664]{1,0:T(8,128)(2,1)S(1)} %fusion.3.refs_0_), channel_id=1, source_target_pairs={{0,4},{1,5},{2,6},{3,7},{4,0},{5,1},{6,2},{7,3},{8,12},{9,13},{10,... | collective-permute-start | bytes 159752 | tf_op jit(solution)/shard_map/ppermute | solution.py:68
  56.7 5.9 %collective-permute-start.14 = (bf16[16,1664]{1,0:T(8,128)(2,1)S(1)}, bf16[16,1664]{1,0:T(8,128)(2,1)S(1)}, u32[]{:S(2)}, u32[]{:S(2)}) collective-permute-start(bf16[16,1664]{1,0:T(8,128)(2,1)S(1)} %fusion.3.refs_0_), channel_id=1, source_target_pairs={{0,1},{1,0},{2,3},{3,2},{4,5},{5,4},{6,7},{7,6},{8,9},{9,8},{10,11... | collective-permute-start | bytes 159752 | tf_op jit(solution)/shard_map/ppermute | solution.py:68
  58.6 4.1 %copy-start.5 = (bf16[16,1664]{1,0:T(8,128)(2,1)}, bf16[16,1664]{1,0:T(8,128)(2,1)S(1)}, u32[]{:S(2)}) copy-start(bf16[16,1664]{1,0:T(8,128)(2,1)S(1)} %collective-permute-done.13.refs_3_) | copy-start | bytes 159748
  58.6 4.1 %collective-permute-start.17 = (bf16[16,1664]{1,0:T(8,128)(2,1)S(1)}, bf16[16,1664]{1,0:T(8,128)(2,1)S(1)}, u32[]{:S(2)}, u32[]{:S(2)}) collective-permute-start(bf16[16,1664]{1,0:T(8,128)(2,1)S(1)} %collective-permute-done.13.refs_3_), channel_id=1, source_target_pairs={{0,1},{1,0},{2,3},{3,2},{4,5},{5,4},{6,7},{7,6},{8,9},{9,8},{10,11... | collective-permute-start | bytes 159752 | tf_op jit(solution)/shard_map/ppermute | solution.py:68
  59.9 2.8 %copy-start.6 = (bf16[16,1664]{1,0:T(8,128)(2,1)}, bf16[16,1664]{1,0:T(8,128)(2,1)S(1)}, u32[]{:S(2)}) copy-start(bf16[16,1664]{1,0:T(8,128)(2,1)S(1)} %collective-permute-done.12.refs_2_) | copy-start | bytes 159748
  59.9 2.7 %collective-permute-start.16 = (bf16[16,1664]{1,0:T(8,128)(2,1)S(1)}, bf16[16,1664]{1,0:T(8,128)(2,1)S(1)}, u32[]{:S(2)}, u32[]{:S(2)}) collective-permute-start(bf16[16,1664]{1,0:T(8,128)(2,1)S(1)} %collective-permute-done.12.refs_2_), channel_id=1, source_target_pairs={{0,1},{1,0},{2,3},{3,2},{4,5},{5,4},{6,7},{7,6},{8,9},{9,8},{10,11... | collective-permute-start | bytes 159752 | tf_op jit(solution)/shard_map/ppermute | solution.py:68
  59.9 2.7 %collective-permute-start.15 = (bf16[16,1664]{1,0:T(8,128)(2,1)S(1)}, bf16[16,1664]{1,0:T(8,128)(2,1)S(1)}, u32[]{:S(2)}, u32[]{:S(2)}) collective-permute-start(bf16[16,1664]{1,0:T(8,128)(2,1)S(1)} %collective-permute-done.11.refs_1_), channel_id=1, source_target_pairs={{0,1},{1,0},{2,3},{3,2},{4,5},{5,4},{6,7},{7,6},{8,9},{9,8},{10,11... | collective-permute-start | bytes 159752 | tf_op jit(solution)/shard_map/ppermute | solution.py:68
  (10 other events, 10.7 us)

commit v3 on v2

--- a/solution.py
+++ b/solution.py
@@ -1,3 +1,5 @@
+import functools
+
 import jax
 import jax.numpy as jnp
 from jax import lax
@@ -9,6 +11,8 @@
 EXTRA = 128
 LANES = 128
 VMEM_BYTES = 56 << 20
+PINNED_BYTES = 24 << 20
+PINNED_TOKENS = 256
 
 sparsity = 0.5
 epsilon = 1e-05
@@ -90,7 +94,7 @@
     return pl.BlockSpec(memory_space=pltpu.SMEM)
 
 
-def call(kernel, name, out_shape, in_specs, out_specs, scratch=(), flops=0, moved=0):
+def launch(limit, kernel, name, out_shape, in_specs, out_specs, scratch=(), flops=0, moved=0):
     return pl.pallas_call(
         kernel,
         name=name,
@@ -98,7 +102,7 @@
         in_specs=in_specs,
         out_specs=out_specs,
         scratch_shapes=list(scratch),
-        compiler_params=pltpu.CompilerParams(vmem_limit_bytes=VMEM_BYTES),
+        compiler_params=pltpu.CompilerParams(vmem_limit_bytes=limit),
         cost_estimate=pl.CostEstimate(flops=flops, bytes_accessed=moved, transcendentals=0),
     )
 
@@ -108,7 +112,7 @@
 
 
 def features_kernel(length, take, wave, first_w, gain, shift, second_hbm, out, second_w, sems):
-    checkpoints, taps_first, channels = first_w.shape
+    taps_first, checkpoints, channels = first_w.shape
     slots, samples = wave.shape
     frames = out.shape[0] // slots
     copies = []
@@ -134,9 +138,9 @@
     ]
     hidden = []
     for c in range(checkpoints):
-        total = taps[0] * first_w[c, 0:1, :]
+        total = taps[0] * first_w[0, c : c + 1, :]
         for k in range(1, taps_first):
-            total = total + taps[k] * first_w[c, k : k + 1, :]
+            total = total + taps[k] * first_w[k, c : c + 1, :]
         total = normalize(total, gain[c, 0:1, :], shift[c, 0:1, :])
         hidden.append(gelu(total).astype(BF16))
     rows = slots * frames
@@ -164,7 +168,7 @@
 def join_kernel(*refs):
     out = refs[-1]
     at = 0
-    for ref in refs[:-1]:
+    for ref in refs[2:-1]:
         out[at : at + ref.shape[0], :] = ref[...]
         at += ref.shape[0]
 
@@ -245,7 +249,7 @@
     send[:, :feature] = part[half:]
     send[:, feature:] = extra[half:]
     chunk = shift.shape[0]
-    shift[:, :feature] = dec_bias[...] - inputs[:chunk].astype(F32)
+    shift[:, :feature] = dec_bias[...].reshape(1, feature) - inputs[:chunk].astype(F32)
     shift[:, feature:] = jnp.zeros((chunk, EXTRA), F32)
 
 
@@ -255,6 +259,13 @@
     latent_t[...] = turned.astype(BF16)
     activity = jnp.sum(turned, axis=1, keepdims=True)
     scale[...] = (sparsity * activity) / jnp.maximum(norms[...], 1e-30)
+
+
+def sum_kernel(*refs):
+    total = refs[1][...]
+    for ref in refs[2:-1]:
+        total = total + ref[...].astype(F32)
+    refs[-1][...] = total
 
 
 def gradients_kernel(count, inner, cells, *refs):
@@ -297,7 +308,7 @@
     squares = tree([w[:, :feature] * w[:, :feature] for w in wide])
     plain = tree([plain[i * ROWS_DEV : (i + 1) * ROWS_DEV] for i in range(inner)])
     squares = tree([squares[i * ROWS_DEV : (i + 1) * ROWS_DEV] for i in range(inner)])
-    dec_bias_out[...] = 2.0 * jnp.sum(plain[:, :feature], axis=0, keepdims=True)
+    dec_bias_out[...] = 2.0 * jnp.sum(plain[:, :feature], axis=0)
     loss = jnp.sum(squares) + sparsity * jnp.sum(plain[:, feature:])
     loss_out[0] = loss / cells
     for copy in copies:
@@ -328,37 +339,49 @@
     frames = (waveforms.shape[1] - 10) // 10
     wide = feature + EXTRA
 
+    pinned = tokens <= PINNED_TOKENS
+    call = functools.partial(launch, PINNED_BYTES if pinned else VMEM_BYTES)
+
+    def fast(dims, kind):
+        return pltpu.VMEM(dims, kind) if pinned else shape(dims, kind)
+
+    def near(value):
+        return pltpu.with_memory_space_constraint(value, pltpu.VMEM) if pinned else value
+
+    encoder = near(enc_weight)
+    decoder = near(dec_weight)
+
     packed = call(
         features_kernel,
         "features",
-        shape((slots * frames, feature), BF16),
+        fast((slots * frames, feature), BF16),
         [smem(), smem(), vmem(), vmem(), vmem(), vmem(), pl.BlockSpec(memory_space=pl.ANY)],
         vmem(),
         [pltpu.VMEM(conv_second.shape, BF16), pltpu.SemaphoreType.DMA((checkpoints,))],
         flops=2 * slots * frames * feature * 3 * channels,
         moved=2 * conv_second.size,
-    )(lengths, take_list, waveforms, conv_first, norm_gain, norm_shift, conv_second)
+    )(lengths, take_list, waveforms, conv_first.transpose(1, 0, 2), norm_gain, norm_shift, conv_second)
 
     norms, weights_sum = call(
         norms_kernel,
         "norms",
-        (shape((latents, LANES), F32), shape((8, latents), F32)),
+        (fast((latents, LANES), F32), fast((8, latents), F32)),
         [vmem()],
         (vmem(), vmem()),
         flops=4 * dec_weight.size,
         moved=2 * dec_weight.size,
-    )(dec_weight)
+    )(decoder)
 
     blocks = [packed] + [exchange(packed, step * k) for k in range(1, outer)]
     pieces = [
         call(
             join_kernel,
             "join",
-            shape((outer * slots * frames, feature), BF16),
-            [vmem()] * outer,
+            fast((outer * slots * frames, feature), BF16),
+            [pl.BlockSpec(memory_space=pl.ANY)] * 2 + [vmem()] * outer,
             vmem(),
             moved=4 * outer * slots * frames * feature,
-        )(*blocks)
+        )(near(norms), encoder, *[near(block) for block in blocks])
     ]
     rel = [0]
     bit = 2
@@ -379,11 +402,11 @@
         encode,
         "encode",
         (
-            shape((half, wide), F32),
-            shape((half, wide), F32),
-            shape((chunk, wide), F32),
-            shape((tokens, feature), BF16),
-            shape((tokens, latents), F32),
+            fast((half, wide), F32),
+            fast((half, wide), F32),
+            fast((chunk, wide), F32),
+            fast((tokens, feature), BF16),
+            fast((tokens, latents), F32),
         ),
         [smem()] + [vmem()] * (len(pieces) + 5),
         (vmem(),) * 5,
@@ -391,30 +414,37 @@
         moved=4 * dec_weight.size,
     )(
         position,
-        *pieces,
-        enc_weight,
+        *[near(piece) for piece in pieces],
+        encoder,
         enc_bias.reshape(1, latents),
-        dec_weight,
-        weights_sum,
-        dec_bias.reshape(1, feature),
+        decoder,
+        near(weights_sum),
+        dec_bias,
     )
 
     inputs_t, latent_t, scale = call(
         turn_kernel,
         "turn",
-        (shape((feature, tokens), BF16), shape((latents, tokens), BF16), shape((latents, LANES), F32)),
+        (fast((feature, tokens), BF16), fast((latents, tokens), BF16), fast((latents, LANES), F32)),
         [vmem()] * 3,
         (vmem(),) * 3,
         flops=2 * tokens * feature,
         moved=4 * tokens * feature,
-    )(inputs, latent, norms)
+    )(near(inputs), near(latent), near(norms))
 
     part = own + exchange(send, 1)
     small = part.astype(BF16)
     blocks = [part[:chunk]]
     for k in range(1, outer):
-        blocks.append(exchange(small[k * chunk : (k + 1) * chunk], step * k).astype(F32))
-    part = sum(blocks[1:], blocks[0])
+        blocks.append(exchange(small[k * chunk : (k + 1) * chunk], step * k))
+    part = call(
+        sum_kernel,
+        "sum",
+        fast((chunk, wide), F32),
+        [pl.BlockSpec(memory_space=pl.ANY)] + [vmem()] * outer,
+        vmem(),
+        moved=8 * chunk * wide,
+    )(near(scale), *[near(block) for block in blocks])
     rows = chunk // inner
     bit = 2
     while bit < step:
@@ -437,7 +467,7 @@
             shape((feature, latents), BF16),
             shape((latents, feature), BF16),
             shape((1, latents), F32),
-            shape((1, feature), F32),
+            shape((feature,), F32),
             shape((1,), F32),
             shape((ROWS_DEV, feature), BF16),
         ),
@@ -450,12 +480,20 @@
         ],
         flops=6 * tokens * feature * latents,
         moved=8 * dec_weight.size,
-    )(*blocks, dec_weight, weights_sum, inputs_t, latent_t, latent, scale)
+    )(
+        *[near(block) for block in blocks],
+        decoder,
+        near(weights_sum),
+        near(inputs_t),
+        near(latent_t),
+        near(latent),
+        near(scale),
+    )
     return (
         enc_grad,
         dec_grad,
         enc_bias_grad.reshape(latents),
-        dec_bias_grad.reshape(feature),
+        dec_bias_grad,
         mean_loss,
         errors_own,
     )

time: 70.3 us -> 60.3 us (0.86)
  Pallas kernels: 21.6 us -> 11.7 us
  other arithmetic: 2.47 us -> 0.09 us
  local copies, waits for them, and re-layouts: 4.8 us -> 6.66 us
    pallas_call x5 -> x6, Pallas kernels: 16.3 us -> 8.22 us  [the longest x1 3.25 us: shards(): call(features_kernel, 'features', fast((slots * frames, feature), BF16),...]
    unnamed x33 -> x22, local copies, waits for them, and re-layouts: 4.13 us -> 6.64 us
    pallas_call x1, Pallas kernels: 5.31 us -> 3.45 us  [shards(): call(gradients, 'gradients', (shape((feature, latents), BF16), shape((lat...]
    pallas_call x1 -> x0, other arithmetic: 1.31 us -> none  [shards(): call(gradients, 'gradients', (shape((feature, latents), BF16), shape((lat...]
    convert_element_type x1, other arithmetic: 1.1 us -> 0.07 us  [shards(): small = part.astype(BF16)]
  transfers between devices with their start and end apart: 18 -> 18, of which waited for: 10 -> 12; matrix products, arithmetic and copies ran while one was open for 1% -> 0% of each run, Pallas kernels for 7% -> 2%
where the time goes in v3:
time: 60.3 us; the launch traced here: 59.9 us
  waiting for transfers between devices  22.3 us (37%)
  starting transfers between devices  18.5 us (31%)
  Pallas kernels  11.7 us (19%)
  local copies, waits for them, and re-layouts  6.66 us (11%)
  between operations  0.74 us (1%)
    ppermute x18, waiting for transfers between devices, exchange(): return lax.ppermute(value, 'utt', [(i, i ^ bit) for i in range(devices)])  22.3 us
    ppermute x18, starting transfers between devices, exchange(): return lax.ppermute(value, 'utt', [(i, i ^ bit) for i in range(devices)])  18.5 us
    unnamed x22, local copies, waits for them, and re-layouts  6.64 us
    pallas_call x1, Pallas kernels, shards(): call(gradients, 'gradients', (shape((feature, latents), BF16), shape((lat...  3.45 us
    pallas_call x1, Pallas kernels, shards(): call(features_kernel, 'features', fast((slots * frames, feature), BF16),...  3.25 us
    pallas_call x1, Pallas kernels, shards(): call(encode, 'encode', (fast((half, wide), F32), fast((half, wide), F32),...  3.22 us
  transfers between devices with their start and end apart: 18, of which 12 were waited for; matrix products, arithmetic and copies ran while one was open for 0% of the time, Pallas kernels for 2%

profile of v3, /device:TPU:0, one launch (start us, length us, event | category | flops | bytes accessed | tf_op | source)
XLA Modules:
  0.0 59.9 jit_solution(4562971773703371226)
XLA Ops:
  0.6 2.3 %copy-done.2 = bf16[3,1536,512]{2,1,0:T(8,128)(2,1)S(1)} copy-done((bf16[3,1536,512]{2,1,0:T(8,128)(2,1)S(1)}, bf16[3,1536,512]{2,1,0:T(8,128)(2,1)}, u32[]{:S(2)}) %copy-start.2) | copy-done | bytes 4718616
  3.0 0.9 %copy-done.3 = f32[3,10,512]{2,0,1:T(4,128)S(1)} copy-done((f32[3,10,512]{2,0,1:T(4,128)S(1)}, f32[3,10,512]{2,0,1:T(4,128)}, u32[]{:S(2)}) %copy-start.3) | copy-done | bytes 61464
  3.9 0.7 %copy-done.4 = f32[3,2,512]{2,1,0:T(2,128)S(1)} copy-done((f32[3,2,512]{2,1,0:T(2,128)S(1)}, f32[3,2,512]{2,1,0:T(2,128)}, u32[]{:S(2)}) %copy-start.4) | copy-done | bytes 12312
  7.3 3.2 %features.1.refs_2_ = bf16[16,1536]{1,0:T(8,128)(2,1)S(1)} custom-call(s32[2]{0:T(128)S(1)} %copy-done.9, s32[2]{0:T(128)S(1)} %copy-done.10, f32[2,90]{1,0:T(2,128)S(1)} %copy-done.8, f32[10,3,512]{2,1,0:T(4,128)S(1)} %bitcast.11, f32[3,2,512]{2,1,0:T(2,128)S(1)} %copy-done.4, f32[3,2,512]{2,1,0:T(2,128)S(1)} %copy-done.5, bf16[3,1536,512]{2,1,0:T(8,128)(2,1)S(1)} %copy-done.2), custom_call_target="tpu_custom_call" | custom-call | flops 75497472 | bytes 4718592 | tf_op jit(solution)/shard_map/features/pallas_call | solution.py:354
  10.6 5.1 %collective-permute-start.2 = (bf16[16,1536]{1,0:T(8,128)(2,1)S(1)}, bf16[16,1536]{1,0:T(8,128)(2,1)S(1)}, u32[]{:S(2)}, u32[]{:S(2)}) collective-permute-start(bf16[16,1536]{1,0:T(8,128)(2,1)S(1)} %features.1.refs_2_), channel_id=1, source_target_pairs={{0,12},{1,13},{2,14},{3,15},{4,8},{5,9},{6,10},{7,11},{8,4},{9,5},... | collective-permute-start | bytes 147464 | tf_op jit(solution)/shard_map/ppermute | solution.py:72
  17.0 0.9 %collective-permute-done.2.refs_5_ = bf16[16,1536]{1,0:T(8,128)(2,1)S(1)} collective-permute-done((bf16[16,1536]{1,0:T(8,128)(2,1)S(1)}, bf16[16,1536]{1,0:T(8,128)(2,1)S(1)}, u32[]{:S(2)}, u32[]{:S(2)}) %collective-permute-start.2) | collective-permute-done | bytes 49184 | tf_op jit(solution)/shard_map/ppermute | solution.py:72
  17.9 2.8 %collective-permute-done.1.refs_4_ = bf16[16,1536]{1,0:T(8,128)(2,1)S(1)} collective-permute-done((bf16[16,1536]{1,0:T(8,128)(2,1)S(1)}, bf16[16,1536]{1,0:T(8,128)(2,1)S(1)}, u32[]{:S(2)}, u32[]{:S(2)}) %collective-permute-start.1) | collective-permute-done | bytes 49184 | tf_op jit(solution)/shard_map/ppermute | solution.py:72
  21.4 1.5 %collective-permute-start.3 = (bf16[64,1536]{1,0:T(8,128)(2,1)}, bf16[64,1536]{1,0:T(8,128)(2,1)}, u32[]{:S(2)}, u32[]{:S(2)}) collective-permute-start(bf16[64,1536]{1,0:T(8,128)(2,1)} %join.1.refs_1_), channel_id=1, source_target_pairs={{0,2},{1,3},{2,0},{3,1},{4,6},{5,7},{6,4},{7,5},{8,10},{9,11},{10,... | collective-permute-start | bytes 589832 | tf_op jit(solution)/shard_map/ppermute | solution.py:72
  22.9 4.5 %collective-permute-done.3.refs_2_ = bf16[64,1536]{1,0:T(8,128)(2,1)} collective-permute-done((bf16[64,1536]{1,0:T(8,128)(2,1)}, bf16[64,1536]{1,0:T(8,128)(2,1)}, u32[]{:S(2)}, u32[]{:S(2)}) %collective-permute-start.3) | collective-permute-done | bytes 196640 | tf_op jit(solution)/shard_map/ppermute | solution.py:72
  27.4 1.8 %collective-permute-done.5.refs_4_ = bf16[64,1536]{1,0:T(8,128)(2,1)} collective-permute-done((bf16[64,1536]{1,0:T(8,128)(2,1)}, bf16[64,1536]{1,0:T(8,128)(2,1)}, u32[]{:S(2)}, u32[]{:S(2)}) %collective-permute-start.5) | collective-permute-done | bytes 196640 | tf_op jit(solution)/shard_map/ppermute | solution.py:72
  29.2 3.2 %encode.1 = (f32[64,1664]{1,0:T(8,128)S(1)}, f32[64,1664]{1,0:T(8,128)S(1)}, f32[16,1664]{1,0:T(8,128)S(1)}, bf16[128,1536]{1,0:T(8,128)(2,1)S(1)}, f32[128,512]{1,0:T(8,128)S(1)}) custom-call(s32[1]{0:T(128)} %bitcast.refs_0_, bf16[64,1536]{1,0:T(8,128)(2,1)} %join.1.refs_1_, bf16[64,1536]{1,0:T(8,128)(2,1)} %collective-permute-done.3.refs_2_, ...), custom_call_target="tpu_custom_call" | custom-call | flops 402653184 | bytes 3145728 | tf_op jit(solution)/shard_map/encode/pallas_call | solution.py:401
  32.7 1.6 %collective-permute-done.6 = f32[64,1664]{1,0:T(8,128)S(1)} collective-permute-done((f32[64,1664]{1,0:T(8,128)S(1)}, f32[64,1664]{1,0:T(8,128)S(1)}, u32[]{:S(2)}, u32[]{:S(2)}) %collective-permute-start.6) | collective-permute-done | bytes 426016 | tf_op jit(solution)/shard_map/ppermute | solution.py:72
  34.4 2.1 %collective-permute-start.9 = (bf16[16,1664]{1,0:T(8,128)(2,1)S(1)}, bf16[16,1664]{1,0:T(8,128)(2,1)S(1)}, u32[]{:S(2)}, u32[]{:S(2)}) collective-permute-start(bf16[16,1664]{1,0:T(8,128)(2,1)S(1)} %get-tuple-element.40), channel_id=1, source_target_pairs={{0,12},{1,13},{2,14},{3,15},{4,8},{5,9},{6,10},{7,11},{8,4},{9,5},... | collective-permute-start | bytes 159752 | tf_op jit(solution)/shard_map/ppermute | solution.py:72
  36.6 2.2 %collective-permute-start.7 = (bf16[16,1664]{1,0:T(8,128)(2,1)S(1)}, bf16[16,1664]{1,0:T(8,128)(2,1)S(1)}, u32[]{:S(2)}, u32[]{:S(2)}) collective-permute-start(bf16[16,1664]{1,0:T(8,128)(2,1)S(1)} %get-tuple-element.42), channel_id=1, source_target_pairs={{0,4},{1,5},{2,6},{3,7},{4,0},{5,1},{6,2},{7,3},{8,12},{9,13},{10,... | collective-permute-start | bytes 159752 | tf_op jit(solution)/shard_map/ppermute | solution.py:72
  39.2 1.8 %collective-permute-done.9.refs_4_ = bf16[16,1664]{1,0:T(8,128)(2,1)S(1)} collective-permute-done((bf16[16,1664]{1,0:T(8,128)(2,1)S(1)}, bf16[16,1664]{1,0:T(8,128)(2,1)S(1)}, u32[]{:S(2)}, u32[]{:S(2)}) %collective-permute-start.9) | collective-permute-done | bytes 53280 | tf_op jit(solution)/shard_map/ppermute | solution.py:72
  41.0 1.6 %collective-permute-done.8.refs_3_ = bf16[16,1664]{1,0:T(8,128)(2,1)S(1)} collective-permute-done((bf16[16,1664]{1,0:T(8,128)(2,1)S(1)}, bf16[16,1664]{1,0:T(8,128)(2,1)S(1)}, u32[]{:S(2)}, u32[]{:S(2)}) %collective-permute-start.8) | collective-permute-done | bytes 53280 | tf_op jit(solution)/shard_map/ppermute | solution.py:72
  42.6 1.6 %collective-permute-start.10 = (f32[16,1664]{1,0:T(8,128)S(1)}, f32[16,1664]{1,0:T(8,128)S(1)}, u32[]{:S(2)}, u32[]{:S(2)}) collective-permute-start(f32[16,1664]{1,0:T(8,128)S(1)} %sum.1), channel_id=1, source_target_pairs={{0,2},{1,3},{2,0},{3,1},{4,6},{5,7},{6,4},{7,5},{8,10},{9,11},{10,... | collective-permute-start | bytes 319496 | tf_op jit(solution)/shard_map/ppermute | solution.py:72
  44.2 3.4 %collective-permute-done.10 = f32[16,1664]{1,0:T(8,128)S(1)} collective-permute-done((f32[16,1664]{1,0:T(8,128)S(1)}, f32[16,1664]{1,0:T(8,128)S(1)}, u32[]{:S(2)}, u32[]{:S(2)}) %collective-permute-start.10) | collective-permute-done | bytes 106528 | tf_op jit(solution)/shard_map/ppermute | solution.py:72
  47.6 2.1 %collective-permute-start.13 = (bf16[16,1664]{1,0:T(8,128)(2,1)S(1)}, bf16[16,1664]{1,0:T(8,128)(2,1)S(1)}, u32[]{:S(2)}, u32[]{:S(2)}) collective-permute-start(bf16[16,1664]{1,0:T(8,128)(2,1)S(1)} %fusion.1.refs_0_), channel_id=1, source_target_pairs={{0,12},{1,13},{2,14},{3,15},{4,8},{5,9},{6,10},{7,11},{8,4},{9,5},... | collective-permute-start | bytes 159752 | tf_op jit(solution)/shard_map/ppermute | solution.py:72
  49.8 2.3 %collective-permute-start.11 = (bf16[16,1664]{1,0:T(8,128)(2,1)S(1)}, bf16[16,1664]{1,0:T(8,128)(2,1)S(1)}, u32[]{:S(2)}, u32[]{:S(2)}) collective-permute-start(bf16[16,1664]{1,0:T(8,128)(2,1)S(1)} %fusion.1.refs_0_), channel_id=1, source_target_pairs={{0,4},{1,5},{2,6},{3,7},{4,0},{5,1},{6,2},{7,3},{8,12},{9,13},{10,... | collective-permute-start | bytes 159752 | tf_op jit(solution)/shard_map/ppermute | solution.py:72
  52.1 2.0 %collective-permute-done.13.refs_3_ = bf16[16,1664]{1,0:T(8,128)(2,1)S(1)} collective-permute-done((bf16[16,1664]{1,0:T(8,128)(2,1)S(1)}, bf16[16,1664]{1,0:T(8,128)(2,1)S(1)}, u32[]{:S(2)}, u32[]{:S(2)}) %collective-permute-start.13) | collective-permute-done | bytes 53280 | tf_op jit(solution)/shard_map/ppermute | solution.py:72
  54.0 1.0 %collective-permute-done.12.refs_2_ = bf16[16,1664]{1,0:T(8,128)(2,1)S(1)} collective-permute-done((bf16[16,1664]{1,0:T(8,128)(2,1)S(1)}, bf16[16,1664]{1,0:T(8,128)(2,1)S(1)}, u32[]{:S(2)}, u32[]{:S(2)}) %collective-permute-start.12) | collective-permute-done | bytes 53280 | tf_op jit(solution)/shard_map/ppermute | solution.py:72
  55.6 0.7 %collective-permute-done.16.refs_6_ = bf16[16,1664]{1,0:T(8,128)(2,1)S(1)} collective-permute-done((bf16[16,1664]{1,0:T(8,128)(2,1)S(1)}, bf16[16,1664]{1,0:T(8,128)(2,1)S(1)}, u32[]{:S(2)}, u32[]{:S(2)}) %collective-permute-start.16) | collective-permute-done | bytes 53280 | tf_op jit(solution)/shard_map/ppermute | solution.py:72
  56.5 3.5 %gradients.1 = (bf16[1536,512]{1,0:T(8,128)(2,1)}, bf16[512,1536]{1,0:T(8,128)(2,1)}, f32[1,512]{1,0:T(1,128)}, f32[1536]{0:T(1024)}, f32[1]{0:T(128)}, /*index=5*/bf16[8,1536]{1,0:T(8,128)(2,1)}) custom-call(bf16[16,1664]{1,0:T(8,128)(2,1)S(1)} %fusion.1.refs_0_, bf16[16,1664]{1,0:T(8,128)(2,1)S(1)} %collective-permute-done.11.refs_1_, ...), custom_call_target="tpu_custom_call" | custom-call | flops 603979776 | bytes 6291456 | tf_op jit(solution)/shard_map/gradients/pallas_call | solution.py:463
  (45 shorter events, 6.3 us)
Async XLA Ops:
  0.6 2.3 %copy-start.2 = (bf16[3,1536,512]{2,1,0:T(8,128)(2,1)S(1)}, bf16[3,1536,512]{2,1,0:T(8,128)(2,1)}, u32[]{:S(2)}) copy-start(bf16[3,1536,512]{2,1,0:T(8,128)(2,1)} %second_hbm.1) | copy-start | bytes 14155780
  3.0 0.9 %copy-start.3 = (f32[3,10,512]{2,0,1:T(4,128)S(1)}, f32[3,10,512]{2,0,1:T(4,128)}, u32[]{:S(2)}) copy-start(f32[3,10,512]{2,0,1:T(4,128)} %param.14) | copy-start | bytes 184324
  7.3 9.1 %copy-start = (bf16[512,1536]{1,0:T(8,128)(2,1)S(1)}, bf16[512,1536]{1,0:T(8,128)(2,1)}, u32[]{:S(2)}) copy-start(bf16[512,1536]{1,0:T(8,128)(2,1)} %refs_8_.1) | copy-start | bytes 4718596
  10.5 10.1 %copy-start.1 = (bf16[1536,512]{1,0:T(8,128)(2,1)S(1)}, bf16[1536,512]{1,0:T(8,128)(2,1)}, u32[]{:S(2)}) copy-start(bf16[1536,512]{1,0:T(8,128)(2,1)} %refs_5_.1) | copy-start | bytes 4718596
  10.5 18.7 %copy-start.6 = (f32[1536]{0:T(1024)S(1)}, f32[1536]{0:T(1024)}, u32[]{:S(2)}) copy-start(f32[1536]{0:T(1024)} %refs_9_.1) | copy-start | bytes 18436
  10.5 18.7 %copy-start.7 = (f32[512]{0:T(512)S(1)}, f32[512]{0:T(512)}, u32[]{:S(2)}) copy-start(f32[512]{0:T(512)} %param.19) | copy-start | bytes 6148
  10.6 7.3 %collective-permute-start.2 = (bf16[16,1536]{1,0:T(8,128)(2,1)S(1)}, bf16[16,1536]{1,0:T(8,128)(2,1)S(1)}, u32[]{:S(2)}, u32[]{:S(2)}) collective-permute-start(bf16[16,1536]{1,0:T(8,128)(2,1)S(1)} %features.1.refs_2_), channel_id=1, source_target_pairs={{0,12},{1,13},{2,14},{3,15},{4,8},{5,9},{6,10},{7,11},{8,4},{9,5},... | collective-permute-start | bytes 147464 | tf_op jit(solution)/shard_map/ppermute | solution.py:72
  15.7 5.0 %collective-permute-start.1 = (bf16[16,1536]{1,0:T(8,128)(2,1)S(1)}, bf16[16,1536]{1,0:T(8,128)(2,1)S(1)}, u32[]{:S(2)}, u32[]{:S(2)}) collective-permute-start(bf16[16,1536]{1,0:T(8,128)(2,1)S(1)} %features.1.refs_2_), channel_id=1, source_target_pairs={{0,8},{1,9},{2,10},{3,11},{4,12},{5,13},{6,14},{7,15},{8,0},{9,1},... | collective-permute-start | bytes 147464 | tf_op jit(solution)/shard_map/ppermute | solution.py:72
  15.7 5.0 %collective-permute-start = (bf16[16,1536]{1,0:T(8,128)(2,1)S(1)}, bf16[16,1536]{1,0:T(8,128)(2,1)S(1)}, u32[]{:S(2)}, u32[]{:S(2)}) collective-permute-start(bf16[16,1536]{1,0:T(8,128)(2,1)S(1)} %features.1.refs_2_), channel_id=1, source_target_pairs={{0,4},{1,5},{2,6},{3,7},{4,0},{5,1},{6,2},{7,3},{8,12},{9,13},{10,... | collective-permute-start | bytes 147464 | tf_op jit(solution)/shard_map/ppermute | solution.py:72
  21.4 6.1 %collective-permute-start.3 = (bf16[64,1536]{1,0:T(8,128)(2,1)}, bf16[64,1536]{1,0:T(8,128)(2,1)}, u32[]{:S(2)}, u32[]{:S(2)}) collective-permute-start(bf16[64,1536]{1,0:T(8,128)(2,1)} %join.1.refs_1_), channel_id=1, source_target_pairs={{0,2},{1,3},{2,0},{3,1},{4,6},{5,7},{6,4},{7,5},{8,10},{9,11},{10,... | collective-permute-start | bytes 589832 | tf_op jit(solution)/shard_map/ppermute | solution.py:72
  22.9 4.6 %collective-permute-start.4 = (bf16[64,1536]{1,0:T(8,128)(2,1)}, bf16[64,1536]{1,0:T(8,128)(2,1)}, u32[]{:S(2)}, u32[]{:S(2)}) collective-permute-start(bf16[64,1536]{1,0:T(8,128)(2,1)} %join.1.refs_1_), channel_id=1, source_target_pairs={{0,1},{1,0},{2,3},{3,2},{4,5},{5,4},{6,7},{7,6},{8,9},{9,8},{10,11... | collective-permute-start | bytes 589832 | tf_op jit(solution)/shard_map/ppermute | solution.py:72
  27.4 1.8 %collective-permute-start.5 = (bf16[64,1536]{1,0:T(8,128)(2,1)}, bf16[64,1536]{1,0:T(8,128)(2,1)}, u32[]{:S(2)}, u32[]{:S(2)}) collective-permute-start(bf16[64,1536]{1,0:T(8,128)(2,1)} %collective-permute-done.3.refs_2_), channel_id=1, source_target_pairs={{0,1},{1,0},{2,3},{3,2},{4,5},{5,4},{6,7},{7,6},{8,9},{9,8},{10,11... | collective-permute-start | bytes 589832 | tf_op jit(solution)/shard_map/ppermute | solution.py:72
  32.5 1.8 %collective-permute-start.6 = (f32[64,1664]{1,0:T(8,128)S(1)}, f32[64,1664]{1,0:T(8,128)S(1)}, u32[]{:S(2)}, u32[]{:S(2)}) collective-permute-start(f32[64,1664]{1,0:T(8,128)S(1)} %get-tuple-element.28), channel_id=1, source_target_pairs={{0,1},{1,0},{2,3},{3,2},{4,5},{5,4},{6,7},{7,6},{8,9},{9,8},{10,11... | collective-permute-start | bytes 1277960 | tf_op jit(solution)/shard_map/ppermute | solution.py:72
  34.4 6.6 %collective-permute-start.9 = (bf16[16,1664]{1,0:T(8,128)(2,1)S(1)}, bf16[16,1664]{1,0:T(8,128)(2,1)S(1)}, u32[]{:S(2)}, u32[]{:S(2)}) collective-permute-start(bf16[16,1664]{1,0:T(8,128)(2,1)S(1)} %get-tuple-element.40), channel_id=1, source_target_pairs={{0,12},{1,13},{2,14},{3,15},{4,8},{5,9},{6,10},{7,11},{8,4},{9,5},... | collective-permute-start | bytes 159752 | tf_op jit(solution)/shard_map/ppermute | solution.py:72
  36.5 6.1 %collective-permute-start.8 = (bf16[16,1664]{1,0:T(8,128)(2,1)S(1)}, bf16[16,1664]{1,0:T(8,128)(2,1)S(1)}, u32[]{:S(2)}, u32[]{:S(2)}) collective-permute-start(bf16[16,1664]{1,0:T(8,128)(2,1)S(1)} %get-tuple-element.41), channel_id=1, source_target_pairs={{0,8},{1,9},{2,10},{3,11},{4,12},{5,13},{6,14},{7,15},{8,0},{9,1},... | collective-permute-start | bytes 159752 | tf_op jit(solution)/shard_map/ppermute | solution.py:72
  36.6 6.0 %collective-permute-start.7 = (bf16[16,1664]{1,0:T(8,128)(2,1)S(1)}, bf16[16,1664]{1,0:T(8,128)(2,1)S(1)}, u32[]{:S(2)}, u32[]{:S(2)}) collective-permute-start(bf16[16,1664]{1,0:T(8,128)(2,1)S(1)} %get-tuple-element.42), channel_id=1, source_target_pairs={{0,4},{1,5},{2,6},{3,7},{4,0},{5,1},{6,2},{7,3},{8,12},{9,13},{10,... | collective-permute-start | bytes 159752 | tf_op jit(solution)/shard_map/ppermute | solution.py:72
  42.6 5.0 %collective-permute-start.10 = (f32[16,1664]{1,0:T(8,128)S(1)}, f32[16,1664]{1,0:T(8,128)S(1)}, u32[]{:S(2)}, u32[]{:S(2)}) collective-permute-start(f32[16,1664]{1,0:T(8,128)S(1)} %sum.1), channel_id=1, source_target_pairs={{0,2},{1,3},{2,0},{3,1},{4,6},{5,7},{6,4},{7,5},{8,10},{9,11},{10,... | collective-permute-start | bytes 319496 | tf_op jit(solution)/shard_map/ppermute | solution.py:72
  47.6 6.4 %collective-permute-start.13 = (bf16[16,1664]{1,0:T(8,128)(2,1)S(1)}, bf16[16,1664]{1,0:T(8,128)(2,1)S(1)}, u32[]{:S(2)}, u32[]{:S(2)}) collective-permute-start(bf16[16,1664]{1,0:T(8,128)(2,1)S(1)} %fusion.1.refs_0_), channel_id=1, source_target_pairs={{0,12},{1,13},{2,14},{3,15},{4,8},{5,9},{6,10},{7,11},{8,4},{9,5},... | collective-permute-start | bytes 159752 | tf_op jit(solution)/shard_map/ppermute | solution.py:72
  49.7 5.3 %collective-permute-start.12 = (bf16[16,1664]{1,0:T(8,128)(2,1)S(1)}, bf16[16,1664]{1,0:T(8,128)(2,1)S(1)}, u32[]{:S(2)}, u32[]{:S(2)}) collective-permute-start(bf16[16,1664]{1,0:T(8,128)(2,1)S(1)} %fusion.1.refs_0_), channel_id=1, source_target_pairs={{0,8},{1,9},{2,10},{3,11},{4,12},{5,13},{6,14},{7,15},{8,0},{9,1},... | collective-permute-start | bytes 159752 | tf_op jit(solution)/shard_map/ppermute | solution.py:72
  49.8 5.3 %collective-permute-start.11 = (bf16[16,1664]{1,0:T(8,128)(2,1)S(1)}, bf16[16,1664]{1,0:T(8,128)(2,1)S(1)}, u32[]{:S(2)}, u32[]{:S(2)}) collective-permute-start(bf16[16,1664]{1,0:T(8,128)(2,1)S(1)} %fusion.1.refs_0_), channel_id=1, source_target_pairs={{0,4},{1,5},{2,6},{3,7},{4,0},{5,1},{6,2},{7,3},{8,12},{9,13},{10,... | collective-permute-start | bytes 159752 | tf_op jit(solution)/shard_map/ppermute | solution.py:72
  52.1 3.5 %collective-permute-start.14 = (bf16[16,1664]{1,0:T(8,128)(2,1)S(1)}, bf16[16,1664]{1,0:T(8,128)(2,1)S(1)}, u32[]{:S(2)}, u32[]{:S(2)}) collective-permute-start(bf16[16,1664]{1,0:T(8,128)(2,1)S(1)} %fusion.1.refs_0_), channel_id=1, source_target_pairs={{0,1},{1,0},{2,3},{3,2},{4,5},{5,4},{6,7},{7,6},{8,9},{9,8},{10,11... | collective-permute-start | bytes 159752 | tf_op jit(solution)/shard_map/ppermute | solution.py:72
  54.0 1.6 %collective-permute-start.17 = (bf16[16,1664]{1,0:T(8,128)(2,1)S(1)}, bf16[16,1664]{1,0:T(8,128)(2,1)S(1)}, u32[]{:S(2)}, u32[]{:S(2)}) collective-permute-start(bf16[16,1664]{1,0:T(8,128)(2,1)S(1)} %collective-permute-done.13.refs_3_), channel_id=1, source_target_pairs={{0,1},{1,0},{2,3},{3,2},{4,5},{5,4},{6,7},{7,6},{8,9},{9,8},{10,11... | collective-permute-start | bytes 159752 | tf_op jit(solution)/shard_map/ppermute | solution.py:72
  55.1 1.2 %collective-permute-start.16 = (bf16[16,1664]{1,0:T(8,128)(2,1)S(1)}, bf16[16,1664]{1,0:T(8,128)(2,1)S(1)}, u32[]{:S(2)}, u32[]{:S(2)}) collective-permute-start(bf16[16,1664]{1,0:T(8,128)(2,1)S(1)} %collective-permute-done.12.refs_2_), channel_id=1, source_target_pairs={{0,1},{1,0},{2,3},{3,2},{4,5},{5,4},{6,7},{7,6},{8,9},{9,8},{10,11... | collective-permute-start | bytes 159752 | tf_op jit(solution)/shard_map/ppermute | solution.py:72
  55.1 1.4 %collective-permute-start.15 = (bf16[16,1664]{1,0:T(8,128)(2,1)S(1)}, bf16[16,1664]{1,0:T(8,128)(2,1)S(1)}, u32[]{:S(2)}, u32[]{:S(2)}) collective-permute-start(bf16[16,1664]{1,0:T(8,128)(2,1)S(1)} %collective-permute-done.11.refs_1_), channel_id=1, source_target_pairs={{0,1},{1,0},{2,3},{3,2},{4,5},{5,4},{6,7},{7,6},{8,9},{9,8},{10,11... | collective-permute-start | bytes 159752 | tf_op jit(solution)/shard_map/ppermute | solution.py:72
  (5 other events, 3.4 us)

commit v4 on v3

--- a/solution.py
+++ b/solution.py
@@ -111,14 +111,21 @@
     return jax.ShapeDtypeStruct(dims, kind)
 
 
-def features_kernel(length, take, wave, first_w, gain, shift, second_hbm, out, second_w, sems):
+def features_kernel(*refs):
+    sources, out, held, second_w, sems, more = refs[:7], refs[7], refs[8:14], refs[14], refs[15], refs[16]
+    small = [pltpu.make_async_copy(sources[i], held[i], sems.at[i]) for i in range(6)]
+    for copy in small:
+        copy.start()
+    length, take, wave, first_w, gain, shift = held
     taps_first, checkpoints, channels = first_w.shape
     slots, samples = wave.shape
     frames = out.shape[0] // slots
     copies = []
     for c in range(checkpoints):
-        copies.append(pltpu.make_async_copy(second_hbm.at[c], second_w.at[c], sems.at[c]))
+        copies.append(pltpu.make_async_copy(sources[6].at[c], second_w.at[c], more.at[c]))
         copies[-1].start()
+    for copy in small:
+        copy.wait()
     lane = iota((frames, samples), 1)
     start = iota((frames, samples), 0) * 10
     columns = []
@@ -168,7 +175,7 @@
 def join_kernel(*refs):
     out = refs[-1]
     at = 0
-    for ref in refs[2:-1]:
+    for ref in refs[1:-1]:
         out[at : at + ref.shape[0], :] = ref[...]
         at += ref.shape[0]
 
@@ -211,7 +218,7 @@
     kinds = iota(takes.shape, 0) & (slots - 1)
     r = iota((tokens, 1), 0) >> log2(ROWS_DEV)
     holder = (
-        ((r >> log2(inner)) & (outer - 1)) * step + (r & (inner - 1)) * 2 + (r >> log2(outer * inner))
+        (r & (outer - 1)) * step + ((r >> log2(outer)) & (inner - 1)) * 2 + (r >> log2(outer * inner))
     )
     token = (me ^ holder) * ROWS_DEV + (iota((tokens, 1), 0) & (ROWS_DEV - 1))
     lane = iota((1, rows), 1)
@@ -262,17 +269,25 @@
 
 
 def sum_kernel(*refs):
-    total = refs[1][...]
-    for ref in refs[2:-1]:
-        total = total + ref[...].astype(F32)
-    refs[-1][...] = total
-
-
-def gradients_kernel(count, inner, cells, *refs):
+    shift, parts, out, own = refs[1], refs[2:-2], refs[-2], refs[-1]
+    wide = [part[...].astype(F32) for part in parts]
+    blocks = []
+    for p in range(len(parts)):
+        terms = []
+        for k in range(len(parts)):
+            at = (p ^ k) * ROWS_DEV
+            terms.append(wide[k][at : at + ROWS_DEV])
+        blocks.append(tree(terms))
+    errors = (jnp.concatenate(blocks, axis=0) + shift[...]).astype(BF16)
+    out[...] = errors
+    own[...] = errors[:ROWS_DEV, : own.shape[1]]
+
+
+def gradients_kernel(count, outer, cells, *refs):
     pieces = refs[:count]
     dec, weights_sum, inputs_t, latent_t, latent, scale = refs[count : count + 6]
-    enc_out, dec_out, enc_bias_out, dec_bias_out, loss_out, errors_out = refs[count + 6 : count + 12]
-    enc_buf, dec_buf, sems = refs[count + 12 :]
+    enc_out, dec_out, enc_bias_out, dec_bias_out, loss_out = refs[count + 6 : count + 11]
+    enc_buf, dec_buf, sems = refs[count + 11 :]
     latents, feature = dec.shape
     channels = 512
     errors = jnp.concatenate([piece[:, :feature] for piece in pieces], axis=0)
@@ -302,12 +317,11 @@
         enc_buf[at] = grad.astype(BF16)
         copies.append(pltpu.make_async_copy(enc_buf.at[at], enc_out.at[at], sems.at[parts + i]))
         copies[-1].start()
-    errors_out[...] = pieces[0][:ROWS_DEV, :feature]
     wide = [piece[...].astype(F32) for piece in pieces]
     plain = tree(wide)
     squares = tree([w[:, :feature] * w[:, :feature] for w in wide])
-    plain = tree([plain[i * ROWS_DEV : (i + 1) * ROWS_DEV] for i in range(inner)])
-    squares = tree([squares[i * ROWS_DEV : (i + 1) * ROWS_DEV] for i in range(inner)])
+    plain = tree([plain[i * ROWS_DEV : (i + 1) * ROWS_DEV] for i in range(outer)])
+    squares = tree([squares[i * ROWS_DEV : (i + 1) * ROWS_DEV] for i in range(outer)])
     dec_bias_out[...] = 2.0 * jnp.sum(plain[:, :feature], axis=0)
     loss = jnp.sum(squares) + sparsity * jnp.sum(plain[:, feature:])
     loss_out[0] = loss / cells
@@ -348,6 +362,10 @@
     def near(value):
         return pltpu.with_memory_space_constraint(value, pltpu.VMEM) if pinned else value
 
+    def far(value):
+        return pltpu.with_memory_space_constraint(value, pltpu.HBM)
+
+    kernels = conv_first.transpose(1, 0, 2)
     encoder = near(enc_weight)
     decoder = near(dec_weight)
 
@@ -355,12 +373,27 @@
         features_kernel,
         "features",
         fast((slots * frames, feature), BF16),
-        [smem(), smem(), vmem(), vmem(), vmem(), vmem(), pl.BlockSpec(memory_space=pl.ANY)],
+        [pl.BlockSpec(memory_space=pl.ANY)] * 7,
         vmem(),
-        [pltpu.VMEM(conv_second.shape, BF16), pltpu.SemaphoreType.DMA((checkpoints,))],
+        [
+            pltpu.SMEM(lengths.shape, jnp.int32),
+            pltpu.SMEM(take_list.shape, jnp.int32),
+            pltpu.VMEM(waveforms.shape, F32),
+            pltpu.VMEM(kernels.shape, F32),
+            pltpu.VMEM(norm_gain.shape, F32),
+            pltpu.VMEM(norm_shift.shape, F32),
+            pltpu.VMEM(conv_second.shape, BF16),
+            pltpu.SemaphoreType.DMA((6,)),
+            pltpu.SemaphoreType.DMA((checkpoints,)),
+        ],
         flops=2 * slots * frames * feature * 3 * channels,
         moved=2 * conv_second.size,
-    )(lengths, take_list, waveforms, conv_first.transpose(1, 0, 2), norm_gain, norm_shift, conv_second)
+    )(
+        *[
+            far(value)
+            for value in (lengths, take_list, waveforms, kernels, norm_gain, norm_shift, conv_second)
+        ]
+    )
 
     norms, weights_sum = call(
         norms_kernel,
@@ -378,10 +411,10 @@
             join_kernel,
             "join",
             fast((outer * slots * frames, feature), BF16),
-            [pl.BlockSpec(memory_space=pl.ANY)] * 2 + [vmem()] * outer,
+            [pl.BlockSpec(memory_space=pl.ANY)] + [vmem()] * outer,
             vmem(),
             moved=4 * outer * slots * frames * feature,
-        )(near(norms), encoder, *[near(block) for block in blocks])
+        )(near(norms), *[near(block) for block in blocks])
     ]
     rel = [0]
     bit = 2
@@ -393,7 +426,7 @@
     rel += [r ^ 1 for r in rel]
 
     half = tokens // 2
-    chunk = half // outer
+    chunk = half // inner
 
     def encode(*refs):
         encode_kernel(len(pieces), outer, inner, slots, frames, rel, *refs)
@@ -434,33 +467,31 @@
 
     part = own + exchange(send, 1)
     small = part.astype(BF16)
-    blocks = [part[:chunk]]
-    for k in range(1, outer):
-        blocks.append(exchange(small[k * chunk : (k + 1) * chunk], step * k))
-    part = call(
+    total = part[:chunk]
+    for k in range(1, inner):
+        total = total + exchange(small[k * chunk : (k + 1) * chunk], 2 * k).astype(F32)
+    total = total.astype(BF16)
+    blocks = [total] + [exchange(total, step * k) for k in range(1, outer)]
+    errors, errors_own = call(
         sum_kernel,
         "sum",
-        fast((chunk, wide), F32),
-        [pl.BlockSpec(memory_space=pl.ANY)] + [vmem()] * outer,
-        vmem(),
+        (fast((chunk, wide), BF16), shape((ROWS_DEV, feature), BF16)),
+        [pl.BlockSpec(memory_space=pl.ANY)] + [vmem()] * (1 + outer),
+        (vmem(), vmem()),
         moved=8 * chunk * wide,
-    )(near(scale), *[near(block) for block in blocks])
-    rows = chunk // inner
+    )(near(scale), near(shift), *[near(block) for block in blocks])
+    blocks = [errors]
     bit = 2
     while bit < step:
-        width = (bit // 2) * rows
-        other = exchange(part, bit).reshape(-1, 2, width, wide)
-        part = part + other[:, ::-1].reshape(chunk, wide)
+        blocks += [exchange(block, bit) for block in blocks]
         bit *= 2
-    errors = (part + shift).astype(BF16)
-    blocks = [errors] + [exchange(errors, step * k) for k in range(1, outer)]
     blocks += [exchange(block, 1) for block in blocks]
 
     def gradients(*refs):
-        gradients_kernel(len(blocks), inner, float(tokens * feature), *refs)
+        gradients_kernel(len(blocks), outer, float(tokens * feature), *refs)
 
     any_space = pl.BlockSpec(memory_space=pl.ANY)
-    enc_grad, dec_grad, enc_bias_grad, dec_bias_grad, mean_loss, errors_own = call(
+    enc_grad, dec_grad, enc_bias_grad, dec_bias_grad, mean_loss = call(
         gradients,
         "gradients",
         (
@@ -469,10 +500,9 @@
             shape((1, latents), F32),
             shape((feature,), F32),
             shape((1,), F32),
-            shape((ROWS_DEV, feature), BF16),
         ),
         [vmem()] * (len(blocks) + 6),
-        (any_space, any_space, vmem(), vmem(), smem(), vmem()),
+        (any_space, any_space, vmem(), vmem(), smem()),
         [
             pltpu.VMEM((feature, latents), BF16),
             pltpu.VMEM((latents, feature), BF16),

time: 60.3 us -> 55.8 us (0.925)
  local copies, waits for them, and re-layouts: 6.66 us -> 0.04 us
  waiting for transfers between devices: 22.3 us -> 26.6 us
  starting transfers between devices: 18.5 us -> 15 us
  Pallas kernels: 11.7 us -> 13.3 us
    unnamed x22 -> x8, local copies, waits for them, and re-layouts: 6.64 us -> 0.02 us
    ppermute x18 -> x14, waiting for transfers between devices: 22.3 us -> 26.6 us  [exchange(): return lax.ppermute(value, 'utt', [(i, i ^ bit) for i in range(devices)])]
    ppermute x18 -> x14, starting transfers between devices: 18.5 us -> 15 us  [exchange(): return lax.ppermute(value, 'utt', [(i, i ^ bit) for i in range(devices)])]
    pallas_call x1, Pallas kernels: 3.25 us -> 4.29 us  [shards(): call(features_kernel, 'features', fast((slots * frames, feature), BF16),...]
    pallas_call x1, Pallas kernels: 0.03 us -> 0.64 us  [shards(): call(sum_kernel, 'sum', (fast((chunk, wide), BF16), shape((ROWS_DEV, feat...]
  transfers between devices with their start and end apart: 18 -> 14, of which waited for: 12 -> 10; matrix products, arithmetic and copies ran while one was open for 0% -> 0% of each run, Pallas kernels for 2% -> 2%
where the time goes in v4:
time: 55.8 us; the launch traced here: 55.7 us
  waiting for transfers between devices  26.6 us (48%)
  starting transfers between devices  15 us (27%)
  Pallas kernels  13.3 us (24%)
  between operations  0.72 us (1%)
    ppermute x14, waiting for transfers between devices, exchange(): return lax.ppermute(value, 'utt', [(i, i ^ bit) for i in range(devices)])  26.6 us
    ppermute x14, starting transfers between devices, exchange(): return lax.ppermute(value, 'utt', [(i, i ^ bit) for i in range(devices)])  15 us
    pallas_call x1, Pallas kernels, shards(): call(features_kernel, 'features', fast((slots * frames, feature), BF16),...  4.29 us
    pallas_call x1, Pallas kernels, shards(): call(gradients, 'gradients', (shape((feature, latents), BF16), shape((lat...  3.38 us
    pallas_call x1, Pallas kernels, shards(): call(encode, 'encode', (fast((half, wide), F32), fast((half, wide), F32),...  3.23 us
  transfers between devices with their start and end apart: 14, of which 10 were waited for; matrix products, arithmetic and copies ran while one was open for 0% of the time, Pallas kernels for 2%

profile of v4, /device:TPU:0, one launch (start us, length us, event | category | flops | bytes accessed | tf_op | source)
XLA Modules:
  0.0 55.7 jit_solution(6505663210545498723)
XLA Ops:
  0.6 4.3 %features.1.refs_1_ = bf16[16,1536]{1,0:T(8,128)(2,1)S(1)} custom-call(s32[2]{0:T(128)} %refs_0_.1, s32[2]{0:T(128)} %refs_1_.1, f32[2,90]{1,0:T(2,128)} %refs_2_.1, f32[10,3,512]{2,1,0:T(4,128)} %bitcast.5, f32[3,2,512]{2,1,0:T(2,128)} %refs_4_.2, f32[3,2,512]{2,1,0:T(2,128)} %refs_5_.2, bf16[3,1536,512]{2,1,0:T(8,128)(2,1)} %refs_6_.1), custom_call_target="tpu_custom_call" | custom-call | flops 75497472 | bytes 4718592 | tf_op jit(solution)/shard_map/features/pallas_call | solution.py:372
  5.0 5.1 %collective-permute-start.2 = (bf16[16,1536]{1,0:T(8,128)(2,1)S(1)}, bf16[16,1536]{1,0:T(8,128)(2,1)S(1)}, u32[]{:S(2)}, u32[]{:S(2)}) collective-permute-start(bf16[16,1536]{1,0:T(8,128)(2,1)S(1)} %features.1.refs_1_), channel_id=1, source_target_pairs={{0,12},{1,13},{2,14},{3,15},{4,8},{5,9},{6,10},{7,11},{8,4},{9,5},... | collective-permute-start | bytes 147464 | tf_op jit(solution)/shard_map/ppermute | solution.py:72
  10.1 0.6 %collective-permute-start = (bf16[16,1536]{1,0:T(8,128)(2,1)S(1)}, bf16[16,1536]{1,0:T(8,128)(2,1)S(1)}, u32[]{:S(2)}, u32[]{:S(2)}) collective-permute-start(bf16[16,1536]{1,0:T(8,128)(2,1)S(1)} %features.1.refs_1_), channel_id=1, source_target_pairs={{0,4},{1,5},{2,6},{3,7},{4,0},{5,1},{6,2},{7,3},{8,12},{9,13},{10,... | collective-permute-start | bytes 147464 | tf_op jit(solution)/shard_map/ppermute | solution.py:72
  10.7 0.7 %norms.1 = (f32[512,128]{1,0:T(8,128)S(1)}, f32[8,512]{1,0:T(8,128)S(1)}) custom-call(bf16[512,1536]{1,0:T(8,128)(2,1)S(1)} %copy-done), custom_call_target="tpu_custom_call" | custom-call | flops 3145728 | bytes 1572864 | tf_op jit(solution)/shard_map/norms/pallas_call | solution.py:398
  11.4 0.9 %collective-permute-done.2.refs_4_ = bf16[16,1536]{1,0:T(8,128)(2,1)S(1)} collective-permute-done((bf16[16,1536]{1,0:T(8,128)(2,1)S(1)}, bf16[16,1536]{1,0:T(8,128)(2,1)S(1)}, u32[]{:S(2)}, u32[]{:S(2)}) %collective-permute-start.2) | collective-permute-done | bytes 49184 | tf_op jit(solution)/shard_map/ppermute | solution.py:72
  12.3 2.8 %collective-permute-done.1.refs_3_ = bf16[16,1536]{1,0:T(8,128)(2,1)S(1)} collective-permute-done((bf16[16,1536]{1,0:T(8,128)(2,1)S(1)}, bf16[16,1536]{1,0:T(8,128)(2,1)S(1)}, u32[]{:S(2)}, u32[]{:S(2)}) %collective-permute-start.1) | collective-permute-done | bytes 49184 | tf_op jit(solution)/shard_map/ppermute | solution.py:72
  15.1 0.7 %join.1.refs_1_ = bf16[64,1536]{1,0:T(8,128)(2,1)} custom-call(f32[512,128]{1,0:T(8,128)S(1)} %get-tuple-element.23.refs_0_.norms, bf16[16,1536]{1,0:T(8,128)(2,1)S(1)} %features.1.refs_1_, bf16[16,1536]{1,0:T(8,128)(2,1)S(1)} %collective-permute-done.refs_2_, bf16[16,1536]{1,0:T(8,128)(2,1)S(1)} %collective-permute-done.1.refs_3_, ...), custom_call_target="tpu_custom_call" | custom-call | bytes 393216 | tf_op jit(solution)/shard_map/join/pallas_call | solution.py:410
  15.8 1.5 %collective-permute-start.3 = (bf16[64,1536]{1,0:T(8,128)(2,1)}, bf16[64,1536]{1,0:T(8,128)(2,1)}, u32[]{:S(2)}, u32[]{:S(2)}) collective-permute-start(bf16[64,1536]{1,0:T(8,128)(2,1)} %join.1.refs_1_), channel_id=1, source_target_pairs={{0,2},{1,3},{2,0},{3,1},{4,6},{5,7},{6,4},{7,5},{8,10},{9,11},{10,... | collective-permute-start | bytes 589832 | tf_op jit(solution)/shard_map/ppermute | solution.py:72
  17.3 4.5 %collective-permute-done.3.refs_2_ = bf16[64,1536]{1,0:T(8,128)(2,1)} collective-permute-done((bf16[64,1536]{1,0:T(8,128)(2,1)}, bf16[64,1536]{1,0:T(8,128)(2,1)}, u32[]{:S(2)}, u32[]{:S(2)}) %collective-permute-start.3) | collective-permute-done | bytes 196640 | tf_op jit(solution)/shard_map/ppermute | solution.py:72
  21.9 1.8 %collective-permute-done.5.refs_4_ = bf16[64,1536]{1,0:T(8,128)(2,1)} collective-permute-done((bf16[64,1536]{1,0:T(8,128)(2,1)}, bf16[64,1536]{1,0:T(8,128)(2,1)}, u32[]{:S(2)}, u32[]{:S(2)}) %collective-permute-start.5) | collective-permute-done | bytes 196640 | tf_op jit(solution)/shard_map/ppermute | solution.py:72
  23.6 3.2 %encode.1 = (f32[64,1664]{1,0:T(8,128)S(1)}, f32[64,1664]{1,0:T(8,128)S(1)}, f32[32,1664]{1,0:T(8,128)S(1)}, bf16[128,1536]{1,0:T(8,128)(2,1)S(1)}, f32[128,512]{1,0:T(8,128)S(1)}) custom-call(s32[1]{0:T(128)} %bitcast.refs_0_, bf16[64,1536]{1,0:T(8,128)(2,1)} %join.1.refs_1_, bf16[64,1536]{1,0:T(8,128)(2,1)} %collective-permute-done.3.refs_2_, ...), custom_call_target="tpu_custom_call" | custom-call | flops 402653184 | bytes 3145728 | tf_op jit(solution)/shard_map/encode/pallas_call | solution.py:434
  27.1 1.6 %collective-permute-done.6 = f32[64,1664]{1,0:T(8,128)S(1)} collective-permute-done((f32[64,1664]{1,0:T(8,128)S(1)}, f32[64,1664]{1,0:T(8,128)S(1)}, u32[]{:S(2)}, u32[]{:S(2)}) %collective-permute-start.6) | collective-permute-done | bytes 426016 | tf_op jit(solution)/shard_map/ppermute | solution.py:72
  28.8 1.6 %collective-permute-start.7 = (bf16[32,1664]{1,0:T(8,128)(2,1)S(1)}, bf16[32,1664]{1,0:T(8,128)(2,1)S(1)}, u32[]{:S(2)}, u32[]{:S(2)}) collective-permute-start(bf16[32,1664]{1,0:T(8,128)(2,1)S(1)} %slice.14), channel_id=1, source_target_pairs={{0,2},{1,3},{2,0},{3,1},{4,6},{5,7},{6,4},{7,5},{8,10},{9,11},{10,... | collective-permute-start | bytes 319496 | tf_op jit(solution)/shard_map/ppermute | solution.py:72
  30.4 3.5 %collective-permute-done.7 = bf16[32,1664]{1,0:T(8,128)(2,1)S(1)} collective-permute-done((bf16[32,1664]{1,0:T(8,128)(2,1)S(1)}, bf16[32,1664]{1,0:T(8,128)(2,1)S(1)}, u32[]{:S(2)}, u32[]{:S(2)}) %collective-permute-start.7) | collective-permute-done | bytes 106528 | tf_op jit(solution)/shard_map/ppermute | solution.py:72
  33.9 2.1 %collective-permute-start.10 = (bf16[32,1664]{1,0:T(8,128)(2,1)S(1)}, bf16[32,1664]{1,0:T(8,128)(2,1)S(1)}, u32[]{:S(2)}, u32[]{:S(2)}) collective-permute-start(bf16[32,1664]{1,0:T(8,128)(2,1)S(1)} %fusion.refs_2_), channel_id=1, source_target_pairs={{0,12},{1,13},{2,14},{3,15},{4,8},{5,9},{6,10},{7,11},{8,4},{9,5},... | collective-permute-start | bytes 319496 | tf_op jit(solution)/shard_map/ppermute | solution.py:72
  36.1 2.2 %collective-permute-start.8 = (bf16[32,1664]{1,0:T(8,128)(2,1)S(1)}, bf16[32,1664]{1,0:T(8,128)(2,1)S(1)}, u32[]{:S(2)}, u32[]{:S(2)}) collective-permute-start(bf16[32,1664]{1,0:T(8,128)(2,1)S(1)} %fusion.refs_2_), channel_id=1, source_target_pairs={{0,4},{1,5},{2,6},{3,7},{4,0},{5,1},{6,2},{7,3},{8,12},{9,13},{10,... | collective-permute-start | bytes 319496 | tf_op jit(solution)/shard_map/ppermute | solution.py:72
  38.3 0.3 turn.1
  38.7 3.0 %collective-permute-done.10.refs_5_ = bf16[32,1664]{1,0:T(8,128)(2,1)S(1)} collective-permute-done((bf16[32,1664]{1,0:T(8,128)(2,1)S(1)}, bf16[32,1664]{1,0:T(8,128)(2,1)S(1)}, u32[]{:S(2)}, u32[]{:S(2)}) %collective-permute-start.10) | collective-permute-done | bytes 106528 | tf_op jit(solution)/shard_map/ppermute | solution.py:72
  41.7 3.9 %collective-permute-done.9.refs_4_ = bf16[32,1664]{1,0:T(8,128)(2,1)S(1)} collective-permute-done((bf16[32,1664]{1,0:T(8,128)(2,1)S(1)}, bf16[32,1664]{1,0:T(8,128)(2,1)S(1)}, u32[]{:S(2)}, u32[]{:S(2)}) %collective-permute-start.9) | collective-permute-done | bytes 106528 | tf_op jit(solution)/shard_map/ppermute | solution.py:72
  45.6 0.6 %sum.1 = (bf16[32,1664]{1,0:T(8,128)(2,1)S(1)}, bf16[8,1536]{1,0:T(8,128)(2,1)}) custom-call(f32[512,128]{1,0:T(8,128)S(1)} %get-tuple-element.27.refs_0_.refs_9_, f32[32,1664]{1,0:T(8,128)S(1)} %get-tuple-element.28.refs_1_, bf16[32,1664]{1,0:T(8,128)(2,1)S(1)} %fusion.refs_2_, bf16[32,1664]{1,0:T(8,128)(2,1)S(1)} %collective-permute-done.8.refs_3_, ...), custom_call_target="tpu_custom_call" | custom-call | bytes 425984 | tf_op jit(solution)/shard_map/sum/pallas_call | solution.py:475
  46.3 1.5 %collective-permute-start.11 = (bf16[32,1664]{1,0:T(8,128)(2,1)S(1)}, bf16[32,1664]{1,0:T(8,128)(2,1)S(1)}, u32[]{:S(2)}, u32[]{:S(2)}) collective-permute-start(bf16[32,1664]{1,0:T(8,128)(2,1)S(1)} %get-tuple-element.31.refs_0_), channel_id=1, source_target_pairs={{0,2},{1,3},{2,0},{3,1},{4,6},{5,7},{6,4},{7,5},{8,10},{9,11},{10,... | collective-permute-start | bytes 319496 | tf_op jit(solution)/shard_map/ppermute | solution.py:72
  47.8 3.2 %collective-permute-done.11.refs_1_ = bf16[32,1664]{1,0:T(8,128)(2,1)S(1)} collective-permute-done((bf16[32,1664]{1,0:T(8,128)(2,1)S(1)}, bf16[32,1664]{1,0:T(8,128)(2,1)S(1)}, u32[]{:S(2)}, u32[]{:S(2)}) %collective-permute-start.11) | collective-permute-done | bytes 106528 | tf_op jit(solution)/shard_map/ppermute | solution.py:72
  51.0 1.3 %collective-permute-done.13.refs_3_ = bf16[32,1664]{1,0:T(8,128)(2,1)S(1)} collective-permute-done((bf16[32,1664]{1,0:T(8,128)(2,1)S(1)}, bf16[32,1664]{1,0:T(8,128)(2,1)S(1)}, u32[]{:S(2)}, u32[]{:S(2)}) %collective-permute-start.13) | collective-permute-done | bytes 106528 | tf_op jit(solution)/shard_map/ppermute | solution.py:72
  52.3 3.4 %gradients.1 = (bf16[1536,512]{1,0:T(8,128)(2,1)}, bf16[512,1536]{1,0:T(8,128)(2,1)}, f32[1,512]{1,0:T(1,128)}, f32[1536]{0:T(1024)}, f32[1]{0:T(128)}) custom-call(bf16[32,1664]{1,0:T(8,128)(2,1)S(1)} %get-tuple-element.31.refs_0_, bf16[32,1664]{1,0:T(8,128)(2,1)S(1)} %collective-permute-done.11.refs_1_, ...), custom_call_target="tpu_custom_call" | custom-call | flops 603979776 | bytes 6291456 | tf_op jit(solution)/shard_map/gradients/pallas_call | solution.py:494
  (22 shorter events, 0.5 us)
Async XLA Ops:
  0.6 10.1 %copy-start = (bf16[512,1536]{1,0:T(8,128)(2,1)S(1)}, bf16[512,1536]{1,0:T(8,128)(2,1)}, u32[]{:S(2)}) copy-start(bf16[512,1536]{1,0:T(8,128)(2,1)} %refs_4_.3) | copy-start | bytes 4718596
  4.9 18.7 %copy-start.1 = (bf16[1536,512]{1,0:T(8,128)(2,1)S(1)}, bf16[1536,512]{1,0:T(8,128)(2,1)}, u32[]{:S(2)}) copy-start(bf16[1536,512]{1,0:T(8,128)(2,1)} %refs_5_.3) | copy-start | bytes 4718596
  5.0 18.7 %copy-start.2 = (f32[1536]{0:T(1024)S(1)}, f32[1536]{0:T(1024)}, u32[]{:S(2)}) copy-start(f32[1536]{0:T(1024)} %refs_9_.1) | copy-start | bytes 18436
  5.0 18.7 %copy-start.3 = (f32[512]{0:T(512)S(1)}, f32[512]{0:T(512)}, u32[]{:S(2)}) copy-start(f32[512]{0:T(512)} %param.19) | copy-start | bytes 6148
  5.0 7.3 %collective-permute-start.2 = (bf16[16,1536]{1,0:T(8,128)(2,1)S(1)}, bf16[16,1536]{1,0:T(8,128)(2,1)S(1)}, u32[]{:S(2)}, u32[]{:S(2)}) collective-permute-start(bf16[16,1536]{1,0:T(8,128)(2,1)S(1)} %features.1.refs_1_), channel_id=1, source_target_pairs={{0,12},{1,13},{2,14},{3,15},{4,8},{5,9},{6,10},{7,11},{8,4},{9,5},... | collective-permute-start | bytes 147464 | tf_op jit(solution)/shard_map/ppermute | solution.py:72
  10.1 5.0 %collective-permute-start.1 = (bf16[16,1536]{1,0:T(8,128)(2,1)S(1)}, bf16[16,1536]{1,0:T(8,128)(2,1)S(1)}, u32[]{:S(2)}, u32[]{:S(2)}) collective-permute-start(bf16[16,1536]{1,0:T(8,128)(2,1)S(1)} %features.1.refs_1_), channel_id=1, source_target_pairs={{0,8},{1,9},{2,10},{3,11},{4,12},{5,13},{6,14},{7,15},{8,0},{9,1},... | collective-permute-start | bytes 147464 | tf_op jit(solution)/shard_map/ppermute | solution.py:72
  10.1 5.0 %collective-permute-start = (bf16[16,1536]{1,0:T(8,128)(2,1)S(1)}, bf16[16,1536]{1,0:T(8,128)(2,1)S(1)}, u32[]{:S(2)}, u32[]{:S(2)}) collective-permute-start(bf16[16,1536]{1,0:T(8,128)(2,1)S(1)} %features.1.refs_1_), channel_id=1, source_target_pairs={{0,4},{1,5},{2,6},{3,7},{4,0},{5,1},{6,2},{7,3},{8,12},{9,13},{10,... | collective-permute-start | bytes 147464 | tf_op jit(solution)/shard_map/ppermute | solution.py:72
  15.8 6.1 %collective-permute-start.3 = (bf16[64,1536]{1,0:T(8,128)(2,1)}, bf16[64,1536]{1,0:T(8,128)(2,1)}, u32[]{:S(2)}, u32[]{:S(2)}) collective-permute-start(bf16[64,1536]{1,0:T(8,128)(2,1)} %join.1.refs_1_), channel_id=1, source_target_pairs={{0,2},{1,3},{2,0},{3,1},{4,6},{5,7},{6,4},{7,5},{8,10},{9,11},{10,... | collective-permute-start | bytes 589832 | tf_op jit(solution)/shard_map/ppermute | solution.py:72
  17.3 4.6 %collective-permute-start.4 = (bf16[64,1536]{1,0:T(8,128)(2,1)}, bf16[64,1536]{1,0:T(8,128)(2,1)}, u32[]{:S(2)}, u32[]{:S(2)}) collective-permute-start(bf16[64,1536]{1,0:T(8,128)(2,1)} %join.1.refs_1_), channel_id=1, source_target_pairs={{0,1},{1,0},{2,3},{3,2},{4,5},{5,4},{6,7},{7,6},{8,9},{9,8},{10,11... | collective-permute-start | bytes 589832 | tf_op jit(solution)/shard_map/ppermute | solution.py:72
  21.8 1.8 %collective-permute-start.5 = (bf16[64,1536]{1,0:T(8,128)(2,1)}, bf16[64,1536]{1,0:T(8,128)(2,1)}, u32[]{:S(2)}, u32[]{:S(2)}) collective-permute-start(bf16[64,1536]{1,0:T(8,128)(2,1)} %collective-permute-done.3.refs_2_), channel_id=1, source_target_pairs={{0,1},{1,0},{2,3},{3,2},{4,5},{5,4},{6,7},{7,6},{8,9},{9,8},{10,11... | collective-permute-start | bytes 589832 | tf_op jit(solution)/shard_map/ppermute | solution.py:72
  26.9 1.8 %collective-permute-start.6 = (f32[64,1664]{1,0:T(8,128)S(1)}, f32[64,1664]{1,0:T(8,128)S(1)}, u32[]{:S(2)}, u32[]{:S(2)}) collective-permute-start(f32[64,1664]{1,0:T(8,128)S(1)} %get-tuple-element.30), channel_id=1, source_target_pairs={{0,1},{1,0},{2,3},{3,2},{4,5},{5,4},{6,7},{7,6},{8,9},{9,8},{10,11... | collective-permute-start | bytes 1277960 | tf_op jit(solution)/shard_map/ppermute | solution.py:72
  28.8 5.1 %collective-permute-start.7 = (bf16[32,1664]{1,0:T(8,128)(2,1)S(1)}, bf16[32,1664]{1,0:T(8,128)(2,1)S(1)}, u32[]{:S(2)}, u32[]{:S(2)}) collective-permute-start(bf16[32,1664]{1,0:T(8,128)(2,1)S(1)} %slice.14), channel_id=1, source_target_pairs={{0,2},{1,3},{2,0},{3,1},{4,6},{5,7},{6,4},{7,5},{8,10},{9,11},{10,... | collective-permute-start | bytes 319496 | tf_op jit(solution)/shard_map/ppermute | solution.py:72
  33.9 7.8 %collective-permute-start.10 = (bf16[32,1664]{1,0:T(8,128)(2,1)S(1)}, bf16[32,1664]{1,0:T(8,128)(2,1)S(1)}, u32[]{:S(2)}, u32[]{:S(2)}) collective-permute-start(bf16[32,1664]{1,0:T(8,128)(2,1)S(1)} %fusion.refs_2_), channel_id=1, source_target_pairs={{0,12},{1,13},{2,14},{3,15},{4,8},{5,9},{6,10},{7,11},{8,4},{9,5},... | collective-permute-start | bytes 319496 | tf_op jit(solution)/shard_map/ppermute | solution.py:72
  36.0 9.7 %collective-permute-start.9 = (bf16[32,1664]{1,0:T(8,128)(2,1)S(1)}, bf16[32,1664]{1,0:T(8,128)(2,1)S(1)}, u32[]{:S(2)}, u32[]{:S(2)}) collective-permute-start(bf16[32,1664]{1,0:T(8,128)(2,1)S(1)} %fusion.refs_2_), channel_id=1, source_target_pairs={{0,8},{1,9},{2,10},{3,11},{4,12},{5,13},{6,14},{7,15},{8,0},{9,1},... | collective-permute-start | bytes 319496 | tf_op jit(solution)/shard_map/ppermute | solution.py:72
  36.1 9.5 %collective-permute-start.8 = (bf16[32,1664]{1,0:T(8,128)(2,1)S(1)}, bf16[32,1664]{1,0:T(8,128)(2,1)S(1)}, u32[]{:S(2)}, u32[]{:S(2)}) collective-permute-start(bf16[32,1664]{1,0:T(8,128)(2,1)S(1)} %fusion.refs_2_), channel_id=1, source_target_pairs={{0,4},{1,5},{2,6},{3,7},{4,0},{5,1},{6,2},{7,3},{8,12},{9,13},{10,... | collective-permute-start | bytes 319496 | tf_op jit(solution)/shard_map/ppermute | solution.py:72
  46.3 4.7 %collective-permute-start.11 = (bf16[32,1664]{1,0:T(8,128)(2,1)S(1)}, bf16[32,1664]{1,0:T(8,128)(2,1)S(1)}, u32[]{:S(2)}, u32[]{:S(2)}) collective-permute-start(bf16[32,1664]{1,0:T(8,128)(2,1)S(1)} %get-tuple-element.31.refs_0_), channel_id=1, source_target_pairs={{0,2},{1,3},{2,0},{3,1},{4,6},{5,7},{6,4},{7,5},{8,10},{9,11},{10,... | collective-permute-start | bytes 319496 | tf_op jit(solution)/shard_map/ppermute | solution.py:72
  47.8 3.2 %collective-permute-start.12 = (bf16[32,1664]{1,0:T(8,128)(2,1)S(1)}, bf16[32,1664]{1,0:T(8,128)(2,1)S(1)}, u32[]{:S(2)}, u32[]{:S(2)}) collective-permute-start(bf16[32,1664]{1,0:T(8,128)(2,1)S(1)} %get-tuple-element.31.refs_0_), channel_id=1, source_target_pairs={{0,1},{1,0},{2,3},{3,2},{4,5},{5,4},{6,7},{7,6},{8,9},{9,8},{10,11... | collective-permute-start | bytes 319496 | tf_op jit(solution)/shard_map/ppermute | solution.py:72
  51.0 1.3 %collective-permute-start.13 = (bf16[32,1664]{1,0:T(8,128)(2,1)S(1)}, bf16[32,1664]{1,0:T(8,128)(2,1)S(1)}, u32[]{:S(2)}, u32[]{:S(2)}) collective-permute-start(bf16[32,1664]{1,0:T(8,128)(2,1)S(1)} %collective-permute-done.11.refs_1_), channel_id=1, source_target_pairs={{0,1},{1,0},{2,3},{3,2},{4,5},{5,4},{6,7},{7,6},{8,9},{9,8},{10,11... | collective-permute-start | bytes 319496 | tf_op jit(solution)/shard_map/ppermute | solution.py:72

commit v5 on v3

--- a/solution.py
+++ b/solution.py
@@ -111,14 +111,21 @@
     return jax.ShapeDtypeStruct(dims, kind)
 
 
-def features_kernel(length, take, wave, first_w, gain, shift, second_hbm, out, second_w, sems):
+def features_kernel(*refs):
+    sources, out, held, second_w, sems, more = refs[:7], refs[7], refs[8:14], refs[14], refs[15], refs[16]
+    small = [pltpu.make_async_copy(sources[i], held[i], sems.at[i]) for i in range(6)]
+    for copy in small:
+        copy.start()
+    length, take, wave, first_w, gain, shift = held
     taps_first, checkpoints, channels = first_w.shape
     slots, samples = wave.shape
     frames = out.shape[0] // slots
     copies = []
     for c in range(checkpoints):
-        copies.append(pltpu.make_async_copy(second_hbm.at[c], second_w.at[c], sems.at[c]))
+        copies.append(pltpu.make_async_copy(sources[6].at[c], second_w.at[c], more.at[c]))
         copies[-1].start()
+    for copy in small:
+        copy.wait()
     lane = iota((frames, samples), 1)
     start = iota((frames, samples), 0) * 10
     columns = []
@@ -136,39 +143,52 @@
         )
         for k in range(taps_first)
     ]
-    hidden = []
-    for c in range(checkpoints):
+
+    def layer_one(c):
         total = taps[0] * first_w[0, c : c + 1, :]
         for k in range(1, taps_first):
             total = total + taps[k] * first_w[k, c : c + 1, :]
-        total = normalize(total, gain[c, 0:1, :], shift[c, 0:1, :])
-        hidden.append(gelu(total).astype(BF16))
+        return gelu(normalize(total, gain[c, 0:1, :], shift[c, 0:1, :])).astype(BF16)
+
     rows = slots * frames
-    for c in range(checkpoints):
-        copies[c].wait()
+
+    def layer_two(c, hidden):
         total = jnp.zeros((rows, channels), F32)
         for tap in range(3):
             total = total + jnp.dot(
-                hidden[c][tap * rows : (tap + 1) * rows],
+                hidden[tap * rows : (tap + 1) * rows],
                 second_w[c, tap * channels : (tap + 1) * channels, :],
                 preferred_element_type=F32,
             )
+        return total
+
+    def finish(c, total):
         total = gelu(normalize(total, gain[c, 1:2, :], shift[c, 1:2, :]))
         if c == 0:
             spot = iota((rows, channels), 1)
             line = iota((rows, channels), 0)
             for s in range(slots):
-                note = jnp.where(
-                    spot == 0, length[s].astype(F32), take[s].astype(F32)
-                )
+                note = jnp.where(spot == 0, length[s].astype(F32), take[s].astype(F32))
                 total = jnp.where(line == (s + 1) * frames - 1, note, total)
         out[:, c * channels : (c + 1) * channels] = total.astype(BF16)
+
+    hidden = layer_one(0)
+    held_back = None
+    for c in range(checkpoints):
+        copies[c].wait()
+        total = layer_two(c, hidden)
+        if c + 1 < checkpoints:
+            hidden = layer_one(c + 1)
+        if held_back is not None:
+            finish(c - 1, held_back)
+        held_back = total
+    finish(checkpoints - 1, held_back)
 
 
 def join_kernel(*refs):
     out = refs[-1]
     at = 0
-    for ref in refs[2:-1]:
+    for ref in refs[1:-1]:
         out[at : at + ref.shape[0], :] = ref[...]
         at += ref.shape[0]
 
@@ -265,7 +285,7 @@
     total = refs[1][...]
     for ref in refs[2:-1]:
         total = total + ref[...].astype(F32)
-    refs[-1][...] = total
+    refs[-1][...] = total.astype(BF16)
 
 
 def gradients_kernel(count, inner, cells, *refs):
@@ -348,6 +368,10 @@
     def near(value):
         return pltpu.with_memory_space_constraint(value, pltpu.VMEM) if pinned else value
 
+    def far(value):
+        return pltpu.with_memory_space_constraint(value, pltpu.HBM)
+
+    kernels = conv_first.transpose(1, 0, 2)
     encoder = near(enc_weight)
     decoder = near(dec_weight)
 
@@ -355,12 +379,27 @@
         features_kernel,
         "features",
         fast((slots * frames, feature), BF16),
-        [smem(), smem(), vmem(), vmem(), vmem(), vmem(), pl.BlockSpec(memory_space=pl.ANY)],
+        [pl.BlockSpec(memory_space=pl.ANY)] * 7,
         vmem(),
-        [pltpu.VMEM(conv_second.shape, BF16), pltpu.SemaphoreType.DMA((checkpoints,))],
+        [
+            pltpu.SMEM(lengths.shape, jnp.int32),
+            pltpu.SMEM(take_list.shape, jnp.int32),
+            pltpu.VMEM(waveforms.shape, F32),
+            pltpu.VMEM(kernels.shape, F32),
+            pltpu.VMEM(norm_gain.shape, F32),
+            pltpu.VMEM(norm_shift.shape, F32),
+            pltpu.VMEM(conv_second.shape, BF16),
+            pltpu.SemaphoreType.DMA((6,)),
+            pltpu.SemaphoreType.DMA((checkpoints,)),
+        ],
         flops=2 * slots * frames * feature * 3 * channels,
         moved=2 * conv_second.size,
-    )(lengths, take_list, waveforms, conv_first.transpose(1, 0, 2), norm_gain, norm_shift, conv_second)
+    )(
+        *[
+            far(value)
+            for value in (lengths, take_list, waveforms, kernels, norm_gain, norm_shift, conv_second)
+        ]
+    )
 
     norms, weights_sum = call(
         norms_kernel,
@@ -378,10 +417,10 @@
             join_kernel,
             "join",
             fast((outer * slots * frames, feature), BF16),
-            [pl.BlockSpec(memory_space=pl.ANY)] * 2 + [vmem()] * outer,
+            [pl.BlockSpec(memory_space=pl.ANY)] + [vmem()] * outer,
             vmem(),
             moved=4 * outer * slots * frames * feature,
-        )(near(norms), encoder, *[near(block) for block in blocks])
+        )(near(norms), *[near(block) for block in blocks])
     ]
     rel = [0]
     bit = 2
@@ -437,20 +476,20 @@
     blocks = [part[:chunk]]
     for k in range(1, outer):
         blocks.append(exchange(small[k * chunk : (k + 1) * chunk], step * k))
-    part = call(
+    total = call(
         sum_kernel,
         "sum",
-        fast((chunk, wide), F32),
+        fast((chunk, wide), BF16),
         [pl.BlockSpec(memory_space=pl.ANY)] + [vmem()] * outer,
         vmem(),
         moved=8 * chunk * wide,
     )(near(scale), *[near(block) for block in blocks])
-    rows = chunk // inner
     bit = 2
     while bit < step:
-        width = (bit // 2) * rows
-        other = exchange(part, bit).reshape(-1, 2, width, wide)
-        part = part + other[:, ::-1].reshape(chunk, wide)
+        width = (bit // 2) * ROWS_DEV
+        other = exchange(total, bit).astype(F32).reshape(-1, 2, width, wide)
+        part = total.astype(F32) + other[:, ::-1].reshape(chunk, wide)
+        total = part.astype(BF16)
         bit *= 2
     errors = (part + shift).astype(BF16)
     blocks = [errors] + [exchange(errors, step * k) for k in range(1, outer)]

time: 60.3 us -> 53.2 us (0.88)
  local copies, waits for them, and re-layouts: 6.66 us -> 0.05 us
    unnamed x22 -> x8, local copies, waits for them, and re-layouts: 6.64 us -> 0.02 us
where the time goes in v5:
time: 53.2 us; the launch traced here: 53.1 us
  waiting for transfers between devices  21.7 us (41%)
  starting transfers between devices  18.5 us (35%)
  Pallas kernels  12 us (23%)
  between operations  0.74 us (1%)
    ppermute x18, waiting for transfers between devices, exchange(): return lax.ppermute(value, 'utt', [(i, i ^ bit) for i in range(devices)])  21.7 us
    ppermute x18, starting transfers between devices, exchange(): return lax.ppermute(value, 'utt', [(i, i ^ bit) for i in range(devices)])  18.5 us
    pallas_call x1, Pallas kernels, shards(): call(features_kernel, 'features', fast((slots * frames, feature), BF16),...  3.64 us
    pallas_call x1, Pallas kernels, shards(): call(gradients, 'gradients', (shape((feature, latents), BF16), shape((lat...  3.42 us
    pallas_call x1, Pallas kernels, shards(): call(encode, 'encode', (fast((half, wide), F32), fast((half, wide), F32),...  3.22 us
  transfers between devices with their start and end apart: 18, of which 12 were waited for; matrix products, arithmetic and copies ran while one was open for 0% of the time, Pallas kernels for 2%

profile of v5, /device:TPU:0, one launch (start us, length us, event | category | flops | bytes accessed | tf_op | source)
XLA Modules:
  0.0 53.1 jit_solution(9264083393381265885)
XLA Ops:
  0.6 3.6 %features.1.refs_1_ = bf16[16,1536]{1,0:T(8,128)(2,1)S(1)} custom-call(s32[2]{0:T(128)} %refs_0_.1, s32[2]{0:T(128)} %refs_1_.1, f32[2,90]{1,0:T(2,128)} %refs_2_.1, f32[10,3,512]{2,1,0:T(4,128)} %bitcast.14, f32[3,2,512]{2,1,0:T(2,128)} %refs_4_.1, f32[3,2,512]{2,1,0:T(2,128)} %refs_5_.2, bf16[3,1536,512]{2,1,0:T(8,128)(2,1)} %refs_6_.1), custom_call_target="tpu_custom_call" | custom-call | flops 75497472 | bytes 4718592 | tf_op jit(solution)/shard_map/features/pallas_call | solution.py:378
  4.3 5.1 %collective-permute-start.2 = (bf16[16,1536]{1,0:T(8,128)(2,1)S(1)}, bf16[16,1536]{1,0:T(8,128)(2,1)S(1)}, u32[]{:S(2)}, u32[]{:S(2)}) collective-permute-start(bf16[16,1536]{1,0:T(8,128)(2,1)S(1)} %features.1.refs_1_), channel_id=1, source_target_pairs={{0,12},{1,13},{2,14},{3,15},{4,8},{5,9},{6,10},{7,11},{8,4},{9,5},... | collective-permute-start | bytes 147464 | tf_op jit(solution)/shard_map/ppermute | solution.py:72
  9.5 0.6 %collective-permute-start = (bf16[16,1536]{1,0:T(8,128)(2,1)S(1)}, bf16[16,1536]{1,0:T(8,128)(2,1)S(1)}, u32[]{:S(2)}, u32[]{:S(2)}) collective-permute-start(bf16[16,1536]{1,0:T(8,128)(2,1)S(1)} %features.1.refs_1_), channel_id=1, source_target_pairs={{0,4},{1,5},{2,6},{3,7},{4,0},{5,1},{6,2},{7,3},{8,12},{9,13},{10,... | collective-permute-start | bytes 147464 | tf_op jit(solution)/shard_map/ppermute | solution.py:72
  10.1 0.7 %norms.1 = (f32[512,128]{1,0:T(8,128)S(1)}, f32[8,512]{1,0:T(8,128)S(1)}) custom-call(bf16[512,1536]{1,0:T(8,128)(2,1)S(1)} %copy-done), custom_call_target="tpu_custom_call" | custom-call | flops 3145728 | bytes 1572864 | tf_op jit(solution)/shard_map/norms/pallas_call | solution.py:404
  10.8 0.9 %collective-permute-done.2.refs_4_ = bf16[16,1536]{1,0:T(8,128)(2,1)S(1)} collective-permute-done((bf16[16,1536]{1,0:T(8,128)(2,1)S(1)}, bf16[16,1536]{1,0:T(8,128)(2,1)S(1)}, u32[]{:S(2)}, u32[]{:S(2)}) %collective-permute-start.2) | collective-permute-done | bytes 49184 | tf_op jit(solution)/shard_map/ppermute | solution.py:72
  11.7 2.8 %collective-permute-done.1.refs_3_ = bf16[16,1536]{1,0:T(8,128)(2,1)S(1)} collective-permute-done((bf16[16,1536]{1,0:T(8,128)(2,1)S(1)}, bf16[16,1536]{1,0:T(8,128)(2,1)S(1)}, u32[]{:S(2)}, u32[]{:S(2)}) %collective-permute-start.1) | collective-permute-done | bytes 49184 | tf_op jit(solution)/shard_map/ppermute | solution.py:72
  14.4 0.7 %join.1.refs_1_ = bf16[64,1536]{1,0:T(8,128)(2,1)} custom-call(f32[512,128]{1,0:T(8,128)S(1)} %get-tuple-element.22.refs_0_.norms, bf16[16,1536]{1,0:T(8,128)(2,1)S(1)} %features.1.refs_1_, bf16[16,1536]{1,0:T(8,128)(2,1)S(1)} %collective-permute-done.refs_2_, bf16[16,1536]{1,0:T(8,128)(2,1)S(1)} %collective-permute-done.1.refs_3_, ...), custom_call_target="tpu_custom_call" | custom-call | bytes 393216 | tf_op jit(solution)/shard_map/join/pallas_call | solution.py:416
  15.1 1.5 %collective-permute-start.3 = (bf16[64,1536]{1,0:T(8,128)(2,1)}, bf16[64,1536]{1,0:T(8,128)(2,1)}, u32[]{:S(2)}, u32[]{:S(2)}) collective-permute-start(bf16[64,1536]{1,0:T(8,128)(2,1)} %join.1.refs_1_), channel_id=1, source_target_pairs={{0,2},{1,3},{2,0},{3,1},{4,6},{5,7},{6,4},{7,5},{8,10},{9,11},{10,... | collective-permute-start | bytes 589832 | tf_op jit(solution)/shard_map/ppermute | solution.py:72
  16.7 4.5 %collective-permute-done.3.refs_2_ = bf16[64,1536]{1,0:T(8,128)(2,1)} collective-permute-done((bf16[64,1536]{1,0:T(8,128)(2,1)}, bf16[64,1536]{1,0:T(8,128)(2,1)}, u32[]{:S(2)}, u32[]{:S(2)}) %collective-permute-start.3) | collective-permute-done | bytes 196640 | tf_op jit(solution)/shard_map/ppermute | solution.py:72
  21.2 1.8 %collective-permute-done.5.refs_4_ = bf16[64,1536]{1,0:T(8,128)(2,1)} collective-permute-done((bf16[64,1536]{1,0:T(8,128)(2,1)}, bf16[64,1536]{1,0:T(8,128)(2,1)}, u32[]{:S(2)}, u32[]{:S(2)}) %collective-permute-start.5) | collective-permute-done | bytes 196640 | tf_op jit(solution)/shard_map/ppermute | solution.py:72
  23.0 3.2 %encode.1 = (f32[64,1664]{1,0:T(8,128)S(1)}, f32[64,1664]{1,0:T(8,128)S(1)}, f32[16,1664]{1,0:T(8,128)S(1)}, bf16[128,1536]{1,0:T(8,128)(2,1)S(1)}, f32[128,512]{1,0:T(8,128)S(1)}) custom-call(s32[1]{0:T(128)} %bitcast.refs_0_, bf16[64,1536]{1,0:T(8,128)(2,1)} %join.1.refs_1_, bf16[64,1536]{1,0:T(8,128)(2,1)} %collective-permute-done.3.refs_2_, ...), custom_call_target="tpu_custom_call" | custom-call | flops 402653184 | bytes 3145728 | tf_op jit(solution)/shard_map/encode/pallas_call | solution.py:440
  26.4 1.6 %collective-permute-done.6 = f32[64,1664]{1,0:T(8,128)S(1)} collective-permute-done((f32[64,1664]{1,0:T(8,128)S(1)}, f32[64,1664]{1,0:T(8,128)S(1)}, u32[]{:S(2)}, u32[]{:S(2)}) %collective-permute-start.6) | collective-permute-done | bytes 426016 | tf_op jit(solution)/shard_map/ppermute | solution.py:72
  28.1 2.1 %collective-permute-start.9 = (bf16[16,1664]{1,0:T(8,128)(2,1)S(1)}, bf16[16,1664]{1,0:T(8,128)(2,1)S(1)}, u32[]{:S(2)}, u32[]{:S(2)}) collective-permute-start(bf16[16,1664]{1,0:T(8,128)(2,1)S(1)} %get-tuple-element.40), channel_id=1, source_target_pairs={{0,12},{1,13},{2,14},{3,15},{4,8},{5,9},{6,10},{7,11},{8,4},{9,5},... | collective-permute-start | bytes 159752 | tf_op jit(solution)/shard_map/ppermute | solution.py:72
  30.4 2.2 %collective-permute-start.7 = (bf16[16,1664]{1,0:T(8,128)(2,1)S(1)}, bf16[16,1664]{1,0:T(8,128)(2,1)S(1)}, u32[]{:S(2)}, u32[]{:S(2)}) collective-permute-start(bf16[16,1664]{1,0:T(8,128)(2,1)S(1)} %get-tuple-element.42), channel_id=1, source_target_pairs={{0,4},{1,5},{2,6},{3,7},{4,0},{5,1},{6,2},{7,3},{8,12},{9,13},{10,... | collective-permute-start | bytes 159752 | tf_op jit(solution)/shard_map/ppermute | solution.py:72
  32.9 1.8 %collective-permute-done.9.refs_4_ = bf16[16,1664]{1,0:T(8,128)(2,1)S(1)} collective-permute-done((bf16[16,1664]{1,0:T(8,128)(2,1)S(1)}, bf16[16,1664]{1,0:T(8,128)(2,1)S(1)}, u32[]{:S(2)}, u32[]{:S(2)}) %collective-permute-start.9) | collective-permute-done | bytes 53280 | tf_op jit(solution)/shard_map/ppermute | solution.py:72
  34.8 1.6 %collective-permute-done.8.refs_3_ = bf16[16,1664]{1,0:T(8,128)(2,1)S(1)} collective-permute-done((bf16[16,1664]{1,0:T(8,128)(2,1)S(1)}, bf16[16,1664]{1,0:T(8,128)(2,1)S(1)}, u32[]{:S(2)}, u32[]{:S(2)}) %collective-permute-start.8) | collective-permute-done | bytes 53280 | tf_op jit(solution)/shard_map/ppermute | solution.py:72
  36.4 1.6 %collective-permute-start.10 = (bf16[16,1664]{1,0:T(8,128)(2,1)S(1)}, bf16[16,1664]{1,0:T(8,128)(2,1)S(1)}, u32[]{:S(2)}, u32[]{:S(2)}) collective-permute-start(bf16[16,1664]{1,0:T(8,128)(2,1)S(1)} %sum.1), channel_id=1, source_target_pairs={{0,2},{1,3},{2,0},{3,1},{4,6},{5,7},{6,4},{7,5},{8,10},{9,11},{10,... | collective-permute-start | bytes 159752 | tf_op jit(solution)/shard_map/ppermute | solution.py:72
  38.0 2.6 %collective-permute-done.10 = bf16[16,1664]{1,0:T(8,128)(2,1)S(1)} collective-permute-done((bf16[16,1664]{1,0:T(8,128)(2,1)S(1)}, bf16[16,1664]{1,0:T(8,128)(2,1)S(1)}, u32[]{:S(2)}, u32[]{:S(2)}) %collective-permute-start.10) | collective-permute-done | bytes 53280 | tf_op jit(solution)/shard_map/ppermute | solution.py:72
  40.6 2.3 %collective-permute-start.13 = (bf16[16,1664]{1,0:T(8,128)(2,1)S(1)}, bf16[16,1664]{1,0:T(8,128)(2,1)S(1)}, u32[]{:S(2)}, u32[]{:S(2)}) collective-permute-start(bf16[16,1664]{1,0:T(8,128)(2,1)S(1)} %fusion.1.refs_0_), channel_id=1, source_target_pairs={{0,12},{1,13},{2,14},{3,15},{4,8},{5,9},{6,10},{7,11},{8,4},{9,5},... | collective-permute-start | bytes 159752 | tf_op jit(solution)/shard_map/ppermute | solution.py:72
  43.0 2.1 %collective-permute-start.11 = (bf16[16,1664]{1,0:T(8,128)(2,1)S(1)}, bf16[16,1664]{1,0:T(8,128)(2,1)S(1)}, u32[]{:S(2)}, u32[]{:S(2)}) collective-permute-start(bf16[16,1664]{1,0:T(8,128)(2,1)S(1)} %fusion.1.refs_0_), channel_id=1, source_target_pairs={{0,4},{1,5},{2,6},{3,7},{4,0},{5,1},{6,2},{7,3},{8,12},{9,13},{10,... | collective-permute-start | bytes 159752 | tf_op jit(solution)/shard_map/ppermute | solution.py:72
  45.1 2.0 %collective-permute-done.13.refs_3_ = bf16[16,1664]{1,0:T(8,128)(2,1)S(1)} collective-permute-done((bf16[16,1664]{1,0:T(8,128)(2,1)S(1)}, bf16[16,1664]{1,0:T(8,128)(2,1)S(1)}, u32[]{:S(2)}, u32[]{:S(2)}) %collective-permute-start.13) | collective-permute-done | bytes 53280 | tf_op jit(solution)/shard_map/ppermute | solution.py:72
  47.1 1.1 %collective-permute-done.12.refs_2_ = bf16[16,1664]{1,0:T(8,128)(2,1)S(1)} collective-permute-done((bf16[16,1664]{1,0:T(8,128)(2,1)S(1)}, bf16[16,1664]{1,0:T(8,128)(2,1)S(1)}, u32[]{:S(2)}, u32[]{:S(2)}) %collective-permute-start.12) | collective-permute-done | bytes 53280 | tf_op jit(solution)/shard_map/ppermute | solution.py:72
  48.8 0.7 %collective-permute-done.16.refs_6_ = bf16[16,1664]{1,0:T(8,128)(2,1)S(1)} collective-permute-done((bf16[16,1664]{1,0:T(8,128)(2,1)S(1)}, bf16[16,1664]{1,0:T(8,128)(2,1)S(1)}, u32[]{:S(2)}, u32[]{:S(2)}) %collective-permute-start.16) | collective-permute-done | bytes 53280 | tf_op jit(solution)/shard_map/ppermute | solution.py:72
  49.7 3.4 %gradients.1 = (bf16[1536,512]{1,0:T(8,128)(2,1)}, bf16[512,1536]{1,0:T(8,128)(2,1)}, f32[1,512]{1,0:T(1,128)}, f32[1536]{0:T(1024)}, f32[1]{0:T(128)}, /*index=5*/bf16[8,1536]{1,0:T(8,128)(2,1)}) custom-call(bf16[16,1664]{1,0:T(8,128)(2,1)S(1)} %fusion.1.refs_0_, bf16[16,1664]{1,0:T(8,128)(2,1)S(1)} %collective-permute-done.11.refs_1_, ...), custom_call_target="tpu_custom_call" | custom-call | flops 603979776 | bytes 6291456 | tf_op jit(solution)/shard_map/gradients/pallas_call | solution.py:502
  (32 shorter events, 1.6 us)
Async XLA Ops:
  0.6 9.5 %copy-start = (bf16[512,1536]{1,0:T(8,128)(2,1)S(1)}, bf16[512,1536]{1,0:T(8,128)(2,1)}, u32[]{:S(2)}) copy-start(bf16[512,1536]{1,0:T(8,128)(2,1)} %refs_8_.1) | copy-start | bytes 4718596
  4.3 18.7 %copy-start.1 = (bf16[1536,512]{1,0:T(8,128)(2,1)S(1)}, bf16[1536,512]{1,0:T(8,128)(2,1)}, u32[]{:S(2)}) copy-start(bf16[1536,512]{1,0:T(8,128)(2,1)} %refs_5_.3) | copy-start | bytes 4718596
  4.3 18.7 %copy-start.2 = (f32[1536]{0:T(1024)S(1)}, f32[1536]{0:T(1024)}, u32[]{:S(2)}) copy-start(f32[1536]{0:T(1024)} %refs_9_.1) | copy-start | bytes 18436
  4.3 18.7 %copy-start.3 = (f32[512]{0:T(512)S(1)}, f32[512]{0:T(512)}, u32[]{:S(2)}) copy-start(f32[512]{0:T(512)} %param.19) | copy-start | bytes 6148
  4.3 7.3 %collective-permute-start.2 = (bf16[16,1536]{1,0:T(8,128)(2,1)S(1)}, bf16[16,1536]{1,0:T(8,128)(2,1)S(1)}, u32[]{:S(2)}, u32[]{:S(2)}) collective-permute-start(bf16[16,1536]{1,0:T(8,128)(2,1)S(1)} %features.1.refs_1_), channel_id=1, source_target_pairs={{0,12},{1,13},{2,14},{3,15},{4,8},{5,9},{6,10},{7,11},{8,4},{9,5},... | collective-permute-start | bytes 147464 | tf_op jit(solution)/shard_map/ppermute | solution.py:72
  9.4 5.0 %collective-permute-start.1 = (bf16[16,1536]{1,0:T(8,128)(2,1)S(1)}, bf16[16,1536]{1,0:T(8,128)(2,1)S(1)}, u32[]{:S(2)}, u32[]{:S(2)}) collective-permute-start(bf16[16,1536]{1,0:T(8,128)(2,1)S(1)} %features.1.refs_1_), channel_id=1, source_target_pairs={{0,8},{1,9},{2,10},{3,11},{4,12},{5,13},{6,14},{7,15},{8,0},{9,1},... | collective-permute-start | bytes 147464 | tf_op jit(solution)/shard_map/ppermute | solution.py:72
  9.5 5.0 %collective-permute-start = (bf16[16,1536]{1,0:T(8,128)(2,1)S(1)}, bf16[16,1536]{1,0:T(8,128)(2,1)S(1)}, u32[]{:S(2)}, u32[]{:S(2)}) collective-permute-start(bf16[16,1536]{1,0:T(8,128)(2,1)S(1)} %features.1.refs_1_), channel_id=1, source_target_pairs={{0,4},{1,5},{2,6},{3,7},{4,0},{5,1},{6,2},{7,3},{8,12},{9,13},{10,... | collective-permute-start | bytes 147464 | tf_op jit(solution)/shard_map/ppermute | solution.py:72
  15.1 6.1 %collective-permute-start.3 = (bf16[64,1536]{1,0:T(8,128)(2,1)}, bf16[64,1536]{1,0:T(8,128)(2,1)}, u32[]{:S(2)}, u32[]{:S(2)}) collective-permute-start(bf16[64,1536]{1,0:T(8,128)(2,1)} %join.1.refs_1_), channel_id=1, source_target_pairs={{0,2},{1,3},{2,0},{3,1},{4,6},{5,7},{6,4},{7,5},{8,10},{9,11},{10,... | collective-permute-start | bytes 589832 | tf_op jit(solution)/shard_map/ppermute | solution.py:72
  16.7 4.6 %collective-permute-start.4 = (bf16[64,1536]{1,0:T(8,128)(2,1)}, bf16[64,1536]{1,0:T(8,128)(2,1)}, u32[]{:S(2)}, u32[]{:S(2)}) collective-permute-start(bf16[64,1536]{1,0:T(8,128)(2,1)} %join.1.refs_1_), channel_id=1, source_target_pairs={{0,1},{1,0},{2,3},{3,2},{4,5},{5,4},{6,7},{7,6},{8,9},{9,8},{10,11... | collective-permute-start | bytes 589832 | tf_op jit(solution)/shard_map/ppermute | solution.py:72
  21.2 1.8 %collective-permute-start.5 = (bf16[64,1536]{1,0:T(8,128)(2,1)}, bf16[64,1536]{1,0:T(8,128)(2,1)}, u32[]{:S(2)}, u32[]{:S(2)}) collective-permute-start(bf16[64,1536]{1,0:T(8,128)(2,1)} %collective-permute-done.3.refs_2_), channel_id=1, source_target_pairs={{0,1},{1,0},{2,3},{3,2},{4,5},{5,4},{6,7},{7,6},{8,9},{9,8},{10,11... | collective-permute-start | bytes 589832 | tf_op jit(solution)/shard_map/ppermute | solution.py:72
  26.2 1.8 %collective-permute-start.6 = (f32[64,1664]{1,0:T(8,128)S(1)}, f32[64,1664]{1,0:T(8,128)S(1)}, u32[]{:S(2)}, u32[]{:S(2)}) collective-permute-start(f32[64,1664]{1,0:T(8,128)S(1)} %get-tuple-element.28), channel_id=1, source_target_pairs={{0,1},{1,0},{2,3},{3,2},{4,5},{5,4},{6,7},{7,6},{8,9},{9,8},{10,11... | collective-permute-start | bytes 1277960 | tf_op jit(solution)/shard_map/ppermute | solution.py:72
  28.1 6.6 %collective-permute-start.9 = (bf16[16,1664]{1,0:T(8,128)(2,1)S(1)}, bf16[16,1664]{1,0:T(8,128)(2,1)S(1)}, u32[]{:S(2)}, u32[]{:S(2)}) collective-permute-start(bf16[16,1664]{1,0:T(8,128)(2,1)S(1)} %get-tuple-element.40), channel_id=1, source_target_pairs={{0,12},{1,13},{2,14},{3,15},{4,8},{5,9},{6,10},{7,11},{8,4},{9,5},... | collective-permute-start | bytes 159752 | tf_op jit(solution)/shard_map/ppermute | solution.py:72
  30.2 6.1 %collective-permute-start.8 = (bf16[16,1664]{1,0:T(8,128)(2,1)S(1)}, bf16[16,1664]{1,0:T(8,128)(2,1)S(1)}, u32[]{:S(2)}, u32[]{:S(2)}) collective-permute-start(bf16[16,1664]{1,0:T(8,128)(2,1)S(1)} %get-tuple-element.41), channel_id=1, source_target_pairs={{0,8},{1,9},{2,10},{3,11},{4,12},{5,13},{6,14},{7,15},{8,0},{9,1},... | collective-permute-start | bytes 159752 | tf_op jit(solution)/shard_map/ppermute | solution.py:72
  30.4 6.0 %collective-permute-start.7 = (bf16[16,1664]{1,0:T(8,128)(2,1)S(1)}, bf16[16,1664]{1,0:T(8,128)(2,1)S(1)}, u32[]{:S(2)}, u32[]{:S(2)}) collective-permute-start(bf16[16,1664]{1,0:T(8,128)(2,1)S(1)} %get-tuple-element.42), channel_id=1, source_target_pairs={{0,4},{1,5},{2,6},{3,7},{4,0},{5,1},{6,2},{7,3},{8,12},{9,13},{10,... | collective-permute-start | bytes 159752 | tf_op jit(solution)/shard_map/ppermute | solution.py:72
  36.4 4.2 %collective-permute-start.10 = (bf16[16,1664]{1,0:T(8,128)(2,1)S(1)}, bf16[16,1664]{1,0:T(8,128)(2,1)S(1)}, u32[]{:S(2)}, u32[]{:S(2)}) collective-permute-start(bf16[16,1664]{1,0:T(8,128)(2,1)S(1)} %sum.1), channel_id=1, source_target_pairs={{0,2},{1,3},{2,0},{3,1},{4,6},{5,7},{6,4},{7,5},{8,10},{9,11},{10,... | collective-permute-start | bytes 159752 | tf_op jit(solution)/shard_map/ppermute | solution.py:72
  40.6 6.5 %collective-permute-start.13 = (bf16[16,1664]{1,0:T(8,128)(2,1)S(1)}, bf16[16,1664]{1,0:T(8,128)(2,1)S(1)}, u32[]{:S(2)}, u32[]{:S(2)}) collective-permute-start(bf16[16,1664]{1,0:T(8,128)(2,1)S(1)} %fusion.1.refs_0_), channel_id=1, source_target_pairs={{0,12},{1,13},{2,14},{3,15},{4,8},{5,9},{6,10},{7,11},{8,4},{9,5},... | collective-permute-start | bytes 159752 | tf_op jit(solution)/shard_map/ppermute | solution.py:72
  43.0 5.3 %collective-permute-start.12 = (bf16[16,1664]{1,0:T(8,128)(2,1)S(1)}, bf16[16,1664]{1,0:T(8,128)(2,1)S(1)}, u32[]{:S(2)}, u32[]{:S(2)}) collective-permute-start(bf16[16,1664]{1,0:T(8,128)(2,1)S(1)} %fusion.1.refs_0_), channel_id=1, source_target_pairs={{0,8},{1,9},{2,10},{3,11},{4,12},{5,13},{6,14},{7,15},{8,0},{9,1},... | collective-permute-start | bytes 159752 | tf_op jit(solution)/shard_map/ppermute | solution.py:72
  43.0 5.3 %collective-permute-start.11 = (bf16[16,1664]{1,0:T(8,128)(2,1)S(1)}, bf16[16,1664]{1,0:T(8,128)(2,1)S(1)}, u32[]{:S(2)}, u32[]{:S(2)}) collective-permute-start(bf16[16,1664]{1,0:T(8,128)(2,1)S(1)} %fusion.1.refs_0_), channel_id=1, source_target_pairs={{0,4},{1,5},{2,6},{3,7},{4,0},{5,1},{6,2},{7,3},{8,12},{9,13},{10,... | collective-permute-start | bytes 159752 | tf_op jit(solution)/shard_map/ppermute | solution.py:72
  45.1 3.7 %collective-permute-start.14 = (bf16[16,1664]{1,0:T(8,128)(2,1)S(1)}, bf16[16,1664]{1,0:T(8,128)(2,1)S(1)}, u32[]{:S(2)}, u32[]{:S(2)}) collective-permute-start(bf16[16,1664]{1,0:T(8,128)(2,1)S(1)} %fusion.1.refs_0_), channel_id=1, source_target_pairs={{0,1},{1,0},{2,3},{3,2},{4,5},{5,4},{6,7},{7,6},{8,9},{9,8},{10,11... | collective-permute-start | bytes 159752 | tf_op jit(solution)/shard_map/ppermute | solution.py:72
  47.1 1.7 %collective-permute-start.17 = (bf16[16,1664]{1,0:T(8,128)(2,1)S(1)}, bf16[16,1664]{1,0:T(8,128)(2,1)S(1)}, u32[]{:S(2)}, u32[]{:S(2)}) collective-permute-start(bf16[16,1664]{1,0:T(8,128)(2,1)S(1)} %collective-permute-done.13.refs_3_), channel_id=1, source_target_pairs={{0,1},{1,0},{2,3},{3,2},{4,5},{5,4},{6,7},{7,6},{8,9},{9,8},{10,11... | collective-permute-start | bytes 159752 | tf_op jit(solution)/shard_map/ppermute | solution.py:72
  48.3 1.2 %collective-permute-start.16 = (bf16[16,1664]{1,0:T(8,128)(2,1)S(1)}, bf16[16,1664]{1,0:T(8,128)(2,1)S(1)}, u32[]{:S(2)}, u32[]{:S(2)}) collective-permute-start(bf16[16,1664]{1,0:T(8,128)(2,1)S(1)} %collective-permute-done.12.refs_2_), channel_id=1, source_target_pairs={{0,1},{1,0},{2,3},{3,2},{4,5},{5,4},{6,7},{7,6},{8,9},{9,8},{10,11... | collective-permute-start | bytes 159752 | tf_op jit(solution)/shard_map/ppermute | solution.py:72
  48.3 1.4 %collective-permute-start.15 = (bf16[16,1664]{1,0:T(8,128)(2,1)S(1)}, bf16[16,1664]{1,0:T(8,128)(2,1)S(1)}, u32[]{:S(2)}, u32[]{:S(2)}) collective-permute-start(bf16[16,1664]{1,0:T(8,128)(2,1)S(1)} %collective-permute-done.11.refs_1_), channel_id=1, source_target_pairs={{0,1},{1,0},{2,3},{3,2},{4,5},{5,4},{6,7},{7,6},{8,9},{9,8},{10,11... | collective-permute-start | bytes 159752 | tf_op jit(solution)/shard_map/ppermute | solution.py:72

commit v6 on v5

--- a/solution.py
+++ b/solution.py
@@ -13,6 +13,7 @@
 VMEM_BYTES = 56 << 20
 PINNED_BYTES = 24 << 20
 PINNED_TOKENS = 256
+GROUP_ROWS = 256
 
 sparsity = 0.5
 epsilon = 1e-05
@@ -188,7 +189,7 @@
 def join_kernel(*refs):
     out = refs[-1]
     at = 0
-    for ref in refs[1:-1]:
+    for ref in refs[:-1]:
         out[at : at + ref.shape[0], :] = ref[...]
         at += ref.shape[0]
 
@@ -208,7 +209,7 @@
     row[...] = jnp.broadcast_to(total, (latents, LANES)).T[:8]
 
 
-def encode_kernel(count, outer, inner, slots, frames, rel, *refs):
+def encode_kernel(count, outer, inner, slots, frames, *refs):
     me_ref = refs[0]
     pieces = refs[1 : 1 + count]
     enc, bias, dec, weights_sum, dec_bias = refs[1 + count : 6 + count]
@@ -217,15 +218,27 @@
     step = 2 * inner
     tokens, feature = inputs_out.shape
     rows = pieces[0].shape[0]
-    held = rows // frames
+    group = max(GROUP_ROWS // rows, 1)
+    width = group * rows
+    held = width // frames
     shift_frames, shift_slots = log2(frames), log2(slots)
-    choose = (iota((held, rows), 1) == iota((held, rows), 0) * frames + frames - 1).astype(BF16)
-    takes, starts = [], []
-    for piece, bits in zip(pieces, rel):
-        notes = jnp.dot(choose, piece[:, :LANES], preferred_element_type=F32)
+
+    def device_of(place):
+        bits = (place & (outer - 1)) * step
+        bits = bits + ((place >> log2(outer)) & (inner - 1)) * 2 + (place >> log2(outer * inner))
+        return me ^ bits
+
+    choose = (iota((held, width), 1) == iota((held, width), 0) * frames + frames - 1).astype(BF16)
+    last = (iota((width, width), 0) == (iota((width, width), 1) | (frames - 1))).astype(BF16)
+    ident = (iota((16, LANES), 0) == iota((16, LANES), 1)).astype(BF16)
+    groups, takes, starts = [], [], []
+    for g in range(0, len(pieces), group):
+        parts = [piece[...] for piece in pieces[g : g + group]]
+        groups.append(parts[0] if group == 1 else jnp.concatenate(parts, axis=0))
+        notes = jnp.dot(choose, groups[-1][:, :LANES], preferred_element_type=F32)
         takes.append(notes[:, 1:2].astype(jnp.int32))
-        device = me ^ ((iota((held, 1), 0) >> shift_slots) * step + bits)
-        starts.append(device * ROWS_DEV)
+        slot = g * rows // frames + iota((held, 1), 0)
+        starts.append(device_of(slot >> shift_slots) * ROWS_DEV)
     takes = jnp.concatenate(takes, axis=0)
     starts = jnp.concatenate(starts, axis=0)
     kinds = iota(takes.shape, 0) & (slots - 1)
@@ -234,18 +247,16 @@
         ((r >> log2(inner)) & (outer - 1)) * step + (r & (inner - 1)) * 2 + (r >> log2(outer * inner))
     )
     token = (me ^ holder) * ROWS_DEV + (iota((tokens, 1), 0) & (ROWS_DEV - 1))
-    lane = iota((1, rows), 1)
+    lane = iota((1, width), 1)
     frame = lane & (frames - 1)
-    last = (iota((rows, rows), 0) == (iota((rows, rows), 1) | (frames - 1))).astype(BF16)
-    ident = (iota((16, LANES), 0) == iota((16, LANES), 1)).astype(BF16)
     total = jnp.zeros((tokens, feature), F32)
-    for piece, bits in zip(pieces, rel):
+    for g, block in enumerate(groups):
         turned = lax.dot_general(
-            ident, piece[:, :LANES], (((1,), (1,)), ((), ())), preferred_element_type=F32
+            ident, block[:, :LANES], (((1,), (1,)), ((), ())), preferred_element_type=F32
         )
         turned = jnp.dot(turned.astype(BF16), last, preferred_element_type=F32)
         size = turned[0:1, :].astype(jnp.int32)
-        device = me ^ ((lane >> (shift_frames + shift_slots)) * step + bits)
+        device = device_of((g * width + lane) >> (shift_frames + shift_slots))
         label = device * slots + ((lane >> shift_frames) & (slots - 1))
         match = takes == label
         begin = jnp.sum(jnp.where(match, starts, 0), axis=0, keepdims=True)
@@ -253,7 +264,7 @@
         target = begin + second * (ROWS_DEV - size) + frame
         target = jnp.where(frame < size, target, -1)
         pick = jnp.where(token == target, 1.0, 0.0).astype(BF16)
-        total = total + jnp.dot(pick, piece[...], preferred_element_type=F32)
+        total = total + jnp.dot(pick, block, preferred_element_type=F32)
     inputs = total.astype(BF16)
     inputs_out[...] = inputs
     latent = jnp.maximum(jnp.dot(inputs, enc[...], preferred_element_type=F32) + bias[...], 0.0)
@@ -412,30 +423,29 @@
     )(decoder)
 
     blocks = [packed] + [exchange(packed, step * k) for k in range(1, outer)]
-    pieces = [
-        call(
-            join_kernel,
-            "join",
-            fast((outer * slots * frames, feature), BF16),
-            [pl.BlockSpec(memory_space=pl.ANY)] + [vmem()] * outer,
-            vmem(),
-            moved=4 * outer * slots * frames * feature,
-        )(near(norms), *[near(block) for block in blocks])
-    ]
-    rel = [0]
+    pieces = blocks
+    if not pinned:
+        pieces = [
+            call(
+                join_kernel,
+                "join",
+                shape((outer * slots * frames, feature), BF16),
+                [vmem()] * outer,
+                vmem(),
+                moved=4 * outer * slots * frames * feature,
+            )(*blocks)
+        ]
     bit = 2
     while bit < step:
-        pieces += [exchange(piece, bit) for piece in pieces]
-        rel += [r ^ bit for r in rel]
+        pieces = pieces + [exchange(piece, bit) for piece in pieces]
         bit *= 2
-    pieces += [exchange(piece, 1) for piece in pieces]
-    rel += [r ^ 1 for r in rel]
+    pieces = pieces + [exchange(piece, 1) for piece in pieces]
 
     half = tokens // 2
     chunk = half // outer
 
     def encode(*refs):
-        encode_kernel(len(pieces), outer, inner, slots, frames, rel, *refs)
+        encode_kernel(len(pieces), outer, inner, slots, frames, *refs)
 
     own, send, shift, inputs, latent = call(
         encode,

time: 53.2 us -> 51.5 us (0.968)
  starting transfers between devices: 18.5 us -> 21.3 us
  waiting for transfers between devices: 21.7 us -> 18.9 us
  Pallas kernels: 12 us -> 10.2 us
    ppermute x18 -> x27, starting transfers between devices: 18.5 us -> 21.3 us  [exchange(): return lax.ppermute(value, 'utt', [(i, i ^ bit) for i in range(devices)])]
    ppermute x18 -> x27, waiting for transfers between devices: 21.7 us -> 18.9 us  [exchange(): return lax.ppermute(value, 'utt', [(i, i ^ bit) for i in range(devices)])]
    pallas_call x1, Pallas kernels: 3.22 us -> 2.05 us  [shards(): call(encode, 'encode', (fast((half, wide), F32), fast((half, wide), F32),...]
    pallas_call x1 -> x0, Pallas kernels: 0.69 us -> none  [shards(): call(join_kernel, 'join', fast((outer * slots * frames, feature), BF16),...]
  transfers between devices with their start and end apart: 18 -> 27, of which waited for: 12 -> 15; matrix products, arithmetic and copies ran while one was open for 0% -> 0% of each run, Pallas kernels for 2% -> 2%
where the time goes in v6:
time: 51.5 us; the launch traced here: 51.3 us
  starting transfers between devices  21.3 us (41%)
  waiting for transfers between devices  18.9 us (37%)
  Pallas kernels  10.2 us (20%)
  between operations  0.75 us (1%)
    ppermute x27, starting transfers between devices, exchange(): return lax.ppermute(value, 'utt', [(i, i ^ bit) for i in range(devices)])  21.3 us
    ppermute x27, waiting for transfers between devices, exchange(): return lax.ppermute(value, 'utt', [(i, i ^ bit) for i in range(devices)])  18.9 us
    pallas_call x1, Pallas kernels, shards(): call(features_kernel, 'features', fast((slots * frames, feature), BF16),...  3.64 us
    pallas_call x1, Pallas kernels, shards(): call(gradients, 'gradients', (shape((feature, latents), BF16), shape((lat...  3.43 us
    pallas_call x1, Pallas kernels, shards(): call(encode, 'encode', (fast((half, wide), F32), fast((half, wide), F32),...  2.05 us
  transfers between devices with their start and end apart: 27, of which 15 were waited for; matrix products, arithmetic and copies ran while one was open for 0% of the time, Pallas kernels for 2%

profile of v6, /device:TPU:0, one launch (start us, length us, event | category | flops | bytes accessed | tf_op | source)
XLA Modules:
  0.0 51.3 jit_solution(10722425163784602514)
XLA Ops:
  0.6 3.6 %features.1.refs_1_ = bf16[16,1536]{1,0:T(8,128)(2,1)S(1)} custom-call(s32[2]{0:T(128)} %refs_0_.1, s32[2]{0:T(128)} %refs_1_.1, f32[2,90]{1,0:T(2,128)} %refs_2_.1, f32[10,3,512]{2,1,0:T(4,128)} %bitcast.14, f32[3,2,512]{2,1,0:T(2,128)} %refs_4_.1, f32[3,2,512]{2,1,0:T(2,128)} %refs_5_.1, bf16[3,1536,512]{2,1,0:T(8,128)(2,1)} %refs_6_.1), custom_call_target="tpu_custom_call" | custom-call | flops 75497472 | bytes 4718592 | tf_op jit(solution)/shard_map/features/pallas_call | solution.py:389
  4.3 3.0 %collective-permute-start.3 = (bf16[16,1536]{1,0:T(8,128)(2,1)S(1)}, bf16[16,1536]{1,0:T(8,128)(2,1)S(1)}, u32[]{:S(2)}, u32[]{:S(2)}) collective-permute-start(bf16[16,1536]{1,0:T(8,128)(2,1)S(1)} %features.1.refs_1_), channel_id=1, source_target_pairs={{0,2},{1,3},{2,0},{3,1},{4,6},{5,7},{6,4},{7,5},{8,10},{9,11},{10,... | collective-permute-start | bytes 147464 | tf_op jit(solution)/shard_map/ppermute | solution.py:73
  7.4 3.6 %collective-permute-start.2 = (bf16[16,1536]{1,0:T(8,128)(2,1)S(1)}, bf16[16,1536]{1,0:T(8,128)(2,1)S(1)}, u32[]{:S(2)}, u32[]{:S(2)}) collective-permute-start(bf16[16,1536]{1,0:T(8,128)(2,1)S(1)} %features.1.refs_1_), channel_id=1, source_target_pairs={{0,12},{1,13},{2,14},{3,15},{4,8},{5,9},{6,10},{7,11},{8,4},{9,5},... | collective-permute-start | bytes 147464 | tf_op jit(solution)/shard_map/ppermute | solution.py:73
  11.0 0.8 %collective-permute-start = (bf16[16,1536]{1,0:T(8,128)(2,1)S(1)}, bf16[16,1536]{1,0:T(8,128)(2,1)S(1)}, u32[]{:S(2)}, u32[]{:S(2)}) collective-permute-start(bf16[16,1536]{1,0:T(8,128)(2,1)S(1)} %features.1.refs_1_), channel_id=1, source_target_pairs={{0,4},{1,5},{2,6},{3,7},{4,0},{5,1},{6,2},{7,3},{8,12},{9,13},{10,... | collective-permute-start | bytes 147464 | tf_op jit(solution)/shard_map/ppermute | solution.py:73
  11.8 1.5 %collective-permute-done.2.refs_4_ = bf16[16,1536]{1,0:T(8,128)(2,1)S(1)} collective-permute-done((bf16[16,1536]{1,0:T(8,128)(2,1)S(1)}, bf16[16,1536]{1,0:T(8,128)(2,1)S(1)}, u32[]{:S(2)}, u32[]{:S(2)}) %collective-permute-start.2) | collective-permute-done | bytes 49184 | tf_op jit(solution)/shard_map/ppermute | solution.py:73
  13.6 2.6 %collective-permute-done.1.refs_3_ = bf16[16,1536]{1,0:T(8,128)(2,1)S(1)} collective-permute-done((bf16[16,1536]{1,0:T(8,128)(2,1)S(1)}, bf16[16,1536]{1,0:T(8,128)(2,1)S(1)}, u32[]{:S(2)}, u32[]{:S(2)}) %collective-permute-start.1) | collective-permute-done | bytes 49184 | tf_op jit(solution)/shard_map/ppermute | solution.py:73
  16.7 1.5 %collective-permute-start.4 = (bf16[16,1536]{1,0:T(8,128)(2,1)S(1)}, bf16[16,1536]{1,0:T(8,128)(2,1)}, u32[]{:S(2)}, u32[]{:S(2)}) collective-permute-start(bf16[16,1536]{1,0:T(8,128)(2,1)S(1)} %collective-permute-done.refs_2_), channel_id=1, source_target_pairs={{0,2},{1,3},{2,0},{3,1},{4,6},{5,7},{6,4},{7,5},{8,10},{9,11},{10,... | collective-permute-start | bytes 147464 | tf_op jit(solution)/shard_map/ppermute | solution.py:73
  18.8 1.6 %collective-permute-done.5.refs_7_ = bf16[16,1536]{1,0:T(8,128)(2,1)} collective-permute-done((bf16[16,1536]{1,0:T(8,128)(2,1)S(1)}, bf16[16,1536]{1,0:T(8,128)(2,1)}, u32[]{:S(2)}, u32[]{:S(2)}) %collective-permute-start.5) | collective-permute-done | bytes 49184 | tf_op jit(solution)/shard_map/ppermute | solution.py:73
  20.9 0.7 %norms.1 = (f32[512,128]{1,0:T(8,128)S(1)}, f32[8,512]{1,0:T(8,128)S(1)}) custom-call(bf16[512,1536]{1,0:T(8,128)(2,1)S(1)} %copy-done), custom_call_target="tpu_custom_call" | custom-call | flops 3145728 | bytes 1572864 | tf_op jit(solution)/shard_map/norms/pallas_call | solution.py:415
  21.9 0.5 %collective-permute-done.12.refs_14_ = bf16[16,1536]{1,0:T(8,128)(2,1)} collective-permute-done((bf16[16,1536]{1,0:T(8,128)(2,1)}, bf16[16,1536]{1,0:T(8,128)(2,1)}, u32[]{:S(2)}, u32[]{:S(2)}) %collective-permute-start.12) | collective-permute-done | bytes 49184 | tf_op jit(solution)/shard_map/ppermute | solution.py:73
  22.5 2.0 %encode.1 = (f32[64,1664]{1,0:T(8,128)S(1)}, f32[64,1664]{1,0:T(8,128)S(1)}, f32[16,1664]{1,0:T(8,128)S(1)}, bf16[128,1536]{1,0:T(8,128)(2,1)S(1)}, f32[128,512]{1,0:T(8,128)S(1)}) custom-call(s32[1]{0:T(128)} %bitcast.refs_0_, bf16[16,1536]{1,0:T(8,128)(2,1)S(1)} %features.1.refs_1_, bf16[16,1536]{1,0:T(8,128)(2,1)S(1)} %collective-permute-done.refs_2_, ...), custom_call_target="tpu_custom_call" | custom-call | flops 402653184 | bytes 3145728 | tf_op jit(solution)/shard_map/encode/pallas_call | solution.py:450
  24.7 1.6 %collective-permute-done.15 = f32[64,1664]{1,0:T(8,128)S(1)} collective-permute-done((f32[64,1664]{1,0:T(8,128)S(1)}, f32[64,1664]{1,0:T(8,128)S(1)}, u32[]{:S(2)}, u32[]{:S(2)}) %collective-permute-start.15) | collective-permute-done | bytes 426016 | tf_op jit(solution)/shard_map/ppermute | solution.py:73
  26.5 3.0 %collective-permute-start.18 = (bf16[16,1664]{1,0:T(8,128)(2,1)S(1)}, bf16[16,1664]{1,0:T(8,128)(2,1)S(1)}, u32[]{:S(2)}, u32[]{:S(2)}) collective-permute-start(bf16[16,1664]{1,0:T(8,128)(2,1)S(1)} %get-tuple-element.40), channel_id=1, source_target_pairs={{0,12},{1,13},{2,14},{3,15},{4,8},{5,9},{6,10},{7,11},{8,4},{9,5},... | collective-permute-start | bytes 159752 | tf_op jit(solution)/shard_map/ppermute | solution.py:73
  29.5 1.4 %collective-permute-start.16 = (bf16[16,1664]{1,0:T(8,128)(2,1)S(1)}, bf16[16,1664]{1,0:T(8,128)(2,1)S(1)}, u32[]{:S(2)}, u32[]{:S(2)}) collective-permute-start(bf16[16,1664]{1,0:T(8,128)(2,1)S(1)} %get-tuple-element.42), channel_id=1, source_target_pairs={{0,4},{1,5},{2,6},{3,7},{4,0},{5,1},{6,2},{7,3},{8,12},{9,13},{10,... | collective-permute-start | bytes 159752 | tf_op jit(solution)/shard_map/ppermute | solution.py:73
  31.3 1.6 %collective-permute-done.18.refs_4_ = bf16[16,1664]{1,0:T(8,128)(2,1)S(1)} collective-permute-done((bf16[16,1664]{1,0:T(8,128)(2,1)S(1)}, bf16[16,1664]{1,0:T(8,128)(2,1)S(1)}, u32[]{:S(2)}, u32[]{:S(2)}) %collective-permute-start.18) | collective-permute-done | bytes 53280 | tf_op jit(solution)/shard_map/ppermute | solution.py:73
  32.9 1.7 %collective-permute-done.17.refs_3_ = bf16[16,1664]{1,0:T(8,128)(2,1)S(1)} collective-permute-done((bf16[16,1664]{1,0:T(8,128)(2,1)S(1)}, bf16[16,1664]{1,0:T(8,128)(2,1)S(1)}, u32[]{:S(2)}, u32[]{:S(2)}) %collective-permute-start.17) | collective-permute-done | bytes 53280 | tf_op jit(solution)/shard_map/ppermute | solution.py:73
  34.8 1.3 %collective-permute-start.19 = (bf16[16,1664]{1,0:T(8,128)(2,1)S(1)}, bf16[16,1664]{1,0:T(8,128)(2,1)S(1)}, u32[]{:S(2)}, u32[]{:S(2)}) collective-permute-start(bf16[16,1664]{1,0:T(8,128)(2,1)S(1)} %sum.1), channel_id=1, source_target_pairs={{0,2},{1,3},{2,0},{3,1},{4,6},{5,7},{6,4},{7,5},{8,10},{9,11},{10,... | collective-permute-start | bytes 159752 | tf_op jit(solution)/shard_map/ppermute | solution.py:73
  36.1 2.9 %collective-permute-done.19 = bf16[16,1664]{1,0:T(8,128)(2,1)S(1)} collective-permute-done((bf16[16,1664]{1,0:T(8,128)(2,1)S(1)}, bf16[16,1664]{1,0:T(8,128)(2,1)S(1)}, u32[]{:S(2)}, u32[]{:S(2)}) %collective-permute-start.19) | collective-permute-done | bytes 53280 | tf_op jit(solution)/shard_map/ppermute | solution.py:73
  39.0 2.4 %collective-permute-start.22 = (bf16[16,1664]{1,0:T(8,128)(2,1)S(1)}, bf16[16,1664]{1,0:T(8,128)(2,1)S(1)}, u32[]{:S(2)}, u32[]{:S(2)}) collective-permute-start(bf16[16,1664]{1,0:T(8,128)(2,1)S(1)} %fusion.1.refs_0_), channel_id=1, source_target_pairs={{0,12},{1,13},{2,14},{3,15},{4,8},{5,9},{6,10},{7,11},{8,4},{9,5},... | collective-permute-start | bytes 159752 | tf_op jit(solution)/shard_map/ppermute | solution.py:73
  41.5 2.0 %collective-permute-start.20 = (bf16[16,1664]{1,0:T(8,128)(2,1)S(1)}, bf16[16,1664]{1,0:T(8,128)(2,1)S(1)}, u32[]{:S(2)}, u32[]{:S(2)}) collective-permute-start(bf16[16,1664]{1,0:T(8,128)(2,1)S(1)} %fusion.1.refs_0_), channel_id=1, source_target_pairs={{0,4},{1,5},{2,6},{3,7},{4,0},{5,1},{6,2},{7,3},{8,12},{9,13},{10,... | collective-permute-start | bytes 159752 | tf_op jit(solution)/shard_map/ppermute | solution.py:73
  43.5 1.7 %collective-permute-done.22.refs_3_ = bf16[16,1664]{1,0:T(8,128)(2,1)S(1)} collective-permute-done((bf16[16,1664]{1,0:T(8,128)(2,1)S(1)}, bf16[16,1664]{1,0:T(8,128)(2,1)S(1)}, u32[]{:S(2)}, u32[]{:S(2)}) %collective-permute-start.22) | collective-permute-done | bytes 53280 | tf_op jit(solution)/shard_map/ppermute | solution.py:73
  45.2 1.3 %collective-permute-done.21.refs_2_ = bf16[16,1664]{1,0:T(8,128)(2,1)S(1)} collective-permute-done((bf16[16,1664]{1,0:T(8,128)(2,1)S(1)}, bf16[16,1664]{1,0:T(8,128)(2,1)S(1)}, u32[]{:S(2)}, u32[]{:S(2)}) %collective-permute-start.21) | collective-permute-done | bytes 53280 | tf_op jit(solution)/shard_map/ppermute | solution.py:73
  47.0 0.7 %collective-permute-done.25.refs_6_ = bf16[16,1664]{1,0:T(8,128)(2,1)S(1)} collective-permute-done((bf16[16,1664]{1,0:T(8,128)(2,1)S(1)}, bf16[16,1664]{1,0:T(8,128)(2,1)S(1)}, u32[]{:S(2)}, u32[]{:S(2)}) %collective-permute-start.25) | collective-permute-done | bytes 53280 | tf_op jit(solution)/shard_map/ppermute | solution.py:73
  47.9 3.4 %gradients.1 = (bf16[1536,512]{1,0:T(8,128)(2,1)}, bf16[512,1536]{1,0:T(8,128)(2,1)}, f32[1,512]{1,0:T(1,128)}, f32[1536]{0:T(1024)}, f32[1]{0:T(128)}, /*index=5*/bf16[8,1536]{1,0:T(8,128)(2,1)}) custom-call(bf16[16,1664]{1,0:T(8,128)(2,1)S(1)} %fusion.1.refs_0_, bf16[16,1664]{1,0:T(8,128)(2,1)S(1)} %collective-permute-done.20.refs_1_, ...), custom_call_target="tpu_custom_call" | custom-call | flops 603979776 | bytes 6291456 | tf_op jit(solution)/shard_map/gradients/pallas_call | solution.py:512
  (49 shorter events, 3.9 us)
Async XLA Ops:
  4.3 7.4 %collective-permute-start.3 = (bf16[16,1536]{1,0:T(8,128)(2,1)S(1)}, bf16[16,1536]{1,0:T(8,128)(2,1)S(1)}, u32[]{:S(2)}, u32[]{:S(2)}) collective-permute-start(bf16[16,1536]{1,0:T(8,128)(2,1)S(1)} %features.1.refs_1_), channel_id=1, source_target_pairs={{0,2},{1,3},{2,0},{3,1},{4,6},{5,7},{6,4},{7,5},{8,10},{9,11},{10,... | collective-permute-start | bytes 147464 | tf_op jit(solution)/shard_map/ppermute | solution.py:73
  7.4 5.9 %collective-permute-start.2 = (bf16[16,1536]{1,0:T(8,128)(2,1)S(1)}, bf16[16,1536]{1,0:T(8,128)(2,1)S(1)}, u32[]{:S(2)}, u32[]{:S(2)}) collective-permute-start(bf16[16,1536]{1,0:T(8,128)(2,1)S(1)} %features.1.refs_1_), channel_id=1, source_target_pairs={{0,12},{1,13},{2,14},{3,15},{4,8},{5,9},{6,10},{7,11},{8,4},{9,5},... | collective-permute-start | bytes 147464 | tf_op jit(solution)/shard_map/ppermute | solution.py:73
  11.0 2.3 %collective-permute-start.7 = (bf16[16,1536]{1,0:T(8,128)(2,1)S(1)}, bf16[16,1536]{1,0:T(8,128)(2,1)S(1)}, u32[]{:S(2)}, u32[]{:S(2)}) collective-permute-start(bf16[16,1536]{1,0:T(8,128)(2,1)S(1)} %features.1.refs_1_), channel_id=1, source_target_pairs={{0,1},{1,0},{2,3},{3,2},{4,5},{5,4},{6,7},{7,6},{8,9},{9,8},{10,11... | collective-permute-start | bytes 147464 | tf_op jit(solution)/shard_map/ppermute | solution.py:73
  11.0 5.2 %collective-permute-start.1 = (bf16[16,1536]{1,0:T(8,128)(2,1)S(1)}, bf16[16,1536]{1,0:T(8,128)(2,1)S(1)}, u32[]{:S(2)}, u32[]{:S(2)}) collective-permute-start(bf16[16,1536]{1,0:T(8,128)(2,1)S(1)} %features.1.refs_1_), channel_id=1, source_target_pairs={{0,8},{1,9},{2,10},{3,11},{4,12},{5,13},{6,14},{7,15},{8,0},{9,1},... | collective-permute-start | bytes 147464 | tf_op jit(solution)/shard_map/ppermute | solution.py:73
  11.0 5.7 %collective-permute-start = (bf16[16,1536]{1,0:T(8,128)(2,1)S(1)}, bf16[16,1536]{1,0:T(8,128)(2,1)S(1)}, u32[]{:S(2)}, u32[]{:S(2)}) collective-permute-start(bf16[16,1536]{1,0:T(8,128)(2,1)S(1)} %features.1.refs_1_), channel_id=1, source_target_pairs={{0,4},{1,5},{2,6},{3,7},{4,0},{5,1},{6,2},{7,3},{8,12},{9,13},{10,... | collective-permute-start | bytes 147464 | tf_op jit(solution)/shard_map/ppermute | solution.py:73
  11.8 6.4 %collective-permute-start.11 = (bf16[16,1536]{1,0:T(8,128)(2,1)S(1)}, bf16[16,1536]{1,0:T(8,128)(2,1)S(1)}, u32[]{:S(2)}, u32[]{:S(2)}) collective-permute-start(bf16[16,1536]{1,0:T(8,128)(2,1)S(1)} %collective-permute-done.3.refs_5_), channel_id=1, source_target_pairs={{0,1},{1,0},{2,3},{3,2},{4,5},{5,4},{6,7},{7,6},{8,9},{9,8},{10,11... | collective-permute-start | bytes 147464 | tf_op jit(solution)/shard_map/ppermute | solution.py:73
  13.3 5.0 %collective-permute-start.10 = (bf16[16,1536]{1,0:T(8,128)(2,1)S(1)}, bf16[16,1536]{1,0:T(8,128)(2,1)S(1)}, u32[]{:S(2)}, u32[]{:S(2)}) collective-permute-start(bf16[16,1536]{1,0:T(8,128)(2,1)S(1)} %collective-permute-done.2.refs_4_), channel_id=1, source_target_pairs={{0,1},{1,0},{2,3},{3,2},{4,5},{5,4},{6,7},{7,6},{8,9},{9,8},{10,11... | collective-permute-start | bytes 147464 | tf_op jit(solution)/shard_map/ppermute | solution.py:73
  13.3 5.5 %collective-permute-start.6 = (bf16[16,1536]{1,0:T(8,128)(2,1)S(1)}, bf16[16,1536]{1,0:T(8,128)(2,1)}, u32[]{:S(2)}, u32[]{:S(2)}) collective-permute-start(bf16[16,1536]{1,0:T(8,128)(2,1)S(1)} %collective-permute-done.2.refs_4_), channel_id=1, source_target_pairs={{0,2},{1,3},{2,0},{3,1},{4,6},{5,7},{6,4},{7,5},{8,10},{9,11},{10,... | collective-permute-start | bytes 147464 | tf_op jit(solution)/shard_map/ppermute | solution.py:73
  16.2 4.2 %collective-permute-start.5 = (bf16[16,1536]{1,0:T(8,128)(2,1)S(1)}, bf16[16,1536]{1,0:T(8,128)(2,1)}, u32[]{:S(2)}, u32[]{:S(2)}) collective-permute-start(bf16[16,1536]{1,0:T(8,128)(2,1)S(1)} %collective-permute-done.1.refs_3_), channel_id=1, source_target_pairs={{0,2},{1,3},{2,0},{3,1},{4,6},{5,7},{6,4},{7,5},{8,10},{9,11},{10,... | collective-permute-start | bytes 147464 | tf_op jit(solution)/shard_map/ppermute | solution.py:73
  16.7 4.2 %collective-permute-start.4 = (bf16[16,1536]{1,0:T(8,128)(2,1)S(1)}, bf16[16,1536]{1,0:T(8,128)(2,1)}, u32[]{:S(2)}, u32[]{:S(2)}) collective-permute-start(bf16[16,1536]{1,0:T(8,128)(2,1)S(1)} %collective-permute-done.refs_2_), channel_id=1, source_target_pairs={{0,2},{1,3},{2,0},{3,1},{4,6},{5,7},{6,4},{7,5},{8,10},{9,11},{10,... | collective-permute-start | bytes 147464 | tf_op jit(solution)/shard_map/ppermute | solution.py:73
  18.2 3.4 %collective-permute-start.9 = (bf16[16,1536]{1,0:T(8,128)(2,1)S(1)}, bf16[16,1536]{1,0:T(8,128)(2,1)}, u32[]{:S(2)}, u32[]{:S(2)}) collective-permute-start(bf16[16,1536]{1,0:T(8,128)(2,1)S(1)} %collective-permute-done.1.refs_3_), channel_id=1, source_target_pairs={{0,1},{1,0},{2,3},{3,2},{4,5},{5,4},{6,7},{7,6},{8,9},{9,8},{10,11... | collective-permute-start | bytes 147464 | tf_op jit(solution)/shard_map/ppermute | solution.py:73
  18.2 3.4 %collective-permute-start.8 = (bf16[16,1536]{1,0:T(8,128)(2,1)S(1)}, bf16[16,1536]{1,0:T(8,128)(2,1)}, u32[]{:S(2)}, u32[]{:S(2)}) collective-permute-start(bf16[16,1536]{1,0:T(8,128)(2,1)S(1)} %collective-permute-done.refs_2_), channel_id=1, source_target_pairs={{0,1},{1,0},{2,3},{3,2},{4,5},{5,4},{6,7},{7,6},{8,9},{9,8},{10,11... | collective-permute-start | bytes 147464 | tf_op jit(solution)/shard_map/ppermute | solution.py:73
  18.7 2.9 %collective-permute-start.14 = (bf16[16,1536]{1,0:T(8,128)(2,1)}, bf16[16,1536]{1,0:T(8,128)(2,1)}, u32[]{:S(2)}, u32[]{:S(2)}) collective-permute-start(bf16[16,1536]{1,0:T(8,128)(2,1)} %collective-permute-done.6.refs_8_), channel_id=1, source_target_pairs={{0,1},{1,0},{2,3},{3,2},{4,5},{5,4},{6,7},{7,6},{8,9},{9,8},{10,11... | collective-permute-start | bytes 147464 | tf_op jit(solution)/shard_map/ppermute | solution.py:73
  20.4 1.6 %collective-permute-start.13 = (bf16[16,1536]{1,0:T(8,128)(2,1)}, bf16[16,1536]{1,0:T(8,128)(2,1)}, u32[]{:S(2)}, u32[]{:S(2)}) collective-permute-start(bf16[16,1536]{1,0:T(8,128)(2,1)} %collective-permute-done.5.refs_7_), channel_id=1, source_target_pairs={{0,1},{1,0},{2,3},{3,2},{4,5},{5,4},{6,7},{7,6},{8,9},{9,8},{10,11... | collective-permute-start | bytes 147464 | tf_op jit(solution)/shard_map/ppermute | solution.py:73
  24.5 1.8 %collective-permute-start.15 = (f32[64,1664]{1,0:T(8,128)S(1)}, f32[64,1664]{1,0:T(8,128)S(1)}, u32[]{:S(2)}, u32[]{:S(2)}) collective-permute-start(f32[64,1664]{1,0:T(8,128)S(1)} %get-tuple-element.28), channel_id=1, source_target_pairs={{0,1},{1,0},{2,3},{3,2},{4,5},{5,4},{6,7},{7,6},{8,9},{9,8},{10,11... | collective-permute-start | bytes 1277960 | tf_op jit(solution)/shard_map/ppermute | solution.py:73
  26.5 6.4 %collective-permute-start.18 = (bf16[16,1664]{1,0:T(8,128)(2,1)S(1)}, bf16[16,1664]{1,0:T(8,128)(2,1)S(1)}, u32[]{:S(2)}, u32[]{:S(2)}) collective-permute-start(bf16[16,1664]{1,0:T(8,128)(2,1)S(1)} %get-tuple-element.40), channel_id=1, source_target_pairs={{0,12},{1,13},{2,14},{3,15},{4,8},{5,9},{6,10},{7,11},{8,4},{9,5},... | collective-permute-start | bytes 159752 | tf_op jit(solution)/shard_map/ppermute | solution.py:73
  29.5 5.1 %collective-permute-start.17 = (bf16[16,1664]{1,0:T(8,128)(2,1)S(1)}, bf16[16,1664]{1,0:T(8,128)(2,1)S(1)}, u32[]{:S(2)}, u32[]{:S(2)}) collective-permute-start(bf16[16,1664]{1,0:T(8,128)(2,1)S(1)} %get-tuple-element.41), channel_id=1, source_target_pairs={{0,8},{1,9},{2,10},{3,11},{4,12},{5,13},{6,14},{7,15},{8,0},{9,1},... | collective-permute-start | bytes 159752 | tf_op jit(solution)/shard_map/ppermute | solution.py:73
  29.5 5.3 %collective-permute-start.16 = (bf16[16,1664]{1,0:T(8,128)(2,1)S(1)}, bf16[16,1664]{1,0:T(8,128)(2,1)S(1)}, u32[]{:S(2)}, u32[]{:S(2)}) collective-permute-start(bf16[16,1664]{1,0:T(8,128)(2,1)S(1)} %get-tuple-element.42), channel_id=1, source_target_pairs={{0,4},{1,5},{2,6},{3,7},{4,0},{5,1},{6,2},{7,3},{8,12},{9,13},{10,... | collective-permute-start | bytes 159752 | tf_op jit(solution)/shard_map/ppermute | solution.py:73
  34.8 4.2 %collective-permute-start.19 = (bf16[16,1664]{1,0:T(8,128)(2,1)S(1)}, bf16[16,1664]{1,0:T(8,128)(2,1)S(1)}, u32[]{:S(2)}, u32[]{:S(2)}) collective-permute-start(bf16[16,1664]{1,0:T(8,128)(2,1)S(1)} %sum.1), channel_id=1, source_target_pairs={{0,2},{1,3},{2,0},{3,1},{4,6},{5,7},{6,4},{7,5},{8,10},{9,11},{10,... | collective-permute-start | bytes 159752 | tf_op jit(solution)/shard_map/ppermute | solution.py:73
  39.0 6.1 %collective-permute-start.22 = (bf16[16,1664]{1,0:T(8,128)(2,1)S(1)}, bf16[16,1664]{1,0:T(8,128)(2,1)S(1)}, u32[]{:S(2)}, u32[]{:S(2)}) collective-permute-start(bf16[16,1664]{1,0:T(8,128)(2,1)S(1)} %fusion.1.refs_0_), channel_id=1, source_target_pairs={{0,12},{1,13},{2,14},{3,15},{4,8},{5,9},{6,10},{7,11},{8,4},{9,5},... | collective-permute-start | bytes 159752 | tf_op jit(solution)/shard_map/ppermute | solution.py:73
  41.5 5.0 %collective-permute-start.21 = (bf16[16,1664]{1,0:T(8,128)(2,1)S(1)}, bf16[16,1664]{1,0:T(8,128)(2,1)S(1)}, u32[]{:S(2)}, u32[]{:S(2)}) collective-permute-start(bf16[16,1664]{1,0:T(8,128)(2,1)S(1)} %fusion.1.refs_0_), channel_id=1, source_target_pairs={{0,8},{1,9},{2,10},{3,11},{4,12},{5,13},{6,14},{7,15},{8,0},{9,1},... | collective-permute-start | bytes 159752 | tf_op jit(solution)/shard_map/ppermute | solution.py:73
  41.5 5.0 %collective-permute-start.20 = (bf16[16,1664]{1,0:T(8,128)(2,1)S(1)}, bf16[16,1664]{1,0:T(8,128)(2,1)S(1)}, u32[]{:S(2)}, u32[]{:S(2)}) collective-permute-start(bf16[16,1664]{1,0:T(8,128)(2,1)S(1)} %fusion.1.refs_0_), channel_id=1, source_target_pairs={{0,4},{1,5},{2,6},{3,7},{4,0},{5,1},{6,2},{7,3},{8,12},{9,13},{10,... | collective-permute-start | bytes 159752 | tf_op jit(solution)/shard_map/ppermute | solution.py:73
  43.5 3.5 %collective-permute-start.23 = (bf16[16,1664]{1,0:T(8,128)(2,1)S(1)}, bf16[16,1664]{1,0:T(8,128)(2,1)S(1)}, u32[]{:S(2)}, u32[]{:S(2)}) collective-permute-start(bf16[16,1664]{1,0:T(8,128)(2,1)S(1)} %fusion.1.refs_0_), channel_id=1, source_target_pairs={{0,1},{1,0},{2,3},{3,2},{4,5},{5,4},{6,7},{7,6},{8,9},{9,8},{10,11... | collective-permute-start | bytes 159752 | tf_op jit(solution)/shard_map/ppermute | solution.py:73
  45.2 1.9 %collective-permute-start.26 = (bf16[16,1664]{1,0:T(8,128)(2,1)S(1)}, bf16[16,1664]{1,0:T(8,128)(2,1)S(1)}, u32[]{:S(2)}, u32[]{:S(2)}) collective-permute-start(bf16[16,1664]{1,0:T(8,128)(2,1)S(1)} %collective-permute-done.22.refs_3_), channel_id=1, source_target_pairs={{0,1},{1,0},{2,3},{3,2},{4,5},{5,4},{6,7},{7,6},{8,9},{9,8},{10,11... | collective-permute-start | bytes 159752 | tf_op jit(solution)/shard_map/ppermute | solution.py:73
  (7 other events, 79.0 us)

commit v7 on v6

--- a/solution.py
+++ b/solution.py
@@ -95,7 +95,9 @@
     return pl.BlockSpec(memory_space=pltpu.SMEM)
 
 
-def launch(limit, kernel, name, out_shape, in_specs, out_specs, scratch=(), flops=0, moved=0):
+def launch(
+    kernel, name, out_shape, in_specs, out_specs, scratch=(), flops=0, moved=0, limit=0, aliases=None
+):
     return pl.pallas_call(
         kernel,
         name=name,
@@ -103,6 +105,7 @@
         in_specs=in_specs,
         out_specs=out_specs,
         scratch_shapes=list(scratch),
+        input_output_aliases=aliases or {},
         compiler_params=pltpu.CompilerParams(vmem_limit_bytes=limit),
         cost_estimate=pl.CostEstimate(flops=flops, bytes_accessed=moved, transcendentals=0),
     )
@@ -122,8 +125,9 @@
     slots, samples = wave.shape
     frames = out.shape[0] // slots
     copies = []
-    for c in range(checkpoints):
-        copies.append(pltpu.make_async_copy(sources[6].at[c], second_w.at[c], more.at[c]))
+    for i in range(checkpoints * 3):
+        at = (i // 3, pl.ds((i % 3) * channels, channels))
+        copies.append(pltpu.make_async_copy(sources[6].at[at], second_w.at[at], more.at[i]))
         copies[-1].start()
     for copy in small:
         copy.wait()
@@ -176,7 +180,8 @@
     hidden = layer_one(0)
     held_back = None
     for c in range(checkpoints):
-        copies[c].wait()
+        for tap in range(3):
+            copies[3 * c + tap].wait()
         total = layer_two(c, hidden)
         if c + 1 < checkpoints:
             hidden = layer_one(c + 1)
@@ -192,6 +197,10 @@
     for ref in refs[:-1]:
         out[at : at + ref.shape[0], :] = ref[...]
         at += ref.shape[0]
+
+
+def pass_kernel(*_):
+    pass
 
 
 def norms_kernel(dec, norms, row):
@@ -213,7 +222,9 @@
     me_ref = refs[0]
     pieces = refs[1 : 1 + count]
     enc, bias, dec, weights_sum, dec_bias = refs[1 + count : 6 + count]
-    own, send, shift, inputs_out, latent_out = refs[6 + count :]
+    own, send, shift, inputs_out, latent_out, enc_buf, sem = refs[6 + count :]
+    fetch = pltpu.make_async_copy(enc, enc_buf, sem)
+    fetch.start()
     me = me_ref[0]
     step = 2 * inner
     tokens, feature = inputs_out.shape
@@ -267,7 +278,8 @@
         total = total + jnp.dot(pick, block, preferred_element_type=F32)
     inputs = total.astype(BF16)
     inputs_out[...] = inputs
-    latent = jnp.maximum(jnp.dot(inputs, enc[...], preferred_element_type=F32) + bias[...], 0.0)
+    fetch.wait()
+    latent = jnp.maximum(jnp.dot(inputs, enc_buf[...], preferred_element_type=F32) + bias[...], 0.0)
     latent_out[...] = latent
     part = jnp.dot(latent.astype(BF16), dec[...], preferred_element_type=F32)
     weighted = latent * weights_sum[0:1, :]
@@ -284,12 +296,15 @@
     shift[:, feature:] = jnp.zeros((chunk, EXTRA), F32)
 
 
-def turn_kernel(inputs, latent, norms, inputs_t, latent_t, scale):
+def turn_kernel(inputs, latent, norms, dec, inputs_t, latent_t, term):
     inputs_t[...] = inputs[...].astype(F32).T.astype(BF16)
     turned = latent[...].T
-    latent_t[...] = turned.astype(BF16)
-    activity = jnp.sum(turned, axis=1, keepdims=True)
-    scale[...] = (sparsity * activity) / jnp.maximum(norms[...], 1e-30)
+    latent_t[...] = (2.0 * turned).astype(BF16)
+    activity = sparsity * jnp.sum(turned, axis=1, keepdims=True)
+    channels = 512
+    for c in range(dec.shape[1] // channels):
+        lanes = slice(c * channels, (c + 1) * channels)
+        term[:, lanes] = (activity / norms[:, c : c + 1]) * dec[:, lanes].astype(F32)
 
 
 def sum_kernel(*refs):
@@ -301,22 +316,18 @@
 
 def gradients_kernel(count, inner, cells, *refs):
     pieces = refs[:count]
-    dec, weights_sum, inputs_t, latent_t, latent, scale = refs[count : count + 6]
+    dec, weights_sum, inputs_t, latent_t, latent, term = refs[count : count + 6]
     enc_out, dec_out, enc_bias_out, dec_bias_out, loss_out, errors_out = refs[count + 6 : count + 12]
     enc_buf, dec_buf, sems = refs[count + 12 :]
     latents, feature = dec.shape
-    channels = 512
     errors = jnp.concatenate([piece[:, :feature] for piece in pieces], axis=0)
     copies = []
     parts = 4
     size = latents // parts
     for i in range(parts):
         at = slice(i * size, (i + 1) * size)
-        grad = 2.0 * jnp.dot(latent_t[at], errors, preferred_element_type=F32)
-        for c in range(feature // channels):
-            lanes = slice(c * channels, (c + 1) * channels)
-            term = scale[at, c : c + 1] * dec[at, lanes].astype(F32)
-            dec_buf[at, lanes] = (grad[:, lanes] + term).astype(BF16)
+        grad = jnp.dot(latent_t[at], errors, preferred_element_type=F32)
+        dec_buf[at] = (grad + term[at]).astype(BF16)
         copies.append(pltpu.make_async_copy(dec_buf.at[at], dec_out.at[at], sems.at[i]))
         copies[-1].start()
     upstream = lax.dot_general(
@@ -371,7 +382,7 @@
     wide = feature + EXTRA
 
     pinned = tokens <= PINNED_TOKENS
-    call = functools.partial(launch, PINNED_BYTES if pinned else VMEM_BYTES)
+    call = functools.partial(launch, limit=PINNED_BYTES if pinned else VMEM_BYTES)
 
     def fast(dims, kind):
         return pltpu.VMEM(dims, kind) if pinned else shape(dims, kind)
@@ -383,7 +394,7 @@
         return pltpu.with_memory_space_constraint(value, pltpu.HBM)
 
     kernels = conv_first.transpose(1, 0, 2)
-    encoder = near(enc_weight)
+    encoder = far(enc_weight)
     decoder = near(dec_weight)
 
     packed = call(
@@ -401,7 +412,7 @@
             pltpu.VMEM(norm_shift.shape, F32),
             pltpu.VMEM(conv_second.shape, BF16),
             pltpu.SemaphoreType.DMA((6,)),
-            pltpu.SemaphoreType.DMA((checkpoints,)),
+            pltpu.SemaphoreType.DMA((3 * checkpoints,)),
         ],
         flops=2 * slots * frames * feature * 3 * channels,
         moved=2 * conv_second.size,
@@ -423,6 +434,15 @@
     )(decoder)
 
     blocks = [packed] + [exchange(packed, step * k) for k in range(1, outer)]
+    if pinned:
+        blocks[1] = call(
+            pass_kernel,
+            "pass",
+            fast(packed.shape, BF16),
+            [pl.BlockSpec(memory_space=pl.ANY)] * 2,
+            pl.BlockSpec(memory_space=pl.ANY),
+            aliases={1: 0},
+        )(near(norms), near(blocks[1]))
     pieces = blocks
     if not pinned:
         pieces = [
@@ -457,8 +477,13 @@
             fast((tokens, feature), BF16),
             fast((tokens, latents), F32),
         ),
-        [smem()] + [vmem()] * (len(pieces) + 5),
+        [smem()]
+        + [vmem()] * len(pieces)
+        + [pl.BlockSpec(memory_space=pl.ANY)]
+        + [vmem()] * 4,
         (vmem(),) * 5,
+        [pltpu.VMEM(enc_weight.shape, BF16), pltpu.SemaphoreType.DMA],
+        limit=VMEM_BYTES,
         flops=4 * tokens * feature * latents,
         moved=4 * dec_weight.size,
     )(
@@ -471,15 +496,15 @@
         dec_bias,
     )
 
-    inputs_t, latent_t, scale = call(
+    inputs_t, latent_t, term = call(
         turn_kernel,
         "turn",
-        (fast((feature, tokens), BF16), fast((latents, tokens), BF16), fast((latents, LANES), F32)),
-        [vmem()] * 3,
+        (fast((feature, tokens), BF16), fast((latents, tokens), BF16), fast((latents, feature), F32)),
+        [vmem()] * 4,
         (vmem(),) * 3,
         flops=2 * tokens * feature,
         moved=4 * tokens * feature,
-    )(near(inputs), near(latent), near(norms))
+    )(near(inputs), near(latent), near(norms), decoder)
 
     part = own + exchange(send, 1)
     small = part.astype(BF16)
@@ -493,7 +518,7 @@
         [pl.BlockSpec(memory_space=pl.ANY)] + [vmem()] * outer,
         vmem(),
         moved=8 * chunk * wide,
-    )(near(scale), *[near(block) for block in blocks])
+    )(near(term), *[near(block) for block in blocks])
     bit = 2
     while bit < step:
         width = (bit // 2) * ROWS_DEV
@@ -536,7 +561,7 @@
         near(inputs_t),
         near(latent_t),
         near(latent),
-        near(scale),
+        near(term),
     )
     return (
         enc_grad,

time: 51.5 us -> 53.2 us (1.033)
  Pallas kernels: 10.2 us -> 11.7 us
    pallas_call x1, Pallas kernels: 2.05 us -> 3.16 us  [shards(): call(encode, 'encode', (fast((half, wide), F32), fast((half, wide), F32),...]
  transfers between devices with their start and end apart: 27 -> 27, of which waited for: 15 -> 14; matrix products, arithmetic and copies ran while one was open for 0% -> 0% of each run, Pallas kernels for 2% -> 2%
where the time goes in v7:
time: 53.2 us; the launch traced here: 53 us
  starting transfers between devices  21.3 us (40%)
  waiting for transfers between devices  19.2 us (36%)
  Pallas kernels  11.7 us (22%)
  between operations  0.75 us (1%)
    ppermute x27, starting transfers between devices, exchange(): return lax.ppermute(value, 'utt', [(i, i ^ bit) for i in range(devices)])  21.3 us
    ppermute x27, waiting for transfers between devices, exchange(): return lax.ppermute(value, 'utt', [(i, i ^ bit) for i in range(devices)])  19.2 us
    pallas_call x1, Pallas kernels, shards(): call(features_kernel, 'features', fast((slots * frames, feature), BF16),...  3.99 us
    pallas_call x1, Pallas kernels, shards(): call(gradients, 'gradients', (shape((feature, latents), BF16), shape((lat...  3.24 us
    pallas_call x1, Pallas kernels, shards(): call(encode, 'encode', (fast((half, wide), F32), fast((half, wide), F32),...  3.16 us
  transfers between devices with their start and end apart: 27, of which 14 were waited for; matrix products, arithmetic and copies ran while one was open for 0% of the time, Pallas kernels for 2%

profile of v7, /device:TPU:0, one launch (start us, length us, event | category | flops | bytes accessed | tf_op | source)
XLA Modules:
  0.0 53.0 jit_solution(14573899666937263469)
XLA Ops:
  0.6 4.0 %features.1.refs_1_ = bf16[16,1536]{1,0:T(8,128)(2,1)S(1)} custom-call(s32[2]{0:T(128)} %refs_0_.1, s32[2]{0:T(128)} %refs_1_.1, f32[2,90]{1,0:T(2,128)} %refs_2_.1, f32[10,3,512]{2,1,0:T(4,128)} %bitcast.13, f32[3,2,512]{2,1,0:T(2,128)} %refs_4_.1, f32[3,2,512]{2,1,0:T(2,128)} %refs_5_.1, bf16[3,1536,512]{2,1,0:T(8,128)(2,1)} %refs_6_.1), custom_call_target="tpu_custom_call" | custom-call | flops 75497472 | bytes 4718592 | tf_op jit(solution)/shard_map/features/pallas_call | solution.py:400
  4.6 3.0 %collective-permute-start.3 = (bf16[16,1536]{1,0:T(8,128)(2,1)S(1)}, bf16[16,1536]{1,0:T(8,128)(2,1)S(1)}, u32[]{:S(2)}, u32[]{:S(2)}) collective-permute-start(bf16[16,1536]{1,0:T(8,128)(2,1)S(1)} %features.1.refs_1_), channel_id=1, source_target_pairs={{0,2},{1,3},{2,0},{3,1},{4,6},{5,7},{6,4},{7,5},{8,10},{9,11},{10,... | collective-permute-start | bytes 147464 | tf_op jit(solution)/shard_map/ppermute | solution.py:73
  7.7 3.6 %collective-permute-start.2 = (bf16[16,1536]{1,0:T(8,128)(2,1)S(1)}, bf16[16,1536]{1,0:T(8,128)(2,1)S(1)}, u32[]{:S(2)}, u32[]{:S(2)}) collective-permute-start(bf16[16,1536]{1,0:T(8,128)(2,1)S(1)} %features.1.refs_1_), channel_id=1, source_target_pairs={{0,12},{1,13},{2,14},{3,15},{4,8},{5,9},{6,10},{7,11},{8,4},{9,5},... | collective-permute-start | bytes 147464 | tf_op jit(solution)/shard_map/ppermute | solution.py:73
  11.3 0.8 %collective-permute-start = (bf16[16,1536]{1,0:T(8,128)(2,1)S(1)}, bf16[16,1536]{1,0:T(8,128)(2,1)S(1)}, u32[]{:S(2)}, u32[]{:S(2)}) collective-permute-start(bf16[16,1536]{1,0:T(8,128)(2,1)S(1)} %features.1.refs_1_), channel_id=1, source_target_pairs={{0,4},{1,5},{2,6},{3,7},{4,0},{5,1},{6,2},{7,3},{8,12},{9,13},{10,... | collective-permute-start | bytes 147464 | tf_op jit(solution)/shard_map/ppermute | solution.py:73
  12.1 0.7 %norms.1 = (f32[512,128]{1,0:T(8,128)S(1)}, f32[8,512]{1,0:T(8,128)S(1)}) custom-call(bf16[512,1536]{1,0:T(8,128)(2,1)S(1)} %copy-done), custom_call_target="tpu_custom_call" | custom-call | flops 3145728 | bytes 1572864 | tf_op jit(solution)/shard_map/norms/pallas_call | solution.py:426
  13.3 0.8 %collective-permute-done.2.refs_4_ = bf16[16,1536]{1,0:T(8,128)(2,1)S(1)} collective-permute-done((bf16[16,1536]{1,0:T(8,128)(2,1)S(1)}, bf16[16,1536]{1,0:T(8,128)(2,1)S(1)}, u32[]{:S(2)}, u32[]{:S(2)}) %collective-permute-start.2) | collective-permute-done | bytes 49184 | tf_op jit(solution)/shard_map/ppermute | solution.py:73
  14.1 2.2 %collective-permute-done.1.refs_3_ = bf16[16,1536]{1,0:T(8,128)(2,1)S(1)} collective-permute-done((bf16[16,1536]{1,0:T(8,128)(2,1)S(1)}, bf16[16,1536]{1,0:T(8,128)(2,1)S(1)}, u32[]{:S(2)}, u32[]{:S(2)}) %collective-permute-start.1) | collective-permute-done | bytes 49184 | tf_op jit(solution)/shard_map/ppermute | solution.py:73
  16.8 1.5 %collective-permute-start.5 = (bf16[16,1536]{1,0:T(8,128)(2,1)S(1)}, bf16[16,1536]{1,0:T(8,128)(2,1)S(1)}, u32[]{:S(2)}, u32[]{:S(2)}) collective-permute-start(bf16[16,1536]{1,0:T(8,128)(2,1)S(1)} %collective-permute-done.1.refs_3_), channel_id=1, source_target_pairs={{0,2},{1,3},{2,0},{3,1},{4,6},{5,7},{6,4},{7,5},{8,10},{9,11},{10,... | collective-permute-start | bytes 147464 | tf_op jit(solution)/shard_map/ppermute | solution.py:73
  19.3 1.0 %collective-permute-done.6.refs_8_ = bf16[16,1536]{1,0:T(8,128)(2,1)S(1)} collective-permute-done((bf16[16,1536]{1,0:T(8,128)(2,1)S(1)}, bf16[16,1536]{1,0:T(8,128)(2,1)S(1)}, u32[]{:S(2)}, u32[]{:S(2)}) %collective-permute-start.6) | collective-permute-done | bytes 49184 | tf_op jit(solution)/shard_map/ppermute | solution.py:73
  20.9 1.5 %collective-permute-done.4.refs_6_ = bf16[16,1536]{1,0:T(8,128)(2,1)S(1)} collective-permute-done((bf16[16,1536]{1,0:T(8,128)(2,1)S(1)}, bf16[16,1536]{1,0:T(8,128)(2,1)S(1)}, u32[]{:S(2)}, u32[]{:S(2)}) %collective-permute-start.4) | collective-permute-done | bytes 49184 | tf_op jit(solution)/shard_map/ppermute | solution.py:73
  22.4 1.2 %collective-permute-done.12.refs_14_ = bf16[16,1536]{1,0:T(8,128)(2,1)S(1)} collective-permute-done((bf16[16,1536]{1,0:T(8,128)(2,1)S(1)}, bf16[16,1536]{1,0:T(8,128)(2,1)S(1)}, u32[]{:S(2)}, u32[]{:S(2)}) %collective-permute-start.12) | collective-permute-done | bytes 49184 | tf_op jit(solution)/shard_map/ppermute | solution.py:73
  23.6 3.2 %encode.1 = (f32[64,1664]{1,0:T(8,128)S(1)}, f32[64,1664]{1,0:T(8,128)S(1)}, f32[16,1664]{1,0:T(8,128)S(1)}, bf16[128,1536]{1,0:T(8,128)(2,1)S(1)}, f32[128,512]{1,0:T(8,128)S(1)}) custom-call(s32[1]{0:T(128)} %bitcast.refs_0_, bf16[16,1536]{1,0:T(8,128)(2,1)S(1)} %features.1.refs_1_, bf16[16,1536]{1,0:T(8,128)(2,1)S(1)} %pass.1.refs_2_, ...), custom_call_target="tpu_custom_call" | custom-call | flops 402653184 | bytes 3145728 | tf_op jit(solution)/shard_map/encode/pallas_call | solution.py:470
  27.0 1.6 %collective-permute-done.15 = f32[64,1664]{1,0:T(8,128)S(1)} collective-permute-done((f32[64,1664]{1,0:T(8,128)S(1)}, f32[64,1664]{1,0:T(8,128)S(1)}, u32[]{:S(2)}, u32[]{:S(2)}) %collective-permute-start.15) | collective-permute-done | bytes 426016 | tf_op jit(solution)/shard_map/ppermute | solution.py:73
  28.7 1.8 %collective-permute-start.18 = (bf16[16,1664]{1,0:T(8,128)(2,1)S(1)}, bf16[16,1664]{1,0:T(8,128)(2,1)S(1)}, u32[]{:S(2)}, u32[]{:S(2)}) collective-permute-start(bf16[16,1664]{1,0:T(8,128)(2,1)S(1)} %get-tuple-element.40), channel_id=1, source_target_pairs={{0,12},{1,13},{2,14},{3,15},{4,8},{5,9},{6,10},{7,11},{8,4},{9,5},... | collective-permute-start | bytes 159752 | tf_op jit(solution)/shard_map/ppermute | solution.py:73
  30.5 2.6 %collective-permute-start.16 = (bf16[16,1664]{1,0:T(8,128)(2,1)S(1)}, bf16[16,1664]{1,0:T(8,128)(2,1)S(1)}, u32[]{:S(2)}, u32[]{:S(2)}) collective-permute-start(bf16[16,1664]{1,0:T(8,128)(2,1)S(1)} %get-tuple-element.42), channel_id=1, source_target_pairs={{0,4},{1,5},{2,6},{3,7},{4,0},{5,1},{6,2},{7,3},{8,12},{9,13},{10,... | collective-permute-start | bytes 159752 | tf_op jit(solution)/shard_map/ppermute | solution.py:73
  33.8 1.4 %collective-permute-done.18.refs_4_ = bf16[16,1664]{1,0:T(8,128)(2,1)S(1)} collective-permute-done((bf16[16,1664]{1,0:T(8,128)(2,1)S(1)}, bf16[16,1664]{1,0:T(8,128)(2,1)S(1)}, u32[]{:S(2)}, u32[]{:S(2)}) %collective-permute-start.18) | collective-permute-done | bytes 53280 | tf_op jit(solution)/shard_map/ppermute | solution.py:73
  35.2 1.6 %collective-permute-done.17.refs_3_ = bf16[16,1664]{1,0:T(8,128)(2,1)S(1)} collective-permute-done((bf16[16,1664]{1,0:T(8,128)(2,1)S(1)}, bf16[16,1664]{1,0:T(8,128)(2,1)S(1)}, u32[]{:S(2)}, u32[]{:S(2)}) %collective-permute-start.17) | collective-permute-done | bytes 53280 | tf_op jit(solution)/shard_map/ppermute | solution.py:73
  37.4 3.6 %collective-permute-done.19 = bf16[16,1664]{1,0:T(8,128)(2,1)S(1)} collective-permute-done((bf16[16,1664]{1,0:T(8,128)(2,1)S(1)}, bf16[16,1664]{1,0:T(8,128)(2,1)S(1)}, u32[]{:S(2)}, u32[]{:S(2)}) %collective-permute-start.19) | collective-permute-done | bytes 53280 | tf_op jit(solution)/shard_map/ppermute | solution.py:73
  41.0 1.8 %collective-permute-start.22 = (bf16[16,1664]{1,0:T(8,128)(2,1)S(1)}, bf16[16,1664]{1,0:T(8,128)(2,1)S(1)}, u32[]{:S(2)}, u32[]{:S(2)}) collective-permute-start(bf16[16,1664]{1,0:T(8,128)(2,1)S(1)} %fusion.1.refs_0_), channel_id=1, source_target_pairs={{0,12},{1,13},{2,14},{3,15},{4,8},{5,9},{6,10},{7,11},{8,4},{9,5},... | collective-permute-start | bytes 159752 | tf_op jit(solution)/shard_map/ppermute | solution.py:73
  43.1 2.4 %collective-permute-start.20 = (bf16[16,1664]{1,0:T(8,128)(2,1)S(1)}, bf16[16,1664]{1,0:T(8,128)(2,1)S(1)}, u32[]{:S(2)}, u32[]{:S(2)}) collective-permute-start(bf16[16,1664]{1,0:T(8,128)(2,1)S(1)} %fusion.1.refs_0_), channel_id=1, source_target_pairs={{0,4},{1,5},{2,6},{3,7},{4,0},{5,1},{6,2},{7,3},{8,12},{9,13},{10,... | collective-permute-start | bytes 159752 | tf_op jit(solution)/shard_map/ppermute | solution.py:73
  45.5 1.8 %collective-permute-done.22.refs_3_ = bf16[16,1664]{1,0:T(8,128)(2,1)S(1)} collective-permute-done((bf16[16,1664]{1,0:T(8,128)(2,1)S(1)}, bf16[16,1664]{1,0:T(8,128)(2,1)S(1)}, u32[]{:S(2)}, u32[]{:S(2)}) %collective-permute-start.22) | collective-permute-done | bytes 53280 | tf_op jit(solution)/shard_map/ppermute | solution.py:73
  47.3 1.1 %collective-permute-done.21.refs_2_ = bf16[16,1664]{1,0:T(8,128)(2,1)S(1)} collective-permute-done((bf16[16,1664]{1,0:T(8,128)(2,1)S(1)}, bf16[16,1664]{1,0:T(8,128)(2,1)S(1)}, u32[]{:S(2)}, u32[]{:S(2)}) %collective-permute-start.21) | collective-permute-done | bytes 53280 | tf_op jit(solution)/shard_map/ppermute | solution.py:73
  48.9 0.7 %collective-permute-done.25.refs_6_ = bf16[16,1664]{1,0:T(8,128)(2,1)S(1)} collective-permute-done((bf16[16,1664]{1,0:T(8,128)(2,1)S(1)}, bf16[16,1664]{1,0:T(8,128)(2,1)S(1)}, u32[]{:S(2)}, u32[]{:S(2)}) %collective-permute-start.25) | collective-permute-done | bytes 53280 | tf_op jit(solution)/shard_map/ppermute | solution.py:73
  49.8 3.2 %gradients.1 = (bf16[1536,512]{1,0:T(8,128)(2,1)}, bf16[512,1536]{1,0:T(8,128)(2,1)}, f32[1,512]{1,0:T(1,128)}, f32[1536]{0:T(1024)}, f32[1]{0:T(128)}, /*index=5*/bf16[8,1536]{1,0:T(8,128)(2,1)}) custom-call(bf16[16,1664]{1,0:T(8,128)(2,1)S(1)} %fusion.1.refs_0_, bf16[16,1664]{1,0:T(8,128)(2,1)S(1)} %collective-permute-done.20.refs_1_, ...), custom_call_target="tpu_custom_call" | custom-call | flops 603979776 | bytes 6291456 | tf_op jit(solution)/shard_map/gradients/pallas_call | solution.py:537
  (44 shorter events, 5.1 us)
Async XLA Ops:
  4.6 8.1 %collective-permute-start.3 = (bf16[16,1536]{1,0:T(8,128)(2,1)S(1)}, bf16[16,1536]{1,0:T(8,128)(2,1)S(1)}, u32[]{:S(2)}, u32[]{:S(2)}) collective-permute-start(bf16[16,1536]{1,0:T(8,128)(2,1)S(1)} %features.1.refs_1_), channel_id=1, source_target_pairs={{0,2},{1,3},{2,0},{3,1},{4,6},{5,7},{6,4},{7,5},{8,10},{9,11},{10,... | collective-permute-start | bytes 147464 | tf_op jit(solution)/shard_map/ppermute | solution.py:73
  7.7 6.4 %collective-permute-start.2 = (bf16[16,1536]{1,0:T(8,128)(2,1)S(1)}, bf16[16,1536]{1,0:T(8,128)(2,1)S(1)}, u32[]{:S(2)}, u32[]{:S(2)}) collective-permute-start(bf16[16,1536]{1,0:T(8,128)(2,1)S(1)} %features.1.refs_1_), channel_id=1, source_target_pairs={{0,12},{1,13},{2,14},{3,15},{4,8},{5,9},{6,10},{7,11},{8,4},{9,5},... | collective-permute-start | bytes 147464 | tf_op jit(solution)/shard_map/ppermute | solution.py:73
  11.3 5.0 %collective-permute-start.1 = (bf16[16,1536]{1,0:T(8,128)(2,1)S(1)}, bf16[16,1536]{1,0:T(8,128)(2,1)S(1)}, u32[]{:S(2)}, u32[]{:S(2)}) collective-permute-start(bf16[16,1536]{1,0:T(8,128)(2,1)S(1)} %features.1.refs_1_), channel_id=1, source_target_pairs={{0,8},{1,9},{2,10},{3,11},{4,12},{5,13},{6,14},{7,15},{8,0},{9,1},... | collective-permute-start | bytes 147464 | tf_op jit(solution)/shard_map/ppermute | solution.py:73
  11.3 5.5 %collective-permute-start = (bf16[16,1536]{1,0:T(8,128)(2,1)S(1)}, bf16[16,1536]{1,0:T(8,128)(2,1)S(1)}, u32[]{:S(2)}, u32[]{:S(2)}) collective-permute-start(bf16[16,1536]{1,0:T(8,128)(2,1)S(1)} %features.1.refs_1_), channel_id=1, source_target_pairs={{0,4},{1,5},{2,6},{3,7},{4,0},{5,1},{6,2},{7,3},{8,12},{9,13},{10,... | collective-permute-start | bytes 147464 | tf_op jit(solution)/shard_map/ppermute | solution.py:73
  12.1 6.2 %collective-permute-start.7 = (bf16[16,1536]{1,0:T(8,128)(2,1)S(1)}, bf16[16,1536]{1,0:T(8,128)(2,1)S(1)}, u32[]{:S(2)}, u32[]{:S(2)}) collective-permute-start(bf16[16,1536]{1,0:T(8,128)(2,1)S(1)} %features.1.refs_1_), channel_id=1, source_target_pairs={{0,1},{1,0},{2,3},{3,2},{4,5},{5,4},{6,7},{7,6},{8,9},{9,8},{10,11... | collective-permute-start | bytes 147464 | tf_op jit(solution)/shard_map/ppermute | solution.py:73
  12.8 6.0 %collective-permute-start.11 = (bf16[16,1536]{1,0:T(8,128)(2,1)S(1)}, bf16[16,1536]{1,0:T(8,128)(2,1)S(1)}, u32[]{:S(2)}, u32[]{:S(2)}) collective-permute-start(bf16[16,1536]{1,0:T(8,128)(2,1)S(1)} %collective-permute-done.3.refs_5_), channel_id=1, source_target_pairs={{0,1},{1,0},{2,3},{3,2},{4,5},{5,4},{6,7},{7,6},{8,9},{9,8},{10,11... | collective-permute-start | bytes 147464 | tf_op jit(solution)/shard_map/ppermute | solution.py:73
  14.1 4.7 %collective-permute-start.10 = (bf16[16,1536]{1,0:T(8,128)(2,1)S(1)}, bf16[16,1536]{1,0:T(8,128)(2,1)S(1)}, u32[]{:S(2)}, u32[]{:S(2)}) collective-permute-start(bf16[16,1536]{1,0:T(8,128)(2,1)S(1)} %collective-permute-done.2.refs_4_), channel_id=1, source_target_pairs={{0,1},{1,0},{2,3},{3,2},{4,5},{5,4},{6,7},{7,6},{8,9},{9,8},{10,11... | collective-permute-start | bytes 147464 | tf_op jit(solution)/shard_map/ppermute | solution.py:73
  16.3 4.1 %collective-permute-start.6 = (bf16[16,1536]{1,0:T(8,128)(2,1)S(1)}, bf16[16,1536]{1,0:T(8,128)(2,1)S(1)}, u32[]{:S(2)}, u32[]{:S(2)}) collective-permute-start(bf16[16,1536]{1,0:T(8,128)(2,1)S(1)} %collective-permute-done.2.refs_4_), channel_id=1, source_target_pairs={{0,2},{1,3},{2,0},{3,1},{4,6},{5,7},{6,4},{7,5},{8,10},{9,11},{10,... | collective-permute-start | bytes 147464 | tf_op jit(solution)/shard_map/ppermute | solution.py:73
  16.8 4.1 %collective-permute-start.5 = (bf16[16,1536]{1,0:T(8,128)(2,1)S(1)}, bf16[16,1536]{1,0:T(8,128)(2,1)S(1)}, u32[]{:S(2)}, u32[]{:S(2)}) collective-permute-start(bf16[16,1536]{1,0:T(8,128)(2,1)S(1)} %collective-permute-done.1.refs_3_), channel_id=1, source_target_pairs={{0,2},{1,3},{2,0},{3,1},{4,6},{5,7},{6,4},{7,5},{8,10},{9,11},{10,... | collective-permute-start | bytes 147464 | tf_op jit(solution)/shard_map/ppermute | solution.py:73
  18.3 4.1 %collective-permute-start.4 = (bf16[16,1536]{1,0:T(8,128)(2,1)S(1)}, bf16[16,1536]{1,0:T(8,128)(2,1)S(1)}, u32[]{:S(2)}, u32[]{:S(2)}) collective-permute-start(bf16[16,1536]{1,0:T(8,128)(2,1)S(1)} %pass.1.refs_2_), channel_id=1, source_target_pairs={{0,2},{1,3},{2,0},{3,1},{4,6},{5,7},{6,4},{7,5},{8,10},{9,11},{10,... | collective-permute-start | bytes 147464 | tf_op jit(solution)/shard_map/ppermute | solution.py:73
  18.8 3.6 %collective-permute-start.8 = (bf16[16,1536]{1,0:T(8,128)(2,1)S(1)}, bf16[16,1536]{1,0:T(8,128)(2,1)S(1)}, u32[]{:S(2)}, u32[]{:S(2)}) collective-permute-start(bf16[16,1536]{1,0:T(8,128)(2,1)S(1)} %pass.1.refs_2_), channel_id=1, source_target_pairs={{0,1},{1,0},{2,3},{3,2},{4,5},{5,4},{6,7},{7,6},{8,9},{9,8},{10,11... | collective-permute-start | bytes 147464 | tf_op jit(solution)/shard_map/ppermute | solution.py:73
  18.8 3.6 %collective-permute-start.9 = (bf16[16,1536]{1,0:T(8,128)(2,1)S(1)}, bf16[16,1536]{1,0:T(8,128)(2,1)S(1)}, u32[]{:S(2)}, u32[]{:S(2)}) collective-permute-start(bf16[16,1536]{1,0:T(8,128)(2,1)S(1)} %collective-permute-done.1.refs_3_), channel_id=1, source_target_pairs={{0,1},{1,0},{2,3},{3,2},{4,5},{5,4},{6,7},{7,6},{8,9},{9,8},{10,11... | collective-permute-start | bytes 147464 | tf_op jit(solution)/shard_map/ppermute | solution.py:73
  20.4 2.1 %collective-permute-start.14 = (bf16[16,1536]{1,0:T(8,128)(2,1)S(1)}, bf16[16,1536]{1,0:T(8,128)(2,1)S(1)}, u32[]{:S(2)}, u32[]{:S(2)}) collective-permute-start(bf16[16,1536]{1,0:T(8,128)(2,1)S(1)} %collective-permute-done.6.refs_8_), channel_id=1, source_target_pairs={{0,1},{1,0},{2,3},{3,2},{4,5},{5,4},{6,7},{7,6},{8,9},{9,8},{10,11... | collective-permute-start | bytes 147464 | tf_op jit(solution)/shard_map/ppermute | solution.py:73
  20.9 1.5 %collective-permute-start.13 = (bf16[16,1536]{1,0:T(8,128)(2,1)S(1)}, bf16[16,1536]{1,0:T(8,128)(2,1)S(1)}, u32[]{:S(2)}, u32[]{:S(2)}) collective-permute-start(bf16[16,1536]{1,0:T(8,128)(2,1)S(1)} %collective-permute-done.5.refs_7_), channel_id=1, source_target_pairs={{0,1},{1,0},{2,3},{3,2},{4,5},{5,4},{6,7},{7,6},{8,9},{9,8},{10,11... | collective-permute-start | bytes 147464 | tf_op jit(solution)/shard_map/ppermute | solution.py:73
  26.8 1.8 %collective-permute-start.15 = (f32[64,1664]{1,0:T(8,128)S(1)}, f32[64,1664]{1,0:T(8,128)S(1)}, u32[]{:S(2)}, u32[]{:S(2)}) collective-permute-start(f32[64,1664]{1,0:T(8,128)S(1)} %get-tuple-element.28), channel_id=1, source_target_pairs={{0,1},{1,0},{2,3},{3,2},{4,5},{5,4},{6,7},{7,6},{8,9},{9,8},{10,11... | collective-permute-start | bytes 1277960 | tf_op jit(solution)/shard_map/ppermute | solution.py:73
  28.7 6.4 %collective-permute-start.18 = (bf16[16,1664]{1,0:T(8,128)(2,1)S(1)}, bf16[16,1664]{1,0:T(8,128)(2,1)S(1)}, u32[]{:S(2)}, u32[]{:S(2)}) collective-permute-start(bf16[16,1664]{1,0:T(8,128)(2,1)S(1)} %get-tuple-element.40), channel_id=1, source_target_pairs={{0,12},{1,13},{2,14},{3,15},{4,8},{5,9},{6,10},{7,11},{8,4},{9,5},... | collective-permute-start | bytes 159752 | tf_op jit(solution)/shard_map/ppermute | solution.py:73
  30.5 6.2 %collective-permute-start.17 = (bf16[16,1664]{1,0:T(8,128)(2,1)S(1)}, bf16[16,1664]{1,0:T(8,128)(2,1)S(1)}, u32[]{:S(2)}, u32[]{:S(2)}) collective-permute-start(bf16[16,1664]{1,0:T(8,128)(2,1)S(1)} %get-tuple-element.41), channel_id=1, source_target_pairs={{0,8},{1,9},{2,10},{3,11},{4,12},{5,13},{6,14},{7,15},{8,0},{9,1},... | collective-permute-start | bytes 159752 | tf_op jit(solution)/shard_map/ppermute | solution.py:73
  30.5 6.2 %collective-permute-start.16 = (bf16[16,1664]{1,0:T(8,128)(2,1)S(1)}, bf16[16,1664]{1,0:T(8,128)(2,1)S(1)}, u32[]{:S(2)}, u32[]{:S(2)}) collective-permute-start(bf16[16,1664]{1,0:T(8,128)(2,1)S(1)} %get-tuple-element.42), channel_id=1, source_target_pairs={{0,4},{1,5},{2,6},{3,7},{4,0},{5,1},{6,2},{7,3},{8,12},{9,13},{10,... | collective-permute-start | bytes 159752 | tf_op jit(solution)/shard_map/ppermute | solution.py:73
  36.8 4.2 %collective-permute-start.19 = (bf16[16,1664]{1,0:T(8,128)(2,1)S(1)}, bf16[16,1664]{1,0:T(8,128)(2,1)S(1)}, u32[]{:S(2)}, u32[]{:S(2)}) collective-permute-start(bf16[16,1664]{1,0:T(8,128)(2,1)S(1)} %sum.1), channel_id=1, source_target_pairs={{0,2},{1,3},{2,0},{3,1},{4,6},{5,7},{6,4},{7,5},{8,10},{9,11},{10,... | collective-permute-start | bytes 159752 | tf_op jit(solution)/shard_map/ppermute | solution.py:73
  41.0 6.2 %collective-permute-start.22 = (bf16[16,1664]{1,0:T(8,128)(2,1)S(1)}, bf16[16,1664]{1,0:T(8,128)(2,1)S(1)}, u32[]{:S(2)}, u32[]{:S(2)}) collective-permute-start(bf16[16,1664]{1,0:T(8,128)(2,1)S(1)} %fusion.1.refs_0_), channel_id=1, source_target_pairs={{0,12},{1,13},{2,14},{3,15},{4,8},{5,9},{6,10},{7,11},{8,4},{9,5},... | collective-permute-start | bytes 159752 | tf_op jit(solution)/shard_map/ppermute | solution.py:73
  42.8 5.5 %collective-permute-start.21 = (bf16[16,1664]{1,0:T(8,128)(2,1)S(1)}, bf16[16,1664]{1,0:T(8,128)(2,1)S(1)}, u32[]{:S(2)}, u32[]{:S(2)}) collective-permute-start(bf16[16,1664]{1,0:T(8,128)(2,1)S(1)} %fusion.1.refs_0_), channel_id=1, source_target_pairs={{0,8},{1,9},{2,10},{3,11},{4,12},{5,13},{6,14},{7,15},{8,0},{9,1},... | collective-permute-start | bytes 159752 | tf_op jit(solution)/shard_map/ppermute | solution.py:73
  43.1 5.3 %collective-permute-start.20 = (bf16[16,1664]{1,0:T(8,128)(2,1)S(1)}, bf16[16,1664]{1,0:T(8,128)(2,1)S(1)}, u32[]{:S(2)}, u32[]{:S(2)}) collective-permute-start(bf16[16,1664]{1,0:T(8,128)(2,1)S(1)} %fusion.1.refs_0_), channel_id=1, source_target_pairs={{0,4},{1,5},{2,6},{3,7},{4,0},{5,1},{6,2},{7,3},{8,12},{9,13},{10,... | collective-permute-start | bytes 159752 | tf_op jit(solution)/shard_map/ppermute | solution.py:73
  45.5 3.4 %collective-permute-start.23 = (bf16[16,1664]{1,0:T(8,128)(2,1)S(1)}, bf16[16,1664]{1,0:T(8,128)(2,1)S(1)}, u32[]{:S(2)}, u32[]{:S(2)}) collective-permute-start(bf16[16,1664]{1,0:T(8,128)(2,1)S(1)} %fusion.1.refs_0_), channel_id=1, source_target_pairs={{0,1},{1,0},{2,3},{3,2},{4,5},{5,4},{6,7},{7,6},{8,9},{9,8},{10,11... | collective-permute-start | bytes 159752 | tf_op jit(solution)/shard_map/ppermute | solution.py:73
  47.3 1.6 %collective-permute-start.26 = (bf16[16,1664]{1,0:T(8,128)(2,1)S(1)}, bf16[16,1664]{1,0:T(8,128)(2,1)S(1)}, u32[]{:S(2)}, u32[]{:S(2)}) collective-permute-start(bf16[16,1664]{1,0:T(8,128)(2,1)S(1)} %collective-permute-done.22.refs_3_), channel_id=1, source_target_pairs={{0,1},{1,0},{2,3},{3,2},{4,5},{5,4},{6,7},{7,6},{8,9},{9,8},{10,11... | collective-permute-start | bytes 159752 | tf_op jit(solution)/shard_map/ppermute | solution.py:73
  (4 other events, 15.3 us)

commit v8 on v6

--- a/solution.py
+++ b/solution.py
@@ -95,7 +95,9 @@
     return pl.BlockSpec(memory_space=pltpu.SMEM)
 
 
-def launch(limit, kernel, name, out_shape, in_specs, out_specs, scratch=(), flops=0, moved=0):
+def launch(
+    kernel, name, out_shape, in_specs, out_specs, scratch=(), flops=0, moved=0, limit=0, aliases=None
+):
     return pl.pallas_call(
         kernel,
         name=name,
@@ -103,6 +105,7 @@
         in_specs=in_specs,
         out_specs=out_specs,
         scratch_shapes=list(scratch),
+        input_output_aliases=aliases or {},
         compiler_params=pltpu.CompilerParams(vmem_limit_bytes=limit),
         cost_estimate=pl.CostEstimate(flops=flops, bytes_accessed=moved, transcendentals=0),
     )
@@ -194,6 +197,10 @@
         at += ref.shape[0]
 
 
+def pass_kernel(*_):
+    pass
+
+
 def norms_kernel(dec, norms, row):
     latents, feature = dec.shape
     channels = 512
@@ -212,8 +219,10 @@
 def encode_kernel(count, outer, inner, slots, frames, *refs):
     me_ref = refs[0]
     pieces = refs[1 : 1 + count]
-    enc, bias, dec, weights_sum, dec_bias = refs[1 + count : 6 + count]
-    own, send, shift, inputs_out, latent_out = refs[6 + count :]
+    enc, bias, dec_hbm, weights_sum, dec_bias = refs[1 + count : 6 + count]
+    own, send, shift, inputs_out, latent_out, dec, sem = refs[6 + count :]
+    fetch = pltpu.make_async_copy(dec_hbm, dec, sem)
+    fetch.start()
     me = me_ref[0]
     step = 2 * inner
     tokens, feature = inputs_out.shape
@@ -269,6 +278,7 @@
     inputs_out[...] = inputs
     latent = jnp.maximum(jnp.dot(inputs, enc[...], preferred_element_type=F32) + bias[...], 0.0)
     latent_out[...] = latent
+    fetch.wait()
     part = jnp.dot(latent.astype(BF16), dec[...], preferred_element_type=F32)
     weighted = latent * weights_sum[0:1, :]
     extra = weighted[:, :LANES]
@@ -287,14 +297,14 @@
 def turn_kernel(inputs, latent, norms, inputs_t, latent_t, scale):
     inputs_t[...] = inputs[...].astype(F32).T.astype(BF16)
     turned = latent[...].T
-    latent_t[...] = turned.astype(BF16)
+    latent_t[...] = (2.0 * turned).astype(BF16)
     activity = jnp.sum(turned, axis=1, keepdims=True)
     scale[...] = (sparsity * activity) / jnp.maximum(norms[...], 1e-30)
 
 
 def sum_kernel(*refs):
-    total = refs[1][...]
-    for ref in refs[2:-1]:
+    total = refs[2][...]
+    for ref in refs[3:-1]:
         total = total + ref[...].astype(F32)
     refs[-1][...] = total.astype(BF16)
 
@@ -312,7 +322,7 @@
     size = latents // parts
     for i in range(parts):
         at = slice(i * size, (i + 1) * size)
-        grad = 2.0 * jnp.dot(latent_t[at], errors, preferred_element_type=F32)
+        grad = jnp.dot(latent_t[at], errors, preferred_element_type=F32)
         for c in range(feature // channels):
             lanes = slice(c * channels, (c + 1) * channels)
             term = scale[at, c : c + 1] * dec[at, lanes].astype(F32)
@@ -371,7 +381,7 @@
     wide = feature + EXTRA
 
     pinned = tokens <= PINNED_TOKENS
-    call = functools.partial(launch, PINNED_BYTES if pinned else VMEM_BYTES)
+    call = functools.partial(launch, limit=PINNED_BYTES if pinned else VMEM_BYTES)
 
     def fast(dims, kind):
         return pltpu.VMEM(dims, kind) if pinned else shape(dims, kind)
@@ -420,9 +430,18 @@
         (vmem(), vmem()),
         flops=4 * dec_weight.size,
         moved=2 * dec_weight.size,
-    )(decoder)
+    )(far(dec_weight))
 
     blocks = [packed] + [exchange(packed, step * k) for k in range(1, outer)]
+    if pinned:
+        blocks[1] = call(
+            pass_kernel,
+            "pass",
+            fast(packed.shape, BF16),
+            [pl.BlockSpec(memory_space=pl.ANY)] * 3,
+            pl.BlockSpec(memory_space=pl.ANY),
+            aliases={2: 0},
+        )(near(norms), encoder, near(blocks[1]))
     pieces = blocks
     if not pinned:
         pieces = [
@@ -457,8 +476,9 @@
             fast((tokens, feature), BF16),
             fast((tokens, latents), F32),
         ),
-        [smem()] + [vmem()] * (len(pieces) + 5),
+        [smem()] + [vmem()] * (len(pieces) + 2) + [pl.BlockSpec(memory_space=pl.ANY)] + [vmem()] * 2,
         (vmem(),) * 5,
+        [pltpu.VMEM(dec_weight.shape, BF16), pltpu.SemaphoreType.DMA],
         flops=4 * tokens * feature * latents,
         moved=4 * dec_weight.size,
     )(
@@ -466,7 +486,7 @@
         *[near(piece) for piece in pieces],
         encoder,
         enc_bias.reshape(1, latents),
-        decoder,
+        far(dec_weight),
         near(weights_sum),
         dec_bias,
     )
@@ -490,10 +510,10 @@
         sum_kernel,
         "sum",
         fast((chunk, wide), BF16),
-        [pl.BlockSpec(memory_space=pl.ANY)] + [vmem()] * outer,
+        [pl.BlockSpec(memory_space=pl.ANY)] * 2 + [vmem()] * outer,
         vmem(),
         moved=8 * chunk * wide,
-    )(near(scale), *[near(block) for block in blocks])
+    )(near(scale), decoder, *[near(block) for block in blocks])
     bit = 2
     while bit < step:
         width = (bit // 2) * ROWS_DEV

time: 51.5 us -> 52.5 us (1.019)
  Pallas kernels: 10.2 us -> 11.7 us
  waiting for transfers between devices: 18.9 us -> 18.3 us
    pallas_call x1, Pallas kernels: 0.7 us -> 2.11 us  [shards(): call(norms_kernel, 'norms', (fast((latents, LANES), F32), fast((8, latent...]
    ppermute x27, waiting for transfers between devices: 18.9 us -> 18.3 us  [exchange(): return lax.ppermute(value, 'utt', [(i, i ^ bit) for i in range(devices)])]
  transfers between devices with their start and end apart: 27 -> 27, of which waited for: 15 -> 13; matrix products, arithmetic and copies ran while one was open for 0% -> 0% of each run, Pallas kernels for 2% -> 5%
where the time goes in v8:
time: 52.5 us; the launch traced here: 52.3 us
  starting transfers between devices  21.3 us (41%)
  waiting for transfers between devices  18.3 us (35%)
  Pallas kernels  11.7 us (22%)
  between operations  0.77 us (1%)
    ppermute x27, starting transfers between devices, exchange(): return lax.ppermute(value, 'utt', [(i, i ^ bit) for i in range(devices)])  21.3 us
    ppermute x27, waiting for transfers between devices, exchange(): return lax.ppermute(value, 'utt', [(i, i ^ bit) for i in range(devices)])  18.3 us
    pallas_call x1, Pallas kernels, shards(): call(features_kernel, 'features', fast((slots * frames, feature), BF16),...  3.53 us
    pallas_call x1, Pallas kernels, shards(): call(gradients, 'gradients', (shape((feature, latents), BF16), shape((lat...  3.31 us
    pallas_call x1, Pallas kernels, shards(): call(encode, 'encode', (fast((half, wide), F32), fast((half, wide), F32),...  2.42 us
    pallas_call x1, Pallas kernels, shards(): call(norms_kernel, 'norms', (fast((latents, LANES), F32), fast((8, latent...  2.11 us
  transfers between devices with their start and end apart: 27, of which 13 were waited for; matrix products, arithmetic and copies ran while one was open for 0% of the time, Pallas kernels for 5%

profile of v8, /device:TPU:0, one launch (start us, length us, event | category | flops | bytes accessed | tf_op | source)
XLA Modules:
  0.0 52.3 jit_solution(6245737916107144032)
XLA Ops:
  0.6 3.5 %features.1.refs_1_ = bf16[16,1536]{1,0:T(8,128)(2,1)S(1)} custom-call(s32[2]{0:T(128)} %refs_0_.1, s32[2]{0:T(128)} %refs_1_.2, f32[2,90]{1,0:T(2,128)} %refs_2_.1, f32[10,3,512]{2,1,0:T(4,128)} %bitcast.14, f32[3,2,512]{2,1,0:T(2,128)} %refs_4_.1, f32[3,2,512]{2,1,0:T(2,128)} %refs_5_.1, bf16[3,1536,512]{2,1,0:T(8,128)(2,1)} %refs_6_.1), custom_call_target="tpu_custom_call" | custom-call | flops 75497472 | bytes 4718592 | tf_op jit(solution)/shard_map/features/pallas_call | solution.py:399
  4.2 3.0 %collective-permute-start.3 = (bf16[16,1536]{1,0:T(8,128)(2,1)S(1)}, bf16[16,1536]{1,0:T(8,128)(2,1)S(1)}, u32[]{:S(2)}, u32[]{:S(2)}) collective-permute-start(bf16[16,1536]{1,0:T(8,128)(2,1)S(1)} %features.1.refs_1_), channel_id=1, source_target_pairs={{0,2},{1,3},{2,0},{3,1},{4,6},{5,7},{6,4},{7,5},{8,10},{9,11},{10,... | collective-permute-start | bytes 147464 | tf_op jit(solution)/shard_map/ppermute | solution.py:73
  7.2 3.6 %collective-permute-start.2 = (bf16[16,1536]{1,0:T(8,128)(2,1)S(1)}, bf16[16,1536]{1,0:T(8,128)(2,1)S(1)}, u32[]{:S(2)}, u32[]{:S(2)}) collective-permute-start(bf16[16,1536]{1,0:T(8,128)(2,1)S(1)} %features.1.refs_1_), channel_id=1, source_target_pairs={{0,12},{1,13},{2,14},{3,15},{4,8},{5,9},{6,10},{7,11},{8,4},{9,5},... | collective-permute-start | bytes 147464 | tf_op jit(solution)/shard_map/ppermute | solution.py:73
  10.8 0.8 %collective-permute-start = (bf16[16,1536]{1,0:T(8,128)(2,1)S(1)}, bf16[16,1536]{1,0:T(8,128)(2,1)S(1)}, u32[]{:S(2)}, u32[]{:S(2)}) collective-permute-start(bf16[16,1536]{1,0:T(8,128)(2,1)S(1)} %features.1.refs_1_), channel_id=1, source_target_pairs={{0,4},{1,5},{2,6},{3,7},{4,0},{5,1},{6,2},{7,3},{8,12},{9,13},{10,... | collective-permute-start | bytes 147464 | tf_op jit(solution)/shard_map/ppermute | solution.py:73
  11.6 2.1 %norms.1 = (f32[512,128]{1,0:T(8,128)S(1)}, f32[8,512]{1,0:T(8,128)S(1)}) custom-call(bf16[512,1536]{1,0:T(8,128)(2,1)} %refs_8_.1), custom_call_target="tpu_custom_call" | custom-call | flops 3145728 | bytes 1572864 | tf_op jit(solution)/shard_map/norms/pallas_call | solution.py:425
  14.4 1.5 %collective-permute-done.1.refs_3_ = bf16[16,1536]{1,0:T(8,128)(2,1)S(1)} collective-permute-done((bf16[16,1536]{1,0:T(8,128)(2,1)S(1)}, bf16[16,1536]{1,0:T(8,128)(2,1)S(1)}, u32[]{:S(2)}, u32[]{:S(2)}) %collective-permute-start.1) | collective-permute-done | bytes 49184 | tf_op jit(solution)/shard_map/ppermute | solution.py:73
  16.3 1.5 %collective-permute-start.5 = (bf16[16,1536]{1,0:T(8,128)(2,1)S(1)}, bf16[16,1536]{1,0:T(8,128)(2,1)S(1)}, u32[]{:S(2)}, u32[]{:S(2)}) collective-permute-start(bf16[16,1536]{1,0:T(8,128)(2,1)S(1)} %collective-permute-done.1.refs_3_), channel_id=1, source_target_pairs={{0,2},{1,3},{2,0},{3,1},{4,6},{5,7},{6,4},{7,5},{8,10},{9,11},{10,... | collective-permute-start | bytes 147464 | tf_op jit(solution)/shard_map/ppermute | solution.py:73
  18.9 1.0 %collective-permute-done.6.refs_8_ = bf16[16,1536]{1,0:T(8,128)(2,1)S(1)} collective-permute-done((bf16[16,1536]{1,0:T(8,128)(2,1)S(1)}, bf16[16,1536]{1,0:T(8,128)(2,1)S(1)}, u32[]{:S(2)}, u32[]{:S(2)}) %collective-permute-start.6) | collective-permute-done | bytes 49184 | tf_op jit(solution)/shard_map/ppermute | solution.py:73
  20.5 1.5 %collective-permute-done.4.refs_6_ = bf16[16,1536]{1,0:T(8,128)(2,1)S(1)} collective-permute-done((bf16[16,1536]{1,0:T(8,128)(2,1)S(1)}, bf16[16,1536]{1,0:T(8,128)(2,1)S(1)}, u32[]{:S(2)}, u32[]{:S(2)}) %collective-permute-start.4) | collective-permute-done | bytes 49184 | tf_op jit(solution)/shard_map/ppermute | solution.py:73
  22.0 1.2 %collective-permute-done.12.refs_14_ = bf16[16,1536]{1,0:T(8,128)(2,1)S(1)} collective-permute-done((bf16[16,1536]{1,0:T(8,128)(2,1)S(1)}, bf16[16,1536]{1,0:T(8,128)(2,1)S(1)}, u32[]{:S(2)}, u32[]{:S(2)}) %collective-permute-start.12) | collective-permute-done | bytes 49184 | tf_op jit(solution)/shard_map/ppermute | solution.py:73
  23.2 2.4 %encode.1 = (f32[64,1664]{1,0:T(8,128)S(1)}, f32[64,1664]{1,0:T(8,128)S(1)}, f32[16,1664]{1,0:T(8,128)S(1)}, bf16[128,1536]{1,0:T(8,128)(2,1)S(1)}, f32[128,512]{1,0:T(8,128)S(1)}) custom-call(s32[1]{0:T(128)} %bitcast.refs_0_, bf16[16,1536]{1,0:T(8,128)(2,1)S(1)} %features.1.refs_1_, bf16[16,1536]{1,0:T(8,128)(2,1)S(1)} %pass.1.refs_2_, ...), custom_call_target="tpu_custom_call" | custom-call | flops 402653184 | bytes 3145728 | tf_op jit(solution)/shard_map/encode/pallas_call | solution.py:469
  25.8 1.6 %collective-permute-done.15 = f32[64,1664]{1,0:T(8,128)S(1)} collective-permute-done((f32[64,1664]{1,0:T(8,128)S(1)}, f32[64,1664]{1,0:T(8,128)S(1)}, u32[]{:S(2)}, u32[]{:S(2)}) %collective-permute-start.15) | collective-permute-done | bytes 426016 | tf_op jit(solution)/shard_map/ppermute | solution.py:73
  27.5 2.3 %collective-permute-start.18 = (bf16[16,1664]{1,0:T(8,128)(2,1)S(1)}, bf16[16,1664]{1,0:T(8,128)(2,1)S(1)}, u32[]{:S(2)}, u32[]{:S(2)}) collective-permute-start(bf16[16,1664]{1,0:T(8,128)(2,1)S(1)} %get-tuple-element.40), channel_id=1, source_target_pairs={{0,12},{1,13},{2,14},{3,15},{4,8},{5,9},{6,10},{7,11},{8,4},{9,5},... | collective-permute-start | bytes 159752 | tf_op jit(solution)/shard_map/ppermute | solution.py:73
  29.8 2.2 %collective-permute-start.16 = (bf16[16,1664]{1,0:T(8,128)(2,1)S(1)}, bf16[16,1664]{1,0:T(8,128)(2,1)S(1)}, u32[]{:S(2)}, u32[]{:S(2)}) collective-permute-start(bf16[16,1664]{1,0:T(8,128)(2,1)S(1)} %get-tuple-element.42), channel_id=1, source_target_pairs={{0,4},{1,5},{2,6},{3,7},{4,0},{5,1},{6,2},{7,3},{8,12},{9,13},{10,... | collective-permute-start | bytes 159752 | tf_op jit(solution)/shard_map/ppermute | solution.py:73
  32.4 1.6 %collective-permute-done.18.refs_5_ = bf16[16,1664]{1,0:T(8,128)(2,1)S(1)} collective-permute-done((bf16[16,1664]{1,0:T(8,128)(2,1)S(1)}, bf16[16,1664]{1,0:T(8,128)(2,1)S(1)}, u32[]{:S(2)}, u32[]{:S(2)}) %collective-permute-start.18) | collective-permute-done | bytes 53280 | tf_op jit(solution)/shard_map/ppermute | solution.py:73
  34.0 1.6 %collective-permute-done.17.refs_4_ = bf16[16,1664]{1,0:T(8,128)(2,1)S(1)} collective-permute-done((bf16[16,1664]{1,0:T(8,128)(2,1)S(1)}, bf16[16,1664]{1,0:T(8,128)(2,1)S(1)}, u32[]{:S(2)}, u32[]{:S(2)}) %collective-permute-start.17) | collective-permute-done | bytes 53280 | tf_op jit(solution)/shard_map/ppermute | solution.py:73
  35.6 0.6 %collective-permute-start.19 = (bf16[16,1664]{1,0:T(8,128)(2,1)S(1)}, bf16[16,1664]{1,0:T(8,128)(2,1)S(1)}, u32[]{:S(2)}, u32[]{:S(2)}) collective-permute-start(bf16[16,1664]{1,0:T(8,128)(2,1)S(1)} %sum.1), channel_id=1, source_target_pairs={{0,2},{1,3},{2,0},{3,1},{4,6},{5,7},{6,4},{7,5},{8,10},{9,11},{10,... | collective-permute-start | bytes 159752 | tf_op jit(solution)/shard_map/ppermute | solution.py:73
  36.2 3.6 %collective-permute-done.19 = bf16[16,1664]{1,0:T(8,128)(2,1)S(1)} collective-permute-done((bf16[16,1664]{1,0:T(8,128)(2,1)S(1)}, bf16[16,1664]{1,0:T(8,128)(2,1)S(1)}, u32[]{:S(2)}, u32[]{:S(2)}) %collective-permute-start.19) | collective-permute-done | bytes 53280 | tf_op jit(solution)/shard_map/ppermute | solution.py:73
  39.9 2.3 %collective-permute-start.22 = (bf16[16,1664]{1,0:T(8,128)(2,1)S(1)}, bf16[16,1664]{1,0:T(8,128)(2,1)S(1)}, u32[]{:S(2)}, u32[]{:S(2)}) collective-permute-start(bf16[16,1664]{1,0:T(8,128)(2,1)S(1)} %fusion.1.refs_0_), channel_id=1, source_target_pairs={{0,12},{1,13},{2,14},{3,15},{4,8},{5,9},{6,10},{7,11},{8,4},{9,5},... | collective-permute-start | bytes 159752 | tf_op jit(solution)/shard_map/ppermute | solution.py:73
  42.1 2.2 %collective-permute-start.20 = (bf16[16,1664]{1,0:T(8,128)(2,1)S(1)}, bf16[16,1664]{1,0:T(8,128)(2,1)S(1)}, u32[]{:S(2)}, u32[]{:S(2)}) collective-permute-start(bf16[16,1664]{1,0:T(8,128)(2,1)S(1)} %fusion.1.refs_0_), channel_id=1, source_target_pairs={{0,4},{1,5},{2,6},{3,7},{4,0},{5,1},{6,2},{7,3},{8,12},{9,13},{10,... | collective-permute-start | bytes 159752 | tf_op jit(solution)/shard_map/ppermute | solution.py:73
  44.3 2.0 %collective-permute-done.22.refs_3_ = bf16[16,1664]{1,0:T(8,128)(2,1)S(1)} collective-permute-done((bf16[16,1664]{1,0:T(8,128)(2,1)S(1)}, bf16[16,1664]{1,0:T(8,128)(2,1)S(1)}, u32[]{:S(2)}, u32[]{:S(2)}) %collective-permute-start.22) | collective-permute-done | bytes 53280 | tf_op jit(solution)/shard_map/ppermute | solution.py:73
  46.3 1.3 %collective-permute-done.21.refs_2_ = bf16[16,1664]{1,0:T(8,128)(2,1)S(1)} collective-permute-done((bf16[16,1664]{1,0:T(8,128)(2,1)S(1)}, bf16[16,1664]{1,0:T(8,128)(2,1)S(1)}, u32[]{:S(2)}, u32[]{:S(2)}) %collective-permute-start.21) | collective-permute-done | bytes 53280 | tf_op jit(solution)/shard_map/ppermute | solution.py:73
  48.1 0.7 %collective-permute-done.25.refs_6_ = bf16[16,1664]{1,0:T(8,128)(2,1)S(1)} collective-permute-done((bf16[16,1664]{1,0:T(8,128)(2,1)S(1)}, bf16[16,1664]{1,0:T(8,128)(2,1)S(1)}, u32[]{:S(2)}, u32[]{:S(2)}) %collective-permute-start.25) | collective-permute-done | bytes 53280 | tf_op jit(solution)/shard_map/ppermute | solution.py:73
  49.0 3.3 %gradients.1 = (bf16[1536,512]{1,0:T(8,128)(2,1)}, bf16[512,1536]{1,0:T(8,128)(2,1)}, f32[1,512]{1,0:T(1,128)}, f32[1536]{0:T(1024)}, f32[1]{0:T(128)}, /*index=5*/bf16[8,1536]{1,0:T(8,128)(2,1)}) custom-call(bf16[16,1664]{1,0:T(8,128)(2,1)S(1)} %fusion.1.refs_0_, bf16[16,1664]{1,0:T(8,128)(2,1)S(1)} %collective-permute-done.20.refs_1_, ...), custom_call_target="tpu_custom_call" | custom-call | flops 603979776 | bytes 6291456 | tf_op jit(solution)/shard_map/gradients/pallas_call | solution.py:532
  (50 shorter events, 4.1 us)
Async XLA Ops:
  4.2 9.5 %collective-permute-start.3 = (bf16[16,1536]{1,0:T(8,128)(2,1)S(1)}, bf16[16,1536]{1,0:T(8,128)(2,1)S(1)}, u32[]{:S(2)}, u32[]{:S(2)}) collective-permute-start(bf16[16,1536]{1,0:T(8,128)(2,1)S(1)} %features.1.refs_1_), channel_id=1, source_target_pairs={{0,2},{1,3},{2,0},{3,1},{4,6},{5,7},{6,4},{7,5},{8,10},{9,11},{10,... | collective-permute-start | bytes 147464 | tf_op jit(solution)/shard_map/ppermute | solution.py:73
  7.2 7.1 %collective-permute-start.2 = (bf16[16,1536]{1,0:T(8,128)(2,1)S(1)}, bf16[16,1536]{1,0:T(8,128)(2,1)S(1)}, u32[]{:S(2)}, u32[]{:S(2)}) collective-permute-start(bf16[16,1536]{1,0:T(8,128)(2,1)S(1)} %features.1.refs_1_), channel_id=1, source_target_pairs={{0,12},{1,13},{2,14},{3,15},{4,8},{5,9},{6,10},{7,11},{8,4},{9,5},... | collective-permute-start | bytes 147464 | tf_op jit(solution)/shard_map/ppermute | solution.py:73
  10.8 5.0 %collective-permute-start.1 = (bf16[16,1536]{1,0:T(8,128)(2,1)S(1)}, bf16[16,1536]{1,0:T(8,128)(2,1)S(1)}, u32[]{:S(2)}, u32[]{:S(2)}) collective-permute-start(bf16[16,1536]{1,0:T(8,128)(2,1)S(1)} %features.1.refs_1_), channel_id=1, source_target_pairs={{0,8},{1,9},{2,10},{3,11},{4,12},{5,13},{6,14},{7,15},{8,0},{9,1},... | collective-permute-start | bytes 147464 | tf_op jit(solution)/shard_map/ppermute | solution.py:73
  10.8 5.5 %collective-permute-start = (bf16[16,1536]{1,0:T(8,128)(2,1)S(1)}, bf16[16,1536]{1,0:T(8,128)(2,1)S(1)}, u32[]{:S(2)}, u32[]{:S(2)}) collective-permute-start(bf16[16,1536]{1,0:T(8,128)(2,1)S(1)} %features.1.refs_1_), channel_id=1, source_target_pairs={{0,4},{1,5},{2,6},{3,7},{4,0},{5,1},{6,2},{7,3},{8,12},{9,13},{10,... | collective-permute-start | bytes 147464 | tf_op jit(solution)/shard_map/ppermute | solution.py:73
  11.6 6.2 %collective-permute-start.7 = (bf16[16,1536]{1,0:T(8,128)(2,1)S(1)}, bf16[16,1536]{1,0:T(8,128)(2,1)S(1)}, u32[]{:S(2)}, u32[]{:S(2)}) collective-permute-start(bf16[16,1536]{1,0:T(8,128)(2,1)S(1)} %features.1.refs_1_), channel_id=1, source_target_pairs={{0,1},{1,0},{2,3},{3,2},{4,5},{5,4},{6,7},{7,6},{8,9},{9,8},{10,11... | collective-permute-start | bytes 147464 | tf_op jit(solution)/shard_map/ppermute | solution.py:73
  13.7 4.6 %collective-permute-start.11 = (bf16[16,1536]{1,0:T(8,128)(2,1)S(1)}, bf16[16,1536]{1,0:T(8,128)(2,1)S(1)}, u32[]{:S(2)}, u32[]{:S(2)}) collective-permute-start(bf16[16,1536]{1,0:T(8,128)(2,1)S(1)} %collective-permute-done.3.refs_5_), channel_id=1, source_target_pairs={{0,1},{1,0},{2,3},{3,2},{4,5},{5,4},{6,7},{7,6},{8,9},{9,8},{10,11... | collective-permute-start | bytes 147464 | tf_op jit(solution)/shard_map/ppermute | solution.py:73
  14.3 4.1 %collective-permute-start.10 = (bf16[16,1536]{1,0:T(8,128)(2,1)S(1)}, bf16[16,1536]{1,0:T(8,128)(2,1)S(1)}, u32[]{:S(2)}, u32[]{:S(2)}) collective-permute-start(bf16[16,1536]{1,0:T(8,128)(2,1)S(1)} %collective-permute-done.2.refs_4_), channel_id=1, source_target_pairs={{0,1},{1,0},{2,3},{3,2},{4,5},{5,4},{6,7},{7,6},{8,9},{9,8},{10,11... | collective-permute-start | bytes 147464 | tf_op jit(solution)/shard_map/ppermute | solution.py:73
  15.8 4.1 %collective-permute-start.6 = (bf16[16,1536]{1,0:T(8,128)(2,1)S(1)}, bf16[16,1536]{1,0:T(8,128)(2,1)S(1)}, u32[]{:S(2)}, u32[]{:S(2)}) collective-permute-start(bf16[16,1536]{1,0:T(8,128)(2,1)S(1)} %collective-permute-done.2.refs_4_), channel_id=1, source_target_pairs={{0,2},{1,3},{2,0},{3,1},{4,6},{5,7},{6,4},{7,5},{8,10},{9,11},{10,... | collective-permute-start | bytes 147464 | tf_op jit(solution)/shard_map/ppermute | solution.py:73
  16.3 4.1 %collective-permute-start.5 = (bf16[16,1536]{1,0:T(8,128)(2,1)S(1)}, bf16[16,1536]{1,0:T(8,128)(2,1)S(1)}, u32[]{:S(2)}, u32[]{:S(2)}) collective-permute-start(bf16[16,1536]{1,0:T(8,128)(2,1)S(1)} %collective-permute-done.1.refs_3_), channel_id=1, source_target_pairs={{0,2},{1,3},{2,0},{3,1},{4,6},{5,7},{6,4},{7,5},{8,10},{9,11},{10,... | collective-permute-start | bytes 147464 | tf_op jit(solution)/shard_map/ppermute | solution.py:73
  17.9 4.1 %collective-permute-start.4 = (bf16[16,1536]{1,0:T(8,128)(2,1)S(1)}, bf16[16,1536]{1,0:T(8,128)(2,1)S(1)}, u32[]{:S(2)}, u32[]{:S(2)}) collective-permute-start(bf16[16,1536]{1,0:T(8,128)(2,1)S(1)} %pass.1.refs_2_), channel_id=1, source_target_pairs={{0,2},{1,3},{2,0},{3,1},{4,6},{5,7},{6,4},{7,5},{8,10},{9,11},{10,... | collective-permute-start | bytes 147464 | tf_op jit(solution)/shard_map/ppermute | solution.py:73
  18.4 3.6 %collective-permute-start.8 = (bf16[16,1536]{1,0:T(8,128)(2,1)S(1)}, bf16[16,1536]{1,0:T(8,128)(2,1)S(1)}, u32[]{:S(2)}, u32[]{:S(2)}) collective-permute-start(bf16[16,1536]{1,0:T(8,128)(2,1)S(1)} %pass.1.refs_2_), channel_id=1, source_target_pairs={{0,1},{1,0},{2,3},{3,2},{4,5},{5,4},{6,7},{7,6},{8,9},{9,8},{10,11... | collective-permute-start | bytes 147464 | tf_op jit(solution)/shard_map/ppermute | solution.py:73
  18.4 3.6 %collective-permute-start.9 = (bf16[16,1536]{1,0:T(8,128)(2,1)S(1)}, bf16[16,1536]{1,0:T(8,128)(2,1)S(1)}, u32[]{:S(2)}, u32[]{:S(2)}) collective-permute-start(bf16[16,1536]{1,0:T(8,128)(2,1)S(1)} %collective-permute-done.1.refs_3_), channel_id=1, source_target_pairs={{0,1},{1,0},{2,3},{3,2},{4,5},{5,4},{6,7},{7,6},{8,9},{9,8},{10,11... | collective-permute-start | bytes 147464 | tf_op jit(solution)/shard_map/ppermute | solution.py:73
  19.9 2.0 %collective-permute-start.14 = (bf16[16,1536]{1,0:T(8,128)(2,1)S(1)}, bf16[16,1536]{1,0:T(8,128)(2,1)S(1)}, u32[]{:S(2)}, u32[]{:S(2)}) collective-permute-start(bf16[16,1536]{1,0:T(8,128)(2,1)S(1)} %collective-permute-done.6.refs_8_), channel_id=1, source_target_pairs={{0,1},{1,0},{2,3},{3,2},{4,5},{5,4},{6,7},{7,6},{8,9},{9,8},{10,11... | collective-permute-start | bytes 147464 | tf_op jit(solution)/shard_map/ppermute | solution.py:73
  20.5 1.5 %collective-permute-start.13 = (bf16[16,1536]{1,0:T(8,128)(2,1)S(1)}, bf16[16,1536]{1,0:T(8,128)(2,1)S(1)}, u32[]{:S(2)}, u32[]{:S(2)}) collective-permute-start(bf16[16,1536]{1,0:T(8,128)(2,1)S(1)} %collective-permute-done.5.refs_7_), channel_id=1, source_target_pairs={{0,1},{1,0},{2,3},{3,2},{4,5},{5,4},{6,7},{7,6},{8,9},{9,8},{10,11... | collective-permute-start | bytes 147464 | tf_op jit(solution)/shard_map/ppermute | solution.py:73
  25.6 1.8 %collective-permute-start.15 = (f32[64,1664]{1,0:T(8,128)S(1)}, f32[64,1664]{1,0:T(8,128)S(1)}, u32[]{:S(2)}, u32[]{:S(2)}) collective-permute-start(f32[64,1664]{1,0:T(8,128)S(1)} %get-tuple-element.28), channel_id=1, source_target_pairs={{0,1},{1,0},{2,3},{3,2},{4,5},{5,4},{6,7},{7,6},{8,9},{9,8},{10,11... | collective-permute-start | bytes 1277960 | tf_op jit(solution)/shard_map/ppermute | solution.py:73
  27.5 6.4 %collective-permute-start.18 = (bf16[16,1664]{1,0:T(8,128)(2,1)S(1)}, bf16[16,1664]{1,0:T(8,128)(2,1)S(1)}, u32[]{:S(2)}, u32[]{:S(2)}) collective-permute-start(bf16[16,1664]{1,0:T(8,128)(2,1)S(1)} %get-tuple-element.40), channel_id=1, source_target_pairs={{0,12},{1,13},{2,14},{3,15},{4,8},{5,9},{6,10},{7,11},{8,4},{9,5},... | collective-permute-start | bytes 159752 | tf_op jit(solution)/shard_map/ppermute | solution.py:73
  29.8 5.8 %collective-permute-start.17 = (bf16[16,1664]{1,0:T(8,128)(2,1)S(1)}, bf16[16,1664]{1,0:T(8,128)(2,1)S(1)}, u32[]{:S(2)}, u32[]{:S(2)}) collective-permute-start(bf16[16,1664]{1,0:T(8,128)(2,1)S(1)} %get-tuple-element.41), channel_id=1, source_target_pairs={{0,8},{1,9},{2,10},{3,11},{4,12},{5,13},{6,14},{7,15},{8,0},{9,1},... | collective-permute-start | bytes 159752 | tf_op jit(solution)/shard_map/ppermute | solution.py:73
  29.8 5.8 %collective-permute-start.16 = (bf16[16,1664]{1,0:T(8,128)(2,1)S(1)}, bf16[16,1664]{1,0:T(8,128)(2,1)S(1)}, u32[]{:S(2)}, u32[]{:S(2)}) collective-permute-start(bf16[16,1664]{1,0:T(8,128)(2,1)S(1)} %get-tuple-element.42), channel_id=1, source_target_pairs={{0,4},{1,5},{2,6},{3,7},{4,0},{5,1},{6,2},{7,3},{8,12},{9,13},{10,... | collective-permute-start | bytes 159752 | tf_op jit(solution)/shard_map/ppermute | solution.py:73
  35.6 4.2 %collective-permute-start.19 = (bf16[16,1664]{1,0:T(8,128)(2,1)S(1)}, bf16[16,1664]{1,0:T(8,128)(2,1)S(1)}, u32[]{:S(2)}, u32[]{:S(2)}) collective-permute-start(bf16[16,1664]{1,0:T(8,128)(2,1)S(1)} %sum.1), channel_id=1, source_target_pairs={{0,2},{1,3},{2,0},{3,1},{4,6},{5,7},{6,4},{7,5},{8,10},{9,11},{10,... | collective-permute-start | bytes 159752 | tf_op jit(solution)/shard_map/ppermute | solution.py:73
  39.9 6.4 %collective-permute-start.22 = (bf16[16,1664]{1,0:T(8,128)(2,1)S(1)}, bf16[16,1664]{1,0:T(8,128)(2,1)S(1)}, u32[]{:S(2)}, u32[]{:S(2)}) collective-permute-start(bf16[16,1664]{1,0:T(8,128)(2,1)S(1)} %fusion.1.refs_0_), channel_id=1, source_target_pairs={{0,12},{1,13},{2,14},{3,15},{4,8},{5,9},{6,10},{7,11},{8,4},{9,5},... | collective-permute-start | bytes 159752 | tf_op jit(solution)/shard_map/ppermute | solution.py:73
  42.1 5.4 %collective-permute-start.21 = (bf16[16,1664]{1,0:T(8,128)(2,1)S(1)}, bf16[16,1664]{1,0:T(8,128)(2,1)S(1)}, u32[]{:S(2)}, u32[]{:S(2)}) collective-permute-start(bf16[16,1664]{1,0:T(8,128)(2,1)S(1)} %fusion.1.refs_0_), channel_id=1, source_target_pairs={{0,8},{1,9},{2,10},{3,11},{4,12},{5,13},{6,14},{7,15},{8,0},{9,1},... | collective-permute-start | bytes 159752 | tf_op jit(solution)/shard_map/ppermute | solution.py:73
  42.1 5.4 %collective-permute-start.20 = (bf16[16,1664]{1,0:T(8,128)(2,1)S(1)}, bf16[16,1664]{1,0:T(8,128)(2,1)S(1)}, u32[]{:S(2)}, u32[]{:S(2)}) collective-permute-start(bf16[16,1664]{1,0:T(8,128)(2,1)S(1)} %fusion.1.refs_0_), channel_id=1, source_target_pairs={{0,4},{1,5},{2,6},{3,7},{4,0},{5,1},{6,2},{7,3},{8,12},{9,13},{10,... | collective-permute-start | bytes 159752 | tf_op jit(solution)/shard_map/ppermute | solution.py:73
  44.3 3.8 %collective-permute-start.23 = (bf16[16,1664]{1,0:T(8,128)(2,1)S(1)}, bf16[16,1664]{1,0:T(8,128)(2,1)S(1)}, u32[]{:S(2)}, u32[]{:S(2)}) collective-permute-start(bf16[16,1664]{1,0:T(8,128)(2,1)S(1)} %fusion.1.refs_0_), channel_id=1, source_target_pairs={{0,1},{1,0},{2,3},{3,2},{4,5},{5,4},{6,7},{7,6},{8,9},{9,8},{10,11... | collective-permute-start | bytes 159752 | tf_op jit(solution)/shard_map/ppermute | solution.py:73
  46.3 1.8 %collective-permute-start.26 = (bf16[16,1664]{1,0:T(8,128)(2,1)S(1)}, bf16[16,1664]{1,0:T(8,128)(2,1)S(1)}, u32[]{:S(2)}, u32[]{:S(2)}) collective-permute-start(bf16[16,1664]{1,0:T(8,128)(2,1)S(1)} %collective-permute-done.22.refs_3_), channel_id=1, source_target_pairs={{0,1},{1,0},{2,3},{3,2},{4,5},{5,4},{6,7},{7,6},{8,9},{9,8},{10,11... | collective-permute-start | bytes 159752 | tf_op jit(solution)/shard_map/ppermute | solution.py:73
  (7 other events, 65.5 us)

commit v9 on v8

--- a/solution.py
+++ b/solution.py
@@ -14,6 +14,7 @@
 PINNED_BYTES = 24 << 20
 PINNED_TOKENS = 256
 GROUP_ROWS = 256
+DEC_PARTS = 2
 
 sparsity = 0.5
 epsilon = 1e-05
@@ -96,7 +97,7 @@
 
 
 def launch(
-    kernel, name, out_shape, in_specs, out_specs, scratch=(), flops=0, moved=0, limit=0, aliases=None
+    kernel, name, out_shape, in_specs, out_specs, scratch=(), flops=0, moved=0, limit=0
 ):
     return pl.pallas_call(
         kernel,
@@ -105,7 +106,6 @@
         in_specs=in_specs,
         out_specs=out_specs,
         scratch_shapes=list(scratch),
-        input_output_aliases=aliases or {},
         compiler_params=pltpu.CompilerParams(vmem_limit_bytes=limit),
         cost_estimate=pl.CostEstimate(flops=flops, bytes_accessed=moved, transcendentals=0),
     )
@@ -192,13 +192,9 @@
 def join_kernel(*refs):
     out = refs[-1]
     at = 0
-    for ref in refs[:-1]:
+    for ref in refs[2:-1]:
         out[at : at + ref.shape[0], :] = ref[...]
         at += ref.shape[0]
-
-
-def pass_kernel(*_):
-    pass
 
 
 def norms_kernel(dec, norms, row):
@@ -220,9 +216,13 @@
     me_ref = refs[0]
     pieces = refs[1 : 1 + count]
     enc, bias, dec_hbm, weights_sum, dec_bias = refs[1 + count : 6 + count]
-    own, send, shift, inputs_out, latent_out, dec, sem = refs[6 + count :]
-    fetch = pltpu.make_async_copy(dec_hbm, dec, sem)
-    fetch.start()
+    own, send, shift, inputs_out, latent_out, dec, sems = refs[6 + count :]
+    quarter = dec.shape[0] // DEC_PARTS
+    fetches = []
+    for i in range(DEC_PARTS):
+        at = pl.ds(i * quarter, quarter)
+        fetches.append(pltpu.make_async_copy(dec_hbm.at[at], dec.at[at], sems.at[i]))
+        fetches[-1].start()
     me = me_ref[0]
     step = 2 * inner
     tokens, feature = inputs_out.shape
@@ -278,8 +278,12 @@
     inputs_out[...] = inputs
     latent = jnp.maximum(jnp.dot(inputs, enc[...], preferred_element_type=F32) + bias[...], 0.0)
     latent_out[...] = latent
-    fetch.wait()
-    part = jnp.dot(latent.astype(BF16), dec[...], preferred_element_type=F32)
+    rounded = latent.astype(BF16)
+    part = jnp.zeros((tokens, feature), F32)
+    for i in range(DEC_PARTS):
+        fetches[i].wait()
+        at = slice(i * quarter, (i + 1) * quarter)
+        part = part + jnp.dot(rounded[:, at], dec[at], preferred_element_type=F32)
     weighted = latent * weights_sum[0:1, :]
     extra = weighted[:, :LANES]
     for q in range(1, weighted.shape[1] // LANES):
@@ -287,8 +291,8 @@
     half = tokens // 2
     own[:, :feature] = part[:half]
     own[:, feature:] = extra[:half]
-    send[:, :feature] = part[half:]
-    send[:, feature:] = extra[half:]
+    send[:, :feature] = part[half:].astype(BF16)
+    send[:, feature:] = extra[half:].astype(BF16)
     chunk = shift.shape[0]
     shift[:, :feature] = dec_bias[...].reshape(1, feature) - inputs[:chunk].astype(F32)
     shift[:, feature:] = jnp.zeros((chunk, EXTRA), F32)
@@ -430,30 +434,19 @@
         (vmem(), vmem()),
         flops=4 * dec_weight.size,
         moved=2 * dec_weight.size,
-    )(far(dec_weight))
+    )(decoder)
 
     blocks = [packed] + [exchange(packed, step * k) for k in range(1, outer)]
-    if pinned:
-        blocks[1] = call(
-            pass_kernel,
-            "pass",
-            fast(packed.shape, BF16),
-            [pl.BlockSpec(memory_space=pl.ANY)] * 3,
-            pl.BlockSpec(memory_space=pl.ANY),
-            aliases={2: 0},
-        )(near(norms), encoder, near(blocks[1]))
-    pieces = blocks
-    if not pinned:
-        pieces = [
-            call(
-                join_kernel,
-                "join",
-                shape((outer * slots * frames, feature), BF16),
-                [vmem()] * outer,
-                vmem(),
-                moved=4 * outer * slots * frames * feature,
-            )(*blocks)
-        ]
+    pieces = [
+        call(
+            join_kernel,
+            "join",
+            fast((outer * slots * frames, feature), BF16),
+            [pl.BlockSpec(memory_space=pl.ANY)] * 2 + [vmem()] * outer,
+            vmem(),
+            moved=4 * outer * slots * frames * feature,
+        )(near(norms), encoder, *[near(block) for block in blocks])
+    ]
     bit = 2
     while bit < step:
         pieces = pieces + [exchange(piece, bit) for piece in pieces]
@@ -471,14 +464,14 @@
         "encode",
         (
             fast((half, wide), F32),
-            fast((half, wide), F32),
+            fast((half, wide), BF16),
             fast((chunk, wide), F32),
             fast((tokens, feature), BF16),
             fast((tokens, latents), F32),
         ),
         [smem()] + [vmem()] * (len(pieces) + 2) + [pl.BlockSpec(memory_space=pl.ANY)] + [vmem()] * 2,
         (vmem(),) * 5,
-        [pltpu.VMEM(dec_weight.shape, BF16), pltpu.SemaphoreType.DMA],
+        [pltpu.VMEM(dec_weight.shape, BF16), pltpu.SemaphoreType.DMA((DEC_PARTS,))],
         flops=4 * tokens * feature * latents,
         moved=4 * dec_weight.size,
     )(
@@ -501,7 +494,7 @@
         moved=4 * tokens * feature,
     )(near(inputs), near(latent), near(norms))
 
-    part = own + exchange(send, 1)
+    part = own + exchange(send, 1).astype(F32)
     small = part.astype(BF16)
     blocks = [part[:chunk]]
     for k in range(1, outer):

time: 52.5 us -> 50.7 us (0.966)
  starting transfers between devices: 21.3 us -> 18.5 us
  waiting for transfers between devices: 18.3 us -> 20.7 us
  Pallas kernels: 11.7 us -> 10.4 us
    ppermute x27 -> x18, starting transfers between devices: 21.3 us -> 18.5 us  [exchange(): return lax.ppermute(value, 'utt', [(i, i ^ bit) for i in range(devices)])]
    ppermute x27 -> x18, waiting for transfers between devices: 18.3 us -> 20.7 us  [exchange(): return lax.ppermute(value, 'utt', [(i, i ^ bit) for i in range(devices)])]
    pallas_call x1, Pallas kernels: 2.11 us -> 0.7 us  [shards(): call(norms_kernel, 'norms', (fast((latents, LANES), F32), fast((8, latent...]
  transfers between devices with their start and end apart: 27 -> 18, of which waited for: 13 -> 12; matrix products, arithmetic and copies ran while one was open for 0% -> 0% of each run, Pallas kernels for 5% -> 2%
where the time goes in v9:
time: 50.7 us; the launch traced here: 50.6 us
  waiting for transfers between devices  20.7 us (41%)
  starting transfers between devices  18.5 us (36%)
  Pallas kernels  10.4 us (21%)
  between operations  0.75 us (1%)
    ppermute x18, waiting for transfers between devices, exchange(): return lax.ppermute(value, 'utt', [(i, i ^ bit) for i in range(devices)])  20.7 us
    ppermute x18, starting transfers between devices, exchange(): return lax.ppermute(value, 'utt', [(i, i ^ bit) for i in range(devices)])  18.5 us
    pallas_call x1, Pallas kernels, shards(): call(features_kernel, 'features', fast((slots * frames, feature), BF16),...  3.64 us
    pallas_call x1, Pallas kernels, shards(): call(gradients, 'gradients', (shape((feature, latents), BF16), shape((lat...  3.33 us
    pallas_call x1, Pallas kernels, shards(): call(encode, 'encode', (fast((half, wide), F32), fast((half, wide), BF16)...  2.37 us
  transfers between devices with their start and end apart: 18, of which 12 were waited for; matrix products, arithmetic and copies ran while one was open for 0% of the time, Pallas kernels for 2%

profile of v9, /device:TPU:0, one launch (start us, length us, event | category | flops | bytes accessed | tf_op | source)
XLA Modules:
  0.0 50.6 jit_solution(13389829700787259765)
XLA Ops:
  0.6 3.6 %features.1.refs_2_ = bf16[16,1536]{1,0:T(8,128)(2,1)S(1)} custom-call(s32[2]{0:T(128)} %refs_0_.1, s32[2]{0:T(128)} %refs_1_.3, f32[2,90]{1,0:T(2,128)} %refs_2_.1, f32[10,3,512]{2,1,0:T(4,128)} %bitcast.14, f32[3,2,512]{2,1,0:T(2,128)} %refs_4_.1, f32[3,2,512]{2,1,0:T(2,128)} %refs_5_.2, bf16[3,1536,512]{2,1,0:T(8,128)(2,1)} %refs_6_.1), custom_call_target="tpu_custom_call" | custom-call | flops 75497472 | bytes 4718592 | tf_op jit(solution)/shard_map/features/pallas_call | solution.py:403
  4.3 5.1 %collective-permute-start.2 = (bf16[16,1536]{1,0:T(8,128)(2,1)S(1)}, bf16[16,1536]{1,0:T(8,128)(2,1)S(1)}, u32[]{:S(2)}, u32[]{:S(2)}) collective-permute-start(bf16[16,1536]{1,0:T(8,128)(2,1)S(1)} %features.1.refs_2_), channel_id=1, source_target_pairs={{0,12},{1,13},{2,14},{3,15},{4,8},{5,9},{6,10},{7,11},{8,4},{9,5},... | collective-permute-start | bytes 147464 | tf_op jit(solution)/shard_map/ppermute | solution.py:74
  9.5 0.6 %collective-permute-start = (bf16[16,1536]{1,0:T(8,128)(2,1)S(1)}, bf16[16,1536]{1,0:T(8,128)(2,1)S(1)}, u32[]{:S(2)}, u32[]{:S(2)}) collective-permute-start(bf16[16,1536]{1,0:T(8,128)(2,1)S(1)} %features.1.refs_2_), channel_id=1, source_target_pairs={{0,4},{1,5},{2,6},{3,7},{4,0},{5,1},{6,2},{7,3},{8,12},{9,13},{10,... | collective-permute-start | bytes 147464 | tf_op jit(solution)/shard_map/ppermute | solution.py:74
  10.1 0.7 %norms.1 = (f32[512,128]{1,0:T(8,128)S(1)}, f32[8,512]{1,0:T(8,128)S(1)}) custom-call(bf16[512,1536]{1,0:T(8,128)(2,1)S(1)} %copy-done), custom_call_target="tpu_custom_call" | custom-call | flops 3145728 | bytes 1572864 | tf_op jit(solution)/shard_map/norms/pallas_call | solution.py:429
  10.8 0.9 %collective-permute-done.2.refs_5_ = bf16[16,1536]{1,0:T(8,128)(2,1)S(1)} collective-permute-done((bf16[16,1536]{1,0:T(8,128)(2,1)S(1)}, bf16[16,1536]{1,0:T(8,128)(2,1)S(1)}, u32[]{:S(2)}, u32[]{:S(2)}) %collective-permute-start.2) | collective-permute-done | bytes 49184 | tf_op jit(solution)/shard_map/ppermute | solution.py:74
  11.7 2.8 %collective-permute-done.1.refs_4_ = bf16[16,1536]{1,0:T(8,128)(2,1)S(1)} collective-permute-done((bf16[16,1536]{1,0:T(8,128)(2,1)S(1)}, bf16[16,1536]{1,0:T(8,128)(2,1)S(1)}, u32[]{:S(2)}, u32[]{:S(2)}) %collective-permute-start.1) | collective-permute-done | bytes 49184 | tf_op jit(solution)/shard_map/ppermute | solution.py:74
  14.5 1.6 %collective-permute-start.3 = (bf16[64,1536]{1,0:T(8,128)(2,1)S(1)}, bf16[64,1536]{1,0:T(8,128)(2,1)S(1)}, u32[]{:S(2)}, u32[]{:S(2)}) collective-permute-start(bf16[64,1536]{1,0:T(8,128)(2,1)S(1)} %join.1.refs_1_), channel_id=1, source_target_pairs={{0,2},{1,3},{2,0},{3,1},{4,6},{5,7},{6,4},{7,5},{8,10},{9,11},{10,... | collective-permute-start | bytes 589832 | tf_op jit(solution)/shard_map/ppermute | solution.py:74
  16.1 4.2 %collective-permute-done.3.refs_2_ = bf16[64,1536]{1,0:T(8,128)(2,1)S(1)} collective-permute-done((bf16[64,1536]{1,0:T(8,128)(2,1)S(1)}, bf16[64,1536]{1,0:T(8,128)(2,1)S(1)}, u32[]{:S(2)}, u32[]{:S(2)}) %collective-permute-start.3) | collective-permute-done | bytes 196640 | tf_op jit(solution)/shard_map/ppermute | solution.py:74
  20.3 1.4 %collective-permute-done.5.refs_4_ = bf16[64,1536]{1,0:T(8,128)(2,1)S(1)} collective-permute-done((bf16[64,1536]{1,0:T(8,128)(2,1)S(1)}, bf16[64,1536]{1,0:T(8,128)(2,1)S(1)}, u32[]{:S(2)}, u32[]{:S(2)}) %collective-permute-start.5) | collective-permute-done | bytes 196640 | tf_op jit(solution)/shard_map/ppermute | solution.py:74
  21.7 2.4 %encode.1 = (f32[64,1664]{1,0:T(8,128)S(1)}, bf16[64,1664]{1,0:T(8,128)(2,1)S(1)}, f32[16,1664]{1,0:T(8,128)S(1)}, bf16[128,1536]{1,0:T(8,128)(2,1)S(1)}, f32[128,512]{1,0:T(8,128)S(1)}) custom-call(s32[1]{0:T(128)} %bitcast.refs_0_, bf16[64,1536]{1,0:T(8,128)(2,1)S(1)} %join.1.refs_1_, bf16[64,1536]{1,0:T(8,128)(2,1)S(1)} %collective-permute-done.3.refs_2_, ...), custom_call_target="tpu_custom_call" | custom-call | flops 402653184 | bytes 3145728 | tf_op jit(solution)/shard_map/encode/pallas_call | solution.py:462
  24.3 1.3 %collective-permute-done.6 = bf16[64,1664]{1,0:T(8,128)(2,1)S(1)} collective-permute-done((bf16[64,1664]{1,0:T(8,128)(2,1)S(1)}, bf16[64,1664]{1,0:T(8,128)(2,1)S(1)}, u32[]{:S(2)}, u32[]{:S(2)}) %collective-permute-start.6) | collective-permute-done | bytes 213024 | tf_op jit(solution)/shard_map/ppermute | solution.py:74
  25.7 2.1 %collective-permute-start.9 = (bf16[16,1664]{1,0:T(8,128)(2,1)S(1)}, bf16[16,1664]{1,0:T(8,128)(2,1)S(1)}, u32[]{:S(2)}, u32[]{:S(2)}) collective-permute-start(bf16[16,1664]{1,0:T(8,128)(2,1)S(1)} %get-tuple-element.40), channel_id=1, source_target_pairs={{0,12},{1,13},{2,14},{3,15},{4,8},{5,9},{6,10},{7,11},{8,4},{9,5},... | collective-permute-start | bytes 159752 | tf_op jit(solution)/shard_map/ppermute | solution.py:74
  28.0 2.2 %collective-permute-start.7 = (bf16[16,1664]{1,0:T(8,128)(2,1)S(1)}, bf16[16,1664]{1,0:T(8,128)(2,1)S(1)}, u32[]{:S(2)}, u32[]{:S(2)}) collective-permute-start(bf16[16,1664]{1,0:T(8,128)(2,1)S(1)} %get-tuple-element.42), channel_id=1, source_target_pairs={{0,4},{1,5},{2,6},{3,7},{4,0},{5,1},{6,2},{7,3},{8,12},{9,13},{10,... | collective-permute-start | bytes 159752 | tf_op jit(solution)/shard_map/ppermute | solution.py:74
  30.5 1.8 %collective-permute-done.9.refs_5_ = bf16[16,1664]{1,0:T(8,128)(2,1)S(1)} collective-permute-done((bf16[16,1664]{1,0:T(8,128)(2,1)S(1)}, bf16[16,1664]{1,0:T(8,128)(2,1)S(1)}, u32[]{:S(2)}, u32[]{:S(2)}) %collective-permute-start.9) | collective-permute-done | bytes 53280 | tf_op jit(solution)/shard_map/ppermute | solution.py:74
  32.3 1.6 %collective-permute-done.8.refs_4_ = bf16[16,1664]{1,0:T(8,128)(2,1)S(1)} collective-permute-done((bf16[16,1664]{1,0:T(8,128)(2,1)S(1)}, bf16[16,1664]{1,0:T(8,128)(2,1)S(1)}, u32[]{:S(2)}, u32[]{:S(2)}) %collective-permute-start.8) | collective-permute-done | bytes 53280 | tf_op jit(solution)/shard_map/ppermute | solution.py:74
  34.0 1.6 %collective-permute-start.10 = (bf16[16,1664]{1,0:T(8,128)(2,1)S(1)}, bf16[16,1664]{1,0:T(8,128)(2,1)S(1)}, u32[]{:S(2)}, u32[]{:S(2)}) collective-permute-start(bf16[16,1664]{1,0:T(8,128)(2,1)S(1)} %sum.1), channel_id=1, source_target_pairs={{0,2},{1,3},{2,0},{3,1},{4,6},{5,7},{6,4},{7,5},{8,10},{9,11},{10,... | collective-permute-start | bytes 159752 | tf_op jit(solution)/shard_map/ppermute | solution.py:74
  35.6 2.6 %collective-permute-done.10 = bf16[16,1664]{1,0:T(8,128)(2,1)S(1)} collective-permute-done((bf16[16,1664]{1,0:T(8,128)(2,1)S(1)}, bf16[16,1664]{1,0:T(8,128)(2,1)S(1)}, u32[]{:S(2)}, u32[]{:S(2)}) %collective-permute-start.10) | collective-permute-done | bytes 53280 | tf_op jit(solution)/shard_map/ppermute | solution.py:74
  38.2 2.3 %collective-permute-start.13 = (bf16[16,1664]{1,0:T(8,128)(2,1)S(1)}, bf16[16,1664]{1,0:T(8,128)(2,1)S(1)}, u32[]{:S(2)}, u32[]{:S(2)}) collective-permute-start(bf16[16,1664]{1,0:T(8,128)(2,1)S(1)} %fusion.1.refs_0_), channel_id=1, source_target_pairs={{0,12},{1,13},{2,14},{3,15},{4,8},{5,9},{6,10},{7,11},{8,4},{9,5},... | collective-permute-start | bytes 159752 | tf_op jit(solution)/shard_map/ppermute | solution.py:74
  40.5 2.1 %collective-permute-start.11 = (bf16[16,1664]{1,0:T(8,128)(2,1)S(1)}, bf16[16,1664]{1,0:T(8,128)(2,1)S(1)}, u32[]{:S(2)}, u32[]{:S(2)}) collective-permute-start(bf16[16,1664]{1,0:T(8,128)(2,1)S(1)} %fusion.1.refs_0_), channel_id=1, source_target_pairs={{0,4},{1,5},{2,6},{3,7},{4,0},{5,1},{6,2},{7,3},{8,12},{9,13},{10,... | collective-permute-start | bytes 159752 | tf_op jit(solution)/shard_map/ppermute | solution.py:74
  42.7 2.0 %collective-permute-done.13.refs_3_ = bf16[16,1664]{1,0:T(8,128)(2,1)S(1)} collective-permute-done((bf16[16,1664]{1,0:T(8,128)(2,1)S(1)}, bf16[16,1664]{1,0:T(8,128)(2,1)S(1)}, u32[]{:S(2)}, u32[]{:S(2)}) %collective-permute-start.13) | collective-permute-done | bytes 53280 | tf_op jit(solution)/shard_map/ppermute | solution.py:74
  44.7 1.1 %collective-permute-done.12.refs_2_ = bf16[16,1664]{1,0:T(8,128)(2,1)S(1)} collective-permute-done((bf16[16,1664]{1,0:T(8,128)(2,1)S(1)}, bf16[16,1664]{1,0:T(8,128)(2,1)S(1)}, u32[]{:S(2)}, u32[]{:S(2)}) %collective-permute-start.12) | collective-permute-done | bytes 53280 | tf_op jit(solution)/shard_map/ppermute | solution.py:74
  45.9 0.5 %collective-permute-start.15 = (bf16[16,1664]{1,0:T(8,128)(2,1)S(1)}, bf16[16,1664]{1,0:T(8,128)(2,1)S(1)}, u32[]{:S(2)}, u32[]{:S(2)}) collective-permute-start(bf16[16,1664]{1,0:T(8,128)(2,1)S(1)} %collective-permute-done.11.refs_1_), channel_id=1, source_target_pairs={{0,1},{1,0},{2,3},{3,2},{4,5},{5,4},{6,7},{7,6},{8,9},{9,8},{10,11... | collective-permute-start | bytes 159752 | tf_op jit(solution)/shard_map/ppermute | solution.py:74
  46.4 0.7 %collective-permute-done.16.refs_6_ = bf16[16,1664]{1,0:T(8,128)(2,1)S(1)} collective-permute-done((bf16[16,1664]{1,0:T(8,128)(2,1)S(1)}, bf16[16,1664]{1,0:T(8,128)(2,1)S(1)}, u32[]{:S(2)}, u32[]{:S(2)}) %collective-permute-start.16) | collective-permute-done | bytes 53280 | tf_op jit(solution)/shard_map/ppermute | solution.py:74
  47.3 3.3 %gradients.1 = (bf16[1536,512]{1,0:T(8,128)(2,1)}, bf16[512,1536]{1,0:T(8,128)(2,1)}, f32[1,512]{1,0:T(1,128)}, f32[1536]{0:T(1024)}, f32[1]{0:T(128)}, /*index=5*/bf16[8,1536]{1,0:T(8,128)(2,1)}) custom-call(bf16[16,1664]{1,0:T(8,128)(2,1)S(1)} %fusion.1.refs_0_, bf16[16,1664]{1,0:T(8,128)(2,1)S(1)} %collective-permute-done.11.refs_1_, ...), custom_call_target="tpu_custom_call" | custom-call | flops 603979776 | bytes 6291456 | tf_op jit(solution)/shard_map/gradients/pallas_call | solution.py:525
  (34 shorter events, 1.0 us)
Async XLA Ops:
  0.6 9.5 %copy-start = (bf16[512,1536]{1,0:T(8,128)(2,1)S(1)}, bf16[512,1536]{1,0:T(8,128)(2,1)}, u32[]{:S(2)}) copy-start(bf16[512,1536]{1,0:T(8,128)(2,1)} %refs_8_.1) | copy-start | bytes 4718596
  4.3 10.1 %copy-start.2 = (bf16[1536,512]{1,0:T(8,128)(2,1)S(1)}, bf16[1536,512]{1,0:T(8,128)(2,1)}, u32[]{:S(2)}) copy-start(bf16[1536,512]{1,0:T(8,128)(2,1)} %refs_5_.3) | copy-start | bytes 4718596
  4.3 17.4 %copy-start.3 = (f32[1536]{0:T(1024)S(1)}, f32[1536]{0:T(1024)}, u32[]{:S(2)}) copy-start(f32[1536]{0:T(1024)} %refs_9_.1) | copy-start | bytes 18436
  4.3 17.4 %copy-start.4 = (f32[512]{0:T(512)S(1)}, f32[512]{0:T(512)}, u32[]{:S(2)}) copy-start(f32[512]{0:T(512)} %param.19) | copy-start | bytes 6148
  4.3 7.3 %collective-permute-start.2 = (bf16[16,1536]{1,0:T(8,128)(2,1)S(1)}, bf16[16,1536]{1,0:T(8,128)(2,1)S(1)}, u32[]{:S(2)}, u32[]{:S(2)}) collective-permute-start(bf16[16,1536]{1,0:T(8,128)(2,1)S(1)} %features.1.refs_2_), channel_id=1, source_target_pairs={{0,12},{1,13},{2,14},{3,15},{4,8},{5,9},{6,10},{7,11},{8,4},{9,5},... | collective-permute-start | bytes 147464 | tf_op jit(solution)/shard_map/ppermute | solution.py:74
  9.4 5.0 %collective-permute-start.1 = (bf16[16,1536]{1,0:T(8,128)(2,1)S(1)}, bf16[16,1536]{1,0:T(8,128)(2,1)S(1)}, u32[]{:S(2)}, u32[]{:S(2)}) collective-permute-start(bf16[16,1536]{1,0:T(8,128)(2,1)S(1)} %features.1.refs_2_), channel_id=1, source_target_pairs={{0,8},{1,9},{2,10},{3,11},{4,12},{5,13},{6,14},{7,15},{8,0},{9,1},... | collective-permute-start | bytes 147464 | tf_op jit(solution)/shard_map/ppermute | solution.py:74
  9.5 5.0 %collective-permute-start = (bf16[16,1536]{1,0:T(8,128)(2,1)S(1)}, bf16[16,1536]{1,0:T(8,128)(2,1)S(1)}, u32[]{:S(2)}, u32[]{:S(2)}) collective-permute-start(bf16[16,1536]{1,0:T(8,128)(2,1)S(1)} %features.1.refs_2_), channel_id=1, source_target_pairs={{0,4},{1,5},{2,6},{3,7},{4,0},{5,1},{6,2},{7,3},{8,12},{9,13},{10,... | collective-permute-start | bytes 147464 | tf_op jit(solution)/shard_map/ppermute | solution.py:74
  14.5 5.8 %collective-permute-start.3 = (bf16[64,1536]{1,0:T(8,128)(2,1)S(1)}, bf16[64,1536]{1,0:T(8,128)(2,1)S(1)}, u32[]{:S(2)}, u32[]{:S(2)}) collective-permute-start(bf16[64,1536]{1,0:T(8,128)(2,1)S(1)} %join.1.refs_1_), channel_id=1, source_target_pairs={{0,2},{1,3},{2,0},{3,1},{4,6},{5,7},{6,4},{7,5},{8,10},{9,11},{10,... | collective-permute-start | bytes 589832 | tf_op jit(solution)/shard_map/ppermute | solution.py:74
  16.0 4.2 %collective-permute-start.4 = (bf16[64,1536]{1,0:T(8,128)(2,1)S(1)}, bf16[64,1536]{1,0:T(8,128)(2,1)S(1)}, u32[]{:S(2)}, u32[]{:S(2)}) collective-permute-start(bf16[64,1536]{1,0:T(8,128)(2,1)S(1)} %join.1.refs_1_), channel_id=1, source_target_pairs={{0,1},{1,0},{2,3},{3,2},{4,5},{5,4},{6,7},{7,6},{8,9},{9,8},{10,11... | collective-permute-start | bytes 589832 | tf_op jit(solution)/shard_map/ppermute | solution.py:74
  20.3 1.4 %collective-permute-start.5 = (bf16[64,1536]{1,0:T(8,128)(2,1)S(1)}, bf16[64,1536]{1,0:T(8,128)(2,1)S(1)}, u32[]{:S(2)}, u32[]{:S(2)}) collective-permute-start(bf16[64,1536]{1,0:T(8,128)(2,1)S(1)} %collective-permute-done.3.refs_2_), channel_id=1, source_target_pairs={{0,1},{1,0},{2,3},{3,2},{4,5},{5,4},{6,7},{7,6},{8,9},{9,8},{10,11... | collective-permute-start | bytes 589832 | tf_op jit(solution)/shard_map/ppermute | solution.py:74
  24.1 9.8 %copy-start.1 = (bf16[512,1536]{1,0:T(8,128)(2,1)S(1)}, bf16[512,1536]{1,0:T(8,128)(2,1)}, u32[]{:S(2)}) copy-start(bf16[512,1536]{1,0:T(8,128)(2,1)} %refs_8_.1) | copy-start | bytes 4718596
  24.1 1.5 %collective-permute-start.6 = (bf16[64,1664]{1,0:T(8,128)(2,1)S(1)}, bf16[64,1664]{1,0:T(8,128)(2,1)S(1)}, u32[]{:S(2)}, u32[]{:S(2)}) collective-permute-start(bf16[64,1664]{1,0:T(8,128)(2,1)S(1)} %get-tuple-element.28), channel_id=1, source_target_pairs={{0,1},{1,0},{2,3},{3,2},{4,5},{5,4},{6,7},{7,6},{8,9},{9,8},{10,11... | collective-permute-start | bytes 638984 | tf_op jit(solution)/shard_map/ppermute | solution.py:74
  25.7 6.6 %collective-permute-start.9 = (bf16[16,1664]{1,0:T(8,128)(2,1)S(1)}, bf16[16,1664]{1,0:T(8,128)(2,1)S(1)}, u32[]{:S(2)}, u32[]{:S(2)}) collective-permute-start(bf16[16,1664]{1,0:T(8,128)(2,1)S(1)} %get-tuple-element.40), channel_id=1, source_target_pairs={{0,12},{1,13},{2,14},{3,15},{4,8},{5,9},{6,10},{7,11},{8,4},{9,5},... | collective-permute-start | bytes 159752 | tf_op jit(solution)/shard_map/ppermute | solution.py:74
  27.8 6.1 %collective-permute-start.8 = (bf16[16,1664]{1,0:T(8,128)(2,1)S(1)}, bf16[16,1664]{1,0:T(8,128)(2,1)S(1)}, u32[]{:S(2)}, u32[]{:S(2)}) collective-permute-start(bf16[16,1664]{1,0:T(8,128)(2,1)S(1)} %get-tuple-element.41), channel_id=1, source_target_pairs={{0,8},{1,9},{2,10},{3,11},{4,12},{5,13},{6,14},{7,15},{8,0},{9,1},... | collective-permute-start | bytes 159752 | tf_op jit(solution)/shard_map/ppermute | solution.py:74
  28.0 6.0 %collective-permute-start.7 = (bf16[16,1664]{1,0:T(8,128)(2,1)S(1)}, bf16[16,1664]{1,0:T(8,128)(2,1)S(1)}, u32[]{:S(2)}, u32[]{:S(2)}) collective-permute-start(bf16[16,1664]{1,0:T(8,128)(2,1)S(1)} %get-tuple-element.42), channel_id=1, source_target_pairs={{0,4},{1,5},{2,6},{3,7},{4,0},{5,1},{6,2},{7,3},{8,12},{9,13},{10,... | collective-permute-start | bytes 159752 | tf_op jit(solution)/shard_map/ppermute | solution.py:74
  34.0 4.2 %collective-permute-start.10 = (bf16[16,1664]{1,0:T(8,128)(2,1)S(1)}, bf16[16,1664]{1,0:T(8,128)(2,1)S(1)}, u32[]{:S(2)}, u32[]{:S(2)}) collective-permute-start(bf16[16,1664]{1,0:T(8,128)(2,1)S(1)} %sum.1), channel_id=1, source_target_pairs={{0,2},{1,3},{2,0},{3,1},{4,6},{5,7},{6,4},{7,5},{8,10},{9,11},{10,... | collective-permute-start | bytes 159752 | tf_op jit(solution)/shard_map/ppermute | solution.py:74
  38.2 6.5 %collective-permute-start.13 = (bf16[16,1664]{1,0:T(8,128)(2,1)S(1)}, bf16[16,1664]{1,0:T(8,128)(2,1)S(1)}, u32[]{:S(2)}, u32[]{:S(2)}) collective-permute-start(bf16[16,1664]{1,0:T(8,128)(2,1)S(1)} %fusion.1.refs_0_), channel_id=1, source_target_pairs={{0,12},{1,13},{2,14},{3,15},{4,8},{5,9},{6,10},{7,11},{8,4},{9,5},... | collective-permute-start | bytes 159752 | tf_op jit(solution)/shard_map/ppermute | solution.py:74
  40.5 5.3 %collective-permute-start.12 = (bf16[16,1664]{1,0:T(8,128)(2,1)S(1)}, bf16[16,1664]{1,0:T(8,128)(2,1)S(1)}, u32[]{:S(2)}, u32[]{:S(2)}) collective-permute-start(bf16[16,1664]{1,0:T(8,128)(2,1)S(1)} %fusion.1.refs_0_), channel_id=1, source_target_pairs={{0,8},{1,9},{2,10},{3,11},{4,12},{5,13},{6,14},{7,15},{8,0},{9,1},... | collective-permute-start | bytes 159752 | tf_op jit(solution)/shard_map/ppermute | solution.py:74
  40.5 5.3 %collective-permute-start.11 = (bf16[16,1664]{1,0:T(8,128)(2,1)S(1)}, bf16[16,1664]{1,0:T(8,128)(2,1)S(1)}, u32[]{:S(2)}, u32[]{:S(2)}) collective-permute-start(bf16[16,1664]{1,0:T(8,128)(2,1)S(1)} %fusion.1.refs_0_), channel_id=1, source_target_pairs={{0,4},{1,5},{2,6},{3,7},{4,0},{5,1},{6,2},{7,3},{8,12},{9,13},{10,... | collective-permute-start | bytes 159752 | tf_op jit(solution)/shard_map/ppermute | solution.py:74
  42.7 3.7 %collective-permute-start.14 = (bf16[16,1664]{1,0:T(8,128)(2,1)S(1)}, bf16[16,1664]{1,0:T(8,128)(2,1)S(1)}, u32[]{:S(2)}, u32[]{:S(2)}) collective-permute-start(bf16[16,1664]{1,0:T(8,128)(2,1)S(1)} %fusion.1.refs_0_), channel_id=1, source_target_pairs={{0,1},{1,0},{2,3},{3,2},{4,5},{5,4},{6,7},{7,6},{8,9},{9,8},{10,11... | collective-permute-start | bytes 159752 | tf_op jit(solution)/shard_map/ppermute | solution.py:74
  44.7 1.7 %collective-permute-start.17 = (bf16[16,1664]{1,0:T(8,128)(2,1)S(1)}, bf16[16,1664]{1,0:T(8,128)(2,1)S(1)}, u32[]{:S(2)}, u32[]{:S(2)}) collective-permute-start(bf16[16,1664]{1,0:T(8,128)(2,1)S(1)} %collective-permute-done.13.refs_3_), channel_id=1, source_target_pairs={{0,1},{1,0},{2,3},{3,2},{4,5},{5,4},{6,7},{7,6},{8,9},{9,8},{10,11... | collective-permute-start | bytes 159752 | tf_op jit(solution)/shard_map/ppermute | solution.py:74
  45.8 1.2 %collective-permute-start.16 = (bf16[16,1664]{1,0:T(8,128)(2,1)S(1)}, bf16[16,1664]{1,0:T(8,128)(2,1)S(1)}, u32[]{:S(2)}, u32[]{:S(2)}) collective-permute-start(bf16[16,1664]{1,0:T(8,128)(2,1)S(1)} %collective-permute-done.12.refs_2_), channel_id=1, source_target_pairs={{0,1},{1,0},{2,3},{3,2},{4,5},{5,4},{6,7},{7,6},{8,9},{9,8},{10,11... | collective-permute-start | bytes 159752 | tf_op jit(solution)/shard_map/ppermute | solution.py:74
  45.9 1.4 %collective-permute-start.15 = (bf16[16,1664]{1,0:T(8,128)(2,1)S(1)}, bf16[16,1664]{1,0:T(8,128)(2,1)S(1)}, u32[]{:S(2)}, u32[]{:S(2)}) collective-permute-start(bf16[16,1664]{1,0:T(8,128)(2,1)S(1)} %collective-permute-done.11.refs_1_), channel_id=1, source_target_pairs={{0,1},{1,0},{2,3},{3,2},{4,5},{5,4},{6,7},{7,6},{8,9},{9,8},{10,11... | collective-permute-start | bytes 159752 | tf_op jit(solution)/shard_map/ppermute | solution.py:74

commit v10 on v9

--- a/solution.py
+++ b/solution.py
@@ -14,7 +14,7 @@
 PINNED_BYTES = 24 << 20
 PINNED_TOKENS = 256
 GROUP_ROWS = 256
-DEC_PARTS = 2
+DEC_PARTS = 3
 
 sparsity = 0.5
 epsilon = 1e-05
@@ -215,12 +215,12 @@
 def encode_kernel(count, outer, inner, slots, frames, *refs):
     me_ref = refs[0]
     pieces = refs[1 : 1 + count]
-    enc, bias, dec_hbm, weights_sum, dec_bias = refs[1 + count : 6 + count]
-    own, send, shift, inputs_out, latent_out, dec, sems = refs[6 + count :]
-    quarter = dec.shape[0] // DEC_PARTS
+    enc, bias, dec_hbm, weights_sum = refs[1 + count : 5 + count]
+    send, inputs_out, latent_out, dec, sems = refs[5 + count :]
+    part_width = dec.shape[1] // DEC_PARTS
     fetches = []
     for i in range(DEC_PARTS):
-        at = pl.ds(i * quarter, quarter)
+        at = (slice(None), pl.ds(i * part_width, part_width))
         fetches.append(pltpu.make_async_copy(dec_hbm.at[at], dec.at[at], sems.at[i]))
         fetches[-1].start()
     me = me_ref[0]
@@ -278,22 +278,29 @@
     inputs_out[...] = inputs
     latent = jnp.maximum(jnp.dot(inputs, enc[...], preferred_element_type=F32) + bias[...], 0.0)
     latent_out[...] = latent
-    rounded = latent.astype(BF16)
-    part = jnp.zeros((tokens, feature), F32)
+    half = tokens // 2
+    rounded = latent[half:].astype(BF16)
     for i in range(DEC_PARTS):
         fetches[i].wait()
-        at = slice(i * quarter, (i + 1) * quarter)
-        part = part + jnp.dot(rounded[:, at], dec[at], preferred_element_type=F32)
-    weighted = latent * weights_sum[0:1, :]
+        at = slice(i * part_width, (i + 1) * part_width)
+        part = jnp.dot(rounded, dec[:, at], preferred_element_type=F32)
+        send[:, at] = part.astype(BF16)
+    send[:, feature:] = lane_sums(latent[half:] * weights_sum[0:1, :]).astype(BF16)
+
+
+def lane_sums(weighted):
     extra = weighted[:, :LANES]
     for q in range(1, weighted.shape[1] // LANES):
         extra = extra + weighted[:, q * LANES : (q + 1) * LANES]
-    half = tokens // 2
-    own[:, :feature] = part[:half]
-    own[:, feature:] = extra[:half]
-    send[:, :feature] = part[half:].astype(BF16)
-    send[:, feature:] = extra[half:].astype(BF16)
-    chunk = shift.shape[0]
+    return extra
+
+
+def own_kernel(inputs, latent, dec, weights_sum, dec_bias, own, shift):
+    half, chunk = own.shape[0], shift.shape[0]
+    feature = dec.shape[1]
+    kept = latent[:half]
+    own[:, :feature] = jnp.dot(kept.astype(BF16), dec[...], preferred_element_type=F32)
+    own[:, feature:] = lane_sums(kept * weights_sum[0:1, :])
     shift[:, :feature] = dec_bias[...].reshape(1, feature) - inputs[:chunk].astype(F32)
     shift[:, feature:] = jnp.zeros((chunk, EXTRA), F32)
 
@@ -307,8 +314,8 @@
 
 
 def sum_kernel(*refs):
-    total = refs[2][...]
-    for ref in refs[3:-1]:
+    total = refs[1][...]
+    for ref in refs[2:-1]:
         total = total + ref[...].astype(F32)
     refs[-1][...] = total.astype(BF16)
 
@@ -459,20 +466,19 @@
     def encode(*refs):
         encode_kernel(len(pieces), outer, inner, slots, frames, *refs)
 
-    own, send, shift, inputs, latent = call(
+    send, inputs, latent, decoder = call(
         encode,
         "encode",
         (
-            fast((half, wide), F32),
             fast((half, wide), BF16),
-            fast((chunk, wide), F32),
             fast((tokens, feature), BF16),
             fast((tokens, latents), F32),
+            fast(dec_weight.shape, BF16),
         ),
-        [smem()] + [vmem()] * (len(pieces) + 2) + [pl.BlockSpec(memory_space=pl.ANY)] + [vmem()] * 2,
-        (vmem(),) * 5,
-        [pltpu.VMEM(dec_weight.shape, BF16), pltpu.SemaphoreType.DMA((DEC_PARTS,))],
-        flops=4 * tokens * feature * latents,
+        [smem()] + [vmem()] * (len(pieces) + 2) + [pl.BlockSpec(memory_space=pl.ANY), vmem()],
+        (vmem(),) * 4,
+        [pltpu.SemaphoreType.DMA((DEC_PARTS,))],
+        flops=3 * tokens * feature * latents,
         moved=4 * dec_weight.size,
     )(
         position,
@@ -481,8 +487,18 @@
         enc_bias.reshape(1, latents),
         far(dec_weight),
         near(weights_sum),
-        dec_bias,
-    )
+    )
+    received = exchange(send, 1)
+    decoder = near(decoder)
+    own, shift = call(
+        own_kernel,
+        "own",
+        (fast((half, wide), F32), fast((chunk, wide), F32)),
+        [vmem()] * 5,
+        (vmem(),) * 2,
+        flops=tokens * feature * latents,
+        moved=2 * dec_weight.size,
+    )(near(inputs), near(latent), decoder, near(weights_sum), dec_bias)
 
     inputs_t, latent_t, scale = call(
         turn_kernel,
@@ -494,7 +510,7 @@
         moved=4 * tokens * feature,
     )(near(inputs), near(latent), near(norms))
 
-    part = own + exchange(send, 1).astype(F32)
+    part = own + received.astype(F32)
     small = part.astype(BF16)
     blocks = [part[:chunk]]
     for k in range(1, outer):
@@ -503,10 +519,10 @@
         sum_kernel,
         "sum",
         fast((chunk, wide), BF16),
-        [pl.BlockSpec(memory_space=pl.ANY)] * 2 + [vmem()] * outer,
+        [pl.BlockSpec(memory_space=pl.ANY)] + [vmem()] * outer,
         vmem(),
         moved=8 * chunk * wide,
-    )(near(scale), decoder, *[near(block) for block in blocks])
+    )(near(scale), *[near(block) for block in blocks])
     bit = 2
     while bit < step:
         width = (bit // 2) * ROWS_DEV

time: 50.7 us -> 50.6 us (level)
    pallas_call x1 -> x2, Pallas kernels: 2.37 us -> 2.6 us  [the longest x1 2.22 us: shards(): call(encode, 'encode', (fast((half, wide), BF16), fast((tokens, feature),...]
  transfers between devices with their start and end apart: 18 -> 18, of which waited for: 12 -> 12; matrix products, arithmetic and copies ran while one was open for 0% -> 0% of each run, Pallas kernels for 2% -> 3%
where the time goes in v10:
time: 50.6 us; the launch traced here: 50.4 us
  waiting for transfers between devices  20.3 us (40%)
  starting transfers between devices  18.6 us (37%)
  Pallas kernels  10.7 us (21%)
  between operations  0.74 us (1%)
    ppermute x18, waiting for transfers between devices, exchange(): return lax.ppermute(value, 'utt', [(i, i ^ bit) for i in range(devices)])  20.3 us
    ppermute x18, starting transfers between devices, exchange(): return lax.ppermute(value, 'utt', [(i, i ^ bit) for i in range(devices)])  18.6 us
    pallas_call x1, Pallas kernels, shards(): call(features_kernel, 'features', fast((slots * frames, feature), BF16),...  3.64 us
    pallas_call x1, Pallas kernels, shards(): call(gradients, 'gradients', (shape((feature, latents), BF16), shape((lat...  3.35 us
    pallas_call x1, Pallas kernels, shards(): call(encode, 'encode', (fast((half, wide), BF16), fast((tokens, feature),...  2.22 us
  transfers between devices with their start and end apart: 18, of which 12 were waited for; matrix products, arithmetic and copies ran while one was open for 0% of the time, Pallas kernels for 3%

profile of v10, /device:TPU:0, one launch (start us, length us, event | category | flops | bytes accessed | tf_op | source)
XLA Modules:
  0.0 50.4 jit_solution(15976326945691619674)
XLA Ops:
  0.6 3.6 %features.1.refs_2_ = bf16[16,1536]{1,0:T(8,128)(2,1)S(1)} custom-call(s32[2]{0:T(128)} %refs_0_.1, s32[2]{0:T(128)} %refs_1_.2, f32[2,90]{1,0:T(2,128)} %refs_2_.1, f32[10,3,512]{2,1,0:T(4,128)} %bitcast.14, f32[3,2,512]{2,1,0:T(2,128)} %refs_4_.1, f32[3,2,512]{2,1,0:T(2,128)} %refs_5_.2, bf16[3,1536,512]{2,1,0:T(8,128)(2,1)} %refs_6_.1), custom_call_target="tpu_custom_call" | custom-call | flops 75497472 | bytes 4718592 | tf_op jit(solution)/shard_map/features/pallas_call | solution.py:410
  4.3 5.1 %collective-permute-start.2 = (bf16[16,1536]{1,0:T(8,128)(2,1)S(1)}, bf16[16,1536]{1,0:T(8,128)(2,1)S(1)}, u32[]{:S(2)}, u32[]{:S(2)}) collective-permute-start(bf16[16,1536]{1,0:T(8,128)(2,1)S(1)} %features.1.refs_2_), channel_id=1, source_target_pairs={{0,12},{1,13},{2,14},{3,15},{4,8},{5,9},{6,10},{7,11},{8,4},{9,5},... | collective-permute-start | bytes 147464 | tf_op jit(solution)/shard_map/ppermute | solution.py:74
  9.4 0.6 %collective-permute-start = (bf16[16,1536]{1,0:T(8,128)(2,1)S(1)}, bf16[16,1536]{1,0:T(8,128)(2,1)S(1)}, u32[]{:S(2)}, u32[]{:S(2)}) collective-permute-start(bf16[16,1536]{1,0:T(8,128)(2,1)S(1)} %features.1.refs_2_), channel_id=1, source_target_pairs={{0,4},{1,5},{2,6},{3,7},{4,0},{5,1},{6,2},{7,3},{8,12},{9,13},{10,... | collective-permute-start | bytes 147464 | tf_op jit(solution)/shard_map/ppermute | solution.py:74
  10.1 0.7 %norms.1 = (f32[512,128]{1,0:T(8,128)S(1)}, f32[8,512]{1,0:T(8,128)S(1)}) custom-call(bf16[512,1536]{1,0:T(8,128)(2,1)S(1)} %copy-done), custom_call_target="tpu_custom_call" | custom-call | flops 3145728 | bytes 1572864 | tf_op jit(solution)/shard_map/norms/pallas_call | solution.py:436
  10.8 0.9 %collective-permute-done.2.refs_5_ = bf16[16,1536]{1,0:T(8,128)(2,1)S(1)} collective-permute-done((bf16[16,1536]{1,0:T(8,128)(2,1)S(1)}, bf16[16,1536]{1,0:T(8,128)(2,1)S(1)}, u32[]{:S(2)}, u32[]{:S(2)}) %collective-permute-start.2) | collective-permute-done | bytes 49184 | tf_op jit(solution)/shard_map/ppermute | solution.py:74
  11.7 2.8 %collective-permute-done.1.refs_4_ = bf16[16,1536]{1,0:T(8,128)(2,1)S(1)} collective-permute-done((bf16[16,1536]{1,0:T(8,128)(2,1)S(1)}, bf16[16,1536]{1,0:T(8,128)(2,1)S(1)}, u32[]{:S(2)}, u32[]{:S(2)}) %collective-permute-start.1) | collective-permute-done | bytes 49184 | tf_op jit(solution)/shard_map/ppermute | solution.py:74
  14.5 1.6 %collective-permute-start.3 = (bf16[64,1536]{1,0:T(8,128)(2,1)S(1)}, bf16[64,1536]{1,0:T(8,128)(2,1)S(1)}, u32[]{:S(2)}, u32[]{:S(2)}) collective-permute-start(bf16[64,1536]{1,0:T(8,128)(2,1)S(1)} %join.1.refs_1_), channel_id=1, source_target_pairs={{0,2},{1,3},{2,0},{3,1},{4,6},{5,7},{6,4},{7,5},{8,10},{9,11},{10,... | collective-permute-start | bytes 589832 | tf_op jit(solution)/shard_map/ppermute | solution.py:74
  16.0 4.2 %collective-permute-done.3.refs_2_ = bf16[64,1536]{1,0:T(8,128)(2,1)S(1)} collective-permute-done((bf16[64,1536]{1,0:T(8,128)(2,1)S(1)}, bf16[64,1536]{1,0:T(8,128)(2,1)S(1)}, u32[]{:S(2)}, u32[]{:S(2)}) %collective-permute-start.3) | collective-permute-done | bytes 196640 | tf_op jit(solution)/shard_map/ppermute | solution.py:74
  20.3 1.4 %collective-permute-done.5.refs_4_ = bf16[64,1536]{1,0:T(8,128)(2,1)S(1)} collective-permute-done((bf16[64,1536]{1,0:T(8,128)(2,1)S(1)}, bf16[64,1536]{1,0:T(8,128)(2,1)S(1)}, u32[]{:S(2)}, u32[]{:S(2)}) %collective-permute-start.5) | collective-permute-done | bytes 196640 | tf_op jit(solution)/shard_map/ppermute | solution.py:74
  21.7 2.2 %encode.1 = (bf16[64,1664]{1,0:T(8,128)(2,1)S(1)}, bf16[128,1536]{1,0:T(8,128)(2,1)S(1)}, f32[128,512]{1,0:T(8,128)S(1)}, bf16[512,1536]{1,0:T(8,128)(2,1)S(1)}) custom-call(s32[1]{0:T(128)} %bitcast.refs_0_, bf16[64,1536]{1,0:T(8,128)(2,1)S(1)} %join.1.refs_1_, bf16[64,1536]{1,0:T(8,128)(2,1)S(1)} %collective-permute-done.3.refs_2_, ...), custom_call_target="tpu_custom_call" | custom-call | flops 301989888 | bytes 3145728 | tf_op jit(solution)/shard_map/encode/pallas_call | solution.py:469
  24.5 0.9 %collective-permute-done.6 = bf16[64,1664]{1,0:T(8,128)(2,1)S(1)} collective-permute-done((bf16[64,1664]{1,0:T(8,128)(2,1)S(1)}, bf16[64,1664]{1,0:T(8,128)(2,1)S(1)}, u32[]{:S(2)}, u32[]{:S(2)}) %collective-permute-start.6) | collective-permute-done | bytes 213024 | tf_op jit(solution)/shard_map/ppermute | solution.py:74
  25.6 2.1 %collective-permute-start.9 = (bf16[16,1664]{1,0:T(8,128)(2,1)S(1)}, bf16[16,1664]{1,0:T(8,128)(2,1)S(1)}, u32[]{:S(2)}, u32[]{:S(2)}) collective-permute-start(bf16[16,1664]{1,0:T(8,128)(2,1)S(1)} %get-tuple-element.42), channel_id=1, source_target_pairs={{0,12},{1,13},{2,14},{3,15},{4,8},{5,9},{6,10},{7,11},{8,4},{9,5},... | collective-permute-start | bytes 159752 | tf_op jit(solution)/shard_map/ppermute | solution.py:74
  27.8 2.2 %collective-permute-start.7 = (bf16[16,1664]{1,0:T(8,128)(2,1)S(1)}, bf16[16,1664]{1,0:T(8,128)(2,1)S(1)}, u32[]{:S(2)}, u32[]{:S(2)}) collective-permute-start(bf16[16,1664]{1,0:T(8,128)(2,1)S(1)} %get-tuple-element.44), channel_id=1, source_target_pairs={{0,4},{1,5},{2,6},{3,7},{4,0},{5,1},{6,2},{7,3},{8,12},{9,13},{10,... | collective-permute-start | bytes 159752 | tf_op jit(solution)/shard_map/ppermute | solution.py:74
  30.4 1.8 %collective-permute-done.9.refs_4_ = bf16[16,1664]{1,0:T(8,128)(2,1)S(1)} collective-permute-done((bf16[16,1664]{1,0:T(8,128)(2,1)S(1)}, bf16[16,1664]{1,0:T(8,128)(2,1)S(1)}, u32[]{:S(2)}, u32[]{:S(2)}) %collective-permute-start.9) | collective-permute-done | bytes 53280 | tf_op jit(solution)/shard_map/ppermute | solution.py:74
  32.2 1.6 %collective-permute-done.8.refs_3_ = bf16[16,1664]{1,0:T(8,128)(2,1)S(1)} collective-permute-done((bf16[16,1664]{1,0:T(8,128)(2,1)S(1)}, bf16[16,1664]{1,0:T(8,128)(2,1)S(1)}, u32[]{:S(2)}, u32[]{:S(2)}) %collective-permute-start.8) | collective-permute-done | bytes 53280 | tf_op jit(solution)/shard_map/ppermute | solution.py:74
  33.8 1.6 %collective-permute-start.10 = (bf16[16,1664]{1,0:T(8,128)(2,1)S(1)}, bf16[16,1664]{1,0:T(8,128)(2,1)S(1)}, u32[]{:S(2)}, u32[]{:S(2)}) collective-permute-start(bf16[16,1664]{1,0:T(8,128)(2,1)S(1)} %sum.1), channel_id=1, source_target_pairs={{0,2},{1,3},{2,0},{3,1},{4,6},{5,7},{6,4},{7,5},{8,10},{9,11},{10,... | collective-permute-start | bytes 159752 | tf_op jit(solution)/shard_map/ppermute | solution.py:74
  35.4 2.6 %collective-permute-done.10 = bf16[16,1664]{1,0:T(8,128)(2,1)S(1)} collective-permute-done((bf16[16,1664]{1,0:T(8,128)(2,1)S(1)}, bf16[16,1664]{1,0:T(8,128)(2,1)S(1)}, u32[]{:S(2)}, u32[]{:S(2)}) %collective-permute-start.10) | collective-permute-done | bytes 53280 | tf_op jit(solution)/shard_map/ppermute | solution.py:74
  38.0 2.3 %collective-permute-start.13 = (bf16[16,1664]{1,0:T(8,128)(2,1)S(1)}, bf16[16,1664]{1,0:T(8,128)(2,1)S(1)}, u32[]{:S(2)}, u32[]{:S(2)}) collective-permute-start(bf16[16,1664]{1,0:T(8,128)(2,1)S(1)} %fusion.1.refs_0_), channel_id=1, source_target_pairs={{0,12},{1,13},{2,14},{3,15},{4,8},{5,9},{6,10},{7,11},{8,4},{9,5},... | collective-permute-start | bytes 159752 | tf_op jit(solution)/shard_map/ppermute | solution.py:74
  40.4 2.1 %collective-permute-start.11 = (bf16[16,1664]{1,0:T(8,128)(2,1)S(1)}, bf16[16,1664]{1,0:T(8,128)(2,1)S(1)}, u32[]{:S(2)}, u32[]{:S(2)}) collective-permute-start(bf16[16,1664]{1,0:T(8,128)(2,1)S(1)} %fusion.1.refs_0_), channel_id=1, source_target_pairs={{0,4},{1,5},{2,6},{3,7},{4,0},{5,1},{6,2},{7,3},{8,12},{9,13},{10,... | collective-permute-start | bytes 159752 | tf_op jit(solution)/shard_map/ppermute | solution.py:74
  42.5 2.0 %collective-permute-done.13.refs_3_ = bf16[16,1664]{1,0:T(8,128)(2,1)S(1)} collective-permute-done((bf16[16,1664]{1,0:T(8,128)(2,1)S(1)}, bf16[16,1664]{1,0:T(8,128)(2,1)S(1)}, u32[]{:S(2)}, u32[]{:S(2)}) %collective-permute-start.13) | collective-permute-done | bytes 53280 | tf_op jit(solution)/shard_map/ppermute | solution.py:74
  44.5 1.1 %collective-permute-done.12.refs_2_ = bf16[16,1664]{1,0:T(8,128)(2,1)S(1)} collective-permute-done((bf16[16,1664]{1,0:T(8,128)(2,1)S(1)}, bf16[16,1664]{1,0:T(8,128)(2,1)S(1)}, u32[]{:S(2)}, u32[]{:S(2)}) %collective-permute-start.12) | collective-permute-done | bytes 53280 | tf_op jit(solution)/shard_map/ppermute | solution.py:74
  45.7 0.5 %collective-permute-start.15 = (bf16[16,1664]{1,0:T(8,128)(2,1)S(1)}, bf16[16,1664]{1,0:T(8,128)(2,1)S(1)}, u32[]{:S(2)}, u32[]{:S(2)}) collective-permute-start(bf16[16,1664]{1,0:T(8,128)(2,1)S(1)} %collective-permute-done.11.refs_1_), channel_id=1, source_target_pairs={{0,1},{1,0},{2,3},{3,2},{4,5},{5,4},{6,7},{7,6},{8,9},{9,8},{10,11... | collective-permute-start | bytes 159752 | tf_op jit(solution)/shard_map/ppermute | solution.py:74
  46.2 0.7 %collective-permute-done.16.refs_6_ = bf16[16,1664]{1,0:T(8,128)(2,1)S(1)} collective-permute-done((bf16[16,1664]{1,0:T(8,128)(2,1)S(1)}, bf16[16,1664]{1,0:T(8,128)(2,1)S(1)}, u32[]{:S(2)}, u32[]{:S(2)}) %collective-permute-start.16) | collective-permute-done | bytes 53280 | tf_op jit(solution)/shard_map/ppermute | solution.py:74
  47.1 3.4 %gradients.1 = (bf16[1536,512]{1,0:T(8,128)(2,1)}, bf16[512,1536]{1,0:T(8,128)(2,1)}, f32[1,512]{1,0:T(1,128)}, f32[1536]{0:T(1024)}, f32[1]{0:T(128)}, /*index=5*/bf16[8,1536]{1,0:T(8,128)(2,1)}) custom-call(bf16[16,1664]{1,0:T(8,128)(2,1)S(1)} %fusion.1.refs_0_, bf16[16,1664]{1,0:T(8,128)(2,1)S(1)} %collective-permute-done.11.refs_1_, ...), custom_call_target="tpu_custom_call" | custom-call | flops 603979776 | bytes 6291456 | tf_op jit(solution)/shard_map/gradients/pallas_call | solution.py:541
  (33 shorter events, 1.4 us)
Async XLA Ops:
  0.6 9.4 %copy-start = (bf16[512,1536]{1,0:T(8,128)(2,1)S(1)}, bf16[512,1536]{1,0:T(8,128)(2,1)}, u32[]{:S(2)}) copy-start(bf16[512,1536]{1,0:T(8,128)(2,1)} %refs_7_.1) | copy-start | bytes 4718596
  4.3 10.1 %copy-start.1 = (bf16[1536,512]{1,0:T(8,128)(2,1)S(1)}, bf16[1536,512]{1,0:T(8,128)(2,1)}, u32[]{:S(2)}) copy-start(bf16[1536,512]{1,0:T(8,128)(2,1)} %refs_5_.3) | copy-start | bytes 4718596
  4.3 17.4 %copy-start.3 = (f32[512]{0:T(512)S(1)}, f32[512]{0:T(512)}, u32[]{:S(2)}) copy-start(f32[512]{0:T(512)} %param.19) | copy-start | bytes 6148
  4.3 7.3 %collective-permute-start.2 = (bf16[16,1536]{1,0:T(8,128)(2,1)S(1)}, bf16[16,1536]{1,0:T(8,128)(2,1)S(1)}, u32[]{:S(2)}, u32[]{:S(2)}) collective-permute-start(bf16[16,1536]{1,0:T(8,128)(2,1)S(1)} %features.1.refs_2_), channel_id=1, source_target_pairs={{0,12},{1,13},{2,14},{3,15},{4,8},{5,9},{6,10},{7,11},{8,4},{9,5},... | collective-permute-start | bytes 147464 | tf_op jit(solution)/shard_map/ppermute | solution.py:74
  9.4 5.0 %collective-permute-start.1 = (bf16[16,1536]{1,0:T(8,128)(2,1)S(1)}, bf16[16,1536]{1,0:T(8,128)(2,1)S(1)}, u32[]{:S(2)}, u32[]{:S(2)}) collective-permute-start(bf16[16,1536]{1,0:T(8,128)(2,1)S(1)} %features.1.refs_2_), channel_id=1, source_target_pairs={{0,8},{1,9},{2,10},{3,11},{4,12},{5,13},{6,14},{7,15},{8,0},{9,1},... | collective-permute-start | bytes 147464 | tf_op jit(solution)/shard_map/ppermute | solution.py:74
  9.4 5.0 %collective-permute-start = (bf16[16,1536]{1,0:T(8,128)(2,1)S(1)}, bf16[16,1536]{1,0:T(8,128)(2,1)S(1)}, u32[]{:S(2)}, u32[]{:S(2)}) collective-permute-start(bf16[16,1536]{1,0:T(8,128)(2,1)S(1)} %features.1.refs_2_), channel_id=1, source_target_pairs={{0,4},{1,5},{2,6},{3,7},{4,0},{5,1},{6,2},{7,3},{8,12},{9,13},{10,... | collective-permute-start | bytes 147464 | tf_op jit(solution)/shard_map/ppermute | solution.py:74
  14.5 5.8 %collective-permute-start.3 = (bf16[64,1536]{1,0:T(8,128)(2,1)S(1)}, bf16[64,1536]{1,0:T(8,128)(2,1)S(1)}, u32[]{:S(2)}, u32[]{:S(2)}) collective-permute-start(bf16[64,1536]{1,0:T(8,128)(2,1)S(1)} %join.1.refs_1_), channel_id=1, source_target_pairs={{0,2},{1,3},{2,0},{3,1},{4,6},{5,7},{6,4},{7,5},{8,10},{9,11},{10,... | collective-permute-start | bytes 589832 | tf_op jit(solution)/shard_map/ppermute | solution.py:74
  16.0 4.2 %collective-permute-start.4 = (bf16[64,1536]{1,0:T(8,128)(2,1)S(1)}, bf16[64,1536]{1,0:T(8,128)(2,1)S(1)}, u32[]{:S(2)}, u32[]{:S(2)}) collective-permute-start(bf16[64,1536]{1,0:T(8,128)(2,1)S(1)} %join.1.refs_1_), channel_id=1, source_target_pairs={{0,1},{1,0},{2,3},{3,2},{4,5},{5,4},{6,7},{7,6},{8,9},{9,8},{10,11... | collective-permute-start | bytes 589832 | tf_op jit(solution)/shard_map/ppermute | solution.py:74
  20.3 1.4 %collective-permute-start.5 = (bf16[64,1536]{1,0:T(8,128)(2,1)S(1)}, bf16[64,1536]{1,0:T(8,128)(2,1)S(1)}, u32[]{:S(2)}, u32[]{:S(2)}) collective-permute-start(bf16[64,1536]{1,0:T(8,128)(2,1)S(1)} %collective-permute-done.3.refs_2_), channel_id=1, source_target_pairs={{0,1},{1,0},{2,3},{3,2},{4,5},{5,4},{6,7},{7,6},{8,9},{9,8},{10,11... | collective-permute-start | bytes 589832 | tf_op jit(solution)/shard_map/ppermute | solution.py:74
  21.7 2.4 %copy-start.2 = (f32[1536]{0:T(1024)S(1)}, f32[1536]{0:T(1024)}, u32[]{:S(2)}) copy-start(f32[1536]{0:T(1024)} %dec_bias.1) | copy-start | bytes 18436
  23.9 1.5 %collective-permute-start.6 = (bf16[64,1664]{1,0:T(8,128)(2,1)S(1)}, bf16[64,1664]{1,0:T(8,128)(2,1)S(1)}, u32[]{:S(2)}, u32[]{:S(2)}) collective-permute-start(bf16[64,1664]{1,0:T(8,128)(2,1)S(1)} %get-tuple-element.30), channel_id=1, source_target_pairs={{0,1},{1,0},{2,3},{3,2},{4,5},{5,4},{6,7},{7,6},{8,9},{9,8},{10,11... | collective-permute-start | bytes 638984 | tf_op jit(solution)/shard_map/ppermute | solution.py:74
  25.6 6.6 %collective-permute-start.9 = (bf16[16,1664]{1,0:T(8,128)(2,1)S(1)}, bf16[16,1664]{1,0:T(8,128)(2,1)S(1)}, u32[]{:S(2)}, u32[]{:S(2)}) collective-permute-start(bf16[16,1664]{1,0:T(8,128)(2,1)S(1)} %get-tuple-element.42), channel_id=1, source_target_pairs={{0,12},{1,13},{2,14},{3,15},{4,8},{5,9},{6,10},{7,11},{8,4},{9,5},... | collective-permute-start | bytes 159752 | tf_op jit(solution)/shard_map/ppermute | solution.py:74
  27.6 6.1 %collective-permute-start.8 = (bf16[16,1664]{1,0:T(8,128)(2,1)S(1)}, bf16[16,1664]{1,0:T(8,128)(2,1)S(1)}, u32[]{:S(2)}, u32[]{:S(2)}) collective-permute-start(bf16[16,1664]{1,0:T(8,128)(2,1)S(1)} %get-tuple-element.43), channel_id=1, source_target_pairs={{0,8},{1,9},{2,10},{3,11},{4,12},{5,13},{6,14},{7,15},{8,0},{9,1},... | collective-permute-start | bytes 159752 | tf_op jit(solution)/shard_map/ppermute | solution.py:74
  27.8 6.0 %collective-permute-start.7 = (bf16[16,1664]{1,0:T(8,128)(2,1)S(1)}, bf16[16,1664]{1,0:T(8,128)(2,1)S(1)}, u32[]{:S(2)}, u32[]{:S(2)}) collective-permute-start(bf16[16,1664]{1,0:T(8,128)(2,1)S(1)} %get-tuple-element.44), channel_id=1, source_target_pairs={{0,4},{1,5},{2,6},{3,7},{4,0},{5,1},{6,2},{7,3},{8,12},{9,13},{10,... | collective-permute-start | bytes 159752 | tf_op jit(solution)/shard_map/ppermute | solution.py:74
  33.8 4.2 %collective-permute-start.10 = (bf16[16,1664]{1,0:T(8,128)(2,1)S(1)}, bf16[16,1664]{1,0:T(8,128)(2,1)S(1)}, u32[]{:S(2)}, u32[]{:S(2)}) collective-permute-start(bf16[16,1664]{1,0:T(8,128)(2,1)S(1)} %sum.1), channel_id=1, source_target_pairs={{0,2},{1,3},{2,0},{3,1},{4,6},{5,7},{6,4},{7,5},{8,10},{9,11},{10,... | collective-permute-start | bytes 159752 | tf_op jit(solution)/shard_map/ppermute | solution.py:74
  38.0 6.5 %collective-permute-start.13 = (bf16[16,1664]{1,0:T(8,128)(2,1)S(1)}, bf16[16,1664]{1,0:T(8,128)(2,1)S(1)}, u32[]{:S(2)}, u32[]{:S(2)}) collective-permute-start(bf16[16,1664]{1,0:T(8,128)(2,1)S(1)} %fusion.1.refs_0_), channel_id=1, source_target_pairs={{0,12},{1,13},{2,14},{3,15},{4,8},{5,9},{6,10},{7,11},{8,4},{9,5},... | collective-permute-start | bytes 159752 | tf_op jit(solution)/shard_map/ppermute | solution.py:74
  40.4 5.3 %collective-permute-start.12 = (bf16[16,1664]{1,0:T(8,128)(2,1)S(1)}, bf16[16,1664]{1,0:T(8,128)(2,1)S(1)}, u32[]{:S(2)}, u32[]{:S(2)}) collective-permute-start(bf16[16,1664]{1,0:T(8,128)(2,1)S(1)} %fusion.1.refs_0_), channel_id=1, source_target_pairs={{0,8},{1,9},{2,10},{3,11},{4,12},{5,13},{6,14},{7,15},{8,0},{9,1},... | collective-permute-start | bytes 159752 | tf_op jit(solution)/shard_map/ppermute | solution.py:74
  40.4 5.3 %collective-permute-start.11 = (bf16[16,1664]{1,0:T(8,128)(2,1)S(1)}, bf16[16,1664]{1,0:T(8,128)(2,1)S(1)}, u32[]{:S(2)}, u32[]{:S(2)}) collective-permute-start(bf16[16,1664]{1,0:T(8,128)(2,1)S(1)} %fusion.1.refs_0_), channel_id=1, source_target_pairs={{0,4},{1,5},{2,6},{3,7},{4,0},{5,1},{6,2},{7,3},{8,12},{9,13},{10,... | collective-permute-start | bytes 159752 | tf_op jit(solution)/shard_map/ppermute | solution.py:74
  42.5 3.7 %collective-permute-start.14 = (bf16[16,1664]{1,0:T(8,128)(2,1)S(1)}, bf16[16,1664]{1,0:T(8,128)(2,1)S(1)}, u32[]{:S(2)}, u32[]{:S(2)}) collective-permute-start(bf16[16,1664]{1,0:T(8,128)(2,1)S(1)} %fusion.1.refs_0_), channel_id=1, source_target_pairs={{0,1},{1,0},{2,3},{3,2},{4,5},{5,4},{6,7},{7,6},{8,9},{9,8},{10,11... | collective-permute-start | bytes 159752 | tf_op jit(solution)/shard_map/ppermute | solution.py:74
  44.5 1.7 %collective-permute-start.17 = (bf16[16,1664]{1,0:T(8,128)(2,1)S(1)}, bf16[16,1664]{1,0:T(8,128)(2,1)S(1)}, u32[]{:S(2)}, u32[]{:S(2)}) collective-permute-start(bf16[16,1664]{1,0:T(8,128)(2,1)S(1)} %collective-permute-done.13.refs_3_), channel_id=1, source_target_pairs={{0,1},{1,0},{2,3},{3,2},{4,5},{5,4},{6,7},{7,6},{8,9},{9,8},{10,11... | collective-permute-start | bytes 159752 | tf_op jit(solution)/shard_map/ppermute | solution.py:74
  45.7 1.2 %collective-permute-start.16 = (bf16[16,1664]{1,0:T(8,128)(2,1)S(1)}, bf16[16,1664]{1,0:T(8,128)(2,1)S(1)}, u32[]{:S(2)}, u32[]{:S(2)}) collective-permute-start(bf16[16,1664]{1,0:T(8,128)(2,1)S(1)} %collective-permute-done.12.refs_2_), channel_id=1, source_target_pairs={{0,1},{1,0},{2,3},{3,2},{4,5},{5,4},{6,7},{7,6},{8,9},{9,8},{10,11... | collective-permute-start | bytes 159752 | tf_op jit(solution)/shard_map/ppermute | solution.py:74
  45.7 1.4 %collective-permute-start.15 = (bf16[16,1664]{1,0:T(8,128)(2,1)S(1)}, bf16[16,1664]{1,0:T(8,128)(2,1)S(1)}, u32[]{:S(2)}, u32[]{:S(2)}) collective-permute-start(bf16[16,1664]{1,0:T(8,128)(2,1)S(1)} %collective-permute-done.11.refs_1_), channel_id=1, source_target_pairs={{0,1},{1,0},{2,3},{3,2},{4,5},{5,4},{6,7},{7,6},{8,9},{9,8},{10,11... | collective-permute-start | bytes 159752 | tf_op jit(solution)/shard_map/ppermute | solution.py:74

commit v11 on v10

--- a/solution.py
+++ b/solution.py
@@ -14,7 +14,6 @@
 PINNED_BYTES = 24 << 20
 PINNED_TOKENS = 256
 GROUP_ROWS = 256
-DEC_PARTS = 3
 
 sparsity = 0.5
 epsilon = 1e-05
@@ -197,32 +196,28 @@
         at += ref.shape[0]
 
 
-def norms_kernel(dec, norms, row):
-    latents, feature = dec.shape
+def column_norms(dec):
     channels = 512
-    spot = iota((latents, LANES), 1)
-    packed = jnp.zeros((latents, LANES), F32)
-    total = jnp.zeros((latents, 1), F32)
-    for c in range(feature // channels):
+    columns = []
+    for c in range(dec.shape[1] // channels):
         block = dec[:, c * channels : (c + 1) * channels].astype(F32)
-        norm = jnp.sqrt(jnp.sum(block * block, axis=1, keepdims=True) + 1e-06)
-        total = total + norm
-        packed = jnp.where(spot == c, norm, packed)
-    norms[...] = packed
-    row[...] = jnp.broadcast_to(total, (latents, LANES)).T[:8]
+        columns.append(jnp.sqrt(jnp.sum(block * block, axis=1, keepdims=True) + 1e-06))
+    return columns
+
+
+def norms_kernel(dec, row):
+    total = sum(column_norms(dec))
+    row[...] = jnp.broadcast_to(total, (total.shape[0], LANES)).T[:8]
 
 
 def encode_kernel(count, outer, inner, slots, frames, *refs):
     me_ref = refs[0]
     pieces = refs[1 : 1 + count]
-    enc, bias, dec_hbm, weights_sum = refs[1 + count : 5 + count]
-    send, inputs_out, latent_out, dec, sems = refs[5 + count :]
-    part_width = dec.shape[1] // DEC_PARTS
-    fetches = []
-    for i in range(DEC_PARTS):
-        at = (slice(None), pl.ds(i * part_width, part_width))
-        fetches.append(pltpu.make_async_copy(dec_hbm.at[at], dec.at[at], sems.at[i]))
-        fetches[-1].start()
+    enc, enc_hbm, bias, dec, weights_sum = refs[1 + count : 6 + count]
+    send, inputs_out, latent_out, enc_late, sem = refs[6 + count :]
+    early = enc.shape[0]
+    fetch = pltpu.make_async_copy(enc_hbm.at[pl.ds(early, enc_late.shape[0])], enc_late, sem)
+    fetch.start()
     me = me_ref[0]
     step = 2 * inner
     tokens, feature = inputs_out.shape
@@ -276,15 +271,14 @@
         total = total + jnp.dot(pick, block, preferred_element_type=F32)
     inputs = total.astype(BF16)
     inputs_out[...] = inputs
-    latent = jnp.maximum(jnp.dot(inputs, enc[...], preferred_element_type=F32) + bias[...], 0.0)
+    preact = jnp.dot(inputs[:, :early], enc[...], preferred_element_type=F32)
+    fetch.wait()
+    preact = preact + jnp.dot(inputs[:, early:], enc_late[...], preferred_element_type=F32)
+    latent = jnp.maximum(preact + bias[...], 0.0)
     latent_out[...] = latent
     half = tokens // 2
     rounded = latent[half:].astype(BF16)
-    for i in range(DEC_PARTS):
-        fetches[i].wait()
-        at = slice(i * part_width, (i + 1) * part_width)
-        part = jnp.dot(rounded, dec[:, at], preferred_element_type=F32)
-        send[:, at] = part.astype(BF16)
+    send[:, :feature] = jnp.dot(rounded, dec[...], preferred_element_type=F32).astype(BF16)
     send[:, feature:] = lane_sums(latent[half:] * weights_sum[0:1, :]).astype(BF16)
 
 
@@ -305,12 +299,16 @@
     shift[:, feature:] = jnp.zeros((chunk, EXTRA), F32)
 
 
-def turn_kernel(inputs, latent, norms, inputs_t, latent_t, scale):
+def turn_kernel(inputs, latent, dec, inputs_t, latent_t, scale):
     inputs_t[...] = inputs[...].astype(F32).T.astype(BF16)
     turned = latent[...].T
     latent_t[...] = (2.0 * turned).astype(BF16)
     activity = jnp.sum(turned, axis=1, keepdims=True)
-    scale[...] = (sparsity * activity) / jnp.maximum(norms[...], 1e-30)
+    spot = iota(scale.shape, 1)
+    packed = jnp.zeros(scale.shape, F32)
+    for c, norm in enumerate(column_norms(dec)):
+        packed = jnp.where(spot == c, (sparsity * activity) / norm, packed)
+    scale[...] = packed
 
 
 def sum_kernel(*refs):
@@ -404,7 +402,8 @@
         return pltpu.with_memory_space_constraint(value, pltpu.HBM)
 
     kernels = conv_first.transpose(1, 0, 2)
-    encoder = near(enc_weight)
+    early = 2 * feature // 3
+    encoder = near(enc_weight[:early])
     decoder = near(dec_weight)
 
     packed = call(
@@ -433,12 +432,12 @@
         ]
     )
 
-    norms, weights_sum = call(
+    weights_sum = call(
         norms_kernel,
         "norms",
-        (fast((latents, LANES), F32), fast((8, latents), F32)),
+        fast((8, latents), F32),
         [vmem()],
-        (vmem(), vmem()),
+        vmem(),
         flops=4 * dec_weight.size,
         moved=2 * dec_weight.size,
     )(decoder)
@@ -452,7 +451,7 @@
             [pl.BlockSpec(memory_space=pl.ANY)] * 2 + [vmem()] * outer,
             vmem(),
             moved=4 * outer * slots * frames * feature,
-        )(near(norms), encoder, *[near(block) for block in blocks])
+        )(near(weights_sum), encoder, *[near(block) for block in blocks])
     ]
     bit = 2
     while bit < step:
@@ -466,30 +465,28 @@
     def encode(*refs):
         encode_kernel(len(pieces), outer, inner, slots, frames, *refs)
 
-    send, inputs, latent, decoder = call(
+    send, inputs, latent = call(
         encode,
         "encode",
-        (
-            fast((half, wide), BF16),
-            fast((tokens, feature), BF16),
-            fast((tokens, latents), F32),
-            fast(dec_weight.shape, BF16),
-        ),
-        [smem()] + [vmem()] * (len(pieces) + 2) + [pl.BlockSpec(memory_space=pl.ANY), vmem()],
-        (vmem(),) * 4,
-        [pltpu.SemaphoreType.DMA((DEC_PARTS,))],
+        (fast((half, wide), BF16), fast((tokens, feature), BF16), fast((tokens, latents), F32)),
+        [smem()]
+        + [vmem()] * (len(pieces) + 1)
+        + [pl.BlockSpec(memory_space=pl.ANY)]
+        + [vmem()] * 3,
+        (vmem(),) * 3,
+        [pltpu.VMEM((feature - early, latents), BF16), pltpu.SemaphoreType.DMA],
         flops=3 * tokens * feature * latents,
         moved=4 * dec_weight.size,
     )(
         position,
         *[near(piece) for piece in pieces],
         encoder,
+        far(enc_weight),
         enc_bias.reshape(1, latents),
-        far(dec_weight),
+        decoder,
         near(weights_sum),
     )
     received = exchange(send, 1)
-    decoder = near(decoder)
     own, shift = call(
         own_kernel,
         "own",
@@ -508,7 +505,7 @@
         (vmem(),) * 3,
         flops=2 * tokens * feature,
         moved=4 * tokens * feature,
-    )(near(inputs), near(latent), near(norms))
+    )(near(inputs), near(latent), decoder)
 
     part = own + received.astype(F32)
     small = part.astype(BF16)

time: 50.6 us -> 50.4 us (level)
  waiting for transfers between devices: 20.3 us -> 19.7 us
    ppermute x18, waiting for transfers between devices: 20.3 us -> 19.7 us  [exchange(): return lax.ppermute(value, 'utt', [(i, i ^ bit) for i in range(devices)])]
    pallas_call x1, Pallas kernels: 0.33 us -> 0.87 us  [shards(): call(turn_kernel, 'turn', (fast((feature, tokens), BF16), fast((latents,...]
  transfers between devices with their start and end apart: 18 -> 18, of which waited for: 12 -> 12; matrix products, arithmetic and copies ran while one was open for 0% -> 0% of each run, Pallas kernels for 3% -> 4%
where the time goes in v11:
time: 50.4 us; the launch traced here: 50.3 us
  waiting for transfers between devices  19.7 us (39%)
  starting transfers between devices  18.6 us (37%)
  Pallas kernels  11 us (22%)
  between operations  0.75 us (1%)
    ppermute x18, waiting for transfers between devices, exchange(): return lax.ppermute(value, 'utt', [(i, i ^ bit) for i in range(devices)])  19.7 us
    ppermute x18, starting transfers between devices, exchange(): return lax.ppermute(value, 'utt', [(i, i ^ bit) for i in range(devices)])  18.6 us
    pallas_call x1, Pallas kernels, shards(): call(features_kernel, 'features', fast((slots * frames, feature), BF16),...  3.64 us
    pallas_call x1, Pallas kernels, shards(): call(gradients, 'gradients', (shape((feature, latents), BF16), shape((lat...  3.32 us
    pallas_call x1, Pallas kernels, shards(): call(encode, 'encode', (fast((half, wide), BF16), fast((tokens, feature),...  2.11 us
  transfers between devices with their start and end apart: 18, of which 12 were waited for; matrix products, arithmetic and copies ran while one was open for 0% of the time, Pallas kernels for 4%

profile of v11, /device:TPU:0, one launch (start us, length us, event | category | flops | bytes accessed | tf_op | source)
XLA Modules:
  0.0 50.3 jit_solution(10441858418618344499)
XLA Ops:
  0.6 3.6 %features.1.refs_2_ = bf16[16,1536]{1,0:T(8,128)(2,1)S(1)} custom-call(s32[2]{0:T(128)} %refs_0_.1, s32[2]{0:T(128)} %refs_1_.1, f32[2,90]{1,0:T(2,128)} %refs_2_.1, f32[10,3,512]{2,1,0:T(4,128)} %bitcast.14, f32[3,2,512]{2,1,0:T(2,128)} %refs_4_.1, f32[3,2,512]{2,1,0:T(2,128)} %refs_5_.1, bf16[3,1536,512]{2,1,0:T(8,128)(2,1)} %refs_6_.2), custom_call_target="tpu_custom_call" | custom-call | flops 75497472 | bytes 4718592 | tf_op jit(solution)/shard_map/features/pallas_call | solution.py:409
  4.3 5.1 %collective-permute-start.2 = (bf16[16,1536]{1,0:T(8,128)(2,1)S(1)}, bf16[16,1536]{1,0:T(8,128)(2,1)S(1)}, u32[]{:S(2)}, u32[]{:S(2)}) collective-permute-start(bf16[16,1536]{1,0:T(8,128)(2,1)S(1)} %features.1.refs_2_), channel_id=1, source_target_pairs={{0,12},{1,13},{2,14},{3,15},{4,8},{5,9},{6,10},{7,11},{8,4},{9,5},... | collective-permute-start | bytes 147464 | tf_op jit(solution)/shard_map/ppermute | solution.py:73
  9.4 0.6 %collective-permute-start = (bf16[16,1536]{1,0:T(8,128)(2,1)S(1)}, bf16[16,1536]{1,0:T(8,128)(2,1)S(1)}, u32[]{:S(2)}, u32[]{:S(2)}) collective-permute-start(bf16[16,1536]{1,0:T(8,128)(2,1)S(1)} %features.1.refs_2_), channel_id=1, source_target_pairs={{0,4},{1,5},{2,6},{3,7},{4,0},{5,1},{6,2},{7,3},{8,12},{9,13},{10,... | collective-permute-start | bytes 147464 | tf_op jit(solution)/shard_map/ppermute | solution.py:73
  10.2 0.7 %norms.1.refs_0_.refs_9_.weights_sum = f32[8,512]{1,0:T(8,128)S(1)} custom-call(bf16[512,1536]{1,0:T(8,128)(2,1)S(1)} %copy-done), custom_call_target="tpu_custom_call" | custom-call | flops 3145728 | bytes 1572864 | tf_op jit(solution)/shard_map/norms/pallas_call | solution.py:435
  10.8 0.8 %collective-permute-done.2.refs_5_ = bf16[16,1536]{1,0:T(8,128)(2,1)S(1)} collective-permute-done((bf16[16,1536]{1,0:T(8,128)(2,1)S(1)}, bf16[16,1536]{1,0:T(8,128)(2,1)S(1)}, u32[]{:S(2)}, u32[]{:S(2)}) %collective-permute-start.2) | collective-permute-done | bytes 49184 | tf_op jit(solution)/shard_map/ppermute | solution.py:73
  11.7 2.8 %collective-permute-done.1.refs_4_ = bf16[16,1536]{1,0:T(8,128)(2,1)S(1)} collective-permute-done((bf16[16,1536]{1,0:T(8,128)(2,1)S(1)}, bf16[16,1536]{1,0:T(8,128)(2,1)S(1)}, u32[]{:S(2)}, u32[]{:S(2)}) %collective-permute-start.1) | collective-permute-done | bytes 49184 | tf_op jit(solution)/shard_map/ppermute | solution.py:73
  14.4 1.6 %collective-permute-start.3 = (bf16[64,1536]{1,0:T(8,128)(2,1)S(1)}, bf16[64,1536]{1,0:T(8,128)(2,1)S(1)}, u32[]{:S(2)}, u32[]{:S(2)}) collective-permute-start(bf16[64,1536]{1,0:T(8,128)(2,1)S(1)} %join.1.refs_1_), channel_id=1, source_target_pairs={{0,2},{1,3},{2,0},{3,1},{4,6},{5,7},{6,4},{7,5},{8,10},{9,11},{10,... | collective-permute-start | bytes 589832 | tf_op jit(solution)/shard_map/ppermute | solution.py:73
  16.0 4.2 %collective-permute-done.3.refs_2_ = bf16[64,1536]{1,0:T(8,128)(2,1)S(1)} collective-permute-done((bf16[64,1536]{1,0:T(8,128)(2,1)S(1)}, bf16[64,1536]{1,0:T(8,128)(2,1)S(1)}, u32[]{:S(2)}, u32[]{:S(2)}) %collective-permute-start.3) | collective-permute-done | bytes 196640 | tf_op jit(solution)/shard_map/ppermute | solution.py:73
  20.3 1.4 %collective-permute-done.5.refs_4_ = bf16[64,1536]{1,0:T(8,128)(2,1)S(1)} collective-permute-done((bf16[64,1536]{1,0:T(8,128)(2,1)S(1)}, bf16[64,1536]{1,0:T(8,128)(2,1)S(1)}, u32[]{:S(2)}, u32[]{:S(2)}) %collective-permute-start.5) | collective-permute-done | bytes 196640 | tf_op jit(solution)/shard_map/ppermute | solution.py:73
  21.7 2.1 %encode.1 = (bf16[64,1664]{1,0:T(8,128)(2,1)S(1)}, bf16[128,1536]{1,0:T(8,128)(2,1)S(1)}, f32[128,512]{1,0:T(8,128)S(1)}) custom-call(s32[1]{0:T(128)} %bitcast.refs_0_, bf16[64,1536]{1,0:T(8,128)(2,1)S(1)} %join.1.refs_1_, bf16[64,1536]{1,0:T(8,128)(2,1)S(1)} %collective-permute-done.3.refs_2_, bf16[64,1536]{1,0:T(8,128)(2,1)S(1)} %collective-permute-done.4.refs_3_, ...), custom_call_target="tpu_custom_call" | custom-call | flops 301989888 | bytes 3145728 | tf_op jit(solution)/shard_map/encode/pallas_call | solution.py:468
  24.4 0.9 %collective-permute-done.6 = bf16[64,1664]{1,0:T(8,128)(2,1)S(1)} collective-permute-done((bf16[64,1664]{1,0:T(8,128)(2,1)S(1)}, bf16[64,1664]{1,0:T(8,128)(2,1)S(1)}, u32[]{:S(2)}, u32[]{:S(2)}) %collective-permute-start.6) | collective-permute-done | bytes 213024 | tf_op jit(solution)/shard_map/ppermute | solution.py:73
  25.4 2.1 %collective-permute-start.9 = (bf16[16,1664]{1,0:T(8,128)(2,1)S(1)}, bf16[16,1664]{1,0:T(8,128)(2,1)S(1)}, u32[]{:S(2)}, u32[]{:S(2)}) collective-permute-start(bf16[16,1664]{1,0:T(8,128)(2,1)S(1)} %get-tuple-element.36), channel_id=1, source_target_pairs={{0,12},{1,13},{2,14},{3,15},{4,8},{5,9},{6,10},{7,11},{8,4},{9,5},... | collective-permute-start | bytes 159752 | tf_op jit(solution)/shard_map/ppermute | solution.py:73
  27.7 2.2 %collective-permute-start.7 = (bf16[16,1664]{1,0:T(8,128)(2,1)S(1)}, bf16[16,1664]{1,0:T(8,128)(2,1)S(1)}, u32[]{:S(2)}, u32[]{:S(2)}) collective-permute-start(bf16[16,1664]{1,0:T(8,128)(2,1)S(1)} %get-tuple-element.38), channel_id=1, source_target_pairs={{0,4},{1,5},{2,6},{3,7},{4,0},{5,1},{6,2},{7,3},{8,12},{9,13},{10,... | collective-permute-start | bytes 159752 | tf_op jit(solution)/shard_map/ppermute | solution.py:73
  29.9 0.9 %turn.1 = (bf16[1536,128]{1,0:T(8,128)(2,1)S(1)}, bf16[512,128]{1,0:T(8,128)(2,1)S(1)}, f32[512,128]{1,0:T(8,128)S(1)}) custom-call(bf16[128,1536]{1,0:T(8,128)(2,1)S(1)} %get-tuple-element.20.inputs, f32[128,512]{1,0:T(8,128)S(1)} %get-tuple-element.21.latent.refs_12_, bf16[512,1536]{1,0:T(8,128)(2,1)S(1)} %copy-done), custom_call_target="tpu_custom_call" | custom-call | flops 393216 | bytes 786432 | tf_op jit(solution)/shard_map/turn/pallas_call | solution.py:500
  30.8 1.3 %collective-permute-done.9.refs_4_ = bf16[16,1664]{1,0:T(8,128)(2,1)S(1)} collective-permute-done((bf16[16,1664]{1,0:T(8,128)(2,1)S(1)}, bf16[16,1664]{1,0:T(8,128)(2,1)S(1)}, u32[]{:S(2)}, u32[]{:S(2)}) %collective-permute-start.9) | collective-permute-done | bytes 53280 | tf_op jit(solution)/shard_map/ppermute | solution.py:73
  32.0 1.6 %collective-permute-done.8.refs_3_ = bf16[16,1664]{1,0:T(8,128)(2,1)S(1)} collective-permute-done((bf16[16,1664]{1,0:T(8,128)(2,1)S(1)}, bf16[16,1664]{1,0:T(8,128)(2,1)S(1)}, u32[]{:S(2)}, u32[]{:S(2)}) %collective-permute-start.8) | collective-permute-done | bytes 53280 | tf_op jit(solution)/shard_map/ppermute | solution.py:73
  33.7 1.6 %collective-permute-start.10 = (bf16[16,1664]{1,0:T(8,128)(2,1)S(1)}, bf16[16,1664]{1,0:T(8,128)(2,1)S(1)}, u32[]{:S(2)}, u32[]{:S(2)}) collective-permute-start(bf16[16,1664]{1,0:T(8,128)(2,1)S(1)} %sum.1), channel_id=1, source_target_pairs={{0,2},{1,3},{2,0},{3,1},{4,6},{5,7},{6,4},{7,5},{8,10},{9,11},{10,... | collective-permute-start | bytes 159752 | tf_op jit(solution)/shard_map/ppermute | solution.py:73
  35.3 2.6 %collective-permute-done.10 = bf16[16,1664]{1,0:T(8,128)(2,1)S(1)} collective-permute-done((bf16[16,1664]{1,0:T(8,128)(2,1)S(1)}, bf16[16,1664]{1,0:T(8,128)(2,1)S(1)}, u32[]{:S(2)}, u32[]{:S(2)}) %collective-permute-start.10) | collective-permute-done | bytes 53280 | tf_op jit(solution)/shard_map/ppermute | solution.py:73
  37.9 2.3 %collective-permute-start.13 = (bf16[16,1664]{1,0:T(8,128)(2,1)S(1)}, bf16[16,1664]{1,0:T(8,128)(2,1)S(1)}, u32[]{:S(2)}, u32[]{:S(2)}) collective-permute-start(bf16[16,1664]{1,0:T(8,128)(2,1)S(1)} %fusion.1.refs_0_), channel_id=1, source_target_pairs={{0,12},{1,13},{2,14},{3,15},{4,8},{5,9},{6,10},{7,11},{8,4},{9,5},... | collective-permute-start | bytes 159752 | tf_op jit(solution)/shard_map/ppermute | solution.py:73
  40.2 2.1 %collective-permute-start.11 = (bf16[16,1664]{1,0:T(8,128)(2,1)S(1)}, bf16[16,1664]{1,0:T(8,128)(2,1)S(1)}, u32[]{:S(2)}, u32[]{:S(2)}) collective-permute-start(bf16[16,1664]{1,0:T(8,128)(2,1)S(1)} %fusion.1.refs_0_), channel_id=1, source_target_pairs={{0,4},{1,5},{2,6},{3,7},{4,0},{5,1},{6,2},{7,3},{8,12},{9,13},{10,... | collective-permute-start | bytes 159752 | tf_op jit(solution)/shard_map/ppermute | solution.py:73
  42.4 2.0 %collective-permute-done.13.refs_3_ = bf16[16,1664]{1,0:T(8,128)(2,1)S(1)} collective-permute-done((bf16[16,1664]{1,0:T(8,128)(2,1)S(1)}, bf16[16,1664]{1,0:T(8,128)(2,1)S(1)}, u32[]{:S(2)}, u32[]{:S(2)}) %collective-permute-start.13) | collective-permute-done | bytes 53280 | tf_op jit(solution)/shard_map/ppermute | solution.py:73
  44.4 1.1 %collective-permute-done.12.refs_2_ = bf16[16,1664]{1,0:T(8,128)(2,1)S(1)} collective-permute-done((bf16[16,1664]{1,0:T(8,128)(2,1)S(1)}, bf16[16,1664]{1,0:T(8,128)(2,1)S(1)}, u32[]{:S(2)}, u32[]{:S(2)}) %collective-permute-start.12) | collective-permute-done | bytes 53280 | tf_op jit(solution)/shard_map/ppermute | solution.py:73
  46.1 0.7 %collective-permute-done.16.refs_6_ = bf16[16,1664]{1,0:T(8,128)(2,1)S(1)} collective-permute-done((bf16[16,1664]{1,0:T(8,128)(2,1)S(1)}, bf16[16,1664]{1,0:T(8,128)(2,1)S(1)}, u32[]{:S(2)}, u32[]{:S(2)}) %collective-permute-start.16) | collective-permute-done | bytes 53280 | tf_op jit(solution)/shard_map/ppermute | solution.py:73
  46.9 3.3 %gradients.1 = (bf16[1536,512]{1,0:T(8,128)(2,1)}, bf16[512,1536]{1,0:T(8,128)(2,1)}, f32[1,512]{1,0:T(1,128)}, f32[1536]{0:T(1024)}, f32[1]{0:T(128)}, /*index=5*/bf16[8,1536]{1,0:T(8,128)(2,1)}) custom-call(bf16[16,1664]{1,0:T(8,128)(2,1)S(1)} %fusion.1.refs_0_, bf16[16,1664]{1,0:T(8,128)(2,1)S(1)} %collective-permute-done.11.refs_1_, ...), custom_call_target="tpu_custom_call" | custom-call | flops 603979776 | bytes 6291456 | tf_op jit(solution)/shard_map/gradients/pallas_call | solution.py:538
  (34 shorter events, 1.7 us)
Async XLA Ops:
  0.6 9.4 %copy-start.3 = (bf16[1536,512]{1,0:T(8,128)(2,1)S(1)}, bf16[1536,512]{1,0:T(8,128)(2,1)}, u32[]{:S(2)}) copy-start(bf16[1536,512]{1,0:T(8,128)(2,1)} %refs_6_.3) | copy-start | bytes 4718596
  4.3 5.8 %copy-start = (bf16[512,1536]{1,0:T(8,128)(2,1)S(1)}, bf16[512,1536]{1,0:T(8,128)(2,1)}, u32[]{:S(2)}) copy-start(bf16[512,1536]{1,0:T(8,128)(2,1)} %refs_8_.3) | copy-start | bytes 4718596
  4.3 7.3 %collective-permute-start.2 = (bf16[16,1536]{1,0:T(8,128)(2,1)S(1)}, bf16[16,1536]{1,0:T(8,128)(2,1)S(1)}, u32[]{:S(2)}, u32[]{:S(2)}) collective-permute-start(bf16[16,1536]{1,0:T(8,128)(2,1)S(1)} %features.1.refs_2_), channel_id=1, source_target_pairs={{0,12},{1,13},{2,14},{3,15},{4,8},{5,9},{6,10},{7,11},{8,4},{9,5},... | collective-permute-start | bytes 147464 | tf_op jit(solution)/shard_map/ppermute | solution.py:73
  9.4 5.0 %collective-permute-start.1 = (bf16[16,1536]{1,0:T(8,128)(2,1)S(1)}, bf16[16,1536]{1,0:T(8,128)(2,1)S(1)}, u32[]{:S(2)}, u32[]{:S(2)}) collective-permute-start(bf16[16,1536]{1,0:T(8,128)(2,1)S(1)} %features.1.refs_2_), channel_id=1, source_target_pairs={{0,8},{1,9},{2,10},{3,11},{4,12},{5,13},{6,14},{7,15},{8,0},{9,1},... | collective-permute-start | bytes 147464 | tf_op jit(solution)/shard_map/ppermute | solution.py:73
  9.4 5.0 %collective-permute-start = (bf16[16,1536]{1,0:T(8,128)(2,1)S(1)}, bf16[16,1536]{1,0:T(8,128)(2,1)S(1)}, u32[]{:S(2)}, u32[]{:S(2)}) collective-permute-start(bf16[16,1536]{1,0:T(8,128)(2,1)S(1)} %features.1.refs_2_), channel_id=1, source_target_pairs={{0,4},{1,5},{2,6},{3,7},{4,0},{5,1},{6,2},{7,3},{8,12},{9,13},{10,... | collective-permute-start | bytes 147464 | tf_op jit(solution)/shard_map/ppermute | solution.py:73
  10.2 11.5 %copy-start.2 = (f32[512]{0:T(512)S(1)}, f32[512]{0:T(512)}, u32[]{:S(2)}) copy-start(f32[512]{0:T(512)} %param.19) | copy-start | bytes 6148
  14.4 5.8 %collective-permute-start.3 = (bf16[64,1536]{1,0:T(8,128)(2,1)S(1)}, bf16[64,1536]{1,0:T(8,128)(2,1)S(1)}, u32[]{:S(2)}, u32[]{:S(2)}) collective-permute-start(bf16[64,1536]{1,0:T(8,128)(2,1)S(1)} %join.1.refs_1_), channel_id=1, source_target_pairs={{0,2},{1,3},{2,0},{3,1},{4,6},{5,7},{6,4},{7,5},{8,10},{9,11},{10,... | collective-permute-start | bytes 589832 | tf_op jit(solution)/shard_map/ppermute | solution.py:73
  16.0 4.2 %collective-permute-start.4 = (bf16[64,1536]{1,0:T(8,128)(2,1)S(1)}, bf16[64,1536]{1,0:T(8,128)(2,1)S(1)}, u32[]{:S(2)}, u32[]{:S(2)}) collective-permute-start(bf16[64,1536]{1,0:T(8,128)(2,1)S(1)} %join.1.refs_1_), channel_id=1, source_target_pairs={{0,1},{1,0},{2,3},{3,2},{4,5},{5,4},{6,7},{7,6},{8,9},{9,8},{10,11... | collective-permute-start | bytes 589832 | tf_op jit(solution)/shard_map/ppermute | solution.py:73
  20.3 1.4 %collective-permute-start.5 = (bf16[64,1536]{1,0:T(8,128)(2,1)S(1)}, bf16[64,1536]{1,0:T(8,128)(2,1)S(1)}, u32[]{:S(2)}, u32[]{:S(2)}) collective-permute-start(bf16[64,1536]{1,0:T(8,128)(2,1)S(1)} %collective-permute-done.3.refs_2_), channel_id=1, source_target_pairs={{0,1},{1,0},{2,3},{3,2},{4,5},{5,4},{6,7},{7,6},{8,9},{9,8},{10,11... | collective-permute-start | bytes 589832 | tf_op jit(solution)/shard_map/ppermute | solution.py:73
  21.7 2.3 %copy-start.1 = (f32[1536]{0:T(1024)S(1)}, f32[1536]{0:T(1024)}, u32[]{:S(2)}) copy-start(f32[1536]{0:T(1024)} %dec_bias.1) | copy-start | bytes 18436
  23.8 1.5 %collective-permute-start.6 = (bf16[64,1664]{1,0:T(8,128)(2,1)S(1)}, bf16[64,1664]{1,0:T(8,128)(2,1)S(1)}, u32[]{:S(2)}, u32[]{:S(2)}) collective-permute-start(bf16[64,1664]{1,0:T(8,128)(2,1)S(1)} %get-tuple-element.24), channel_id=1, source_target_pairs={{0,1},{1,0},{2,3},{3,2},{4,5},{5,4},{6,7},{7,6},{8,9},{9,8},{10,11... | collective-permute-start | bytes 638984 | tf_op jit(solution)/shard_map/ppermute | solution.py:73
  25.4 6.6 %collective-permute-start.9 = (bf16[16,1664]{1,0:T(8,128)(2,1)S(1)}, bf16[16,1664]{1,0:T(8,128)(2,1)S(1)}, u32[]{:S(2)}, u32[]{:S(2)}) collective-permute-start(bf16[16,1664]{1,0:T(8,128)(2,1)S(1)} %get-tuple-element.36), channel_id=1, source_target_pairs={{0,12},{1,13},{2,14},{3,15},{4,8},{5,9},{6,10},{7,11},{8,4},{9,5},... | collective-permute-start | bytes 159752 | tf_op jit(solution)/shard_map/ppermute | solution.py:73
  27.5 6.1 %collective-permute-start.8 = (bf16[16,1664]{1,0:T(8,128)(2,1)S(1)}, bf16[16,1664]{1,0:T(8,128)(2,1)S(1)}, u32[]{:S(2)}, u32[]{:S(2)}) collective-permute-start(bf16[16,1664]{1,0:T(8,128)(2,1)S(1)} %get-tuple-element.37), channel_id=1, source_target_pairs={{0,8},{1,9},{2,10},{3,11},{4,12},{5,13},{6,14},{7,15},{8,0},{9,1},... | collective-permute-start | bytes 159752 | tf_op jit(solution)/shard_map/ppermute | solution.py:73
  27.7 6.0 %collective-permute-start.7 = (bf16[16,1664]{1,0:T(8,128)(2,1)S(1)}, bf16[16,1664]{1,0:T(8,128)(2,1)S(1)}, u32[]{:S(2)}, u32[]{:S(2)}) collective-permute-start(bf16[16,1664]{1,0:T(8,128)(2,1)S(1)} %get-tuple-element.38), channel_id=1, source_target_pairs={{0,4},{1,5},{2,6},{3,7},{4,0},{5,1},{6,2},{7,3},{8,12},{9,13},{10,... | collective-permute-start | bytes 159752 | tf_op jit(solution)/shard_map/ppermute | solution.py:73
  33.7 4.2 %collective-permute-start.10 = (bf16[16,1664]{1,0:T(8,128)(2,1)S(1)}, bf16[16,1664]{1,0:T(8,128)(2,1)S(1)}, u32[]{:S(2)}, u32[]{:S(2)}) collective-permute-start(bf16[16,1664]{1,0:T(8,128)(2,1)S(1)} %sum.1), channel_id=1, source_target_pairs={{0,2},{1,3},{2,0},{3,1},{4,6},{5,7},{6,4},{7,5},{8,10},{9,11},{10,... | collective-permute-start | bytes 159752 | tf_op jit(solution)/shard_map/ppermute | solution.py:73
  37.9 6.5 %collective-permute-start.13 = (bf16[16,1664]{1,0:T(8,128)(2,1)S(1)}, bf16[16,1664]{1,0:T(8,128)(2,1)S(1)}, u32[]{:S(2)}, u32[]{:S(2)}) collective-permute-start(bf16[16,1664]{1,0:T(8,128)(2,1)S(1)} %fusion.1.refs_0_), channel_id=1, source_target_pairs={{0,12},{1,13},{2,14},{3,15},{4,8},{5,9},{6,10},{7,11},{8,4},{9,5},... | collective-permute-start | bytes 159752 | tf_op jit(solution)/shard_map/ppermute | solution.py:73
  40.2 5.3 %collective-permute-start.12 = (bf16[16,1664]{1,0:T(8,128)(2,1)S(1)}, bf16[16,1664]{1,0:T(8,128)(2,1)S(1)}, u32[]{:S(2)}, u32[]{:S(2)}) collective-permute-start(bf16[16,1664]{1,0:T(8,128)(2,1)S(1)} %fusion.1.refs_0_), channel_id=1, source_target_pairs={{0,8},{1,9},{2,10},{3,11},{4,12},{5,13},{6,14},{7,15},{8,0},{9,1},... | collective-permute-start | bytes 159752 | tf_op jit(solution)/shard_map/ppermute | solution.py:73
  40.2 5.3 %collective-permute-start.11 = (bf16[16,1664]{1,0:T(8,128)(2,1)S(1)}, bf16[16,1664]{1,0:T(8,128)(2,1)S(1)}, u32[]{:S(2)}, u32[]{:S(2)}) collective-permute-start(bf16[16,1664]{1,0:T(8,128)(2,1)S(1)} %fusion.1.refs_0_), channel_id=1, source_target_pairs={{0,4},{1,5},{2,6},{3,7},{4,0},{5,1},{6,2},{7,3},{8,12},{9,13},{10,... | collective-permute-start | bytes 159752 | tf_op jit(solution)/shard_map/ppermute | solution.py:73
  42.4 3.7 %collective-permute-start.14 = (bf16[16,1664]{1,0:T(8,128)(2,1)S(1)}, bf16[16,1664]{1,0:T(8,128)(2,1)S(1)}, u32[]{:S(2)}, u32[]{:S(2)}) collective-permute-start(bf16[16,1664]{1,0:T(8,128)(2,1)S(1)} %fusion.1.refs_0_), channel_id=1, source_target_pairs={{0,1},{1,0},{2,3},{3,2},{4,5},{5,4},{6,7},{7,6},{8,9},{9,8},{10,11... | collective-permute-start | bytes 159752 | tf_op jit(solution)/shard_map/ppermute | solution.py:73
  44.4 1.7 %collective-permute-start.17 = (bf16[16,1664]{1,0:T(8,128)(2,1)S(1)}, bf16[16,1664]{1,0:T(8,128)(2,1)S(1)}, u32[]{:S(2)}, u32[]{:S(2)}) collective-permute-start(bf16[16,1664]{1,0:T(8,128)(2,1)S(1)} %collective-permute-done.13.refs_3_), channel_id=1, source_target_pairs={{0,1},{1,0},{2,3},{3,2},{4,5},{5,4},{6,7},{7,6},{8,9},{9,8},{10,11... | collective-permute-start | bytes 159752 | tf_op jit(solution)/shard_map/ppermute | solution.py:73
  45.5 1.2 %collective-permute-start.16 = (bf16[16,1664]{1,0:T(8,128)(2,1)S(1)}, bf16[16,1664]{1,0:T(8,128)(2,1)S(1)}, u32[]{:S(2)}, u32[]{:S(2)}) collective-permute-start(bf16[16,1664]{1,0:T(8,128)(2,1)S(1)} %collective-permute-done.12.refs_2_), channel_id=1, source_target_pairs={{0,1},{1,0},{2,3},{3,2},{4,5},{5,4},{6,7},{7,6},{8,9},{9,8},{10,11... | collective-permute-start | bytes 159752 | tf_op jit(solution)/shard_map/ppermute | solution.py:73
  45.6 1.4 %collective-permute-start.15 = (bf16[16,1664]{1,0:T(8,128)(2,1)S(1)}, bf16[16,1664]{1,0:T(8,128)(2,1)S(1)}, u32[]{:S(2)}, u32[]{:S(2)}) collective-permute-start(bf16[16,1664]{1,0:T(8,128)(2,1)S(1)} %collective-permute-done.11.refs_1_), channel_id=1, source_target_pairs={{0,1},{1,0},{2,3},{3,2},{4,5},{5,4},{6,7},{7,6},{8,9},{9,8},{10,11... | collective-permute-start | bytes 159752 | tf_op jit(solution)/shard_map/ppermute | solution.py:73

commit v12 on v10

--- a/solution.py
+++ b/solution.py
@@ -14,7 +14,7 @@
 PINNED_BYTES = 24 << 20
 PINNED_TOKENS = 256
 GROUP_ROWS = 256
-DEC_PARTS = 3
+DEC_PARTS = 2
 
 sparsity = 0.5
 epsilon = 1e-05
@@ -217,10 +217,10 @@
     pieces = refs[1 : 1 + count]
     enc, bias, dec_hbm, weights_sum = refs[1 + count : 5 + count]
     send, inputs_out, latent_out, dec, sems = refs[5 + count :]
-    part_width = dec.shape[1] // DEC_PARTS
+    part_rows = dec.shape[0] // DEC_PARTS
     fetches = []
     for i in range(DEC_PARTS):
-        at = (slice(None), pl.ds(i * part_width, part_width))
+        at = pl.ds(i * part_rows, part_rows)
         fetches.append(pltpu.make_async_copy(dec_hbm.at[at], dec.at[at], sems.at[i]))
         fetches[-1].start()
     me = me_ref[0]
@@ -280,11 +280,14 @@
     latent_out[...] = latent
     half = tokens // 2
     rounded = latent[half:].astype(BF16)
-    for i in range(DEC_PARTS):
-        fetches[i].wait()
-        at = slice(i * part_width, (i + 1) * part_width)
-        part = jnp.dot(rounded, dec[:, at], preferred_element_type=F32)
-        send[:, at] = part.astype(BF16)
+    middle = dec.shape[0] // 2
+    for fetch in fetches[: DEC_PARTS // 2]:
+        fetch.wait()
+    part = jnp.dot(rounded[:, :middle], dec[:middle], preferred_element_type=F32)
+    for fetch in fetches[DEC_PARTS // 2 :]:
+        fetch.wait()
+    part = part + jnp.dot(rounded[:, middle:], dec[middle:], preferred_element_type=F32)
+    send[:, :feature] = part.astype(BF16)
     send[:, feature:] = lane_sums(latent[half:] * weights_sum[0:1, :]).astype(BF16)
 
 

time: 50.6 us -> 50.2 us (level)
  no operation moved by 1% of the time
where the time goes in v12:
time: 50.2 us; the launch traced here: 50 us
  waiting for transfers between devices  20.3 us (40%)
  starting transfers between devices  18.6 us (37%)
  Pallas kernels  10.2 us (20%)
  between operations  0.74 us (1%)
    ppermute x18, waiting for transfers between devices, exchange(): return lax.ppermute(value, 'utt', [(i, i ^ bit) for i in range(devices)])  20.3 us
    ppermute x18, starting transfers between devices, exchange(): return lax.ppermute(value, 'utt', [(i, i ^ bit) for i in range(devices)])  18.6 us
    pallas_call x1, Pallas kernels, shards(): call(features_kernel, 'features', fast((slots * frames, feature), BF16),...  3.64 us
    pallas_call x1, Pallas kernels, shards(): call(gradients, 'gradients', (shape((feature, latents), BF16), shape((lat...  3.35 us
    pallas_call x1, Pallas kernels, shards(): call(encode, 'encode', (fast((half, wide), BF16), fast((tokens, feature),...  1.79 us
  transfers between devices with their start and end apart: 18, of which 12 were waited for; matrix products, arithmetic and copies ran while one was open for 0% of the time, Pallas kernels for 3%

profile of v12, /device:TPU:0, one launch (start us, length us, event | category | flops | bytes accessed | tf_op | source)
XLA Modules:
  0.0 50.0 jit_solution(6841858326410459981)
XLA Ops:
  0.6 3.6 %features.1.refs_2_ = bf16[16,1536]{1,0:T(8,128)(2,1)S(1)} custom-call(s32[2]{0:T(128)} %refs_0_.1, s32[2]{0:T(128)} %refs_1_.2, f32[2,90]{1,0:T(2,128)} %refs_2_.1, f32[10,3,512]{2,1,0:T(4,128)} %bitcast.14, f32[3,2,512]{2,1,0:T(2,128)} %refs_4_.1, f32[3,2,512]{2,1,0:T(2,128)} %refs_5_.2, bf16[3,1536,512]{2,1,0:T(8,128)(2,1)} %refs_6_.1), custom_call_target="tpu_custom_call" | custom-call | flops 75497472 | bytes 4718592 | tf_op jit(solution)/shard_map/features/pallas_call | solution.py:413
  4.3 5.1 %collective-permute-start.2 = (bf16[16,1536]{1,0:T(8,128)(2,1)S(1)}, bf16[16,1536]{1,0:T(8,128)(2,1)S(1)}, u32[]{:S(2)}, u32[]{:S(2)}) collective-permute-start(bf16[16,1536]{1,0:T(8,128)(2,1)S(1)} %features.1.refs_2_), channel_id=1, source_target_pairs={{0,12},{1,13},{2,14},{3,15},{4,8},{5,9},{6,10},{7,11},{8,4},{9,5},... | collective-permute-start | bytes 147464 | tf_op jit(solution)/shard_map/ppermute | solution.py:74
  9.4 0.6 %collective-permute-start = (bf16[16,1536]{1,0:T(8,128)(2,1)S(1)}, bf16[16,1536]{1,0:T(8,128)(2,1)S(1)}, u32[]{:S(2)}, u32[]{:S(2)}) collective-permute-start(bf16[16,1536]{1,0:T(8,128)(2,1)S(1)} %features.1.refs_2_), channel_id=1, source_target_pairs={{0,4},{1,5},{2,6},{3,7},{4,0},{5,1},{6,2},{7,3},{8,12},{9,13},{10,... | collective-permute-start | bytes 147464 | tf_op jit(solution)/shard_map/ppermute | solution.py:74
  10.1 0.7 %norms.1 = (f32[512,128]{1,0:T(8,128)S(1)}, f32[8,512]{1,0:T(8,128)S(1)}) custom-call(bf16[512,1536]{1,0:T(8,128)(2,1)S(1)} %copy-done), custom_call_target="tpu_custom_call" | custom-call | flops 3145728 | bytes 1572864 | tf_op jit(solution)/shard_map/norms/pallas_call | solution.py:439
  10.8 0.9 %collective-permute-done.2.refs_5_ = bf16[16,1536]{1,0:T(8,128)(2,1)S(1)} collective-permute-done((bf16[16,1536]{1,0:T(8,128)(2,1)S(1)}, bf16[16,1536]{1,0:T(8,128)(2,1)S(1)}, u32[]{:S(2)}, u32[]{:S(2)}) %collective-permute-start.2) | collective-permute-done | bytes 49184 | tf_op jit(solution)/shard_map/ppermute | solution.py:74
  11.7 2.8 %collective-permute-done.1.refs_4_ = bf16[16,1536]{1,0:T(8,128)(2,1)S(1)} collective-permute-done((bf16[16,1536]{1,0:T(8,128)(2,1)S(1)}, bf16[16,1536]{1,0:T(8,128)(2,1)S(1)}, u32[]{:S(2)}, u32[]{:S(2)}) %collective-permute-start.1) | collective-permute-done | bytes 49184 | tf_op jit(solution)/shard_map/ppermute | solution.py:74
  14.5 1.6 %collective-permute-start.3 = (bf16[64,1536]{1,0:T(8,128)(2,1)S(1)}, bf16[64,1536]{1,0:T(8,128)(2,1)S(1)}, u32[]{:S(2)}, u32[]{:S(2)}) collective-permute-start(bf16[64,1536]{1,0:T(8,128)(2,1)S(1)} %join.1.refs_1_), channel_id=1, source_target_pairs={{0,2},{1,3},{2,0},{3,1},{4,6},{5,7},{6,4},{7,5},{8,10},{9,11},{10,... | collective-permute-start | bytes 589832 | tf_op jit(solution)/shard_map/ppermute | solution.py:74
  16.0 4.2 %collective-permute-done.3.refs_2_ = bf16[64,1536]{1,0:T(8,128)(2,1)S(1)} collective-permute-done((bf16[64,1536]{1,0:T(8,128)(2,1)S(1)}, bf16[64,1536]{1,0:T(8,128)(2,1)S(1)}, u32[]{:S(2)}, u32[]{:S(2)}) %collective-permute-start.3) | collective-permute-done | bytes 196640 | tf_op jit(solution)/shard_map/ppermute | solution.py:74
  20.3 1.4 %collective-permute-done.5.refs_4_ = bf16[64,1536]{1,0:T(8,128)(2,1)S(1)} collective-permute-done((bf16[64,1536]{1,0:T(8,128)(2,1)S(1)}, bf16[64,1536]{1,0:T(8,128)(2,1)S(1)}, u32[]{:S(2)}, u32[]{:S(2)}) %collective-permute-start.5) | collective-permute-done | bytes 196640 | tf_op jit(solution)/shard_map/ppermute | solution.py:74
  21.7 1.8 %encode.1 = (bf16[64,1664]{1,0:T(8,128)(2,1)S(1)}, bf16[128,1536]{1,0:T(8,128)(2,1)S(1)}, f32[128,512]{1,0:T(8,128)S(1)}, bf16[512,1536]{1,0:T(8,128)(2,1)S(1)}) custom-call(s32[1]{0:T(128)} %bitcast.refs_0_, bf16[64,1536]{1,0:T(8,128)(2,1)S(1)} %join.1.refs_1_, bf16[64,1536]{1,0:T(8,128)(2,1)S(1)} %collective-permute-done.3.refs_2_, ...), custom_call_target="tpu_custom_call" | custom-call | flops 301989888 | bytes 3145728 | tf_op jit(solution)/shard_map/encode/pallas_call | solution.py:472
  24.1 0.9 %collective-permute-done.6 = bf16[64,1664]{1,0:T(8,128)(2,1)S(1)} collective-permute-done((bf16[64,1664]{1,0:T(8,128)(2,1)S(1)}, bf16[64,1664]{1,0:T(8,128)(2,1)S(1)}, u32[]{:S(2)}, u32[]{:S(2)}) %collective-permute-start.6) | collective-permute-done | bytes 213024 | tf_op jit(solution)/shard_map/ppermute | solution.py:74
  25.1 2.1 %collective-permute-start.9 = (bf16[16,1664]{1,0:T(8,128)(2,1)S(1)}, bf16[16,1664]{1,0:T(8,128)(2,1)S(1)}, u32[]{:S(2)}, u32[]{:S(2)}) collective-permute-start(bf16[16,1664]{1,0:T(8,128)(2,1)S(1)} %get-tuple-element.42), channel_id=1, source_target_pairs={{0,12},{1,13},{2,14},{3,15},{4,8},{5,9},{6,10},{7,11},{8,4},{9,5},... | collective-permute-start | bytes 159752 | tf_op jit(solution)/shard_map/ppermute | solution.py:74
  27.4 2.2 %collective-permute-start.7 = (bf16[16,1664]{1,0:T(8,128)(2,1)S(1)}, bf16[16,1664]{1,0:T(8,128)(2,1)S(1)}, u32[]{:S(2)}, u32[]{:S(2)}) collective-permute-start(bf16[16,1664]{1,0:T(8,128)(2,1)S(1)} %get-tuple-element.44), channel_id=1, source_target_pairs={{0,4},{1,5},{2,6},{3,7},{4,0},{5,1},{6,2},{7,3},{8,12},{9,13},{10,... | collective-permute-start | bytes 159752 | tf_op jit(solution)/shard_map/ppermute | solution.py:74
  29.9 1.8 %collective-permute-done.9.refs_4_ = bf16[16,1664]{1,0:T(8,128)(2,1)S(1)} collective-permute-done((bf16[16,1664]{1,0:T(8,128)(2,1)S(1)}, bf16[16,1664]{1,0:T(8,128)(2,1)S(1)}, u32[]{:S(2)}, u32[]{:S(2)}) %collective-permute-start.9) | collective-permute-done | bytes 53280 | tf_op jit(solution)/shard_map/ppermute | solution.py:74
  31.7 1.6 %collective-permute-done.8.refs_3_ = bf16[16,1664]{1,0:T(8,128)(2,1)S(1)} collective-permute-done((bf16[16,1664]{1,0:T(8,128)(2,1)S(1)}, bf16[16,1664]{1,0:T(8,128)(2,1)S(1)}, u32[]{:S(2)}, u32[]{:S(2)}) %collective-permute-start.8) | collective-permute-done | bytes 53280 | tf_op jit(solution)/shard_map/ppermute | solution.py:74
  33.4 1.6 %collective-permute-start.10 = (bf16[16,1664]{1,0:T(8,128)(2,1)S(1)}, bf16[16,1664]{1,0:T(8,128)(2,1)S(1)}, u32[]{:S(2)}, u32[]{:S(2)}) collective-permute-start(bf16[16,1664]{1,0:T(8,128)(2,1)S(1)} %sum.1), channel_id=1, source_target_pairs={{0,2},{1,3},{2,0},{3,1},{4,6},{5,7},{6,4},{7,5},{8,10},{9,11},{10,... | collective-permute-start | bytes 159752 | tf_op jit(solution)/shard_map/ppermute | solution.py:74
  35.0 2.6 %collective-permute-done.10 = bf16[16,1664]{1,0:T(8,128)(2,1)S(1)} collective-permute-done((bf16[16,1664]{1,0:T(8,128)(2,1)S(1)}, bf16[16,1664]{1,0:T(8,128)(2,1)S(1)}, u32[]{:S(2)}, u32[]{:S(2)}) %collective-permute-start.10) | collective-permute-done | bytes 53280 | tf_op jit(solution)/shard_map/ppermute | solution.py:74
  37.6 2.3 %collective-permute-start.13 = (bf16[16,1664]{1,0:T(8,128)(2,1)S(1)}, bf16[16,1664]{1,0:T(8,128)(2,1)S(1)}, u32[]{:S(2)}, u32[]{:S(2)}) collective-permute-start(bf16[16,1664]{1,0:T(8,128)(2,1)S(1)} %fusion.1.refs_0_), channel_id=1, source_target_pairs={{0,12},{1,13},{2,14},{3,15},{4,8},{5,9},{6,10},{7,11},{8,4},{9,5},... | collective-permute-start | bytes 159752 | tf_op jit(solution)/shard_map/ppermute | solution.py:74
  39.9 2.1 %collective-permute-start.11 = (bf16[16,1664]{1,0:T(8,128)(2,1)S(1)}, bf16[16,1664]{1,0:T(8,128)(2,1)S(1)}, u32[]{:S(2)}, u32[]{:S(2)}) collective-permute-start(bf16[16,1664]{1,0:T(8,128)(2,1)S(1)} %fusion.1.refs_0_), channel_id=1, source_target_pairs={{0,4},{1,5},{2,6},{3,7},{4,0},{5,1},{6,2},{7,3},{8,12},{9,13},{10,... | collective-permute-start | bytes 159752 | tf_op jit(solution)/shard_map/ppermute | solution.py:74
  42.1 2.0 %collective-permute-done.13.refs_3_ = bf16[16,1664]{1,0:T(8,128)(2,1)S(1)} collective-permute-done((bf16[16,1664]{1,0:T(8,128)(2,1)S(1)}, bf16[16,1664]{1,0:T(8,128)(2,1)S(1)}, u32[]{:S(2)}, u32[]{:S(2)}) %collective-permute-start.13) | collective-permute-done | bytes 53280 | tf_op jit(solution)/shard_map/ppermute | solution.py:74
  44.1 1.1 %collective-permute-done.12.refs_2_ = bf16[16,1664]{1,0:T(8,128)(2,1)S(1)} collective-permute-done((bf16[16,1664]{1,0:T(8,128)(2,1)S(1)}, bf16[16,1664]{1,0:T(8,128)(2,1)S(1)}, u32[]{:S(2)}, u32[]{:S(2)}) %collective-permute-start.12) | collective-permute-done | bytes 53280 | tf_op jit(solution)/shard_map/ppermute | solution.py:74
  45.3 0.5 %collective-permute-start.15 = (bf16[16,1664]{1,0:T(8,128)(2,1)S(1)}, bf16[16,1664]{1,0:T(8,128)(2,1)S(1)}, u32[]{:S(2)}, u32[]{:S(2)}) collective-permute-start(bf16[16,1664]{1,0:T(8,128)(2,1)S(1)} %collective-permute-done.11.refs_1_), channel_id=1, source_target_pairs={{0,1},{1,0},{2,3},{3,2},{4,5},{5,4},{6,7},{7,6},{8,9},{9,8},{10,11... | collective-permute-start | bytes 159752 | tf_op jit(solution)/shard_map/ppermute | solution.py:74
  45.8 0.7 %collective-permute-done.16.refs_6_ = bf16[16,1664]{1,0:T(8,128)(2,1)S(1)} collective-permute-done((bf16[16,1664]{1,0:T(8,128)(2,1)S(1)}, bf16[16,1664]{1,0:T(8,128)(2,1)S(1)}, u32[]{:S(2)}, u32[]{:S(2)}) %collective-permute-start.16) | collective-permute-done | bytes 53280 | tf_op jit(solution)/shard_map/ppermute | solution.py:74
  46.6 3.4 %gradients.1 = (bf16[1536,512]{1,0:T(8,128)(2,1)}, bf16[512,1536]{1,0:T(8,128)(2,1)}, f32[1,512]{1,0:T(1,128)}, f32[1536]{0:T(1024)}, f32[1]{0:T(128)}, /*index=5*/bf16[8,1536]{1,0:T(8,128)(2,1)}) custom-call(bf16[16,1664]{1,0:T(8,128)(2,1)S(1)} %fusion.1.refs_0_, bf16[16,1664]{1,0:T(8,128)(2,1)S(1)} %collective-permute-done.11.refs_1_, ...), custom_call_target="tpu_custom_call" | custom-call | flops 603979776 | bytes 6291456 | tf_op jit(solution)/shard_map/gradients/pallas_call | solution.py:544
  (33 shorter events, 1.4 us)
Async XLA Ops:
  0.6 9.4 %copy-start = (bf16[512,1536]{1,0:T(8,128)(2,1)S(1)}, bf16[512,1536]{1,0:T(8,128)(2,1)}, u32[]{:S(2)}) copy-start(bf16[512,1536]{1,0:T(8,128)(2,1)} %refs_7_.1) | copy-start | bytes 4718596
  4.3 10.1 %copy-start.1 = (bf16[1536,512]{1,0:T(8,128)(2,1)S(1)}, bf16[1536,512]{1,0:T(8,128)(2,1)}, u32[]{:S(2)}) copy-start(bf16[1536,512]{1,0:T(8,128)(2,1)} %refs_5_.3) | copy-start | bytes 4718596
  4.3 17.4 %copy-start.3 = (f32[512]{0:T(512)S(1)}, f32[512]{0:T(512)}, u32[]{:S(2)}) copy-start(f32[512]{0:T(512)} %param.19) | copy-start | bytes 6148
  4.3 7.3 %collective-permute-start.2 = (bf16[16,1536]{1,0:T(8,128)(2,1)S(1)}, bf16[16,1536]{1,0:T(8,128)(2,1)S(1)}, u32[]{:S(2)}, u32[]{:S(2)}) collective-permute-start(bf16[16,1536]{1,0:T(8,128)(2,1)S(1)} %features.1.refs_2_), channel_id=1, source_target_pairs={{0,12},{1,13},{2,14},{3,15},{4,8},{5,9},{6,10},{7,11},{8,4},{9,5},... | collective-permute-start | bytes 147464 | tf_op jit(solution)/shard_map/ppermute | solution.py:74
  9.4 5.0 %collective-permute-start.1 = (bf16[16,1536]{1,0:T(8,128)(2,1)S(1)}, bf16[16,1536]{1,0:T(8,128)(2,1)S(1)}, u32[]{:S(2)}, u32[]{:S(2)}) collective-permute-start(bf16[16,1536]{1,0:T(8,128)(2,1)S(1)} %features.1.refs_2_), channel_id=1, source_target_pairs={{0,8},{1,9},{2,10},{3,11},{4,12},{5,13},{6,14},{7,15},{8,0},{9,1},... | collective-permute-start | bytes 147464 | tf_op jit(solution)/shard_map/ppermute | solution.py:74
  9.4 5.0 %collective-permute-start = (bf16[16,1536]{1,0:T(8,128)(2,1)S(1)}, bf16[16,1536]{1,0:T(8,128)(2,1)S(1)}, u32[]{:S(2)}, u32[]{:S(2)}) collective-permute-start(bf16[16,1536]{1,0:T(8,128)(2,1)S(1)} %features.1.refs_2_), channel_id=1, source_target_pairs={{0,4},{1,5},{2,6},{3,7},{4,0},{5,1},{6,2},{7,3},{8,12},{9,13},{10,... | collective-permute-start | bytes 147464 | tf_op jit(solution)/shard_map/ppermute | solution.py:74
  14.5 5.8 %collective-permute-start.3 = (bf16[64,1536]{1,0:T(8,128)(2,1)S(1)}, bf16[64,1536]{1,0:T(8,128)(2,1)S(1)}, u32[]{:S(2)}, u32[]{:S(2)}) collective-permute-start(bf16[64,1536]{1,0:T(8,128)(2,1)S(1)} %join.1.refs_1_), channel_id=1, source_target_pairs={{0,2},{1,3},{2,0},{3,1},{4,6},{5,7},{6,4},{7,5},{8,10},{9,11},{10,... | collective-permute-start | bytes 589832 | tf_op jit(solution)/shard_map/ppermute | solution.py:74
  16.0 4.2 %collective-permute-start.4 = (bf16[64,1536]{1,0:T(8,128)(2,1)S(1)}, bf16[64,1536]{1,0:T(8,128)(2,1)S(1)}, u32[]{:S(2)}, u32[]{:S(2)}) collective-permute-start(bf16[64,1536]{1,0:T(8,128)(2,1)S(1)} %join.1.refs_1_), channel_id=1, source_target_pairs={{0,1},{1,0},{2,3},{3,2},{4,5},{5,4},{6,7},{7,6},{8,9},{9,8},{10,11... | collective-permute-start | bytes 589832 | tf_op jit(solution)/shard_map/ppermute | solution.py:74
  20.3 1.4 %collective-permute-start.5 = (bf16[64,1536]{1,0:T(8,128)(2,1)S(1)}, bf16[64,1536]{1,0:T(8,128)(2,1)S(1)}, u32[]{:S(2)}, u32[]{:S(2)}) collective-permute-start(bf16[64,1536]{1,0:T(8,128)(2,1)S(1)} %collective-permute-done.3.refs_2_), channel_id=1, source_target_pairs={{0,1},{1,0},{2,3},{3,2},{4,5},{5,4},{6,7},{7,6},{8,9},{9,8},{10,11... | collective-permute-start | bytes 589832 | tf_op jit(solution)/shard_map/ppermute | solution.py:74
  21.7 2.0 %copy-start.2 = (f32[1536]{0:T(1024)S(1)}, f32[1536]{0:T(1024)}, u32[]{:S(2)}) copy-start(f32[1536]{0:T(1024)} %dec_bias.1) | copy-start | bytes 18436
  23.5 1.5 %collective-permute-start.6 = (bf16[64,1664]{1,0:T(8,128)(2,1)S(1)}, bf16[64,1664]{1,0:T(8,128)(2,1)S(1)}, u32[]{:S(2)}, u32[]{:S(2)}) collective-permute-start(bf16[64,1664]{1,0:T(8,128)(2,1)S(1)} %get-tuple-element.30), channel_id=1, source_target_pairs={{0,1},{1,0},{2,3},{3,2},{4,5},{5,4},{6,7},{7,6},{8,9},{9,8},{10,11... | collective-permute-start | bytes 638984 | tf_op jit(solution)/shard_map/ppermute | solution.py:74
  25.1 6.6 %collective-permute-start.9 = (bf16[16,1664]{1,0:T(8,128)(2,1)S(1)}, bf16[16,1664]{1,0:T(8,128)(2,1)S(1)}, u32[]{:S(2)}, u32[]{:S(2)}) collective-permute-start(bf16[16,1664]{1,0:T(8,128)(2,1)S(1)} %get-tuple-element.42), channel_id=1, source_target_pairs={{0,12},{1,13},{2,14},{3,15},{4,8},{5,9},{6,10},{7,11},{8,4},{9,5},... | collective-permute-start | bytes 159752 | tf_op jit(solution)/shard_map/ppermute | solution.py:74
  27.2 6.1 %collective-permute-start.8 = (bf16[16,1664]{1,0:T(8,128)(2,1)S(1)}, bf16[16,1664]{1,0:T(8,128)(2,1)S(1)}, u32[]{:S(2)}, u32[]{:S(2)}) collective-permute-start(bf16[16,1664]{1,0:T(8,128)(2,1)S(1)} %get-tuple-element.43), channel_id=1, source_target_pairs={{0,8},{1,9},{2,10},{3,11},{4,12},{5,13},{6,14},{7,15},{8,0},{9,1},... | collective-permute-start | bytes 159752 | tf_op jit(solution)/shard_map/ppermute | solution.py:74
  27.4 6.0 %collective-permute-start.7 = (bf16[16,1664]{1,0:T(8,128)(2,1)S(1)}, bf16[16,1664]{1,0:T(8,128)(2,1)S(1)}, u32[]{:S(2)}, u32[]{:S(2)}) collective-permute-start(bf16[16,1664]{1,0:T(8,128)(2,1)S(1)} %get-tuple-element.44), channel_id=1, source_target_pairs={{0,4},{1,5},{2,6},{3,7},{4,0},{5,1},{6,2},{7,3},{8,12},{9,13},{10,... | collective-permute-start | bytes 159752 | tf_op jit(solution)/shard_map/ppermute | solution.py:74
  33.4 4.2 %collective-permute-start.10 = (bf16[16,1664]{1,0:T(8,128)(2,1)S(1)}, bf16[16,1664]{1,0:T(8,128)(2,1)S(1)}, u32[]{:S(2)}, u32[]{:S(2)}) collective-permute-start(bf16[16,1664]{1,0:T(8,128)(2,1)S(1)} %sum.1), channel_id=1, source_target_pairs={{0,2},{1,3},{2,0},{3,1},{4,6},{5,7},{6,4},{7,5},{8,10},{9,11},{10,... | collective-permute-start | bytes 159752 | tf_op jit(solution)/shard_map/ppermute | solution.py:74
  37.6 6.5 %collective-permute-start.13 = (bf16[16,1664]{1,0:T(8,128)(2,1)S(1)}, bf16[16,1664]{1,0:T(8,128)(2,1)S(1)}, u32[]{:S(2)}, u32[]{:S(2)}) collective-permute-start(bf16[16,1664]{1,0:T(8,128)(2,1)S(1)} %fusion.1.refs_0_), channel_id=1, source_target_pairs={{0,12},{1,13},{2,14},{3,15},{4,8},{5,9},{6,10},{7,11},{8,4},{9,5},... | collective-permute-start | bytes 159752 | tf_op jit(solution)/shard_map/ppermute | solution.py:74
  39.9 5.3 %collective-permute-start.12 = (bf16[16,1664]{1,0:T(8,128)(2,1)S(1)}, bf16[16,1664]{1,0:T(8,128)(2,1)S(1)}, u32[]{:S(2)}, u32[]{:S(2)}) collective-permute-start(bf16[16,1664]{1,0:T(8,128)(2,1)S(1)} %fusion.1.refs_0_), channel_id=1, source_target_pairs={{0,8},{1,9},{2,10},{3,11},{4,12},{5,13},{6,14},{7,15},{8,0},{9,1},... | collective-permute-start | bytes 159752 | tf_op jit(solution)/shard_map/ppermute | solution.py:74
  39.9 5.3 %collective-permute-start.11 = (bf16[16,1664]{1,0:T(8,128)(2,1)S(1)}, bf16[16,1664]{1,0:T(8,128)(2,1)S(1)}, u32[]{:S(2)}, u32[]{:S(2)}) collective-permute-start(bf16[16,1664]{1,0:T(8,128)(2,1)S(1)} %fusion.1.refs_0_), channel_id=1, source_target_pairs={{0,4},{1,5},{2,6},{3,7},{4,0},{5,1},{6,2},{7,3},{8,12},{9,13},{10,... | collective-permute-start | bytes 159752 | tf_op jit(solution)/shard_map/ppermute | solution.py:74
  42.1 3.7 %collective-permute-start.14 = (bf16[16,1664]{1,0:T(8,128)(2,1)S(1)}, bf16[16,1664]{1,0:T(8,128)(2,1)S(1)}, u32[]{:S(2)}, u32[]{:S(2)}) collective-permute-start(bf16[16,1664]{1,0:T(8,128)(2,1)S(1)} %fusion.1.refs_0_), channel_id=1, source_target_pairs={{0,1},{1,0},{2,3},{3,2},{4,5},{5,4},{6,7},{7,6},{8,9},{9,8},{10,11... | collective-permute-start | bytes 159752 | tf_op jit(solution)/shard_map/ppermute | solution.py:74
  44.1 1.7 %collective-permute-start.17 = (bf16[16,1664]{1,0:T(8,128)(2,1)S(1)}, bf16[16,1664]{1,0:T(8,128)(2,1)S(1)}, u32[]{:S(2)}, u32[]{:S(2)}) collective-permute-start(bf16[16,1664]{1,0:T(8,128)(2,1)S(1)} %collective-permute-done.13.refs_3_), channel_id=1, source_target_pairs={{0,1},{1,0},{2,3},{3,2},{4,5},{5,4},{6,7},{7,6},{8,9},{9,8},{10,11... | collective-permute-start | bytes 159752 | tf_op jit(solution)/shard_map/ppermute | solution.py:74
  45.2 1.2 %collective-permute-start.16 = (bf16[16,1664]{1,0:T(8,128)(2,1)S(1)}, bf16[16,1664]{1,0:T(8,128)(2,1)S(1)}, u32[]{:S(2)}, u32[]{:S(2)}) collective-permute-start(bf16[16,1664]{1,0:T(8,128)(2,1)S(1)} %collective-permute-done.12.refs_2_), channel_id=1, source_target_pairs={{0,1},{1,0},{2,3},{3,2},{4,5},{5,4},{6,7},{7,6},{8,9},{9,8},{10,11... | collective-permute-start | bytes 159752 | tf_op jit(solution)/shard_map/ppermute | solution.py:74
  45.3 1.4 %collective-permute-start.15 = (bf16[16,1664]{1,0:T(8,128)(2,1)S(1)}, bf16[16,1664]{1,0:T(8,128)(2,1)S(1)}, u32[]{:S(2)}, u32[]{:S(2)}) collective-permute-start(bf16[16,1664]{1,0:T(8,128)(2,1)S(1)} %collective-permute-done.11.refs_1_), channel_id=1, source_target_pairs={{0,1},{1,0},{2,3},{3,2},{4,5},{5,4},{6,7},{7,6},{8,9},{9,8},{10,11... | collective-permute-start | bytes 159752 | tf_op jit(solution)/shard_map/ppermute | solution.py:74

commit v13 on v12

--- a/solution.py
+++ b/solution.py
@@ -125,8 +125,9 @@
     slots, samples = wave.shape
     frames = out.shape[0] // slots
     copies = []
-    for c in range(checkpoints):
-        copies.append(pltpu.make_async_copy(sources[6].at[c], second_w.at[c], more.at[c]))
+    for c, n in ((0, 1), (1, checkpoints - 1)):
+        at = pl.ds(c, n)
+        copies.append(pltpu.make_async_copy(sources[6].at[at], second_w.at[at], more.at[c]))
         copies[-1].start()
     for copy in small:
         copy.wait()
@@ -179,7 +180,8 @@
     hidden = layer_one(0)
     held_back = None
     for c in range(checkpoints):
-        copies[c].wait()
+        if c < len(copies):
+            copies[c].wait()
         total = layer_two(c, hidden)
         if c + 1 < checkpoints:
             hidden = layer_one(c + 1)

time: 50.2 us -> 49.9 us (level)
  no operation moved by 1% of the time
where the time goes in v13:
time: 49.9 us; the launch traced here: 49.8 us
  waiting for transfers between devices  20.3 us (41%)
  starting transfers between devices  18.6 us (37%)
  Pallas kernels  10 us (20%)
  between operations  0.74 us (1%)
    ppermute x18, waiting for transfers between devices, exchange(): return lax.ppermute(value, 'utt', [(i, i ^ bit) for i in range(devices)])  20.3 us
    ppermute x18, starting transfers between devices, exchange(): return lax.ppermute(value, 'utt', [(i, i ^ bit) for i in range(devices)])  18.6 us
    pallas_call x1, Pallas kernels, shards(): call(features_kernel, 'features', fast((slots * frames, feature), BF16),...  3.4 us
    pallas_call x1, Pallas kernels, shards(): call(gradients, 'gradients', (shape((feature, latents), BF16), shape((lat...  3.35 us
    pallas_call x1, Pallas kernels, shards(): call(encode, 'encode', (fast((half, wide), BF16), fast((tokens, feature),...  1.79 us
  transfers between devices with their start and end apart: 18, of which 12 were waited for; matrix products, arithmetic and copies ran while one was open for 0% of the time, Pallas kernels for 3%

profile of v13, /device:TPU:0, one launch (start us, length us, event | category | flops | bytes accessed | tf_op | source)
XLA Modules:
  0.0 49.8 jit_solution(7479485786663423563)
XLA Ops:
  0.6 3.4 %features.1.refs_2_ = bf16[16,1536]{1,0:T(8,128)(2,1)S(1)} custom-call(s32[2]{0:T(128)} %refs_0_.1, s32[2]{0:T(128)} %refs_1_.2, f32[2,90]{1,0:T(2,128)} %refs_2_.1, f32[10,3,512]{2,1,0:T(4,128)} %bitcast.14, f32[3,2,512]{2,1,0:T(2,128)} %refs_4_.1, f32[3,2,512]{2,1,0:T(2,128)} %refs_5_.2, bf16[3,1536,512]{2,1,0:T(8,128)(2,1)} %refs_6_.1), custom_call_target="tpu_custom_call" | custom-call | flops 75497472 | bytes 4718592 | tf_op jit(solution)/shard_map/features/pallas_call | solution.py:415
  4.1 5.1 %collective-permute-start.2 = (bf16[16,1536]{1,0:T(8,128)(2,1)S(1)}, bf16[16,1536]{1,0:T(8,128)(2,1)S(1)}, u32[]{:S(2)}, u32[]{:S(2)}) collective-permute-start(bf16[16,1536]{1,0:T(8,128)(2,1)S(1)} %features.1.refs_2_), channel_id=1, source_target_pairs={{0,12},{1,13},{2,14},{3,15},{4,8},{5,9},{6,10},{7,11},{8,4},{9,5},... | collective-permute-start | bytes 147464 | tf_op jit(solution)/shard_map/ppermute | solution.py:74
  9.2 0.6 %collective-permute-start = (bf16[16,1536]{1,0:T(8,128)(2,1)S(1)}, bf16[16,1536]{1,0:T(8,128)(2,1)S(1)}, u32[]{:S(2)}, u32[]{:S(2)}) collective-permute-start(bf16[16,1536]{1,0:T(8,128)(2,1)S(1)} %features.1.refs_2_), channel_id=1, source_target_pairs={{0,4},{1,5},{2,6},{3,7},{4,0},{5,1},{6,2},{7,3},{8,12},{9,13},{10,... | collective-permute-start | bytes 147464 | tf_op jit(solution)/shard_map/ppermute | solution.py:74
  9.8 0.7 %norms.1 = (f32[512,128]{1,0:T(8,128)S(1)}, f32[8,512]{1,0:T(8,128)S(1)}) custom-call(bf16[512,1536]{1,0:T(8,128)(2,1)S(1)} %copy-done), custom_call_target="tpu_custom_call" | custom-call | flops 3145728 | bytes 1572864 | tf_op jit(solution)/shard_map/norms/pallas_call | solution.py:441
  10.5 0.9 %collective-permute-done.2.refs_5_ = bf16[16,1536]{1,0:T(8,128)(2,1)S(1)} collective-permute-done((bf16[16,1536]{1,0:T(8,128)(2,1)S(1)}, bf16[16,1536]{1,0:T(8,128)(2,1)S(1)}, u32[]{:S(2)}, u32[]{:S(2)}) %collective-permute-start.2) | collective-permute-done | bytes 49184 | tf_op jit(solution)/shard_map/ppermute | solution.py:74
  11.4 2.8 %collective-permute-done.1.refs_4_ = bf16[16,1536]{1,0:T(8,128)(2,1)S(1)} collective-permute-done((bf16[16,1536]{1,0:T(8,128)(2,1)S(1)}, bf16[16,1536]{1,0:T(8,128)(2,1)S(1)}, u32[]{:S(2)}, u32[]{:S(2)}) %collective-permute-start.1) | collective-permute-done | bytes 49184 | tf_op jit(solution)/shard_map/ppermute | solution.py:74
  14.2 1.6 %collective-permute-start.3 = (bf16[64,1536]{1,0:T(8,128)(2,1)S(1)}, bf16[64,1536]{1,0:T(8,128)(2,1)S(1)}, u32[]{:S(2)}, u32[]{:S(2)}) collective-permute-start(bf16[64,1536]{1,0:T(8,128)(2,1)S(1)} %join.1.refs_1_), channel_id=1, source_target_pairs={{0,2},{1,3},{2,0},{3,1},{4,6},{5,7},{6,4},{7,5},{8,10},{9,11},{10,... | collective-permute-start | bytes 589832 | tf_op jit(solution)/shard_map/ppermute | solution.py:74
  15.8 4.2 %collective-permute-done.3.refs_2_ = bf16[64,1536]{1,0:T(8,128)(2,1)S(1)} collective-permute-done((bf16[64,1536]{1,0:T(8,128)(2,1)S(1)}, bf16[64,1536]{1,0:T(8,128)(2,1)S(1)}, u32[]{:S(2)}, u32[]{:S(2)}) %collective-permute-start.3) | collective-permute-done | bytes 196640 | tf_op jit(solution)/shard_map/ppermute | solution.py:74
  20.0 1.4 %collective-permute-done.5.refs_4_ = bf16[64,1536]{1,0:T(8,128)(2,1)S(1)} collective-permute-done((bf16[64,1536]{1,0:T(8,128)(2,1)S(1)}, bf16[64,1536]{1,0:T(8,128)(2,1)S(1)}, u32[]{:S(2)}, u32[]{:S(2)}) %collective-permute-start.5) | collective-permute-done | bytes 196640 | tf_op jit(solution)/shard_map/ppermute | solution.py:74
  21.5 1.8 %encode.1 = (bf16[64,1664]{1,0:T(8,128)(2,1)S(1)}, bf16[128,1536]{1,0:T(8,128)(2,1)S(1)}, f32[128,512]{1,0:T(8,128)S(1)}, bf16[512,1536]{1,0:T(8,128)(2,1)S(1)}) custom-call(s32[1]{0:T(128)} %bitcast.refs_0_, bf16[64,1536]{1,0:T(8,128)(2,1)S(1)} %join.1.refs_1_, bf16[64,1536]{1,0:T(8,128)(2,1)S(1)} %collective-permute-done.3.refs_2_, ...), custom_call_target="tpu_custom_call" | custom-call | flops 301989888 | bytes 3145728 | tf_op jit(solution)/shard_map/encode/pallas_call | solution.py:474
  23.9 0.9 %collective-permute-done.6 = bf16[64,1664]{1,0:T(8,128)(2,1)S(1)} collective-permute-done((bf16[64,1664]{1,0:T(8,128)(2,1)S(1)}, bf16[64,1664]{1,0:T(8,128)(2,1)S(1)}, u32[]{:S(2)}, u32[]{:S(2)}) %collective-permute-start.6) | collective-permute-done | bytes 213024 | tf_op jit(solution)/shard_map/ppermute | solution.py:74
  24.9 2.1 %collective-permute-start.9 = (bf16[16,1664]{1,0:T(8,128)(2,1)S(1)}, bf16[16,1664]{1,0:T(8,128)(2,1)S(1)}, u32[]{:S(2)}, u32[]{:S(2)}) collective-permute-start(bf16[16,1664]{1,0:T(8,128)(2,1)S(1)} %get-tuple-element.42), channel_id=1, source_target_pairs={{0,12},{1,13},{2,14},{3,15},{4,8},{5,9},{6,10},{7,11},{8,4},{9,5},... | collective-permute-start | bytes 159752 | tf_op jit(solution)/shard_map/ppermute | solution.py:74
  27.1 2.2 %collective-permute-start.7 = (bf16[16,1664]{1,0:T(8,128)(2,1)S(1)}, bf16[16,1664]{1,0:T(8,128)(2,1)S(1)}, u32[]{:S(2)}, u32[]{:S(2)}) collective-permute-start(bf16[16,1664]{1,0:T(8,128)(2,1)S(1)} %get-tuple-element.44), channel_id=1, source_target_pairs={{0,4},{1,5},{2,6},{3,7},{4,0},{5,1},{6,2},{7,3},{8,12},{9,13},{10,... | collective-permute-start | bytes 159752 | tf_op jit(solution)/shard_map/ppermute | solution.py:74
  29.7 1.8 %collective-permute-done.9.refs_4_ = bf16[16,1664]{1,0:T(8,128)(2,1)S(1)} collective-permute-done((bf16[16,1664]{1,0:T(8,128)(2,1)S(1)}, bf16[16,1664]{1,0:T(8,128)(2,1)S(1)}, u32[]{:S(2)}, u32[]{:S(2)}) %collective-permute-start.9) | collective-permute-done | bytes 53280 | tf_op jit(solution)/shard_map/ppermute | solution.py:74
  31.5 1.6 %collective-permute-done.8.refs_3_ = bf16[16,1664]{1,0:T(8,128)(2,1)S(1)} collective-permute-done((bf16[16,1664]{1,0:T(8,128)(2,1)S(1)}, bf16[16,1664]{1,0:T(8,128)(2,1)S(1)}, u32[]{:S(2)}, u32[]{:S(2)}) %collective-permute-start.8) | collective-permute-done | bytes 53280 | tf_op jit(solution)/shard_map/ppermute | solution.py:74
  33.1 1.6 %collective-permute-start.10 = (bf16[16,1664]{1,0:T(8,128)(2,1)S(1)}, bf16[16,1664]{1,0:T(8,128)(2,1)S(1)}, u32[]{:S(2)}, u32[]{:S(2)}) collective-permute-start(bf16[16,1664]{1,0:T(8,128)(2,1)S(1)} %sum.1), channel_id=1, source_target_pairs={{0,2},{1,3},{2,0},{3,1},{4,6},{5,7},{6,4},{7,5},{8,10},{9,11},{10,... | collective-permute-start | bytes 159752 | tf_op jit(solution)/shard_map/ppermute | solution.py:74
  34.7 2.6 %collective-permute-done.10 = bf16[16,1664]{1,0:T(8,128)(2,1)S(1)} collective-permute-done((bf16[16,1664]{1,0:T(8,128)(2,1)S(1)}, bf16[16,1664]{1,0:T(8,128)(2,1)S(1)}, u32[]{:S(2)}, u32[]{:S(2)}) %collective-permute-start.10) | collective-permute-done | bytes 53280 | tf_op jit(solution)/shard_map/ppermute | solution.py:74
  37.4 2.3 %collective-permute-start.13 = (bf16[16,1664]{1,0:T(8,128)(2,1)S(1)}, bf16[16,1664]{1,0:T(8,128)(2,1)S(1)}, u32[]{:S(2)}, u32[]{:S(2)}) collective-permute-start(bf16[16,1664]{1,0:T(8,128)(2,1)S(1)} %fusion.1.refs_0_), channel_id=1, source_target_pairs={{0,12},{1,13},{2,14},{3,15},{4,8},{5,9},{6,10},{7,11},{8,4},{9,5},... | collective-permute-start | bytes 159752 | tf_op jit(solution)/shard_map/ppermute | solution.py:74
  39.7 2.1 %collective-permute-start.11 = (bf16[16,1664]{1,0:T(8,128)(2,1)S(1)}, bf16[16,1664]{1,0:T(8,128)(2,1)S(1)}, u32[]{:S(2)}, u32[]{:S(2)}) collective-permute-start(bf16[16,1664]{1,0:T(8,128)(2,1)S(1)} %fusion.1.refs_0_), channel_id=1, source_target_pairs={{0,4},{1,5},{2,6},{3,7},{4,0},{5,1},{6,2},{7,3},{8,12},{9,13},{10,... | collective-permute-start | bytes 159752 | tf_op jit(solution)/shard_map/ppermute | solution.py:74
  41.8 2.0 %collective-permute-done.13.refs_3_ = bf16[16,1664]{1,0:T(8,128)(2,1)S(1)} collective-permute-done((bf16[16,1664]{1,0:T(8,128)(2,1)S(1)}, bf16[16,1664]{1,0:T(8,128)(2,1)S(1)}, u32[]{:S(2)}, u32[]{:S(2)}) %collective-permute-start.13) | collective-permute-done | bytes 53280 | tf_op jit(solution)/shard_map/ppermute | solution.py:74
  43.9 1.1 %collective-permute-done.12.refs_2_ = bf16[16,1664]{1,0:T(8,128)(2,1)S(1)} collective-permute-done((bf16[16,1664]{1,0:T(8,128)(2,1)S(1)}, bf16[16,1664]{1,0:T(8,128)(2,1)S(1)}, u32[]{:S(2)}, u32[]{:S(2)}) %collective-permute-start.12) | collective-permute-done | bytes 53280 | tf_op jit(solution)/shard_map/ppermute | solution.py:74
  45.0 0.5 %collective-permute-start.15 = (bf16[16,1664]{1,0:T(8,128)(2,1)S(1)}, bf16[16,1664]{1,0:T(8,128)(2,1)S(1)}, u32[]{:S(2)}, u32[]{:S(2)}) collective-permute-start(bf16[16,1664]{1,0:T(8,128)(2,1)S(1)} %collective-permute-done.11.refs_1_), channel_id=1, source_target_pairs={{0,1},{1,0},{2,3},{3,2},{4,5},{5,4},{6,7},{7,6},{8,9},{9,8},{10,11... | collective-permute-start | bytes 159752 | tf_op jit(solution)/shard_map/ppermute | solution.py:74
  45.5 0.7 %collective-permute-done.16.refs_6_ = bf16[16,1664]{1,0:T(8,128)(2,1)S(1)} collective-permute-done((bf16[16,1664]{1,0:T(8,128)(2,1)S(1)}, bf16[16,1664]{1,0:T(8,128)(2,1)S(1)}, u32[]{:S(2)}, u32[]{:S(2)}) %collective-permute-start.16) | collective-permute-done | bytes 53280 | tf_op jit(solution)/shard_map/ppermute | solution.py:74
  46.4 3.4 %gradients.1 = (bf16[1536,512]{1,0:T(8,128)(2,1)}, bf16[512,1536]{1,0:T(8,128)(2,1)}, f32[1,512]{1,0:T(1,128)}, f32[1536]{0:T(1024)}, f32[1]{0:T(128)}, /*index=5*/bf16[8,1536]{1,0:T(8,128)(2,1)}) custom-call(bf16[16,1664]{1,0:T(8,128)(2,1)S(1)} %fusion.1.refs_0_, bf16[16,1664]{1,0:T(8,128)(2,1)S(1)} %collective-permute-done.11.refs_1_, ...), custom_call_target="tpu_custom_call" | custom-call | flops 603979776 | bytes 6291456 | tf_op jit(solution)/shard_map/gradients/pallas_call | solution.py:546
  (33 shorter events, 1.4 us)
Async XLA Ops:
  0.6 9.2 %copy-start = (bf16[512,1536]{1,0:T(8,128)(2,1)S(1)}, bf16[512,1536]{1,0:T(8,128)(2,1)}, u32[]{:S(2)}) copy-start(bf16[512,1536]{1,0:T(8,128)(2,1)} %refs_7_.1) | copy-start | bytes 4718596
  4.1 10.1 %copy-start.1 = (bf16[1536,512]{1,0:T(8,128)(2,1)S(1)}, bf16[1536,512]{1,0:T(8,128)(2,1)}, u32[]{:S(2)}) copy-start(bf16[1536,512]{1,0:T(8,128)(2,1)} %refs_5_.3) | copy-start | bytes 4718596
  4.1 17.4 %copy-start.3 = (f32[512]{0:T(512)S(1)}, f32[512]{0:T(512)}, u32[]{:S(2)}) copy-start(f32[512]{0:T(512)} %param.19) | copy-start | bytes 6148
  4.1 7.3 %collective-permute-start.2 = (bf16[16,1536]{1,0:T(8,128)(2,1)S(1)}, bf16[16,1536]{1,0:T(8,128)(2,1)S(1)}, u32[]{:S(2)}, u32[]{:S(2)}) collective-permute-start(bf16[16,1536]{1,0:T(8,128)(2,1)S(1)} %features.1.refs_2_), channel_id=1, source_target_pairs={{0,12},{1,13},{2,14},{3,15},{4,8},{5,9},{6,10},{7,11},{8,4},{9,5},... | collective-permute-start | bytes 147464 | tf_op jit(solution)/shard_map/ppermute | solution.py:74
  9.2 5.0 %collective-permute-start.1 = (bf16[16,1536]{1,0:T(8,128)(2,1)S(1)}, bf16[16,1536]{1,0:T(8,128)(2,1)S(1)}, u32[]{:S(2)}, u32[]{:S(2)}) collective-permute-start(bf16[16,1536]{1,0:T(8,128)(2,1)S(1)} %features.1.refs_2_), channel_id=1, source_target_pairs={{0,8},{1,9},{2,10},{3,11},{4,12},{5,13},{6,14},{7,15},{8,0},{9,1},... | collective-permute-start | bytes 147464 | tf_op jit(solution)/shard_map/ppermute | solution.py:74
  9.2 5.0 %collective-permute-start = (bf16[16,1536]{1,0:T(8,128)(2,1)S(1)}, bf16[16,1536]{1,0:T(8,128)(2,1)S(1)}, u32[]{:S(2)}, u32[]{:S(2)}) collective-permute-start(bf16[16,1536]{1,0:T(8,128)(2,1)S(1)} %features.1.refs_2_), channel_id=1, source_target_pairs={{0,4},{1,5},{2,6},{3,7},{4,0},{5,1},{6,2},{7,3},{8,12},{9,13},{10,... | collective-permute-start | bytes 147464 | tf_op jit(solution)/shard_map/ppermute | solution.py:74
  14.2 5.8 %collective-permute-start.3 = (bf16[64,1536]{1,0:T(8,128)(2,1)S(1)}, bf16[64,1536]{1,0:T(8,128)(2,1)S(1)}, u32[]{:S(2)}, u32[]{:S(2)}) collective-permute-start(bf16[64,1536]{1,0:T(8,128)(2,1)S(1)} %join.1.refs_1_), channel_id=1, source_target_pairs={{0,2},{1,3},{2,0},{3,1},{4,6},{5,7},{6,4},{7,5},{8,10},{9,11},{10,... | collective-permute-start | bytes 589832 | tf_op jit(solution)/shard_map/ppermute | solution.py:74
  15.8 4.2 %collective-permute-start.4 = (bf16[64,1536]{1,0:T(8,128)(2,1)S(1)}, bf16[64,1536]{1,0:T(8,128)(2,1)S(1)}, u32[]{:S(2)}, u32[]{:S(2)}) collective-permute-start(bf16[64,1536]{1,0:T(8,128)(2,1)S(1)} %join.1.refs_1_), channel_id=1, source_target_pairs={{0,1},{1,0},{2,3},{3,2},{4,5},{5,4},{6,7},{7,6},{8,9},{9,8},{10,11... | collective-permute-start | bytes 589832 | tf_op jit(solution)/shard_map/ppermute | solution.py:74
  20.0 1.4 %collective-permute-start.5 = (bf16[64,1536]{1,0:T(8,128)(2,1)S(1)}, bf16[64,1536]{1,0:T(8,128)(2,1)S(1)}, u32[]{:S(2)}, u32[]{:S(2)}) collective-permute-start(bf16[64,1536]{1,0:T(8,128)(2,1)S(1)} %collective-permute-done.3.refs_2_), channel_id=1, source_target_pairs={{0,1},{1,0},{2,3},{3,2},{4,5},{5,4},{6,7},{7,6},{8,9},{9,8},{10,11... | collective-permute-start | bytes 589832 | tf_op jit(solution)/shard_map/ppermute | solution.py:74
  21.5 2.0 %copy-start.2 = (f32[1536]{0:T(1024)S(1)}, f32[1536]{0:T(1024)}, u32[]{:S(2)}) copy-start(f32[1536]{0:T(1024)} %dec_bias.1) | copy-start | bytes 18436
  23.3 1.5 %collective-permute-start.6 = (bf16[64,1664]{1,0:T(8,128)(2,1)S(1)}, bf16[64,1664]{1,0:T(8,128)(2,1)S(1)}, u32[]{:S(2)}, u32[]{:S(2)}) collective-permute-start(bf16[64,1664]{1,0:T(8,128)(2,1)S(1)} %get-tuple-element.30), channel_id=1, source_target_pairs={{0,1},{1,0},{2,3},{3,2},{4,5},{5,4},{6,7},{7,6},{8,9},{9,8},{10,11... | collective-permute-start | bytes 638984 | tf_op jit(solution)/shard_map/ppermute | solution.py:74
  24.9 6.6 %collective-permute-start.9 = (bf16[16,1664]{1,0:T(8,128)(2,1)S(1)}, bf16[16,1664]{1,0:T(8,128)(2,1)S(1)}, u32[]{:S(2)}, u32[]{:S(2)}) collective-permute-start(bf16[16,1664]{1,0:T(8,128)(2,1)S(1)} %get-tuple-element.42), channel_id=1, source_target_pairs={{0,12},{1,13},{2,14},{3,15},{4,8},{5,9},{6,10},{7,11},{8,4},{9,5},... | collective-permute-start | bytes 159752 | tf_op jit(solution)/shard_map/ppermute | solution.py:74
  27.0 6.1 %collective-permute-start.8 = (bf16[16,1664]{1,0:T(8,128)(2,1)S(1)}, bf16[16,1664]{1,0:T(8,128)(2,1)S(1)}, u32[]{:S(2)}, u32[]{:S(2)}) collective-permute-start(bf16[16,1664]{1,0:T(8,128)(2,1)S(1)} %get-tuple-element.43), channel_id=1, source_target_pairs={{0,8},{1,9},{2,10},{3,11},{4,12},{5,13},{6,14},{7,15},{8,0},{9,1},... | collective-permute-start | bytes 159752 | tf_op jit(solution)/shard_map/ppermute | solution.py:74
  27.1 6.0 %collective-permute-start.7 = (bf16[16,1664]{1,0:T(8,128)(2,1)S(1)}, bf16[16,1664]{1,0:T(8,128)(2,1)S(1)}, u32[]{:S(2)}, u32[]{:S(2)}) collective-permute-start(bf16[16,1664]{1,0:T(8,128)(2,1)S(1)} %get-tuple-element.44), channel_id=1, source_target_pairs={{0,4},{1,5},{2,6},{3,7},{4,0},{5,1},{6,2},{7,3},{8,12},{9,13},{10,... | collective-permute-start | bytes 159752 | tf_op jit(solution)/shard_map/ppermute | solution.py:74
  33.1 4.2 %collective-permute-start.10 = (bf16[16,1664]{1,0:T(8,128)(2,1)S(1)}, bf16[16,1664]{1,0:T(8,128)(2,1)S(1)}, u32[]{:S(2)}, u32[]{:S(2)}) collective-permute-start(bf16[16,1664]{1,0:T(8,128)(2,1)S(1)} %sum.1), channel_id=1, source_target_pairs={{0,2},{1,3},{2,0},{3,1},{4,6},{5,7},{6,4},{7,5},{8,10},{9,11},{10,... | collective-permute-start | bytes 159752 | tf_op jit(solution)/shard_map/ppermute | solution.py:74
  37.4 6.5 %collective-permute-start.13 = (bf16[16,1664]{1,0:T(8,128)(2,1)S(1)}, bf16[16,1664]{1,0:T(8,128)(2,1)S(1)}, u32[]{:S(2)}, u32[]{:S(2)}) collective-permute-start(bf16[16,1664]{1,0:T(8,128)(2,1)S(1)} %fusion.1.refs_0_), channel_id=1, source_target_pairs={{0,12},{1,13},{2,14},{3,15},{4,8},{5,9},{6,10},{7,11},{8,4},{9,5},... | collective-permute-start | bytes 159752 | tf_op jit(solution)/shard_map/ppermute | solution.py:74
  39.7 5.3 %collective-permute-start.12 = (bf16[16,1664]{1,0:T(8,128)(2,1)S(1)}, bf16[16,1664]{1,0:T(8,128)(2,1)S(1)}, u32[]{:S(2)}, u32[]{:S(2)}) collective-permute-start(bf16[16,1664]{1,0:T(8,128)(2,1)S(1)} %fusion.1.refs_0_), channel_id=1, source_target_pairs={{0,8},{1,9},{2,10},{3,11},{4,12},{5,13},{6,14},{7,15},{8,0},{9,1},... | collective-permute-start | bytes 159752 | tf_op jit(solution)/shard_map/ppermute | solution.py:74
  39.7 5.3 %collective-permute-start.11 = (bf16[16,1664]{1,0:T(8,128)(2,1)S(1)}, bf16[16,1664]{1,0:T(8,128)(2,1)S(1)}, u32[]{:S(2)}, u32[]{:S(2)}) collective-permute-start(bf16[16,1664]{1,0:T(8,128)(2,1)S(1)} %fusion.1.refs_0_), channel_id=1, source_target_pairs={{0,4},{1,5},{2,6},{3,7},{4,0},{5,1},{6,2},{7,3},{8,12},{9,13},{10,... | collective-permute-start | bytes 159752 | tf_op jit(solution)/shard_map/ppermute | solution.py:74
  41.8 3.7 %collective-permute-start.14 = (bf16[16,1664]{1,0:T(8,128)(2,1)S(1)}, bf16[16,1664]{1,0:T(8,128)(2,1)S(1)}, u32[]{:S(2)}, u32[]{:S(2)}) collective-permute-start(bf16[16,1664]{1,0:T(8,128)(2,1)S(1)} %fusion.1.refs_0_), channel_id=1, source_target_pairs={{0,1},{1,0},{2,3},{3,2},{4,5},{5,4},{6,7},{7,6},{8,9},{9,8},{10,11... | collective-permute-start | bytes 159752 | tf_op jit(solution)/shard_map/ppermute | solution.py:74
  43.9 1.7 %collective-permute-start.17 = (bf16[16,1664]{1,0:T(8,128)(2,1)S(1)}, bf16[16,1664]{1,0:T(8,128)(2,1)S(1)}, u32[]{:S(2)}, u32[]{:S(2)}) collective-permute-start(bf16[16,1664]{1,0:T(8,128)(2,1)S(1)} %collective-permute-done.13.refs_3_), channel_id=1, source_target_pairs={{0,1},{1,0},{2,3},{3,2},{4,5},{5,4},{6,7},{7,6},{8,9},{9,8},{10,11... | collective-permute-start | bytes 159752 | tf_op jit(solution)/shard_map/ppermute | solution.py:74
  45.0 1.2 %collective-permute-start.16 = (bf16[16,1664]{1,0:T(8,128)(2,1)S(1)}, bf16[16,1664]{1,0:T(8,128)(2,1)S(1)}, u32[]{:S(2)}, u32[]{:S(2)}) collective-permute-start(bf16[16,1664]{1,0:T(8,128)(2,1)S(1)} %collective-permute-done.12.refs_2_), channel_id=1, source_target_pairs={{0,1},{1,0},{2,3},{3,2},{4,5},{5,4},{6,7},{7,6},{8,9},{9,8},{10,11... | collective-permute-start | bytes 159752 | tf_op jit(solution)/shard_map/ppermute | solution.py:74
  45.0 1.4 %collective-permute-start.15 = (bf16[16,1664]{1,0:T(8,128)(2,1)S(1)}, bf16[16,1664]{1,0:T(8,128)(2,1)S(1)}, u32[]{:S(2)}, u32[]{:S(2)}) collective-permute-start(bf16[16,1664]{1,0:T(8,128)(2,1)S(1)} %collective-permute-done.11.refs_1_), channel_id=1, source_target_pairs={{0,1},{1,0},{2,3},{3,2},{4,5},{5,4},{6,7},{7,6},{8,9},{9,8},{10,11... | collective-permute-start | bytes 159752 | tf_op jit(solution)/shard_map/ppermute | solution.py:74
